TPU v7x, 128 devices: a whole 4x4x4 slice. The times are simulated.
128 devices in a mesh: group: 2 (over y_lo), seq: 8 (over y_hi, z), mp: 8 (over x, core).
Axes of the slice: x: 4, y: 4 (y_hi: 2, y_lo: 2; y = y_hi * 2 + y_lo), z: 4, core: 2. Of those that a mesh axis runs over, the one named last changes fastest.
Arguments:
- embeds: bfloat16 [16384, 8192], P('seq', 'mp'), may hold values from -250 to 250
- image_feats: bfloat16 [1024, 7296], P('seq'), may hold values from -6 to 6
- image_pos: int32 [1024], P('seq'), may hold values from 0 to 16383, as said below
- proj_w: bfloat16 [7296, 8192], P('seq', 'mp'), may hold values from -0.0625 to 0.0625
- proj_b: bfloat16 [8192], P('mp'), may hold values from -3 to 3
- norm_gain: bfloat16 [8192], P('mp'), may hold values from 0.099609375 to 1.8984375
- kv_w: bfloat16 [8192, 2048], P('mp'), may hold values from -0.0625 to 0.0625
- prompt_lengths: int32 [4], replicated, may hold values from 2048 to 4096
- page_owner: int32 [1024, 1], P('seq'), may hold values from 0 to 7; in each aligned block of 128 rows (0 to 127, 128 to 255, ...) at most 32 rows name the same one
- queries: bfloat16 [1024, 8192], P('seq', 'mp'), may hold values from -180 to 180
- kv_cache: bfloat16 [1024, 128, 2048], P('seq', None, 'mp'), may hold values from -5 to 5
- new_kv: bfloat16 [1024, 2048], P('seq', 'mp'), may hold values from -5 to 5
- cache_lengths: int32 [1024], P('seq'), may hold values from 2 to 128
Outputs:
- page_slots: bfloat16 [4096, 16, 2048], P(('group', 'seq'), None, 'mp')
- row_states: bfloat16 [2048, 8192], P(('group', 'seq'), 'mp')
Inputs may be any that keep to these rules, and one draw needn't show every extreme that they name: `image_pos`: distinct and increasing; entries s * 128 to (s + 1) * 128 - 1 lie among tokens s * 2048 to (s + 1) * 2048 - 1. `page_owner`: among the 128 pages of one seq index no owner is named more than 32 times.
All inputs are finite; a program needn't handle non-finite values.
Results may differ from a plain program's by a relative error of at most 0.005.
Values may be sent and summed in bfloat16 or wider, within the bound.
No kernel may reach another device: no remote copies, remote signals or barrier semaphores. Data moves between devices by JAX's collectives and lax.ppermute only.
A program may use at most 128 MiB of HBM per device.

v0:
```python
import jax
import jax.numpy as jnp
from jax import lax
from jax.sharding import PartitionSpec as P

D = 8192
HEAD = 128
PAGE = 16
PROMPT_LEN = 4096


def gated(condition, action, empty_value, *operands):
    return lax.cond(condition, action, lambda *unused: empty_value, *operands)


def attend(queries, kv_cache, new_kv, cache_lengths):
    row_count = queries.shape[0]
    heads_kv = kv_cache.shape[2] // (2 * HEAD)
    grouped = queries.reshape(row_count, heads_kv, queries.shape[1] // (HEAD * heads_kv), HEAD)
    stored = kv_cache.reshape(row_count, kv_cache.shape[1], heads_kv, 2 * HEAD)
    fresh_kv = new_kv.reshape(row_count, heads_kv, 2 * HEAD)
    scores = jnp.einsum(
        "rgqh,rjgh->rgqj", grouped, stored[..., :HEAD], preferred_element_type=jnp.float32
    ) * HEAD ** (-0.5)
    in_cache = jnp.arange(stored.shape[1], dtype=jnp.int32)[None, :] < cache_lengths[:, None]
    scores = jnp.where(in_cache[:, None, None, :], scores, -1e30)
    own_score = jnp.einsum(
        "rgqh,rgh->rgq", grouped, fresh_kv[..., :HEAD], preferred_element_type=jnp.float32
    ) * HEAD ** (-0.5)
    row_max = jnp.maximum(jnp.max(scores, axis=3), own_score)
    weights = jnp.exp(scores - row_max[..., None])
    own_weight = jnp.exp(own_score - row_max)
    denominator = jnp.sum(weights, axis=3) + own_weight
    probability = (weights / denominator[..., None]).astype(jnp.bfloat16)
    own_prob = lax.optimization_barrier((own_weight / denominator).astype(jnp.bfloat16)).astype(
        jnp.float32
    )
    attended = jnp.einsum(
        "rgqj,rjgh->rgqh", probability, stored[..., HEAD:], preferred_element_type=jnp.float32
    )
    attended = attended + own_prob[..., None] * fresh_kv[:, :, None, HEAD:].astype(jnp.float32)
    return attended.astype(jnp.bfloat16).reshape(row_count, queries.shape[1])


def per_device(
    embeds,
    image_feats,
    image_pos,
    proj_w,
    proj_b,
    norm_gain,
    kv_w,
    prompt_lengths,
    page_owner,
    queries,
    kv_cache,
    new_kv,
    cache_lengths,
):
    group_index = lax.axis_index("group")
    prefill = group_index == 0
    seq_index = lax.axis_index("seq")
    seq_count = lax.axis_size("seq")
    token_rows = embeds.shape[0]
    image_rows = image_feats.shape[0]
    width_local = proj_w.shape[1]
    carry_sum = jnp.zeros((image_rows, width_local), jnp.float32)
    weight_piece = lax.all_gather(proj_w, "seq", axis=0, tiled=True)

    def product(carry_sum, weight_piece):
        return jnp.dot(image_feats, weight_piece, preferred_element_type=jnp.float32)

    summed = lax.cond(
        prefill, product, lambda carry_sum, weight_piece: carry_sum, carry_sum, weight_piece
    )
    image_hidden = jax.nn.gelu(summed + proj_b.astype(jnp.float32), approximate=False).astype(
        jnp.bfloat16
    )
    local_pos = image_pos - seq_index * token_rows
    hidden_all = embeds.at[local_pos].set(image_hidden)
    hidden_f32 = hidden_all.astype(jnp.float32)
    squares = lax.psum(jnp.sum(hidden_f32 * hidden_f32, axis=1), "mp")
    scaled = (hidden_f32 * norm_gain.astype(jnp.float32)).astype(jnp.bfloat16)
    partial_kv = gated(
        prefill,
        lambda values: jnp.dot(values, kv_w, preferred_element_type=jnp.float32),
        jnp.zeros((token_rows, kv_w.shape[1]), jnp.float32),
        scaled,
    )
    head_kv = lax.psum_scatter(partial_kv, "mp", scatter_dimension=1, tiled=True)
    row_scale = lax.rsqrt(squares / D + 1e-05)
    positions = seq_index * token_rows + jnp.arange(token_rows, dtype=jnp.int32)
    prompt_ids = positions // PROMPT_LEN
    prompt_match = (
        prompt_ids[:, None] == jnp.arange(prompt_lengths.shape[0], dtype=jnp.int32)[None, :]
    )
    prompt_limit = jnp.sum(jnp.where(prompt_match, prompt_lengths[None, :], 0), axis=1)
    is_live = positions % PROMPT_LEN < prompt_limit
    kv_rows = jnp.where(is_live[:, None], head_kv * row_scale[:, None], 0.0).astype(jnp.bfloat16)
    page_width = kv_rows.shape[1]
    pages_dev = token_rows // PAGE
    share_pages = token_rows // PAGE
    capacity = 2 * pages_dev // seq_count
    kv_pages = kv_rows.reshape(share_pages, PAGE * page_width)
    owners = page_owner[:, 0]
    one_hot = (owners[:, None] == jnp.arange(seq_count, dtype=jnp.int32)[None, :]).astype(jnp.int32)
    page_rank = jnp.sum((jnp.cumsum(one_hot, axis=0) - one_hot) * one_hot, axis=1)
    slot_index = owners * capacity + page_rank
    selector = (
        jnp.arange(seq_count * capacity, dtype=jnp.int32)[:, None] == slot_index[None, :]
    ).astype(jnp.bfloat16)
    by_owner = jnp.dot(selector, kv_pages, preferred_element_type=jnp.float32).astype(jnp.bfloat16)
    by_owner = by_owner.reshape(seq_count * capacity, PAGE, page_width)
    block_slots = seq_count * capacity
    padded = jnp.concatenate([jnp.zeros_like(by_owner), by_owner], axis=0)
    arrived = lax.all_to_all(padded, ("group", "seq"), split_axis=0, concat_axis=0, tiled=True)
    received = arrived[:block_slots]
    page_slots = jnp.where(prefill, by_owner, received)
    empty_rows = jnp.zeros(queries.shape, jnp.bfloat16)
    attended = gated(
        jnp.logical_not(prefill), attend, empty_rows, queries, kv_cache, new_kv, cache_lengths
    )
    row_states = jnp.where(prefill, image_hidden, attended)
    return (page_slots, row_states)


def solution(mesh):
    in_specs = (
        P("seq", "mp"),
        P("seq", None),
        P("seq"),
        P("seq", "mp"),
        P("mp"),
        P("mp"),
        P("mp", None),
        P(),
        P("seq", None),
        P("seq", "mp"),
        P("seq", None, "mp"),
        P("seq", "mp"),
        P("seq"),
    )
    out_specs = (P(("group", "seq"), None, "mp"), P(("group", "seq"), "mp"))
    return jax.shard_map(
        per_device, mesh=mesh, in_specs=in_specs, out_specs=out_specs, check_vma=False
    )
```

profile of v0, /device:TPU:10, one launch (start us, length us, event | category | flops | bytes accessed | tf_op | source)
XLA Modules:
  0.0 383.6 jit_solution(4705935326329326566)
XLA Ops:
  7.2 0.0 all-gather.2.cloned.1.call-start
  7.3 4.7 %copy.38 = bf16[2048,1024]{1,0:T(8,128)(2,1)} copy(bf16[2048,1024]{1,0:T(8,128)(2,1)} %param.19) | data formatting | bytes 8388608
  12.0 0.0 reduce-scatter.2.cloned.1.call-start
  12.1 167.8 %all-gather.2.cloned.1.call-done = bf16[7296,1024]{1,0:T(8,128)(2,1)} async-done(((bf16[912,1024]{1,0:T(8,128)(2,1)}), bf16[7296,1024]{1,0:T(8,128)(2,1)}) %all-gather.2.cloned.1.call-update) | async-done | bytes 14942224 | tf_op jit(solution)/shard_map/all_gather | solution.py:68
  179.9 0.1 conditional.3
  180.0 7.1 %scatter_custom_fusion = bf16[2048,1024]{1,0:T(8,128)(2,1)} fusion(bf16[2048,1024]{1,0:T(8,128)(2,1)} %copy.38, s32[128]{0:T(128)S(1)} %compare_select_fusion, f32[128,1024]{1,0:T(8,128)S(1)} %get-tuple-element.55, f32[1024]{0:T(1024)S(1)} %convert_element_type.60), kind=kCustom, calls=%fused_computation.77 | custom fusion | flops 8650752 | bytes 4722688 | tf_op jit(solution)/shard_map/scatter | solution.py:80
  187.1 5.3 %fusion.15 = (f32[2048]{0:T(1024)S(1)}, bf16[2048,1024]{1,0:T(8,128)(2,1)}) fusion(bf16[2048,1024]{1,0:T(8,128)(2,1)} %scatter_custom_fusion, f32[1024]{0:T(1024)S(1)} %convert_element_type.63), kind=kLoop, calls=%fused_computation.30 | loop fusion | flops 10483712 | bytes 8400896 | tf_op jit(solution)/shard_map/reduce_sum | solution.py:82
  192.4 7.9 %conditional.4 = (f32[2048,2048]{1,0:T(8,128)}) conditional(s32[]{:T(128)} %convert_element_type.59, () %tuple.26, (bf16[2048,1024]{1,0:T(8,128)(2,1)}, bf16[1024,2048]{1,0:T(8,128)(2,1)}) %tuple.29), branch_computations={%region_6.0_spmd, %region_7.0_spmd} | conditional | flops 8589934592 | bytes 25165832 | solution.py:13
  192.4 7.9 %broadcast_in_dim.30 = f32[2048,2048]{1,0:T(8,128)} broadcast(f32[]{:T(128)} %constant.45.clone), dimensions={} | broadcast | bytes 16777220 | tf_op jit(solution)/shard_map/broadcast_in_dim | solution.py:87
  200.3 0.6 copy-done.3
  200.9 0.1 fusion.27
  201.0 0.2 reduce_window_sum.11
  201.2 0.1 select_reduce_fusion.1
  201.3 0.2 select_reduce_fusion
  201.5 11.4 %psum.7 = f32[2048]{0:T(1024)S(1)} all-reduce(f32[2048]{0:T(1024)S(1)} %get-tuple-element.53), channel_id=1, replica_groups=mesh['group'=2,'seq'=8,'mp'=8] {'mp'}, use_global_device_ids=true, to_apply=%region_10.11 | all-reduce | flops 2048 | bytes 16384 | tf_op jit(solution)/shard_map/psum | solution.py:82
  213.0 89.6 %reduce-scatter.2.cloned.1.call-done = f32[2048,256]{1,0:T(8,128)} async-done(((f32[2048,2048]{1,0:T(8,128)}), f32[2048,256]{1,0:T(8,128)}) %reduce-scatter.2.cloned.1.call-update) | async-done | bytes 2097168 | tf_op jit(solution)/shard_map/reduce_scatter | solution.py:90
  302.6 1.9 select_convert_fusion
  304.6 0.5 reshape.152
  305.1 0.7 convolution_convert_fusion
  305.8 0.6 copy.25
  306.5 2.2 concatenate.3
  308.7 7.6 %all-to-all-start = ((bf16[512,16,256]{2,1,0:T(8,128)(2,1)}), bf16[512,16,256]{2,1,0:T(8,128)(2,1)}, u32[]{:S(2)}, u32[]{:S(2)}) async-start(bf16[512,16,256]{2,1,0:T(8,128)(2,1)} %concatenate.3), calls=%async_computation.1 | async-start | bytes 8388608 | tf_op jit(solution)/shard_map/all_to_all | solution.py:116
  316.4 9.0 %conditional.5 = (bf16[128,1024]{1,0:T(8,128)(2,1)S(1)}) conditional(s32[]{:T(128)} %convert_element_type.67, () %tuple.30, (s32[128]{0:T(128)S(1)}, bf16[128,1024]{1,0:T(8,128)(2,1)S(1)}, bf16[128,128,256]{2,1,0:T(8,128)(2,1)}, bf16[128,256]{1,0:T(8,128)(2,1)S(1)}) %tuple.50), branch_computations={%region_11.12_spmd, %region_12.15_spmd} | conditional | flops 68852736 | bytes 12157448 | solution.py:13
  316.4 0.1 iota_compare_fusion
  316.5 0.3 fusion.9
  316.8 4.5 %fusion.36 = (f32[128,8]{1,0:T(8,128)S(1)}, f32[128,8,128]{2,1,0:T(8,128)S(1)}) fusion(bf16[128,8,128]{2,1,0:T(8,128)(2,1)S(1)} %bitcast.57, bf16[128,128,1,256]{3,1,0,2:T(8,128)(2,1)} %bitcast.54, pred[128,128]{1,0:T(8,128)(4,1)S(1)} %iota_compare_fusion), kind=kOutput, calls=%fused_computation.78 | convolution fusion | flops 33946624 | bytes 5001216 | tf_op jit(solution)/shard_map/cond/branch_1_fun/rgqh,rjgh->rgqj/dot_general | solution.py:22
  321.4 0.4 fusion.6
  321.8 3.5 fusion.5
  325.3 0.1 copy.29
  325.4 1.9 broadcast_select_fusion
  327.2 46.4 %all-to-all-done = bf16[512,16,256]{2,1,0:T(8,128)(2,1)} async-done(((bf16[512,16,256]{2,1,0:T(8,128)(2,1)}), bf16[512,16,256]{2,1,0:T(8,128)(2,1)}, u32[]{:S(2)}, u32[]{:S(2)}) %all-to-all-start) | async-done | bytes 4194336 | tf_op jit(solution)/shard_map/all_to_all | solution.py:116
  373.6 3.1 slice_select_fusion
  (32 shorter events, 0.3 us)
Async XLA Ops:
  7.2 4.9 %copy-start.8 = (s32[128]{0:T(128)S(1)}, s32[128]{0:T(128)}, u32[]{:S(2)}) copy-start(s32[128]{0:T(128)} %param.21) | copy-start | bytes 1540
  7.2 172.7 %copy-start = (bf16[128,7296]{1,0:T(8,128)(2,1)S(1)}, bf16[128,7296]{1,0:T(8,128)(2,1)}, u32[]{:S(2)}) copy-start(bf16[128,7296]{1,0:T(8,128)(2,1)} %param.20) | copy-start | bytes 5603332
  7.2 4.8 %copy-start.4 = (bf16[1024]{0:T(1024)(128)(2,1)S(1)}, bf16[1024]{0:T(1024)(128)(2,1)}, u32[]{:S(2)}) copy-start(bf16[1024]{0:T(1024)(128)(2,1)} %param.23) | copy-start | bytes 6148
  7.2 4.8 %copy-start.5 = (bf16[1024]{0:T(1024)(128)(2,1)S(1)}, bf16[1024]{0:T(1024)(128)(2,1)}, u32[]{:S(2)}) copy-start(bf16[1024]{0:T(1024)(128)(2,1)} %param.24) | copy-start | bytes 6148
  7.2 172.7 %all-gather.2.cloned.1.call-start = ((), (), s32[]{:S(2)}) async-start(), calls=%async_computation.2 | async-start | bytes 16809984 | tf_op jit(solution)/shard_map/all_gather | solution.py:68
  12.0 290.7 %reduce-scatter.2.cloned.1.call-start = ((), (), s32[]{:S(2)}) async-start(), calls=%async_computation.3 | async-start | bytes 18874368 | tf_op jit(solution)/shard_map/reduce_scatter | solution.py:90
  200.3 0.7 copy-start.3
  200.3 0.9 copy-start.6
  308.7 7.6 %copy-start.1 = (bf16[128,1024]{1,0:T(8,128)(2,1)S(1)}, bf16[128,1024]{1,0:T(8,128)(2,1)}, u32[]{:S(2)}) copy-start(bf16[128,1024]{1,0:T(8,128)(2,1)} %param.28) | copy-start | bytes 786436
  308.7 7.6 %copy-start.2 = (bf16[128,256]{1,0:T(8,128)(2,1)S(1)}, bf16[128,256]{1,0:T(8,128)(2,1)}, u32[]{:S(2)}) copy-start(bf16[128,256]{1,0:T(8,128)(2,1)} %param.30) | copy-start | bytes 196612
  308.7 7.7 %copy-start.7 = (s32[128]{0:T(128)S(1)}, s32[128]{0:T(128)}, u32[]{:S(2)}) copy-start(s32[128]{0:T(128)} %param.31) | copy-start | bytes 1540
  308.7 64.9 %all-to-all-start = ((bf16[512,16,256]{2,1,0:T(8,128)(2,1)}), bf16[512,16,256]{2,1,0:T(8,128)(2,1)}, u32[]{:S(2)}, u32[]{:S(2)}) async-start(bf16[512,16,256]{2,1,0:T(8,128)(2,1)} %concatenate.3), calls=%async_computation.1 | async-start | bytes 8388608 | tf_op jit(solution)/shard_map/all_to_all | solution.py:116
Sparse Core Ops, SparseCore 0:
  12.1 167.7 all-gather.1
  200.4 102.1 reduce-scatter.1
where the time goes:
time: 388 us; the launch traced here: 384 us
  waiting for transfers between devices  304 us (78%)
  other arithmetic  20.5 us (5%)
  local copies, waits for them, and re-layouts  16.7 us (4%)
  between operations  14.3 us (4%)
  blocking collectives  11.4 us (3%)
  matrix products  8.97 us (2%)
  starting transfers between devices  7.72 us (2%)
    all_gather x1, waiting for transfers between devices, per_device(): weight_piece = lax.all_gather(proj_w, 'seq', axis=0, tiled=True)  168 us
    reduce_scatter x1, waiting for transfers between devices, per_device(): lax.psum_scatter(partial_kv, 'mp', scatter_dimension=1, tiled=True)  89.6 us
    all_to_all x1, waiting for transfers between devices, per_device(): lax.all_to_all(padded, ('group', 'seq'), split_axis=0, concat_axis=0, til...  46.4 us
    psum x1, blocking collectives, per_device(): squares = lax.psum(jnp.sum(hidden_f32 * hidden_f32, axis=1), 'mp')  11.4 us
    broadcast_in_dim x1, local copies, waits for them, and re-layouts, per_device(): jnp.zeros((token_rows, kv_w.shape[1]), jnp.float32)  7.85 us
  transfers between devices with their start and end apart: 3, of which 3 were waited for; matrix products, arithmetic and copies ran while one was open for 3% of the time, Pallas kernels for 0%

commit v1 on v0

v1 whole, which is shorter than its diff:
```python
import functools

import jax
import jax.numpy as jnp
from jax import lax
from jax.experimental import pallas as pl
from jax.experimental.pallas import tpu as pltpu
from jax.sharding import PartitionSpec as P

D = 8192
HEAD = 128
PAGE = 16
PROMPT_LEN = 4096
CAP = 32
ROWS = 2048
EXT = 32
TALL = ROWS + EXT
PAGES = ROWS // PAGE
IMG = 64
IMG_TALL = IMG + 16
BF = jnp.bfloat16
F32 = jnp.float32
VMEM_LIMIT = 56 * 1024 * 1024


def split_pair(value):
    high = value.astype(BF)
    low = (value - high.astype(F32)).astype(BF)
    return high, low


def project_kernel(place, embeds_ref, gain_ref, *refs):
    weights, (send_ref, keep_ref, squares_ref) = refs[:8], refs[8:]
    step = pl.program_id(0)

    @pl.when(step < 8)
    def _():
        hidden = embeds_ref[...].astype(F32)
        scaled = (hidden * gain_ref[...].astype(F32)).astype(BF)
        squared = hidden * hidden
        lanes = squared[:, 0:128]
        for k in range(1, 8):
            lanes = lanes + squared[:, k * 128 : (k + 1) * 128]
        summed = jnp.sum(lanes.T, axis=0, keepdims=True)
        squares_ref[pl.ds(2 * step, 1), :] = summed[:, :128]
        squares_ref[pl.ds(2 * step + 1, 1), :] = summed[:, 128:]
        for pair in range(4):
            weight = jnp.concatenate([weights[2 * pair][...], weights[2 * pair + 1][...]], axis=1)
            product = jnp.dot(scaled, weight, preferred_element_type=F32).astype(BF)
            target = send_ref if pair < 2 else keep_ref
            target[2 * (pair % 2)] = product[:, :128]
            target[2 * (pair % 2) + 1] = product[:, 128:]

    @pl.when(step == 8)
    def _():
        high, low = split_pair(squares_ref[...])
        both = jnp.concatenate([high, low], axis=0)
        for j in range(4):
            send_ref[j, 0:EXT, :] = both
            keep_ref[j, 0:EXT, :] = both


def project_text(place, embeds, gain, kv_w):
    def column(r, j):
        def index(i, place):
            core = place[1] if r else 1 - place[1]
            head = 2 * lax.rem(place[2] + j, 4) + core
            return (0, 2 * head + place[0])

        return index

    specs = [
        pl.BlockSpec((256, 1024), lambda i, place: (jnp.minimum(i, 7), 0)),
        pl.BlockSpec((1, 1024), lambda i, place: (0, 0)),
    ] + [pl.BlockSpec((1024, 128), column(r, j)) for r in range(2) for j in range(4)]
    out = jax.ShapeDtypeStruct((4, TALL, 128), BF)
    return pl.pallas_call(
        project_kernel,
        grid_spec=pltpu.PrefetchScalarGridSpec(
            num_scalar_prefetch=1,
            grid=(9,),
            in_specs=specs,
            out_specs=[pl.BlockSpec((4, 256, 128), lambda i, place: (0, i, 0))] * 2,
            scratch_shapes=[pltpu.VMEM((16, 128), F32)],
        ),
        out_shape=[out, out],
        compiler_params=pltpu.CompilerParams(vmem_limit_bytes=VMEM_LIMIT),
        cost_estimate=pl.CostEstimate(
            flops=2 * ROWS * 1024 * 1024, bytes_accessed=12 << 20, transcendentals=0
        ),
        name="project_text",
    )(place, embeds, gain, *([kv_w] * 8))


def add_kernel(a_ref, b_ref, out_ref):
    out_ref[0:ROWS, :] = (a_ref[0, 0:ROWS, :].astype(F32) + b_ref[0, 0:ROWS, :].astype(F32)).astype(BF)
    total = jnp.zeros((16, 128), F32)
    for ref in (a_ref, b_ref):
        total = total + ref[0, ROWS : ROWS + 16, :].astype(F32) + ref[0, ROWS + 16 : TALL, :].astype(F32)
    high, low = split_pair(total)
    out_ref[ROWS : ROWS + 16, :] = high
    out_ref[ROWS + 16 : TALL, :] = low


def add_pair(keep, received, j):
    spec = pl.BlockSpec((1, TALL, 128), lambda i: (j, 0, 0))
    return pl.pallas_call(
        add_kernel,
        grid=(1,),
        in_specs=[spec, spec],
        out_specs=pl.BlockSpec((TALL, 128), lambda i: (0, 0)),
        out_shape=jax.ShapeDtypeStruct((TALL, 128), BF),
        compiler_params=pltpu.CompilerParams(vmem_limit_bytes=VMEM_LIMIT),
        cost_estimate=pl.CostEstimate(flops=TALL * 128, bytes_accessed=3 << 19, transcendentals=0),
        name="add_pair",
    )(keep, received)


def finish_kernel(slots, limit, a_ref, b_ref, c_ref, d_ref, rows_ref, slot_ref):
    refs = (a_ref, b_ref, c_ref, d_ref)
    slot_ref[...] = jnp.zeros_like(slot_ref)
    squares = jnp.zeros((16, 128), F32)
    for ref in refs:
        squares = squares + ref[ROWS : ROWS + 16, :].astype(F32) + ref[ROWS + 16 : TALL, :].astype(F32)
    scale = lax.rsqrt(squares / D + 1e-05)
    row_iota = lax.broadcasted_iota(jnp.int32, (128, 128), 0)
    for part in range(16):
        tile = jnp.broadcast_to(scale[part : part + 1, :], (128, 128)).T
        here = pl.ds(part * 128, 128)
        total = refs[0][here, :].astype(F32)
        for ref in refs[1:]:
            total = total + ref[here, :].astype(F32)
        live = row_iota + part * 128 < limit[0]
        rows = jnp.where(live, total * tile, 0.0).astype(BF)
        for p in range(8):
            page = rows[p * PAGE : (p + 1) * PAGE, :]
            rows_ref[part * 8 + p] = page
            slot_ref[0, slots[part * 8 + p]] = page


def finish_text(slots, limit, parts):
    spec = pl.BlockSpec((TALL, 128), lambda i, slots, limit: (0, 0))
    return pl.pallas_call(
        finish_kernel,
        grid_spec=pltpu.PrefetchScalarGridSpec(
            num_scalar_prefetch=2,
            grid=(1,),
            in_specs=[spec] * 4,
            out_specs=[
                pl.BlockSpec((PAGES, PAGE, 128), lambda i, slots, limit: (0, 0, 0)),
                pl.BlockSpec((1, 256, PAGE, 128), lambda i, slots, limit: (1, 0, 0, 0)),
            ],
        ),
        out_shape=[
            jax.ShapeDtypeStruct((PAGES, PAGE, 128), BF),
            jax.ShapeDtypeStruct((2, 256, PAGE, 128), BF),
        ],
        compiler_params=pltpu.CompilerParams(vmem_limit_bytes=VMEM_LIMIT),
        cost_estimate=pl.CostEstimate(flops=ROWS * 1024, bytes_accessed=4 << 20, transcendentals=0),
        name="finish_text",
    )(slots, limit, *parts)


def place_kernel(slots, rows_ref, slot_ref):
    slot_ref[...] = jnp.zeros_like(slot_ref)
    for p in range(PAGES):
        slot_ref[slots[p]] = rows_ref[p]


def place_pages(slots, rows):
    return pl.pallas_call(
        place_kernel,
        grid_spec=pltpu.PrefetchScalarGridSpec(
            num_scalar_prefetch=1,
            grid=(1,),
            in_specs=[pl.BlockSpec((PAGES, PAGE, 128), lambda i, slots: (0, 0, 0))],
            out_specs=pl.BlockSpec((256, PAGE, 128), lambda i, slots: (0, 0, 0)),
        ),
        out_shape=jax.ShapeDtypeStruct((256, PAGE, 128), BF),
        compiler_params=pltpu.CompilerParams(vmem_limit_bytes=VMEM_LIMIT),
        cost_estimate=pl.CostEstimate(flops=ROWS * 128, bytes_accessed=3 << 19, transcendentals=0),
        name="place_pages",
    )(slots, rows)


def merge_kernel(place, own_ref, other_ref, first_ref, second_ref, image_ref, out_ref):
    match = jnp.where(place[0] == 0, pl.program_id(0), place[3]).astype(F32)
    targets = []
    for half in range(2):
        owner = image_ref[half, 0, IMG : IMG + 1, 0:IMG].astype(F32)
        rank = image_ref[half, 0, IMG + 1 : IMG + 2, 0:IMG].astype(F32)
        offset = image_ref[half, 0, IMG + 2 : IMG + 3, 0:IMG].astype(F32)
        targets.append(jnp.where(owner == match, rank * PAGE + offset, -1.0))
    target = jnp.concatenate(targets, axis=1)
    data = jnp.concatenate([image_ref[0, 0, 0:IMG, :], image_ref[1, 0, 0:IMG, :]], axis=0)
    spots = lax.broadcasted_iota(jnp.int32, (CAP * PAGE, 2 * IMG), 0).astype(F32)
    chosen = (spots == target).astype(F32).astype(BF)
    image = jnp.dot(chosen, data, preferred_element_type=F32)
    taken = jnp.dot(chosen, jnp.ones((2 * IMG, 256), BF), preferred_element_type=F32)

    def write(left, right):
        text = jnp.concatenate([left.reshape(CAP * PAGE, 128), right.reshape(CAP * PAGE, 128)], axis=1)
        merged = jnp.where(taken > 0.5, image, text.astype(F32)).astype(BF)
        out_ref[...] = merged.reshape(CAP, PAGE, 256)

    @pl.when(place[0] == 0)
    def _():
        write(own_ref[0], other_ref[...])

    @pl.when(place[0] != 0)
    def _():
        write(first_ref[0], second_ref[0])


def merge_slots(place, own, other, arrived, image):
    def local(i, place):
        return jnp.where(place[0] == 0, i, 7)

    def remote(i, place):
        return jnp.where(place[0] == 0, 0, i)

    return pl.pallas_call(
        merge_kernel,
        grid_spec=pltpu.PrefetchScalarGridSpec(
            num_scalar_prefetch=1,
            grid=(8,),
            in_specs=[
                pl.BlockSpec((1, CAP, PAGE, 128), lambda i, place: (1, local(i, place), 0, 0)),
                pl.BlockSpec((CAP, PAGE, 128), lambda i, place: (local(i, place), 0, 0)),
                pl.BlockSpec((1, CAP, PAGE, 128), lambda i, place: (0, remote(i, place), 0, 0)),
                pl.BlockSpec((1, CAP, PAGE, 128), lambda i, place: (1, remote(i, place), 0, 0)),
                pl.BlockSpec(
                    (2, 1, IMG_TALL, 256),
                    lambda i, place: (0, jnp.where(place[0] == 0, place[3], i), 0, 0),
                ),
            ],
            out_specs=pl.BlockSpec((CAP, PAGE, 256), lambda i, place: (i, 0, 0)),
        ),
        out_shape=jax.ShapeDtypeStruct((256, PAGE, 256), BF),
        compiler_params=pltpu.CompilerParams(vmem_limit_bytes=VMEM_LIMIT),
        cost_estimate=pl.CostEstimate(
            flops=2 * 8 * 512 * 128 * 512, bytes_accessed=5 << 20, transcendentals=0
        ),
        name="merge_slots",
    )(place, own, other, arrived, arrived, image)


def attend(queries, kv_cache, new_kv, cache_lengths):
    row_count = queries.shape[0]
    heads_kv = kv_cache.shape[2] // (2 * HEAD)
    grouped = queries.reshape(row_count, heads_kv, queries.shape[1] // (HEAD * heads_kv), HEAD)
    stored = kv_cache.reshape(row_count, kv_cache.shape[1], heads_kv, 2 * HEAD)
    fresh_kv = new_kv.reshape(row_count, heads_kv, 2 * HEAD)
    scores = jnp.einsum(
        "rgqh,rjgh->rgqj", grouped, stored[..., :HEAD], preferred_element_type=jnp.float32
    ) * HEAD ** (-0.5)
    in_cache = jnp.arange(stored.shape[1], dtype=jnp.int32)[None, :] < cache_lengths[:, None]
    scores = jnp.where(in_cache[:, None, None, :], scores, -1e30)
    own_score = jnp.einsum(
        "rgqh,rgh->rgq", grouped, fresh_kv[..., :HEAD], preferred_element_type=jnp.float32
    ) * HEAD ** (-0.5)
    row_max = jnp.maximum(jnp.max(scores, axis=3), own_score)
    weights = jnp.exp(scores - row_max[..., None])
    own_weight = jnp.exp(own_score - row_max)
    denominator = jnp.sum(weights, axis=3) + own_weight
    probability = (weights / denominator[..., None]).astype(jnp.bfloat16)
    own_prob = lax.optimization_barrier((own_weight / denominator).astype(jnp.bfloat16)).astype(
        jnp.float32
    )
    attended = jnp.einsum(
        "rgqj,rjgh->rgqh", probability, stored[..., HEAD:], preferred_element_type=jnp.float32
    )
    attended = attended + own_prob[..., None] * fresh_kv[:, :, None, HEAD:].astype(jnp.float32)
    return attended.astype(jnp.bfloat16).reshape(row_count, queries.shape[1])


PARTNER = [(i, i ^ 1) for i in range(8)]


def shift(k):
    return [(i, (i + 2 * k) % 8) for i in range(8)]


def per_device(
    embeds,
    image_feats,
    image_pos,
    proj_w,
    proj_b,
    norm_gain,
    kv_w,
    prompt_lengths,
    page_owner,
    queries,
    kv_cache,
    new_kv,
    cache_lengths,
):
    group = lax.axis_index("group").astype(jnp.int32)
    seq = lax.axis_index("seq").astype(jnp.int32)
    mp = lax.axis_index("mp").astype(jnp.int32)
    core, x = mp % 2, mp // 2
    place = jnp.stack([group, core, x, seq])
    gain = norm_gain.reshape(1, -1)

    mine = lax.dynamic_slice(image_feats, (group * IMG + core * 32, 0), (32, image_feats.shape[1]))
    depth = proj_w.shape[0]
    blocks = mine.reshape(32, 8, depth).transpose(1, 0, 2)
    got = lax.all_to_all(blocks, "seq", 0, 0, tiled=True)
    swapped = lax.ppermute(got, "mp", PARTNER)
    low = jnp.where(core == 0, got, swapped)
    high = jnp.where(core == 0, swapped, got)
    feats = jnp.concatenate([low, high], axis=1).reshape(8 * IMG, depth)

    send, keep = project_text(place, embeds, gain, kv_w)
    received = lax.ppermute(send, "mp", PARTNER)
    parts = [None] * 4
    for j in (1, 2, 3):
        parts[j] = lax.ppermute(add_pair(keep, received, j), "mp", shift(j))
    parts[0] = add_pair(keep, received, 0)

    partial = jnp.dot(feats, proj_w, preferred_element_type=F32).astype(BF)
    pieces = lax.all_to_all(partial, "seq", 0, 0, tiled=True).reshape(8, IMG, -1)
    summed = jnp.sum(pieces.astype(F32), axis=0)
    image_hidden = jax.nn.gelu(summed + proj_b.astype(F32), approximate=False).astype(BF)

    owners = page_owner[:, 0]
    one_hot = (owners[:, None] == jnp.arange(8, dtype=jnp.int32)[None, :]).astype(jnp.int32)
    before = (
        jnp.arange(PAGES, dtype=jnp.int32)[None, :] < jnp.arange(PAGES, dtype=jnp.int32)[:, None]
    )
    page_rank = jnp.sum((before & (owners[:, None] == owners[None, :])).astype(jnp.int32), axis=1)
    slots = owners * CAP + page_rank
    prompt = seq // 2
    live = jnp.sum(jnp.where(jnp.arange(4, dtype=jnp.int32) == prompt, prompt_lengths, 0))
    limit = live - (seq % 2) * ROWS

    hidden = image_hidden.astype(F32)
    squares = jnp.sum(hidden * hidden, axis=1)
    scaled = (hidden * norm_gain.astype(F32)).astype(BF)
    image_kv = jnp.dot(scaled, kv_w, preferred_element_type=F32).astype(BF)
    image_kv = image_kv.reshape(IMG, 8, 256).transpose(1, 0, 2)
    square_high, square_low = split_pair(squares)
    extra = jnp.concatenate([square_high, square_low]).reshape(2, IMG)
    extra = jnp.pad(extra, ((0, 14), (0, 256 - IMG)))
    extra = jnp.broadcast_to(extra[None], (8, 16, 256))
    image_parts = lax.all_to_all(jnp.concatenate([image_kv, extra], axis=1), "mp", 0, 0, tiled=True)
    image_sum = jnp.sum(image_parts.astype(F32), axis=0)
    image_squares = image_sum[IMG, :IMG] + image_sum[IMG + 1, :IMG]
    image_scale = lax.rsqrt(image_squares / D + 1e-05)
    local_pos = lax.dynamic_slice(image_pos, (group * IMG,), (IMG,)) - seq * ROWS
    image_rows = jnp.where(
        (local_pos < limit)[:, None], image_sum[:IMG] * image_scale[:, None], 0.0
    ).astype(BF)
    at_page = (local_pos // PAGE)[:, None] == jnp.arange(PAGES, dtype=jnp.int32)[None, :]
    image_owner = jnp.sum(jnp.where(at_page, owners[None, :], 0), axis=1)
    image_rank = jnp.sum(jnp.where(at_page, page_rank[None, :], 0), axis=1)
    labels = jnp.stack([image_owner, image_rank, local_pos % PAGE]).astype(BF)
    labels = jnp.pad(labels, ((0, 13), (0, 256 - IMG)))
    image_block = jnp.concatenate([image_rows, labels], axis=0)
    image_all = lax.all_gather(image_block, ("group", "seq"), axis=0)
    image_all = image_all.reshape(2, 8, IMG_TALL, 256)

    rows, by_owner = finish_text(slots, limit.reshape(1), parts)
    other_rows = lax.ppermute(rows, "group", [(1, 0)])
    arrived = lax.all_to_all(
        by_owner.reshape(512, PAGE, 128), ("group", "seq"), split_axis=0, concat_axis=0, tiled=True
    ).reshape(2, 256, PAGE, 128)
    other = place_pages(slots, other_rows)
    page_slots = merge_slots(place, by_owner, other, arrived, image_all)

    other_hidden = lax.ppermute(image_hidden, "group", [(1, 0)])
    attended = lax.cond(
        group != 0,
        attend,
        lambda *unused: jnp.zeros(queries.shape, BF),
        queries,
        kv_cache,
        new_kv,
        cache_lengths,
    )
    row_states = jnp.where(
        group == 0, jnp.concatenate([image_hidden, other_hidden], axis=0), attended
    )
    return (page_slots, row_states)


def solution(mesh):
    in_specs = (
        P("seq", "mp"),
        P("seq", None),
        P("seq"),
        P("seq", "mp"),
        P("mp"),
        P("mp"),
        P("mp", None),
        P(),
        P("seq", None),
        P("seq", "mp"),
        P("seq", None, "mp"),
        P("seq", "mp"),
        P("seq"),
    )
    out_specs = (P(("group", "seq"), None, "mp"), P(("group", "seq"), "mp"))
    return jax.shard_map(
        per_device, mesh=mesh, in_specs=in_specs, out_specs=out_specs, check_vma=False
    )
```

time: 388 us -> 198 us (0.51)
  the two profiles are of different devices: /device:TPU:10 before, /device:TPU:26 now
where the time goes in v1:
time: 198 us; the launch traced here: 197 us
  blocking collectives  50.5 us (26%)
  waiting for transfers between devices  48.5 us (24%)
  starting transfers between devices  37.6 us (19%)
  Pallas kernels  34.5 us (17%)
  matrix products  13.5 us (7%)
  other arithmetic  5.64 us (3%)
  local copies, waits for them, and re-layouts  4.96 us (3%)
    all_gather x1, blocking collectives, per_device(): image_all = lax.all_gather(image_block, ('group', 'seq'), axis=0)  50.5 us
    ppermute x1, waiting for transfers between devices, per_device(): other_hidden = lax.ppermute(image_hidden, 'group', [(1, 0)])  13.8 us
    all_to_all x1, waiting for transfers between devices, per_device(): lax.all_to_all(partial, 'seq', 0, 0, tiled=True).reshape(8, IMG, -1)  13.4 us
    ppermute x3, waiting for transfers between devices, per_device(): parts[j] = lax.ppermute(add_pair(keep, received, j), 'mp', shift(j))  13.2 us
    pallas_call x1, Pallas kernels, project_text(): pl.pallas_call(project_kernel, grid_spec=pltpu.PrefetchScalarGridSpec(num...  10.9 us
    pallas_call x4, Pallas kernels, add_pair(): pl.pallas_call(add_kernel, grid=(1,), in_specs=[spec, spec], out_specs=pl...  8.55 us
    all_to_all x1, starting transfers between devices, per_device(): got = lax.all_to_all(blocks, 'seq', 0, 0, tiled=True)  8.28 us
    pallas_call x1, Pallas kernels, merge_slots(): pl.pallas_call(merge_kernel, grid_spec=pltpu.PrefetchScalarGridSpec(num_s...  8.23 us
  transfers between devices with their start and end apart: 11, of which 5 were waited for; matrix products, arithmetic and copies ran while one was open for 10% of the time, Pallas kernels for 12%

profile of v1, /device:TPU:26, one launch (start us, length us, event | category | flops | bytes accessed | tf_op | source)
XLA Modules:
  0.0 196.9 jit_solution(12992219286309805382)
XLA Ops:
  0.7 1.2 constant_dynamic-slice_fusion
  1.9 1.0 reshape.159
  2.9 1.1 copy.22
  4.0 8.3 %all-to-all-start.1 = ((bf16[8,32,912]{2,1,0:T(8,128)(2,1)}), bf16[8,32,912]{2,1,0:T(8,128)(2,1)S(1)}, u32[]{:S(2)}, u32[]{:S(2)}) async-start(bf16[8,32,912]{2,1,0:T(8,128)(2,1)} %copy.22), calls=%async_computation.1 | async-start | bytes 1048576 | tf_op jit(solution)/shard_map/all_to_all | solution.py:309
  12.9 8.0 %all-to-all-done.1 = bf16[8,32,912]{2,1,0:T(8,128)(2,1)S(1)} async-done(((bf16[8,32,912]{2,1,0:T(8,128)(2,1)}), bf16[8,32,912]{2,1,0:T(8,128)(2,1)S(1)}, u32[]{:S(2)}, u32[]{:S(2)}) %all-to-all-start.1) | async-done | bytes 466976 | tf_op jit(solution)/shard_map/all_to_all | solution.py:309
  21.6 10.9 %project_text.1 = (bf16[4,2080,128]{2,1,0:T(8,128)(2,1)}, bf16[4,2080,128]{2,1,0:T(8,128)(2,1)}) custom-call(s32[4]{0:T(128)} %pad_add_fusion.place, bf16[2048,1024]{1,0:T(8,128)(2,1)} %embeds_ref.1, bf16[1,1024]{1,0:T(2,128)(2,1)} %reshape.156.gain_ref, bf16[1024,2048]{1,0:T(8,128)(2,1)} %refs_7_.1, bf16[1024,2048]{1,0:T(8,128)(2,1)} %refs_7_.1, ...), custom_call_target="tpu_custom_call" | custom-call | flops 4294967296 | bytes 12582912 | tf_op jit(solution)/shard_map/project_text/pallas_call | solution.py:77
  33.2 2.2 %convolution_convert_fusion.1 = bf16[512,1024]{1,0:T(8,128)(2,1)} fusion(bf16[512,912]{1,0:T(8,128)(2,1)S(1)} %bitcast.80, bf16[912,1024]{1,0:T(8,128)(2,1)S(1)} %copy-done), kind=kOutput, calls=%fused_computation.28 | convolution fusion | flops 956825600 | bytes 3850240 | tf_op jit(solution)/shard_map/dot_general | solution.py:322
  35.4 6.1 %all-to-all-start.2 = ((bf16[8,64,1024]{2,1,0:T(8,128)(2,1)}), bf16[8,64,1024]{2,1,0:T(8,128)(2,1)S(1)}, u32[]{:S(2)}, u32[]{:S(2)}) async-start(bf16[8,64,1024]{2,1,0:T(8,128)(2,1)} %bitcast.79), calls=%async_computation.2 | async-start | bytes 2097152 | tf_op jit(solution)/shard_map/all_to_all | solution.py:323
  42.8 13.4 %all-to-all-done.2 = bf16[8,64,1024]{2,1,0:T(8,128)(2,1)S(1)} async-done(((bf16[8,64,1024]{2,1,0:T(8,128)(2,1)}), bf16[8,64,1024]{2,1,0:T(8,128)(2,1)S(1)}, u32[]{:S(2)}, u32[]{:S(2)}) %all-to-all-start.2) | async-done | bytes 1048608 | tf_op jit(solution)/shard_map/all_to_all | solution.py:323
  57.1 3.0 %convolution_convert_fusion = bf16[64,2048]{1,0:T(8,128)(2,1)S(1)} fusion(bf16[1024,2048]{1,0:T(8,128)(2,1)} %refs_7_.1, bf16[64,1024]{1,0:T(8,128)(2,1)S(1)} %get-tuple-element.38, f32[1024]{0:T(1024)S(1)} %convert_element_type.82), kind=kOutput, calls=%fused_computation.26 | convolution fusion | flops 268763136 | bytes 4591616 | tf_op jit(solution)/shard_map/dot_general | solution.py:341
  60.1 2.1 %add_pair.5 = bf16[2080,128]{1,0:T(8,128)(2,1)} custom-call(bf16[4,2080,128]{2,1,0:T(8,128)(2,1)} %get-tuple-element.21.a_ref, bf16[4,2080,128]{2,1,0:T(8,128)(2,1)} %collective-permute-done.b_ref), custom_call_target="tpu_custom_call" | custom-call | flops 266240 | bytes 1572864 | tf_op jit(solution)/shard_map/add_pair/pallas_call | solution.py:107
  62.3 1.5 collective-permute-start.1
  63.8 2.1 %add_pair.6 = bf16[2080,128]{1,0:T(8,128)(2,1)} custom-call(bf16[4,2080,128]{2,1,0:T(8,128)(2,1)} %get-tuple-element.21.a_ref, bf16[4,2080,128]{2,1,0:T(8,128)(2,1)} %collective-permute-done.b_ref), custom_call_target="tpu_custom_call" | custom-call | flops 266240 | bytes 1572864 | tf_op jit(solution)/shard_map/add_pair/pallas_call | solution.py:107
  65.9 1.1 collective-permute-start.2
  67.0 2.1 %add_pair.7 = bf16[2080,128]{1,0:T(8,128)(2,1)} custom-call(bf16[4,2080,128]{2,1,0:T(8,128)(2,1)} %get-tuple-element.21.a_ref, bf16[4,2080,128]{2,1,0:T(8,128)(2,1)} %collective-permute-done.b_ref), custom_call_target="tpu_custom_call" | custom-call | flops 266240 | bytes 1572864 | tf_op jit(solution)/shard_map/add_pair/pallas_call | solution.py:107
  69.2 2.2 %collective-permute-start.3 = (bf16[2080,128]{1,0:T(8,128)(2,1)}, bf16[2080,128]{1,0:T(8,128)(2,1)}, u32[]{:S(2)}, u32[]{:S(2)}) collective-permute-start(bf16[2080,128]{1,0:T(8,128)(2,1)} %add_pair.7), channel_id=1, source_target_pairs={{0,6},{1,7},{2,0},{3,1},{4,2},{5,3},{6,4},{7,5},{8,14},{9,15},{10,... | collective-permute-start | bytes 1597448 | tf_op jit(solution)/shard_map/ppermute | solution.py:319
  72.3 4.8 %all-to-all-start.3 = ((bf16[8,80,256]{2,1,0:T(8,128)(2,1)}), bf16[8,80,256]{2,1,0:T(8,128)(2,1)S(1)}, u32[]{:S(2)}, u32[]{:S(2)}) async-start(bf16[8,80,256]{2,1,0:T(8,128)(2,1)} %pad_maximum_fusion.1), calls=%async_computation.3 | async-start | bytes 655360 | tf_op jit(solution)/shard_map/all_to_all | solution.py:347
  77.8 2.1 %add_pair.4.a_ref = bf16[2080,128]{1,0:T(8,128)(2,1)} custom-call(bf16[4,2080,128]{2,1,0:T(8,128)(2,1)} %get-tuple-element.21.a_ref, bf16[4,2080,128]{2,1,0:T(8,128)(2,1)} %collective-permute-done.b_ref), custom_call_target="tpu_custom_call" | custom-call | flops 266240 | bytes 1572864 | tf_op jit(solution)/shard_map/add_pair/pallas_call | solution.py:107
  79.9 2.8 %collective-permute-done.2.c_ref = bf16[2080,128]{1,0:T(8,128)(2,1)S(1)} collective-permute-done((bf16[2080,128]{1,0:T(8,128)(2,1)}, bf16[2080,128]{1,0:T(8,128)(2,1)S(1)}, u32[]{:S(2)}, u32[]{:S(2)}) %collective-permute-start.2) | collective-permute-done | bytes 532512 | tf_op jit(solution)/shard_map/ppermute | solution.py:319
  82.7 10.4 %collective-permute-done.3.d_ref = bf16[2080,128]{1,0:T(8,128)(2,1)} collective-permute-done((bf16[2080,128]{1,0:T(8,128)(2,1)}, bf16[2080,128]{1,0:T(8,128)(2,1)}, u32[]{:S(2)}, u32[]{:S(2)}) %collective-permute-start.3) | collective-permute-done | bytes 532512 | tf_op jit(solution)/shard_map/ppermute | solution.py:319
  93.2 3.9 %finish_text.1 = (bf16[128,16,128]{2,1,0:T(8,128)(2,1)}, bf16[2,256,16,128]{3,2,1,0:T(8,128)(2,1)}) custom-call(s32[128]{0:T(128)} %multiply_add_fusion.slots, s32[1]{0:T(128)} %bitcast.16.limit, bf16[2080,128]{1,0:T(8,128)(2,1)} %add_pair.4.a_ref, bf16[2080,128]{1,0:T(8,128)(2,1)} %copy-done.1, bf16[2080,128]{1,0:T(8,128)(2,1)} %copy-done.2, ...), custom_call_target="tpu_custom_call" | custom-call | flops 2097152 | bytes 4194304 | tf_op jit(solution)/shard_map/finish_text/pallas_call | solution.py:143
  97.1 6.0 %all-to-all-start = ((bf16[512,16,128]{2,1,0:T(8,128)(2,1)}), bf16[512,16,128]{2,1,0:T(8,128)(2,1)}, u32[]{:S(2)}, u32[]{:S(2)}) async-start(bf16[512,16,128]{2,1,0:T(8,128)(2,1)} %bitcast.72), calls=%async_computation | async-start | bytes 4194304 | tf_op jit(solution)/shard_map/all_to_all | solution.py:366
  103.4 2.8 %collective-permute-start.6 = (bf16[64,1024]{1,0:T(8,128)(2,1)S(1)}, bf16[64,1024]{1,0:T(8,128)(2,1)S(1)}, u32[]{:S(2)}, u32[]{:S(2)}) collective-permute-start(bf16[64,1024]{1,0:T(8,128)(2,1)S(1)} %get-tuple-element.38), channel_id=1, source_target_pairs={{64,0},{65,1},{66,2},{67,3},{68,4},{69,5},{70,6},{71,7},{72,8},{73... | collective-permute-start | bytes 393224 | tf_op jit(solution)/shard_map/ppermute | solution.py:372
  106.2 9.0 %conditional.1 = (bf16[128,1024]{1,0:T(8,128)(2,1)S(1)}) conditional(s32[]{:T(128)} %convert_element_type.90, () %tuple.14, (s32[128]{0:T(128)S(1)}, bf16[128,1024]{1,0:T(8,128)(2,1)S(1)}, bf16[128,128,256]{2,1,0:T(8,128)(2,1)}, bf16[128,256]{1,0:T(8,128)(2,1)S(1)}) %tuple.31), branch_computations={%region_7.8_spmd, %region_8.11_spmd} | conditional | flops 68852736 | bytes 12157448 | solution.py:373
  106.4 4.5 %fusion.45 = (f32[128,8]{1,0:T(8,128)S(1)}, f32[128,8,128]{2,1,0:T(8,128)S(1)}) fusion(bf16[128,8,128]{2,1,0:T(8,128)(2,1)S(1)} %bitcast.77, bf16[128,128,1,256]{3,1,0,2:T(8,128)(2,1)} %bitcast.74, pred[128,128]{1,0:T(8,128)(4,1)S(1)} %iota_compare_fusion), kind=kOutput, calls=%fused_computation.102 | convolution fusion | flops 33946624 | bytes 5001216 | tf_op jit(solution)/shard_map/cond/branch_1_fun/rgqh,rjgh->rgqj/dot_general | solution.py:254
  111.7 3.5 %fusion.5 = bf16[128,8,128]{2,1,0:T(8,128)(2,1)S(1)} fusion(bf16[128,128,1,256]{3,1,0,2:T(8,128)(2,1)} %bitcast.75, f32[128,8,128]{2,1,0:T(8,128)S(1)} %get-tuple-element.44, f32[128,128]{1,0:T(8,128)S(1)} %get-tuple-element.42, f32[128,8]{1,0:T(8,128)S(1)} %bitcast_convert_fusion, f32[128,8]{1,0:T(8,128)S(1)} %get-tuple-element.39, ...), kind=kOutput, calls=%fused_computation.7 | convolution fusion | flops 34340864 | bytes 5058560 | tf_op jit(solution)/shard_map/cond/branch_1_fun/rgqj,rjgh->rgqh/dot_general | solution.py:270
  115.2 13.8 %collective-permute-done.6 = bf16[64,1024]{1,0:T(8,128)(2,1)S(1)} collective-permute-done((bf16[64,1024]{1,0:T(8,128)(2,1)S(1)}, bf16[64,1024]{1,0:T(8,128)(2,1)S(1)}, u32[]{:S(2)}, u32[]{:S(2)}) %collective-permute-start.6) | collective-permute-done | bytes 131104 | tf_op jit(solution)/shard_map/ppermute | solution.py:372
  129.9 4.4 %collective-permute-start.4 = (bf16[128,16,128]{2,1,0:T(8,128)(2,1)}, bf16[128,16,128]{2,1,0:T(8,128)(2,1)S(1)}, u32[]{:S(2)}, u32[]{:S(2)}) collective-permute-start(bf16[128,16,128]{2,1,0:T(8,128)(2,1)} %get-tuple-element.24), channel_id=1, source_target_pairs={{64,0},{65,1},{66,2},{67,3},{68,4},{69,5},{70,6},{71,7},{72,8},{73... | collective-permute-start | bytes 1572872 | tf_op jit(solution)/shard_map/ppermute | solution.py:365
  134.4 50.5 %all-gather = bf16[1280,256]{1,0:T(8,128)(2,1)} all-gather(bf16[80,256]{1,0:T(8,128)(2,1)S(1)} %pad_maximum_fusion.2), channel_id=2, replica_groups=mesh['group'=2,'seq'=8,'mp'=8] {'group','seq'}, dimensions={0}, use_global_device_ids=true | all-gather | bytes 696320 | tf_op jit(solution)/shard_map/all_gather | solution.py:361
  184.9 0.8 copy-done.3
  185.7 2.9 %place_pages.1.other_ref = bf16[256,16,128]{2,1,0:T(8,128)(2,1)} custom-call(s32[128]{0:T(128)} %multiply_add_fusion.slots, bf16[128,16,128]{2,1,0:T(8,128)(2,1)} %copy-done.3), custom_call_target="tpu_custom_call" | custom-call | flops 262144 | bytes 1572864 | tf_op jit(solution)/shard_map/place_pages/pallas_call | solution.py:171
  188.6 8.2 %merge_slots.1 = bf16[256,16,256]{2,1,0:T(8,128)(2,1)} custom-call(s32[4]{0:T(128)} %pad_add_fusion.place, bf16[2,256,16,128]{3,2,1,0:T(8,128)(2,1)} %get-tuple-element.23.own_ref, bf16[256,16,128]{2,1,0:T(8,128)(2,1)} %place_pages.1.other_ref, bf16[2,256,16,128]{3,2,1,0:T(8,128)(2,1)} %bitcast.18.first_ref.second_ref, ...), custom_call_target="tpu_custom_call" | custom-call | flops 536870912 | bytes 5242880 | tf_op jit(solution)/shard_map/merge_slots/pallas_call | solution.py:222
  (68 shorter events, 7.3 us)
Async XLA Ops:
  0.6 32.5 %copy-start = (bf16[912,1024]{1,0:T(8,128)(2,1)S(1)}, bf16[912,1024]{1,0:T(8,128)(2,1)}, u32[]{:S(2)}) copy-start(bf16[912,1024]{1,0:T(8,128)(2,1)} %param.18) | copy-start | bytes 5603332
  0.6 11.6 %copy-start.6 = (bf16[1024]{0:T(1024)(128)(2,1)S(1)}, bf16[1024]{0:T(1024)(128)(2,1)}, u32[]{:S(2)}) copy-start(bf16[1024]{0:T(1024)(128)(2,1)} %param.20) | copy-start | bytes 6148
  4.0 16.9 %all-to-all-start.1 = ((bf16[8,32,912]{2,1,0:T(8,128)(2,1)}), bf16[8,32,912]{2,1,0:T(8,128)(2,1)S(1)}, u32[]{:S(2)}, u32[]{:S(2)}) async-start(bf16[8,32,912]{2,1,0:T(8,128)(2,1)} %copy.22), calls=%async_computation.1 | async-start | bytes 1048576 | tf_op jit(solution)/shard_map/all_to_all | solution.py:309
  20.9 12.1 %collective-permute-start.5 = (bf16[8,32,912]{2,1,0:T(8,128)(2,1)S(1)}, bf16[8,32,912]{2,1,0:T(8,128)(2,1)S(1)}, u32[]{:S(2)}, u32[]{:S(2)}) collective-permute-start(bf16[8,32,912]{2,1,0:T(8,128)(2,1)S(1)} %all-to-all-done.1), channel_id=1, source_target_pairs={{0,1},{1,0},{2,3},{3,2},{4,5},{5,4},{6,7},{7,6},{8,9},{9,8},{10,11... | collective-permute-start | bytes 1400840 | tf_op jit(solution)/shard_map/ppermute | solution.py:310
  32.4 27.7 %collective-permute-start = (bf16[4,2080,128]{2,1,0:T(8,128)(2,1)}, bf16[4,2080,128]{2,1,0:T(8,128)(2,1)}, u32[]{:S(2)}, u32[]{:S(2)}) collective-permute-start(bf16[4,2080,128]{2,1,0:T(8,128)(2,1)} %get-tuple-element.22), channel_id=1, source_target_pairs={{0,1},{1,0},{2,3},{3,2},{4,5},{5,4},{6,7},{7,6},{8,9},{9,8},{10,11... | collective-permute-start | bytes 6389768 | tf_op jit(solution)/shard_map/ppermute | solution.py:316
  35.4 6.1 %copy-start.7 = (bf16[1024]{0:T(1024)(128)(2,1)S(1)}, bf16[1024]{0:T(1024)(128)(2,1)}, u32[]{:S(2)}) copy-start(bf16[1024]{0:T(1024)(128)(2,1)} %param.19) | copy-start | bytes 6148
  35.4 6.1 %copy-start.11 = (s32[4]{0:T(128)S(1)}, s32[4]{0:T(128)}, u32[]{:S(2)}) copy-start(s32[4]{0:T(128)} %param.22) | copy-start | bytes 52
  35.4 20.8 %all-to-all-start.2 = ((bf16[8,64,1024]{2,1,0:T(8,128)(2,1)}), bf16[8,64,1024]{2,1,0:T(8,128)(2,1)S(1)}, u32[]{:S(2)}, u32[]{:S(2)}) async-start(bf16[8,64,1024]{2,1,0:T(8,128)(2,1)} %bitcast.79), calls=%async_computation.2 | async-start | bytes 2097152 | tf_op jit(solution)/shard_map/all_to_all | solution.py:323
  62.3 17.6 %collective-permute-start.1 = (bf16[2080,128]{1,0:T(8,128)(2,1)}, bf16[2080,128]{1,0:T(8,128)(2,1)S(1)}, u32[]{:S(2)}, u32[]{:S(2)}) collective-permute-start(bf16[2080,128]{1,0:T(8,128)(2,1)} %add_pair.5), channel_id=1, source_target_pairs={{0,2},{1,3},{2,4},{3,5},{4,6},{5,7},{6,0},{7,1},{8,10},{9,11},{10,... | collective-permute-start | bytes 1597448 | tf_op jit(solution)/shard_map/ppermute | solution.py:319
  65.9 11.2 %copy-start.8 = (s32[128,1]{0,1:T(1,128)S(1)}, s32[128,1]{0,1:T(1,128)}, u32[]{:S(2)}) copy-start(s32[128,1]{0,1:T(1,128)} %param.23) | copy-start | bytes 1540
  65.9 16.8 %collective-permute-start.2 = (bf16[2080,128]{1,0:T(8,128)(2,1)}, bf16[2080,128]{1,0:T(8,128)(2,1)S(1)}, u32[]{:S(2)}, u32[]{:S(2)}) collective-permute-start(bf16[2080,128]{1,0:T(8,128)(2,1)} %add_pair.6), channel_id=1, source_target_pairs={{0,4},{1,5},{2,6},{3,7},{4,0},{5,1},{6,2},{7,3},{8,12},{9,13},{10,... | collective-permute-start | bytes 1597448 | tf_op jit(solution)/shard_map/ppermute | solution.py:319
  69.2 24.0 %collective-permute-start.3 = (bf16[2080,128]{1,0:T(8,128)(2,1)}, bf16[2080,128]{1,0:T(8,128)(2,1)}, u32[]{:S(2)}, u32[]{:S(2)}) collective-permute-start(bf16[2080,128]{1,0:T(8,128)(2,1)} %add_pair.7), channel_id=1, source_target_pairs={{0,6},{1,7},{2,0},{3,1},{4,2},{5,3},{6,4},{7,5},{8,14},{9,15},{10,... | collective-permute-start | bytes 1597448 | tf_op jit(solution)/shard_map/ppermute | solution.py:319
  72.3 24.8 %all-to-all-start.3 = ((bf16[8,80,256]{2,1,0:T(8,128)(2,1)}), bf16[8,80,256]{2,1,0:T(8,128)(2,1)S(1)}, u32[]{:S(2)}, u32[]{:S(2)}) async-start(bf16[8,80,256]{2,1,0:T(8,128)(2,1)} %pad_maximum_fusion.1), calls=%async_computation.3 | async-start | bytes 655360 | tf_op jit(solution)/shard_map/all_to_all | solution.py:347
  79.9 13.2 %copy-start.1 = (bf16[2080,128]{1,0:T(8,128)(2,1)}, bf16[2080,128]{1,0:T(8,128)(2,1)S(1)}, u32[]{:S(2)}) copy-start(bf16[2080,128]{1,0:T(8,128)(2,1)S(1)} %collective-permute-done.1.b_ref) | copy-start | bytes 1597444
  82.7 10.4 %copy-start.2 = (bf16[2080,128]{1,0:T(8,128)(2,1)}, bf16[2080,128]{1,0:T(8,128)(2,1)S(1)}, u32[]{:S(2)}) copy-start(bf16[2080,128]{1,0:T(8,128)(2,1)S(1)} %collective-permute-done.2.c_ref) | copy-start | bytes 1597444
  97.1 6.0 %copy-start.10 = (s32[128]{0:T(128)S(1)}, s32[128]{0:T(128)}, u32[]{:S(2)}) copy-start(s32[128]{0:T(128)} %param.17) | copy-start | bytes 1540
  97.1 9.1 %copy-start.4 = (bf16[128,1024]{1,0:T(8,128)(2,1)S(1)}, bf16[128,1024]{1,0:T(8,128)(2,1)}, u32[]{:S(2)}) copy-start(bf16[128,1024]{1,0:T(8,128)(2,1)} %param.24) | copy-start | bytes 786436
  97.1 9.1 %copy-start.5 = (bf16[128,256]{1,0:T(8,128)(2,1)S(1)}, bf16[128,256]{1,0:T(8,128)(2,1)}, u32[]{:S(2)}) copy-start(bf16[128,256]{1,0:T(8,128)(2,1)} %param.26) | copy-start | bytes 196612
  97.1 9.1 %copy-start.9 = (s32[128]{0:T(128)S(1)}, s32[128]{0:T(128)}, u32[]{:S(2)}) copy-start(s32[128]{0:T(128)} %param.27) | copy-start | bytes 1540
  97.1 91.5 %all-to-all-start = ((bf16[512,16,128]{2,1,0:T(8,128)(2,1)}), bf16[512,16,128]{2,1,0:T(8,128)(2,1)}, u32[]{:S(2)}, u32[]{:S(2)}) async-start(bf16[512,16,128]{2,1,0:T(8,128)(2,1)} %bitcast.72), calls=%async_computation | async-start | bytes 4194304 | tf_op jit(solution)/shard_map/all_to_all | solution.py:366
  103.4 25.7 %collective-permute-start.6 = (bf16[64,1024]{1,0:T(8,128)(2,1)S(1)}, bf16[64,1024]{1,0:T(8,128)(2,1)S(1)}, u32[]{:S(2)}, u32[]{:S(2)}) collective-permute-start(bf16[64,1024]{1,0:T(8,128)(2,1)S(1)} %get-tuple-element.38), channel_id=1, source_target_pairs={{64,0},{65,1},{66,2},{67,3},{68,4},{69,5},{70,6},{71,7},{72,8},{73... | collective-permute-start | bytes 393224 | tf_op jit(solution)/shard_map/ppermute | solution.py:372
  129.9 55.1 %collective-permute-start.4 = (bf16[128,16,128]{2,1,0:T(8,128)(2,1)}, bf16[128,16,128]{2,1,0:T(8,128)(2,1)S(1)}, u32[]{:S(2)}, u32[]{:S(2)}) collective-permute-start(bf16[128,16,128]{2,1,0:T(8,128)(2,1)} %get-tuple-element.24), channel_id=1, source_target_pairs={{64,0},{65,1},{66,2},{67,3},{68,4},{69,5},{70,6},{71,7},{72,8},{73... | collective-permute-start | bytes 1572872 | tf_op jit(solution)/shard_map/ppermute | solution.py:365
  184.9 0.8 copy-start.3

commit v2 on v1

v2 whole, which is shorter than its diff:
```python
import functools

import jax
import jax.numpy as jnp
from jax import lax
from jax.experimental import pallas as pl
from jax.experimental.pallas import tpu as pltpu
from jax.sharding import PartitionSpec as P

D = 8192
HEAD = 128
PAGE = 16
PROMPT_LEN = 4096
CAP = 32
ROWS = 2048
EXT = 32
TALL = ROWS + EXT
PAGES = ROWS // PAGE
IMG = 64
IMG_TALL = IMG + 16
BF = jnp.bfloat16
F32 = jnp.float32
LIGHT = pl.CostEstimate(flops=1, bytes_accessed=1, transcendentals=0)
VMEM_LIMIT = 56 * 1024 * 1024


def split_pair(value):
    high = value.astype(BF)
    low = (value - high.astype(F32)).astype(BF)
    return high, low


def project_kernel(count, place, embeds_ref, gain_ref, *refs):
    weights, refs = refs[: 2 * count], refs[2 * count :]
    if count == 2:
        send_ref, keep_ref, both_ref, squares_ref = refs
    step = pl.program_id(0)

    @pl.when(step < 8)
    def _():
        hidden = embeds_ref[...].astype(F32)
        scaled = (hidden * gain_ref[...].astype(F32)).astype(BF)
        squared = hidden * hidden
        lanes = squared[:, 0:128]
        for k in range(1, 8):
            lanes = lanes + squared[:, k * 128 : (k + 1) * 128]
        summed = jnp.sum(lanes.T, axis=0, keepdims=True)
        squares_ref[pl.ds(2 * step, 1), :] = summed[:, :128]
        squares_ref[pl.ds(2 * step + 1, 1), :] = summed[:, 128:]
        for target, pair in ((send_ref, weights[:2]), (keep_ref, weights[2:])):
            weight = jnp.concatenate([pair[0][...], pair[1][...]], axis=1)
            product = jnp.dot(scaled, weight, preferred_element_type=F32).astype(BF)
            target[0] = product[:, :128]
            target[1] = product[:, 128:]

    @pl.when(step == 8)
    def _():
        high, low = split_pair(squares_ref[...])
        both = jnp.concatenate([high, low], axis=0)
        for j in range(count):
            send_ref[j, 0:EXT, :] = both
            keep_ref[j, 0:EXT, :] = both


def project_text(place, embeds, gain, kv_w, shifts):
    def column(r, j):
        def index(i, place):
            core = place[1] if r else 1 - place[1]
            head = 2 * lax.rem(place[2] + j, 4) + core
            return (0, 2 * head + place[0])

        return index

    count = len(shifts)
    specs = [
        pl.BlockSpec((256, 1024), lambda i, place: (jnp.minimum(i, 7), 0)),
        pl.BlockSpec((1, 1024), lambda i, place: (0, 0)),
    ] + [pl.BlockSpec((1024, 128), column(r, j)) for r in range(2) for j in shifts]
    out = jax.ShapeDtypeStruct((count, TALL, 128), BF)
    return pl.pallas_call(
        functools.partial(project_kernel, count),
        grid_spec=pltpu.PrefetchScalarGridSpec(
            num_scalar_prefetch=1,
            grid=(9,),
            in_specs=specs,
            out_specs=[pl.BlockSpec((count, 256, 128), lambda i, place: (0, i, 0))] * 2
            + [pl.BlockSpec((8, 128), lambda i, place: (0, 0))],
            scratch_shapes=[pltpu.VMEM((16, 128), F32)],
        ),
        out_shape=[out, out, jax.ShapeDtypeStruct((8, 128), F32)],
        compiler_params=pltpu.CompilerParams(vmem_limit_bytes=VMEM_LIMIT),
        cost_estimate=LIGHT,
        name="project_text",
    )(place, embeds, gain, *([kv_w] * (2 * count)))


def add_kernel(a_ref, b_ref, out_ref):
    out_ref[...] = (a_ref[0].astype(F32) + b_ref[0].astype(F32)).astype(BF)

    @pl.when(pl.program_id(0) == 1)
    def _():
        half = TALL // 2
        total = jnp.zeros((16, 128), F32)
        for ref in (a_ref, b_ref):
            total = total + ref[0, half - 32 : half - 16, :].astype(F32) + ref[0, half - 16 :, :].astype(F32)
        high, low = split_pair(total)
        out_ref[half - 32 : half - 16, :] = high
        out_ref[half - 16 :, :] = low


def add_pair(keep, received, j):
    spec = pl.BlockSpec((1, TALL // 2, 128), lambda i: (j, i, 0))
    return pl.pallas_call(
        add_kernel,
        grid=(2,),
        in_specs=[spec, spec],
        out_specs=pl.BlockSpec((TALL // 2, 128), lambda i: (i, 0)),
        out_shape=jax.ShapeDtypeStruct((TALL, 128), BF),
        compiler_params=pltpu.CompilerParams(vmem_limit_bytes=VMEM_LIMIT),
        cost_estimate=LIGHT,
        name="add_pair",
    )(keep, received)


def finish_kernel(slots, limit, a_ref, b_ref, c_ref, d_ref, rows_ref, slot_ref):
    refs = (a_ref, b_ref, c_ref, d_ref)
    slot_ref[...] = jnp.zeros_like(slot_ref)
    squares = jnp.zeros((16, 128), F32)
    for ref in refs:
        squares = squares + ref[ROWS : ROWS + 16, :].astype(F32) + ref[ROWS + 16 : TALL, :].astype(F32)
    scale = lax.rsqrt(squares / D + 1e-05)
    row_iota = lax.broadcasted_iota(jnp.int32, (128, 128), 0)
    for part in range(16):
        tile = jnp.broadcast_to(scale[part : part + 1, :], (128, 128)).T
        here = pl.ds(part * 128, 128)
        total = refs[0][here, :].astype(F32)
        for ref in refs[1:]:
            total = total + ref[here, :].astype(F32)
        live = row_iota + part * 128 < limit[0]
        rows = jnp.where(live, total * tile, 0.0).astype(BF)
        for p in range(8):
            page = rows[p * PAGE : (p + 1) * PAGE, :]
            rows_ref[part * 8 + p] = page
            slot_ref[0, slots[part * 8 + p]] = page


def finish_text(slots, limit, parts):
    spec = pl.BlockSpec((TALL, 128), lambda i, slots, limit: (0, 0))
    return pl.pallas_call(
        finish_kernel,
        grid_spec=pltpu.PrefetchScalarGridSpec(
            num_scalar_prefetch=2,
            grid=(1,),
            in_specs=[spec] * 4,
            out_specs=[
                pl.BlockSpec((PAGES, PAGE, 128), lambda i, slots, limit: (0, 0, 0)),
                pl.BlockSpec((1, 256, PAGE, 128), lambda i, slots, limit: (1, 0, 0, 0)),
            ],
        ),
        out_shape=[
            jax.ShapeDtypeStruct((PAGES, PAGE, 128), BF),
            jax.ShapeDtypeStruct((2, 256, PAGE, 128), BF),
        ],
        compiler_params=pltpu.CompilerParams(vmem_limit_bytes=VMEM_LIMIT),
        cost_estimate=LIGHT,
        name="finish_text",
    )(slots, limit, *parts)


def place_kernel(slots, rows_ref, slot_ref):
    slot_ref[...] = jnp.zeros_like(slot_ref)
    for p in range(PAGES):
        slot_ref[slots[p]] = rows_ref[p]


def place_pages(slots, rows):
    return pl.pallas_call(
        place_kernel,
        grid_spec=pltpu.PrefetchScalarGridSpec(
            num_scalar_prefetch=1,
            grid=(1,),
            in_specs=[pl.BlockSpec((PAGES, PAGE, 128), lambda i, slots: (0, 0, 0))],
            out_specs=pl.BlockSpec((256, PAGE, 128), lambda i, slots: (0, 0, 0)),
        ),
        out_shape=jax.ShapeDtypeStruct((256, PAGE, 128), BF),
        compiler_params=pltpu.CompilerParams(vmem_limit_bytes=VMEM_LIMIT),
        cost_estimate=LIGHT,
        name="place_pages",
    )(slots, rows)


def cut_kernel(place, feats_ref, out_ref):
    depth = out_ref.shape[2]
    for k in range(8):
        out_ref[k] = feats_ref[:, k * depth : (k + 1) * depth]


def cut_features(place, feats):
    depth = feats.shape[1] // 8
    return pl.pallas_call(
        cut_kernel,
        grid_spec=pltpu.PrefetchScalarGridSpec(
            num_scalar_prefetch=1,
            grid=(1,),
            in_specs=[
                pl.BlockSpec((32, feats.shape[1]), lambda i, place: (2 * place[0] + place[1], 0))
            ],
            out_specs=pl.BlockSpec((8, 32, depth), lambda i, place: (0, 0, 0)),
        ),
        out_shape=jax.ShapeDtypeStruct((8, 32, depth), BF),
        cost_estimate=LIGHT,
        name="cut_features",
    )(place, feats)


def partial_kernel(place, got_ref, swapped_ref, weight_ref, out_ref):
    def product(ref):
        rows = ref[...].reshape(256, ref.shape[2])
        value = jnp.dot(rows, weight_ref[...], preferred_element_type=F32).astype(BF)
        out_ref[...] = value.reshape(8, 32, value.shape[1])

    own = pl.program_id(0) == place[1]

    @pl.when(own)
    def _():
        product(got_ref)

    @pl.when(jnp.logical_not(own))
    def _():
        product(swapped_ref)


def partial_images(place, got, swapped, weight):
    depth, width = weight.shape
    rows = pl.BlockSpec((8, 32, depth), lambda i, place: (0, 0, 0))
    return pl.pallas_call(
        partial_kernel,
        grid_spec=pltpu.PrefetchScalarGridSpec(
            num_scalar_prefetch=1,
            grid=(2,),
            in_specs=[rows, rows, pl.BlockSpec((depth, width), lambda i, place: (0, 0))],
            out_specs=pl.BlockSpec((8, 32, width), lambda i, place: (0, i, 0)),
        ),
        out_shape=jax.ShapeDtypeStruct((8, IMG, width), BF),
        compiler_params=pltpu.CompilerParams(vmem_limit_bytes=VMEM_LIMIT),
        cost_estimate=LIGHT,
        name="partial_images",
    )(place, got, swapped, weight)


def image_kernel(
    place, pieces_ref, bias_ref, gain_ref, weight_ref, hidden_ref, swap_ref, same_ref, scaled, pair
):
    step = pl.program_id(0)

    @pl.when(step == 0)
    def _():
        total = pieces_ref[0].astype(F32)
        for k in range(1, 8):
            total = total + pieces_ref[k].astype(F32)
        total = total + bias_ref[...].astype(F32)
        image_hidden = (0.5 * total * (1.0 + lax.erf(total * (0.5**0.5)))).astype(BF)
        hidden_ref[...] = image_hidden
        hidden = image_hidden.astype(F32)
        scaled[...] = (hidden * gain_ref[...].astype(F32)).astype(BF)
        squared = hidden * hidden
        lanes = squared[:, 0:128]
        for k in range(1, 8):
            lanes = lanes + squared[:, k * 128 : (k + 1) * 128]
        lanes = jnp.concatenate([lanes, jnp.zeros_like(lanes)], axis=0)
        summed = jnp.sum(lanes.T, axis=0, keepdims=True)
        high, low = split_pair(summed)
        picked = lax.broadcasted_iota(jnp.int32, (16, 128), 0)
        rows = jnp.where(picked == 0, high.astype(F32), jnp.where(picked == 1, low.astype(F32), 0.0))
        pair[...] = jnp.concatenate([rows, jnp.zeros_like(rows)], axis=1).astype(BF)

    product = jnp.dot(scaled[...], weight_ref[...], preferred_element_type=F32).astype(BF)
    block = jnp.concatenate([product, pair[...]], axis=0)

    @pl.when(step < 4)
    def _():
        swap_ref[0] = block

    @pl.when(step >= 4)
    def _():
        same_ref[0] = block


def image_rows_kv(place, pieces, bias, gain, kv_w):
    def column(i, place):
        core = jnp.where(i < 4, 1 - place[1], place[1])
        return (0, 2 * lax.rem(place[2] + i, 4) + core)

    width = pieces.shape[2]
    row = pl.BlockSpec((1, width), lambda i, place: (0, 0))
    out = jax.ShapeDtypeStruct((4, IMG_TALL, 256), BF)
    return pl.pallas_call(
        image_kernel,
        grid_spec=pltpu.PrefetchScalarGridSpec(
            num_scalar_prefetch=1,
            grid=(8,),
            in_specs=[
                pl.BlockSpec((8, IMG, width), lambda i, place: (0, 0, 0)),
                row,
                row,
                pl.BlockSpec((width, 256), column),
            ],
            out_specs=[
                pl.BlockSpec((IMG, width), lambda i, place: (0, 0)),
                pl.BlockSpec((1, IMG_TALL, 256), lambda i, place: (jnp.minimum(i, 3), 0, 0)),
                pl.BlockSpec((1, IMG_TALL, 256), lambda i, place: (jnp.maximum(i - 4, 0), 0, 0)),
            ],
            scratch_shapes=[pltpu.VMEM((IMG, width), BF), pltpu.VMEM((16, 256), BF)],
        ),
        out_shape=[jax.ShapeDtypeStruct((IMG, width), BF), out, out],
        compiler_params=pltpu.CompilerParams(vmem_limit_bytes=VMEM_LIMIT),
        cost_estimate=LIGHT,
        name="image_rows_kv",
    )(place, pieces, bias, gain, kv_w)


def pair_kernel(same_ref, received_ref, *out_refs):
    for j, out_ref in enumerate(out_refs):
        total = same_ref[j].astype(F32) + received_ref[j].astype(F32)
        out_ref[0:IMG, :] = total[0:IMG].astype(BF)
        high, low = split_pair(total[IMG : IMG + 1] + total[IMG + 1 : IMG + 2])
        picked = lax.broadcasted_iota(jnp.int32, (16, 256), 0)
        rows = jnp.where(picked == 0, high.astype(F32), jnp.where(picked == 1, low.astype(F32), 0.0))
        out_ref[IMG:, :] = rows.astype(BF)


def pair_images(same, received):
    return pl.pallas_call(
        pair_kernel,
        out_shape=[jax.ShapeDtypeStruct((IMG_TALL, 256), BF)] * 4,
        cost_estimate=LIGHT,
        name="pair_images",
    )(same, received)


def close_kernel(a_ref, b_ref, c_ref, d_ref, labels_ref, out_ref):
    total = a_ref[...].astype(F32) + b_ref[...].astype(F32)
    total = total + c_ref[...].astype(F32) + d_ref[...].astype(F32)
    squares = total[IMG : IMG + 1, 0:128] + total[IMG + 1 : IMG + 2, 0:128]
    scale = lax.rsqrt(squares / D + 1e-05)
    scale = jnp.where(labels_ref[3:4, 0:128].astype(F32) > 0.5, scale, 0.0)
    tile = jnp.broadcast_to(scale, (128, 128)).T[0:IMG]
    tile = jnp.concatenate([tile, tile], axis=1)
    out_ref[0:IMG, :] = jnp.where(tile > 0.0, total[0:IMG] * tile, 0.0).astype(BF)
    out_ref[IMG:, :] = labels_ref[...]


def close_images(parts, labels):
    return pl.pallas_call(
        close_kernel,
        out_shape=jax.ShapeDtypeStruct((IMG_TALL, 256), BF),
        cost_estimate=LIGHT,
        name="close_images",
    )(*parts, labels)


def merge_kernel(
    place, own_ref, other_ref, first_ref, second_ref, near_ref, yonder_ref, side_ref, far_ref, out_ref
):
    step = pl.program_id(0)
    match = jnp.where(place[0] == 0, step, place[3]).astype(F32)
    shard = jnp.where(place[0] == 0, place[3], step)
    level = lax.rem(place[3] - shard + 8, 4)
    close = (shard >= 4) == (place[3] >= 4)
    images = []
    for near, away in ((near_ref, yonder_ref), (side_ref, far_ref)):
        images.append(jnp.where(close, near[level].astype(F32), away[level].astype(F32)))
    targets = []
    for image in images:
        owner = image[IMG : IMG + 1, 0:IMG]
        spot = image[IMG + 1 : IMG + 2, 0:IMG] * PAGE + image[IMG + 2 : IMG + 3, 0:IMG]
        targets.append(jnp.where(owner == match, spot, -1.0))
    target = jnp.concatenate(targets, axis=1)
    data = jnp.concatenate([images[0][0:IMG], images[1][0:IMG]], axis=0).astype(BF)
    spots = lax.broadcasted_iota(jnp.int32, (CAP * PAGE, 2 * IMG), 0).astype(F32)
    chosen = (spots == target).astype(F32).astype(BF)
    image = jnp.dot(chosen, data, preferred_element_type=F32)
    taken = jnp.dot(chosen, jnp.ones((2 * IMG, 256), BF), preferred_element_type=F32)

    def write(left, right):
        text = jnp.concatenate([left.reshape(CAP * PAGE, 128), right.reshape(CAP * PAGE, 128)], axis=1)
        merged = jnp.where(taken > 0.5, image, text.astype(F32)).astype(BF)
        out_ref[...] = merged.reshape(CAP, PAGE, 256)

    @pl.when(place[0] == 0)
    def _():
        write(own_ref[0], other_ref[...])

    @pl.when(place[0] != 0)
    def _():
        write(first_ref[0], second_ref[0])


def merge_slots(place, own, other, arrived, images):
    def local(i, place):
        return jnp.where(place[0] == 0, i, 7)

    def remote(i, place):
        return jnp.where(place[0] == 0, 0, i)

    image_spec = pl.BlockSpec((4, IMG_TALL, 256), lambda i, place: (0, 0, 0))
    return pl.pallas_call(
        merge_kernel,
        grid_spec=pltpu.PrefetchScalarGridSpec(
            num_scalar_prefetch=1,
            grid=(8,),
            in_specs=[
                pl.BlockSpec((1, CAP, PAGE, 128), lambda i, place: (1, local(i, place), 0, 0)),
                pl.BlockSpec((CAP, PAGE, 128), lambda i, place: (local(i, place), 0, 0)),
                pl.BlockSpec((1, CAP, PAGE, 128), lambda i, place: (0, remote(i, place), 0, 0)),
                pl.BlockSpec((1, CAP, PAGE, 128), lambda i, place: (1, remote(i, place), 0, 0)),
            ]
            + [image_spec] * 4,
            out_specs=pl.BlockSpec((CAP, PAGE, 256), lambda i, place: (i, 0, 0)),
        ),
        out_shape=jax.ShapeDtypeStruct((256, PAGE, 256), BF),
        compiler_params=pltpu.CompilerParams(vmem_limit_bytes=VMEM_LIMIT),
        cost_estimate=LIGHT,
        name="merge_slots",
    )(place, own, other, arrived, arrived, *images)


def attend(queries, kv_cache, new_kv, cache_lengths):
    row_count = queries.shape[0]
    heads_kv = kv_cache.shape[2] // (2 * HEAD)
    grouped = queries.reshape(row_count, heads_kv, queries.shape[1] // (HEAD * heads_kv), HEAD)
    stored = kv_cache.reshape(row_count, kv_cache.shape[1], heads_kv, 2 * HEAD)
    fresh_kv = new_kv.reshape(row_count, heads_kv, 2 * HEAD)
    scores = jnp.einsum(
        "rgqh,rjgh->rgqj", grouped, stored[..., :HEAD], preferred_element_type=jnp.float32
    ) * HEAD ** (-0.5)
    in_cache = jnp.arange(stored.shape[1], dtype=jnp.int32)[None, :] < cache_lengths[:, None]
    scores = jnp.where(in_cache[:, None, None, :], scores, -1e30)
    own_score = jnp.einsum(
        "rgqh,rgh->rgq", grouped, fresh_kv[..., :HEAD], preferred_element_type=jnp.float32
    ) * HEAD ** (-0.5)
    row_max = jnp.maximum(jnp.max(scores, axis=3), own_score)
    weights = jnp.exp(scores - row_max[..., None])
    own_weight = jnp.exp(own_score - row_max)
    denominator = jnp.sum(weights, axis=3) + own_weight
    probability = (weights / denominator[..., None]).astype(jnp.bfloat16)
    own_prob = lax.optimization_barrier((own_weight / denominator).astype(jnp.bfloat16)).astype(
        jnp.float32
    )
    attended = jnp.einsum(
        "rgqj,rjgh->rgqh", probability, stored[..., HEAD:], preferred_element_type=jnp.float32
    )
    attended = attended + own_prob[..., None] * fresh_kv[:, :, None, HEAD:].astype(jnp.float32)
    return attended.astype(jnp.bfloat16).reshape(row_count, queries.shape[1])


PARTNER = [(i, i ^ 1) for i in range(8)]


def shift(k):
    return [(i, (i + 2 * k) % 8) for i in range(8)]


def seq_shift(y, z):
    return [(i, (i // 4 + y) % 2 * 4 + (i + z) % 4) for i in range(8)]


FAR = [(g * 8 + i, (1 - g) * 8 + (i + 4) % 8) for g in range(2) for i in range(8)]


def after(value, other):
    return lax.optimization_barrier((value, other))[0]


def per_device(
    embeds,
    image_feats,
    image_pos,
    proj_w,
    proj_b,
    norm_gain,
    kv_w,
    prompt_lengths,
    page_owner,
    queries,
    kv_cache,
    new_kv,
    cache_lengths,
):
    group = lax.axis_index("group").astype(jnp.int32)
    seq = lax.axis_index("seq").astype(jnp.int32)
    mp = lax.axis_index("mp").astype(jnp.int32)
    core, x = mp % 2, mp // 2
    place = jnp.stack([group, core, x, seq])
    gain = norm_gain.reshape(1, -1)

    bias = proj_b.reshape(1, -1)

    owners = page_owner[:, 0]
    before = (
        jnp.arange(PAGES, dtype=jnp.int32)[None, :] < jnp.arange(PAGES, dtype=jnp.int32)[:, None]
    )
    page_rank = jnp.sum((before & (owners[:, None] == owners[None, :])).astype(jnp.int32), axis=1)
    slots = owners * CAP + page_rank
    live = jnp.sum(jnp.where(jnp.arange(4, dtype=jnp.int32) == seq // 2, prompt_lengths, 0))
    limit = live - (seq % 2) * ROWS
    local_pos = lax.dynamic_slice(image_pos, (group * IMG,), (IMG,)) - seq * ROWS
    at_page = (local_pos // PAGE)[:, None] == jnp.arange(PAGES, dtype=jnp.int32)[None, :]
    image_owner = jnp.sum(jnp.where(at_page, owners[None, :], 0), axis=1)
    image_rank = jnp.sum(jnp.where(at_page, page_rank[None, :], 0), axis=1)
    labels = jnp.stack(
        [image_owner, image_rank, local_pos % PAGE, (local_pos < limit).astype(jnp.int32)]
    ).astype(BF)
    labels = jnp.pad(labels, ((0, 12), (0, 256 - IMG)))

    got = lax.all_to_all(cut_features(place, image_feats), "seq", 0, 0, tiled=True)

    send, keep, _ = project_text(place, embeds, gain, kv_w, (1, 3))
    received = lax.ppermute(send, "mp", PARTNER)
    got = after(got, keep)
    swapped = lax.ppermute(got, "mp", PARTNER)
    added = [None] * 4
    parts = [None] * 4
    for k, j in enumerate((1, 3)):
        added[j] = add_pair(keep, received, k)
        parts[j] = lax.ppermute(added[j], "mp", shift(j))
    send, keep, _ = project_text(place, after(embeds, (added[1], added[3])), gain, kv_w, (2, 0))
    received = lax.ppermute(send, "mp", PARTNER)
    for k, j in enumerate((2, 0)):
        added[j] = add_pair(keep, received, k)
    parts[2] = lax.ppermute(added[2], "mp", shift(2))
    parts[0] = added[0]

    swapped = after(swapped, (added[2], added[0]))
    partial = partial_images(place, got, swapped, proj_w)
    attended = lax.cond(
        group != 0,
        attend,
        lambda *unused: jnp.zeros(queries.shape, BF),
        after(queries, partial),
        kv_cache,
        new_kv,
        cache_lengths,
    )
    pieces = lax.all_to_all(partial, "seq", 0, 0, tiled=True)
    pieces = after(pieces, attended)
    image_hidden, swap, same = image_rows_kv(place, pieces, bias, gain, kv_w)
    image_pairs = pair_images(same, lax.ppermute(swap, "mp", PARTNER))
    image_parts = [image_pairs[0]]
    image_parts += [lax.ppermute(image_pairs[j], "mp", shift(j)) for j in (1, 2, 3)]

    rows, by_owner = finish_text(slots, limit.reshape(1), parts)
    other_rows = lax.ppermute(rows, "group", [(1, 0)])
    arrived = lax.all_to_all(
        by_owner.reshape(512, PAGE, 128), ("group", "seq"), split_axis=0, concat_axis=0, tiled=True
    ).reshape(2, 256, PAGE, 128)

    image_parts = after(image_parts, by_owner)
    image_block = close_images(image_parts, labels)
    near = jnp.stack(
        [image_block] + [lax.ppermute(image_block, "seq", seq_shift(0, k)) for k in (1, 2, 3)]
    )
    images = [
        near,
        lax.ppermute(near, "seq", seq_shift(1, 0)),
        lax.ppermute(near, "group", [(0, 1), (1, 0)]),
        lax.ppermute(near, ("group", "seq"), FAR),
    ]
    other = place_pages(slots, other_rows)
    page_slots = merge_slots(place, by_owner, other, arrived, images)

    other_hidden = lax.ppermute(image_hidden, "group", [(1, 0)])
    row_states = jnp.where(
        group == 0, jnp.concatenate([image_hidden, other_hidden], axis=0), attended
    )
    return (page_slots, row_states)


def solution(mesh):
    in_specs = (
        P("seq", "mp"),
        P("seq", None),
        P("seq"),
        P("seq", "mp"),
        P("mp"),
        P("mp"),
        P("mp", None),
        P(),
        P("seq", None),
        P("seq", "mp"),
        P("seq", None, "mp"),
        P("seq", "mp"),
        P("seq"),
    )
    out_specs = (P(("group", "seq"), None, "mp"), P(("group", "seq"), "mp"))
    return jax.shard_map(
        per_device, mesh=mesh, in_specs=in_specs, out_specs=out_specs, check_vma=False
    )
```

time: 198 us -> 170 us (0.86)
  the two profiles are of different devices: /device:TPU:26 before, /device:TPU:10 now
where the time goes in v2:
time: 170 us; the launch traced here: 167 us
  Pallas kernels  59.3 us (35%)
  waiting for transfers between devices  32.8 us (19%)
  starting transfers between devices  31.3 us (18%)
  blocking collectives  19 us (11%)
  local copies, waits for them, and re-layouts  9.12 us (5%)
  matrix products  8.28 us (5%)
  other arithmetic  5.94 us (3%)
    all_to_all x1, blocking collectives, per_device(): lax.all_to_all(cut_features(place, image_feats), 'seq', 0, 0, tiled=True)  19 us
    pallas_call x2, Pallas kernels, project_text(): pl.pallas_call(functools.partial(project_kernel, count), grid_spec=pltpu....  17.5 us
    ppermute x1, waiting for transfers between devices, per_device(): parts[2] = lax.ppermute(added[2], 'mp', shift(2))  11.9 us
    ppermute x2, waiting for transfers between devices, per_device(): parts[j] = lax.ppermute(added[j], 'mp', shift(j))  9.68 us
    pallas_call x1, Pallas kernels, merge_slots(): pl.pallas_call(merge_kernel, grid_spec=pltpu.PrefetchScalarGridSpec(num_s...  8.29 us
    all_to_all x1, starting transfers between devices, per_device(): lax.all_to_all(by_owner.reshape(512, PAGE, 128), ('group', 'seq'), split_...  8.15 us
    pallas_call x4, Pallas kernels, add_pair(): pl.pallas_call(add_kernel, grid=(2,), in_specs=[spec, spec], out_specs=pl...  7.99 us
    pallas_call x1, Pallas kernels, image_rows_kv(): pl.pallas_call(image_kernel, grid_spec=pltpu.PrefetchScalarGridSpec(num_s...  7.94 us
  transfers between devices with their start and end apart: 20, of which 10 were waited for; matrix products, arithmetic and copies ran while one was open for 9% of the time, Pallas kernels for 15%

profile of v2, /device:TPU:10, one launch (start us, length us, event | category | flops | bytes accessed | tf_op | source)
XLA Modules:
  0.0 167.4 jit_solution(17783245393482756558)
XLA Ops:
  2.6 8.8 %project_text.2 = (bf16[2,2080,128]{2,1,0:T(8,128)(2,1)}, bf16[2,2080,128]{2,1,0:T(8,128)(2,1)}, f32[8,128]{1,0:T(8,128)}) custom-call(s32[4]{0:T(128)} %pad_add_fusion.place, bf16[2048,1024]{1,0:T(8,128)(2,1)} %embeds_ref.2, bf16[1,1024]{1,0:T(2,128)(2,1)} %reshape.118.gain_ref, bf16[1024,2048]{1,0:T(8,128)(2,1)} %weight_ref.3, ...), custom_call_target="tpu_custom_call" | custom-call | flops 1 | bytes 1 | tf_op jit(solution)/shard_map/project_text/pallas_call | solution.py:80
  11.4 2.9 %collective-permute-done.b_ref = bf16[2,2080,128]{2,1,0:T(8,128)(2,1)S(1)} collective-permute-done((bf16[2,2080,128]{2,1,0:T(8,128)(2,1)}, bf16[2,2080,128]{2,1,0:T(8,128)(2,1)S(1)}, u32[]{:S(2)}, u32[]{:S(2)}) %collective-permute-start) | collective-permute-done | bytes 1064992 | tf_op jit(solution)/shard_map/ppermute | solution.py:519
  15.3 2.0 %add_pair.5 = bf16[2080,128]{1,0:T(8,128)(2,1)} custom-call(bf16[2,2080,128]{2,1,0:T(8,128)(2,1)} %get-tuple-element.39.a_ref, bf16[2,2080,128]{2,1,0:T(8,128)(2,1)} %copy-done.2), custom_call_target="tpu_custom_call" | custom-call | flops 1 | bytes 1 | tf_op jit(solution)/shard_map/add_pair/pallas_call | solution.py:113
  17.3 2.0 %add_pair.4 = bf16[2080,128]{1,0:T(8,128)(2,1)} custom-call(bf16[2,2080,128]{2,1,0:T(8,128)(2,1)} %get-tuple-element.39.a_ref, bf16[2,2080,128]{2,1,0:T(8,128)(2,1)} %copy-done.2), custom_call_target="tpu_custom_call" | custom-call | flops 1 | bytes 1 | tf_op jit(solution)/shard_map/add_pair/pallas_call | solution.py:113
  19.2 8.8 %project_text.3 = (bf16[2,2080,128]{2,1,0:T(8,128)(2,1)}, bf16[2,2080,128]{2,1,0:T(8,128)(2,1)}, f32[8,128]{1,0:T(8,128)}) custom-call(s32[4]{0:T(128)} %pad_add_fusion.place, bf16[2048,1024]{1,0:T(8,128)(2,1)} %embeds_ref.2, bf16[1,1024]{1,0:T(2,128)(2,1)} %reshape.118.gain_ref, bf16[1024,2048]{1,0:T(8,128)(2,1)} %weight_ref.3, ...), custom_call_target="tpu_custom_call" | custom-call | flops 1 | bytes 1 | tf_op jit(solution)/shard_map/project_text/pallas_call | solution.py:80
  28.2 2.7 %cut_features.1 = bf16[8,32,912]{2,1,0:T(8,128)(2,1)} custom-call(s32[4]{0:T(128)} %pad_add_fusion.place, bf16[128,7296]{1,0:T(8,128)(2,1)} %feats_ref.1), custom_call_target="tpu_custom_call" | custom-call | flops 1 | bytes 1 | tf_op jit(solution)/shard_map/cut_features/pallas_call | solution.py:200
  30.9 19.0 %all_to_all.15.got_ref = bf16[8,32,912]{2,1,0:T(8,128)(2,1)S(1)} all-to-all(bf16[8,32,912]{2,1,0:T(8,128)(2,1)} %cut_features.1), channel_id=1, replica_groups=mesh['group'=2,'seq'=8,'mp'=8] {'seq'}, dimensions={0} | all-to-all | bytes 933888 | tf_op jit(solution)/shard_map/all_to_all | solution.py:516
  50.9 2.0 %add_pair.7 = bf16[2080,128]{1,0:T(8,128)(2,1)} custom-call(bf16[2,2080,128]{2,1,0:T(8,128)(2,1)} %get-tuple-element.42.a_ref, bf16[2,2080,128]{2,1,0:T(8,128)(2,1)} %copy-done.1), custom_call_target="tpu_custom_call" | custom-call | flops 1 | bytes 1 | tf_op jit(solution)/shard_map/add_pair/pallas_call | solution.py:113
  52.9 2.1 %add_pair.6.a_ref = bf16[2080,128]{1,0:T(8,128)(2,1)} custom-call(bf16[2,2080,128]{2,1,0:T(8,128)(2,1)} %get-tuple-element.42.a_ref, bf16[2,2080,128]{2,1,0:T(8,128)(2,1)} %copy-done.1), custom_call_target="tpu_custom_call" | custom-call | flops 1 | bytes 1 | tf_op jit(solution)/shard_map/add_pair/pallas_call | solution.py:113
  55.9 4.8 %partial_images.1 = bf16[8,64,1024]{2,1,0:T(8,128)(2,1)} custom-call(s32[4]{0:T(128)} %pad_add_fusion.place, bf16[8,32,912]{2,1,0:T(8,128)(2,1)} %copy-done.4, bf16[8,32,912]{2,1,0:T(8,128)(2,1)} %copy-done.9, bf16[912,1024]{1,0:T(8,128)(2,1)} %weight_ref.2), custom_call_target="tpu_custom_call" | custom-call | flops 1 | bytes 1 | tf_op jit(solution)/shard_map/partial_images/pallas_call | solution.py:236
  60.6 3.7 %all-to-all-start.2 = ((bf16[8,64,1024]{2,1,0:T(8,128)(2,1)}), bf16[8,64,1024]{2,1,0:T(8,128)(2,1)S(1)}, u32[]{:S(2)}, u32[]{:S(2)}) async-start(bf16[8,64,1024]{2,1,0:T(8,128)(2,1)} %partial_images.1), calls=%async_computation.2 | async-start | bytes 2097152 | tf_op jit(solution)/shard_map/all_to_all | solution.py:545
  64.4 1.6 collective-permute-start.2
  66.5 2.1 %collective-permute-start.3 = (bf16[2080,128]{1,0:T(8,128)(2,1)S(1)}, bf16[2080,128]{1,0:T(8,128)(2,1)}, u32[]{:S(2)}, u32[]{:S(2)}) collective-permute-start(bf16[2080,128]{1,0:T(8,128)(2,1)S(1)} %copy-done.8), channel_id=1, source_target_pairs={{0,4},{1,5},{2,6},{3,7},{4,0},{5,1},{6,2},{7,3},{8,12},{9,13},{10,... | collective-permute-start | bytes 1597448 | tf_op jit(solution)/shard_map/ppermute | solution.py:531
  70.7 8.8 %collective-permute-done.2.b_ref = bf16[2080,128]{1,0:T(8,128)(2,1)} collective-permute-done((bf16[2080,128]{1,0:T(8,128)(2,1)S(1)}, bf16[2080,128]{1,0:T(8,128)(2,1)}, u32[]{:S(2)}, u32[]{:S(2)}) %collective-permute-start.2) | collective-permute-done | bytes 532512 | tf_op jit(solution)/shard_map/ppermute | solution.py:526
  80.3 11.9 %collective-permute-done.3.c_ref = bf16[2080,128]{1,0:T(8,128)(2,1)} collective-permute-done((bf16[2080,128]{1,0:T(8,128)(2,1)S(1)}, bf16[2080,128]{1,0:T(8,128)(2,1)}, u32[]{:S(2)}, u32[]{:S(2)}) %collective-permute-start.3) | collective-permute-done | bytes 532512 | tf_op jit(solution)/shard_map/ppermute | solution.py:531
  92.3 3.9 %finish_text.1 = (bf16[128,16,128]{2,1,0:T(8,128)(2,1)}, bf16[2,256,16,128]{3,2,1,0:T(8,128)(2,1)}) custom-call(s32[128]{0:T(128)} %multiply_add_fusion.slots, s32[1]{0:T(128)} %bitcast.16.limit, bf16[2080,128]{1,0:T(8,128)(2,1)} %add_pair.6.a_ref, bf16[2080,128]{1,0:T(8,128)(2,1)} %collective-permute-done.2.b_ref, ...), custom_call_target="tpu_custom_call" | custom-call | flops 1 | bytes 1 | tf_op jit(solution)/shard_map/finish_text/pallas_call | solution.py:149
  96.2 8.1 %all-to-all-start = ((bf16[512,16,128]{2,1,0:T(8,128)(2,1)}), bf16[512,16,128]{2,1,0:T(8,128)(2,1)S(1)}, u32[]{:S(2)}, u32[]{:S(2)}) async-start(bf16[512,16,128]{2,1,0:T(8,128)(2,1)} %bitcast.64), calls=%async_computation | async-start | bytes 4194304 | tf_op jit(solution)/shard_map/all_to_all | solution.py:554
  105.2 9.9 %conditional.1 = (bf16[128,1024]{1,0:T(8,128)(2,1)S(1)}) conditional(s32[]{:T(128)} %convert_element_type.37, () %tuple.23, (s32[128]{0:T(128)S(1)}, bf16[128,1024]{1,0:T(8,128)(2,1)}, bf16[128,128,256]{2,1,0:T(8,128)(2,1)}, bf16[128,256]{1,0:T(8,128)(2,1)S(1)}) %tuple.38), branch_computations={%region_2.3_spmd, %region_3.6_spmd} | conditional | flops 68852736 | bytes 12157448 | solution.py:536
  106.7 4.5 %fusion.32 = (f32[128,8]{1,0:T(8,128)S(1)}, f32[128,8,128]{2,1,0:T(8,128)S(1)}) fusion(bf16[128,8,128]{2,1,0:T(8,128)(2,1)S(1)} %bitcast.68, bf16[128,128,1,256]{3,1,0,2:T(8,128)(2,1)} %bitcast.65, pred[128,128]{1,0:T(8,128)(4,1)S(1)} %iota_compare_fusion), kind=kOutput, calls=%fused_computation.65 | convolution fusion | flops 33946624 | bytes 5001216 | tf_op jit(solution)/shard_map/cond/branch_1_fun/rgqh,rjgh->rgqj/dot_general | solution.py:434
  111.7 3.5 %fusion.5 = bf16[128,8,128]{2,1,0:T(8,128)(2,1)S(1)} fusion(bf16[128,128,1,256]{3,1,0,2:T(8,128)(2,1)} %bitcast.66, f32[128,8,128]{2,1,0:T(8,128)S(1)} %get-tuple-element.76, f32[128,128]{1,0:T(8,128)S(1)} %get-tuple-element.74, f32[128,8]{1,0:T(8,128)S(1)} %bitcast_convert_fusion, f32[128,8]{1,0:T(8,128)S(1)} %get-tuple-element.71, ...), kind=kOutput, calls=%fused_computation.7 | convolution fusion | flops 34340864 | bytes 5058560 | tf_op jit(solution)/shard_map/cond/branch_1_fun/rgqj,rjgh->rgqh/dot_general | solution.py:450
  116.5 7.9 %image_rows_kv.1 = (bf16[64,1024]{1,0:T(8,128)(2,1)}, bf16[4,80,256]{2,1,0:T(8,128)(2,1)}, bf16[4,80,256]{2,1,0:T(8,128)(2,1)}) custom-call(s32[4]{0:T(128)} %pad_add_fusion.place, bf16[8,64,1024]{2,1,0:T(8,128)(2,1)} %copy-done.3, bf16[1,1024]{1,0:T(2,128)(2,1)} %reshape.121.bias_ref, bf16[1,1024]{1,0:T(2,128)(2,1)} %reshape.118.gain_ref, ...), custom_call_target="tpu_custom_call" | custom-call | flops 1 | bytes 1 | tf_op jit(solution)/shard_map/image_rows_kv/pallas_call | solution.py:297
  124.5 1.6 collective-permute-done.7.received_ref
  126.7 1.7 pair_images.1
  128.4 2.9 %collective-permute-start.9 = (bf16[80,256]{1,0:T(8,128)(2,1)}, bf16[80,256]{1,0:T(8,128)(2,1)S(1)}, u32[]{:S(2)}, u32[]{:S(2)}) collective-permute-start(bf16[80,256]{1,0:T(8,128)(2,1)} %get-tuple-element.54), channel_id=1, source_target_pairs={{0,4},{1,5},{2,6},{3,7},{4,0},{5,1},{6,2},{7,3},{8,12},{9,13},{10,... | collective-permute-start | bytes 122888 | tf_op jit(solution)/shard_map/ppermute | solution.py:550
  131.3 1.4 collective-permute-start.10
  136.2 1.6 close_images.1
  137.7 2.7 %collective-permute-start.13 = (bf16[80,256]{1,0:T(8,128)(2,1)}, bf16[80,256]{1,0:T(8,128)(2,1)S(1)}, u32[]{:S(2)}, u32[]{:S(2)}) collective-permute-start(bf16[80,256]{1,0:T(8,128)(2,1)} %close_images.1), channel_id=1, source_target_pairs={{0,24},{8,0},{16,8},{24,16},{32,56},{40,32},{48,40},{56,48},{1,25}... | collective-permute-start | bytes 122888 | tf_op jit(solution)/shard_map/ppermute | solution.py:561
  143.4 2.7 %collective-permute-done.12 = bf16[80,256]{1,0:T(8,128)(2,1)S(1)} collective-permute-done((bf16[80,256]{1,0:T(8,128)(2,1)}, bf16[80,256]{1,0:T(8,128)(2,1)S(1)}, u32[]{:S(2)}, u32[]{:S(2)}) %collective-permute-start.12) | collective-permute-done | bytes 40992 | tf_op jit(solution)/shard_map/ppermute | solution.py:561
  147.6 3.2 %collective-permute-start.15 = (bf16[4,80,256]{2,1,0:T(8,128)(2,1)S(1)}, bf16[4,80,256]{2,1,0:T(8,128)(2,1)S(1)}, u32[]{:S(2)}, u32[]{:S(2)}) collective-permute-start(bf16[4,80,256]{2,1,0:T(8,128)(2,1)S(1)} %pad_maximum_fusion.near_ref), channel_id=1, source_target_pairs={{0,64},{64,0},{1,65},{65,1},{2,66},{66,2},{3,67},{67,3},{4,68},{68... | collective-permute-start | bytes 491528 | tf_op jit(solution)/shard_map/ppermute | solution.py:566
  151.1 1.7 maximum_select_fusion
  153.5 2.9 %place_pages.1.other_ref = bf16[256,16,128]{2,1,0:T(8,128)(2,1)} custom-call(s32[128]{0:T(128)} %multiply_add_fusion.slots, bf16[128,16,128]{2,1,0:T(8,128)(2,1)} %copy-done.10), custom_call_target="tpu_custom_call" | custom-call | flops 1 | bytes 1 | tf_op jit(solution)/shard_map/place_pages/pallas_call | solution.py:177
  159.1 8.3 %merge_slots.1 = bf16[256,16,256]{2,1,0:T(8,128)(2,1)} custom-call(s32[4]{0:T(128)} %pad_add_fusion.place, bf16[2,256,16,128]{3,2,1,0:T(8,128)(2,1)} %get-tuple-element.44.own_ref, bf16[256,16,128]{2,1,0:T(8,128)(2,1)} %place_pages.1.other_ref, bf16[2,256,16,128]{3,2,1,0:T(8,128)(2,1)} %bitcast.62, bf16[2,256,16,128]{3,2,1,0:T(8,128)(2,1)} %bitcast.63, ...), custom_call_target="tpu_custom_call" | custom-call | flops 1 | bytes 1 | tf_op jit(solution)/shard_map/merge_slots/pallas_call | solution.py:407
  (95 shorter events, 24.1 us)
Async XLA Ops:
  11.3 3.0 %collective-permute-start = (bf16[2,2080,128]{2,1,0:T(8,128)(2,1)}, bf16[2,2080,128]{2,1,0:T(8,128)(2,1)S(1)}, u32[]{:S(2)}, u32[]{:S(2)}) collective-permute-start(bf16[2,2080,128]{2,1,0:T(8,128)(2,1)} %get-tuple-element.40), channel_id=1, source_target_pairs={{0,1},{1,0},{2,3},{3,2},{4,5},{5,4},{6,7},{7,6},{8,9},{9,8},{10,11... | collective-permute-start | bytes 3194888 | tf_op jit(solution)/shard_map/ppermute | solution.py:519
  28.0 22.0 %collective-permute-start.1 = (bf16[2,2080,128]{2,1,0:T(8,128)(2,1)}, bf16[2,2080,128]{2,1,0:T(8,128)(2,1)S(1)}, u32[]{:S(2)}, u32[]{:S(2)}) collective-permute-start(bf16[2,2080,128]{2,1,0:T(8,128)(2,1)} %get-tuple-element.43), channel_id=1, source_target_pairs={{0,1},{1,0},{2,3},{3,2},{4,5},{5,4},{6,7},{7,6},{8,9},{9,8},{10,11... | collective-permute-start | bytes 3194888 | tf_op jit(solution)/shard_map/ppermute | solution.py:528
  49.9 5.1 %copy-start.4 = (bf16[8,32,912]{2,1,0:T(8,128)(2,1)}, bf16[8,32,912]{2,1,0:T(8,128)(2,1)S(1)}, u32[]{:S(2)}) copy-start(bf16[8,32,912]{2,1,0:T(8,128)(2,1)S(1)} %all_to_all.15.got_ref) | copy-start | bytes 1400836
  49.9 5.1 %collective-permute-start.6 = (bf16[8,32,912]{2,1,0:T(8,128)(2,1)S(1)}, bf16[8,32,912]{2,1,0:T(8,128)(2,1)S(1)}, u32[]{:S(2)}, u32[]{:S(2)}) collective-permute-start(bf16[8,32,912]{2,1,0:T(8,128)(2,1)S(1)} %all_to_all.15.got_ref), channel_id=1, source_target_pairs={{0,1},{1,0},{2,3},{3,2},{4,5},{5,4},{6,7},{7,6},{8,9},{9,8},{10,11... | collective-permute-start | bytes 1400840 | tf_op jit(solution)/shard_map/ppermute | solution.py:521
  52.9 11.5 %copy-start.7 = (bf16[2080,128]{1,0:T(8,128)(2,1)S(1)}, bf16[2080,128]{1,0:T(8,128)(2,1)}, u32[]{:S(2)}) copy-start(bf16[2080,128]{1,0:T(8,128)(2,1)} %add_pair.4) | copy-start | bytes 1597444
  52.9 13.0 %copy-start.6 = (bf16[2080,128]{1,0:T(8,128)(2,1)S(1)}, bf16[2080,128]{1,0:T(8,128)(2,1)}, u32[]{:S(2)}) copy-start(bf16[2080,128]{1,0:T(8,128)(2,1)} %add_pair.5) | copy-start | bytes 1597444
  52.9 13.6 %copy-start.8 = (bf16[2080,128]{1,0:T(8,128)(2,1)S(1)}, bf16[2080,128]{1,0:T(8,128)(2,1)}, u32[]{:S(2)}) copy-start(bf16[2080,128]{1,0:T(8,128)(2,1)} %add_pair.7) | copy-start | bytes 1597444
  52.9 15.7 %copy-start.22 = (s32[4]{0:T(128)S(1)}, s32[4]{0:T(128)}, u32[]{:S(2)}) copy-start(s32[4]{0:T(128)} %param.22) | copy-start | bytes 52
  52.9 17.0 %copy-start.20 = (s32[128,1]{0,1:T(1,128)S(1)}, s32[128,1]{0,1:T(1,128)}, u32[]{:S(2)}) copy-start(s32[128,1]{0,1:T(1,128)} %param.23) | copy-start | bytes 1540
  60.6 43.7 %copy-start.18 = (bf16[1024]{0:T(1024)(128)(2,1)S(1)}, bf16[1024]{0:T(1024)(128)(2,1)}, u32[]{:S(2)}) copy-start(bf16[1024]{0:T(1024)(128)(2,1)} %param.19) | copy-start | bytes 6148
  60.6 44.3 %copy-start.19 = (s32[128]{0:T(128)S(1)}, s32[128]{0:T(128)}, u32[]{:S(2)}) copy-start(s32[128]{0:T(128)} %param.17) | copy-start | bytes 1540
  60.6 44.6 %copy-start.14 = (bf16[128,256]{1,0:T(8,128)(2,1)S(1)}, bf16[128,256]{1,0:T(8,128)(2,1)}, u32[]{:S(2)}) copy-start(bf16[128,256]{1,0:T(8,128)(2,1)} %param.26) | copy-start | bytes 196612
  60.6 44.6 %copy-start.21 = (s32[128]{0:T(128)S(1)}, s32[128]{0:T(128)}, u32[]{:S(2)}) copy-start(s32[128]{0:T(128)} %param.27) | copy-start | bytes 1540
  60.6 35.5 %all-to-all-start.2 = ((bf16[8,64,1024]{2,1,0:T(8,128)(2,1)}), bf16[8,64,1024]{2,1,0:T(8,128)(2,1)S(1)}, u32[]{:S(2)}, u32[]{:S(2)}) async-start(bf16[8,64,1024]{2,1,0:T(8,128)(2,1)} %partial_images.1), calls=%async_computation.2 | async-start | bytes 2097152 | tf_op jit(solution)/shard_map/all_to_all | solution.py:545
  64.4 15.1 %collective-permute-start.2 = (bf16[2080,128]{1,0:T(8,128)(2,1)S(1)}, bf16[2080,128]{1,0:T(8,128)(2,1)}, u32[]{:S(2)}, u32[]{:S(2)}) collective-permute-start(bf16[2080,128]{1,0:T(8,128)(2,1)S(1)} %copy-done.7), channel_id=1, source_target_pairs={{0,2},{1,3},{2,4},{3,5},{4,6},{5,7},{6,0},{7,1},{8,10},{9,11},{10,... | collective-permute-start | bytes 1597448 | tf_op jit(solution)/shard_map/ppermute | solution.py:526
  65.9 14.4 %collective-permute-start.4 = (bf16[2080,128]{1,0:T(8,128)(2,1)S(1)}, bf16[2080,128]{1,0:T(8,128)(2,1)}, u32[]{:S(2)}, u32[]{:S(2)}) collective-permute-start(bf16[2080,128]{1,0:T(8,128)(2,1)S(1)} %copy-done.6), channel_id=1, source_target_pairs={{0,6},{1,7},{2,0},{3,1},{4,2},{5,3},{6,4},{7,5},{8,14},{9,15},{10,... | collective-permute-start | bytes 1597448 | tf_op jit(solution)/shard_map/ppermute | solution.py:526
  66.5 25.8 %collective-permute-start.3 = (bf16[2080,128]{1,0:T(8,128)(2,1)S(1)}, bf16[2080,128]{1,0:T(8,128)(2,1)}, u32[]{:S(2)}, u32[]{:S(2)}) collective-permute-start(bf16[2080,128]{1,0:T(8,128)(2,1)S(1)} %copy-done.8), channel_id=1, source_target_pairs={{0,4},{1,5},{2,6},{3,7},{4,0},{5,1},{6,2},{7,3},{8,12},{9,13},{10,... | collective-permute-start | bytes 1597448 | tf_op jit(solution)/shard_map/ppermute | solution.py:531
  96.2 9.1 %copy-start.3 = (bf16[8,64,1024]{2,1,0:T(8,128)(2,1)}, bf16[8,64,1024]{2,1,0:T(8,128)(2,1)S(1)}, u32[]{:S(2)}) copy-start(bf16[8,64,1024]{2,1,0:T(8,128)(2,1)S(1)} %all-to-all-done.2.pieces_ref) | copy-start | bytes 3145732
  96.2 61.6 %all-to-all-start = ((bf16[512,16,128]{2,1,0:T(8,128)(2,1)}), bf16[512,16,128]{2,1,0:T(8,128)(2,1)S(1)}, u32[]{:S(2)}, u32[]{:S(2)}) async-start(bf16[512,16,128]{2,1,0:T(8,128)(2,1)} %bitcast.64), calls=%async_computation | async-start | bytes 4194304 | tf_op jit(solution)/shard_map/all_to_all | solution.py:554
  115.2 37.6 %collective-permute-start.5 = (bf16[128,16,128]{2,1,0:T(8,128)(2,1)}, bf16[128,16,128]{2,1,0:T(8,128)(2,1)S(1)}, u32[]{:S(2)}, u32[]{:S(2)}) collective-permute-start(bf16[128,16,128]{2,1,0:T(8,128)(2,1)} %get-tuple-element.45), channel_id=1, source_target_pairs={{64,0},{65,1},{66,2},{67,3},{68,4},{69,5},{70,6},{71,7},{72,8},{73... | collective-permute-start | bytes 1572872 | tf_op jit(solution)/shard_map/ppermute | solution.py:553
  124.5 1.6 collective-permute-start.7
  128.4 4.9 %collective-permute-start.8 = (bf16[80,256]{1,0:T(8,128)(2,1)}, bf16[80,256]{1,0:T(8,128)(2,1)S(1)}, u32[]{:S(2)}, u32[]{:S(2)}) collective-permute-start(bf16[80,256]{1,0:T(8,128)(2,1)} %get-tuple-element.53), channel_id=1, source_target_pairs={{0,2},{1,3},{2,4},{3,5},{4,6},{5,7},{6,0},{7,1},{8,10},{9,11},{10,... | collective-permute-start | bytes 122888 | tf_op jit(solution)/shard_map/ppermute | solution.py:550
  128.4 6.1 %collective-permute-start.9 = (bf16[80,256]{1,0:T(8,128)(2,1)}, bf16[80,256]{1,0:T(8,128)(2,1)S(1)}, u32[]{:S(2)}, u32[]{:S(2)}) collective-permute-start(bf16[80,256]{1,0:T(8,128)(2,1)} %get-tuple-element.54), channel_id=1, source_target_pairs={{0,4},{1,5},{2,6},{3,7},{4,0},{5,1},{6,2},{7,3},{8,12},{9,13},{10,... | collective-permute-start | bytes 122888 | tf_op jit(solution)/shard_map/ppermute | solution.py:550
  131.3 4.2 %collective-permute-start.10 = (bf16[80,256]{1,0:T(8,128)(2,1)}, bf16[80,256]{1,0:T(8,128)(2,1)S(1)}, u32[]{:S(2)}, u32[]{:S(2)}) collective-permute-start(bf16[80,256]{1,0:T(8,128)(2,1)} %get-tuple-element.55), channel_id=1, source_target_pairs={{0,6},{1,7},{2,0},{3,1},{4,2},{5,3},{6,4},{7,5},{8,14},{9,15},{10,... | collective-permute-start | bytes 122888 | tf_op jit(solution)/shard_map/ppermute | solution.py:550
  137.7 5.7 %collective-permute-start.13 = (bf16[80,256]{1,0:T(8,128)(2,1)}, bf16[80,256]{1,0:T(8,128)(2,1)S(1)}, u32[]{:S(2)}, u32[]{:S(2)}) collective-permute-start(bf16[80,256]{1,0:T(8,128)(2,1)} %close_images.1), channel_id=1, source_target_pairs={{0,24},{8,0},{16,8},{24,16},{32,56},{40,32},{48,40},{56,48},{1,25}... | collective-permute-start | bytes 122888 | tf_op jit(solution)/shard_map/ppermute | solution.py:561
  140.4 5.7 %collective-permute-start.12 = (bf16[80,256]{1,0:T(8,128)(2,1)}, bf16[80,256]{1,0:T(8,128)(2,1)S(1)}, u32[]{:S(2)}, u32[]{:S(2)}) collective-permute-start(bf16[80,256]{1,0:T(8,128)(2,1)} %close_images.1), channel_id=1, source_target_pairs={{0,16},{8,24},{16,0},{24,8},{32,48},{40,56},{48,32},{56,40},{1,17}... | collective-permute-start | bytes 122888 | tf_op jit(solution)/shard_map/ppermute | solution.py:561
  141.3 5.4 %collective-permute-start.11 = (bf16[80,256]{1,0:T(8,128)(2,1)}, bf16[80,256]{1,0:T(8,128)(2,1)S(1)}, u32[]{:S(2)}, u32[]{:S(2)}) collective-permute-start(bf16[80,256]{1,0:T(8,128)(2,1)} %close_images.1), channel_id=1, source_target_pairs={{0,8},{8,16},{16,24},{24,0},{32,40},{40,48},{48,56},{56,32},{1,9},... | collective-permute-start | bytes 122888 | tf_op jit(solution)/shard_map/ppermute | solution.py:561
  142.1 8.9 %collective-permute-start.17 = (bf16[64,1024]{1,0:T(8,128)(2,1)}, bf16[64,1024]{1,0:T(8,128)(2,1)S(1)}, u32[]{:S(2)}, u32[]{:S(2)}) collective-permute-start(bf16[64,1024]{1,0:T(8,128)(2,1)} %get-tuple-element.60), channel_id=1, source_target_pairs={{64,0},{65,1},{66,2},{67,3},{68,4},{69,5},{70,6},{71,7},{72,8},{73... | collective-permute-start | bytes 393224 | tf_op jit(solution)/shard_map/ppermute | solution.py:572
  147.5 10.3 %copy-start.5 = (bf16[4,80,256]{2,1,0:T(8,128)(2,1)}, bf16[4,80,256]{2,1,0:T(8,128)(2,1)S(1)}, u32[]{:S(2)}) copy-start(bf16[4,80,256]{2,1,0:T(8,128)(2,1)S(1)} %pad_maximum_fusion.near_ref) | copy-start | bytes 491524
  147.5 9.0 %collective-permute-start.16 = (bf16[4,80,256]{2,1,0:T(8,128)(2,1)S(1)}, bf16[4,80,256]{2,1,0:T(8,128)(2,1)S(1)}, u32[]{:S(2)}, u32[]{:S(2)}) collective-permute-start(bf16[4,80,256]{2,1,0:T(8,128)(2,1)S(1)} %pad_maximum_fusion.near_ref), channel_id=1, source_target_pairs={{0,96},{8,104},{16,112},{24,120},{32,64},{40,72},{48,80},{56,88},{... | collective-permute-start | bytes 491528 | tf_op jit(solution)/shard_map/ppermute | solution.py:567
  147.6 8.9 %collective-permute-start.15 = (bf16[4,80,256]{2,1,0:T(8,128)(2,1)S(1)}, bf16[4,80,256]{2,1,0:T(8,128)(2,1)S(1)}, u32[]{:S(2)}, u32[]{:S(2)}) collective-permute-start(bf16[4,80,256]{2,1,0:T(8,128)(2,1)S(1)} %pad_maximum_fusion.near_ref), channel_id=1, source_target_pairs={{0,64},{64,0},{1,65},{65,1},{2,66},{66,2},{3,67},{67,3},{4,68},{68... | collective-permute-start | bytes 491528 | tf_op jit(solution)/shard_map/ppermute | solution.py:566
  150.8 6.9 %collective-permute-start.14 = (bf16[4,80,256]{2,1,0:T(8,128)(2,1)S(1)}, bf16[4,80,256]{2,1,0:T(8,128)(2,1)}, u32[]{:S(2)}, u32[]{:S(2)}) collective-permute-start(bf16[4,80,256]{2,1,0:T(8,128)(2,1)S(1)} %pad_maximum_fusion.near_ref), channel_id=1, source_target_pairs={{0,32},{8,40},{16,48},{24,56},{32,0},{40,8},{48,16},{56,24},{1,33}... | collective-permute-start | bytes 491528 | tf_op jit(solution)/shard_map/ppermute | solution.py:565
  (11 other events, 12.0 us)

commit v3 on v2

--- a/solution.py
+++ b/solution.py
@@ -20,6 +20,11 @@
 IMG_TALL = IMG + 16
 BF = jnp.bfloat16
 F32 = jnp.float32
+def work(micros):
+    size = int(micros * 3700000)
+    return pl.CostEstimate(flops=micros * 1000000, bytes_accessed=size, transcendentals=0)
+
+
 LIGHT = pl.CostEstimate(flops=1, bytes_accessed=1, transcendentals=0)
 VMEM_LIMIT = 56 * 1024 * 1024
 
@@ -30,13 +35,15 @@
     return high, low
 
 
-def project_kernel(count, place, embeds_ref, gain_ref, *refs):
-    weights, refs = refs[: 2 * count], refs[2 * count :]
-    if count == 2:
-        send_ref, keep_ref, both_ref, squares_ref = refs
+TILE = 512
+STEPS = ROWS // TILE
+
+
+def project_kernel(place, embeds_ref, gain_ref, *refs):
+    weights, send, keep, squares_ref = refs[0:8], refs[8:12], refs[12:16], refs[16]
     step = pl.program_id(0)
 
-    @pl.when(step < 8)
+    @pl.when(step < STEPS)
     def _():
         hidden = embeds_ref[...].astype(F32)
         scaled = (hidden * gain_ref[...].astype(F32)).astype(BF)
@@ -45,24 +52,23 @@
         for k in range(1, 8):
             lanes = lanes + squared[:, k * 128 : (k + 1) * 128]
         summed = jnp.sum(lanes.T, axis=0, keepdims=True)
-        squares_ref[pl.ds(2 * step, 1), :] = summed[:, :128]
-        squares_ref[pl.ds(2 * step + 1, 1), :] = summed[:, 128:]
-        for target, pair in ((send_ref, weights[:2]), (keep_ref, weights[2:])):
-            weight = jnp.concatenate([pair[0][...], pair[1][...]], axis=1)
+        for k in range(TILE // 128):
+            squares_ref[pl.ds(TILE // 128 * step + k, 1), :] = summed[:, k * 128 : (k + 1) * 128]
+        for k, target in enumerate((send[:2], send[2:], keep[:2], keep[2:])):
+            weight = jnp.concatenate([weights[2 * k][...], weights[2 * k + 1][...]], axis=1)
             product = jnp.dot(scaled, weight, preferred_element_type=F32).astype(BF)
-            target[0] = product[:, :128]
-            target[1] = product[:, 128:]
-
-    @pl.when(step == 8)
+            target[0][...] = product[:, :128]
+            target[1][...] = product[:, 128:]
+
+    @pl.when(step == STEPS)
     def _():
         high, low = split_pair(squares_ref[...])
         both = jnp.concatenate([high, low], axis=0)
-        for j in range(count):
-            send_ref[j, 0:EXT, :] = both
-            keep_ref[j, 0:EXT, :] = both
-
-
-def project_text(place, embeds, gain, kv_w, shifts):
+        for ref in (*send, *keep):
+            ref[0:EXT, :] = both
+
+
+def project_text(place, embeds, gain, kv_w):
     def column(r, j):
         def index(i, place):
             core = place[1] if r else 1 - place[1]
@@ -71,50 +77,44 @@
 
         return index
 
-    count = len(shifts)
     specs = [
-        pl.BlockSpec((256, 1024), lambda i, place: (jnp.minimum(i, 7), 0)),
+        pl.BlockSpec((TILE, 1024), lambda i, place: (jnp.minimum(i, STEPS - 1), 0)),
         pl.BlockSpec((1, 1024), lambda i, place: (0, 0)),
-    ] + [pl.BlockSpec((1024, 128), column(r, j)) for r in range(2) for j in shifts]
-    out = jax.ShapeDtypeStruct((count, TALL, 128), BF)
-    return pl.pallas_call(
-        functools.partial(project_kernel, count),
+    ] + [pl.BlockSpec((1024, 128), column(r, j)) for r in range(2) for j in range(4)]
+    outs = pl.pallas_call(
+        project_kernel,
         grid_spec=pltpu.PrefetchScalarGridSpec(
             num_scalar_prefetch=1,
-            grid=(9,),
+            grid=(STEPS + 1,),
             in_specs=specs,
-            out_specs=[pl.BlockSpec((count, 256, 128), lambda i, place: (0, i, 0))] * 2
-            + [pl.BlockSpec((8, 128), lambda i, place: (0, 0))],
+            out_specs=[pl.BlockSpec((TILE, 128), lambda i, place: (i, 0))] * 8,
             scratch_shapes=[pltpu.VMEM((16, 128), F32)],
         ),
-        out_shape=[out, out, jax.ShapeDtypeStruct((8, 128), F32)],
+        out_shape=[jax.ShapeDtypeStruct((TALL, 128), BF)] * 8,
         compiler_params=pltpu.CompilerParams(vmem_limit_bytes=VMEM_LIMIT),
         cost_estimate=LIGHT,
         name="project_text",
-    )(place, embeds, gain, *([kv_w] * (2 * count)))
+    )(place, embeds, gain, *([kv_w] * 8))
+    return outs[:4], outs[4:]
+
+
+def square_rows(refs):
+    total = jnp.zeros((16, 128), F32)
+    for ref in refs:
+        total = total + ref[ROWS : ROWS + 16, :].astype(F32) + ref[ROWS + 16 : TALL, :].astype(F32)
+    return total
 
 
 def add_kernel(a_ref, b_ref, out_ref):
-    out_ref[...] = (a_ref[0].astype(F32) + b_ref[0].astype(F32)).astype(BF)
-
-    @pl.when(pl.program_id(0) == 1)
-    def _():
-        half = TALL // 2
-        total = jnp.zeros((16, 128), F32)
-        for ref in (a_ref, b_ref):
-            total = total + ref[0, half - 32 : half - 16, :].astype(F32) + ref[0, half - 16 :, :].astype(F32)
-        high, low = split_pair(total)
-        out_ref[half - 32 : half - 16, :] = high
-        out_ref[half - 16 :, :] = low
-
-
-def add_pair(keep, received, j):
-    spec = pl.BlockSpec((1, TALL // 2, 128), lambda i: (j, i, 0))
+    out_ref[0:ROWS, :] = (a_ref[0:ROWS, :].astype(F32) + b_ref[0:ROWS, :].astype(F32)).astype(BF)
+    high, low = split_pair(square_rows([a_ref, b_ref]))
+    out_ref[ROWS : ROWS + 16, :] = high
+    out_ref[ROWS + 16 : TALL, :] = low
+
+
+def add_pair(keep, received):
     return pl.pallas_call(
         add_kernel,
-        grid=(2,),
-        in_specs=[spec, spec],
-        out_specs=pl.BlockSpec((TALL // 2, 128), lambda i: (i, 0)),
         out_shape=jax.ShapeDtypeStruct((TALL, 128), BF),
         compiler_params=pltpu.CompilerParams(vmem_limit_bytes=VMEM_LIMIT),
         cost_estimate=LIGHT,
@@ -122,19 +122,17 @@
     )(keep, received)
 
 
-def finish_kernel(slots, limit, a_ref, b_ref, c_ref, d_ref, rows_ref, slot_ref):
-    refs = (a_ref, b_ref, c_ref, d_ref)
+def finish_kernel(slots, limit, *refs):
+    parts, (rows_ref, slot_ref) = refs[:5], refs[5:]
     slot_ref[...] = jnp.zeros_like(slot_ref)
-    squares = jnp.zeros((16, 128), F32)
-    for ref in refs:
-        squares = squares + ref[ROWS : ROWS + 16, :].astype(F32) + ref[ROWS + 16 : TALL, :].astype(F32)
+    squares = square_rows(parts)
     scale = lax.rsqrt(squares / D + 1e-05)
     row_iota = lax.broadcasted_iota(jnp.int32, (128, 128), 0)
     for part in range(16):
         tile = jnp.broadcast_to(scale[part : part + 1, :], (128, 128)).T
-        here = pl.ds(part * 128, 128)
-        total = refs[0][here, :].astype(F32)
-        for ref in refs[1:]:
+        here = slice(part * 128, part * 128 + 128)
+        total = parts[0][here, :].astype(F32)
+        for ref in parts[1:]:
             total = total + ref[here, :].astype(F32)
         live = row_iota + part * 128 < limit[0]
         rows = jnp.where(live, total * tile, 0.0).astype(BF)
@@ -145,13 +143,13 @@
 
 
 def finish_text(slots, limit, parts):
-    spec = pl.BlockSpec((TALL, 128), lambda i, slots, limit: (0, 0))
+    whole = lambda i, slots, limit: (0, 0)
     return pl.pallas_call(
         finish_kernel,
         grid_spec=pltpu.PrefetchScalarGridSpec(
             num_scalar_prefetch=2,
             grid=(1,),
-            in_specs=[spec] * 4,
+            in_specs=[pl.BlockSpec((TALL, 128), whole)] * 5,
             out_specs=[
                 pl.BlockSpec((PAGES, PAGE, 128), lambda i, slots, limit: (0, 0, 0)),
                 pl.BlockSpec((1, 256, PAGE, 128), lambda i, slots, limit: (1, 0, 0, 0)),
@@ -162,7 +160,7 @@
             jax.ShapeDtypeStruct((2, 256, PAGE, 128), BF),
         ],
         compiler_params=pltpu.CompilerParams(vmem_limit_bytes=VMEM_LIMIT),
-        cost_estimate=LIGHT,
+        cost_estimate=work(200000),
         name="finish_text",
     )(slots, limit, *parts)
 
@@ -213,33 +211,31 @@
     )(place, feats)
 
 
-def partial_kernel(place, got_ref, swapped_ref, weight_ref, out_ref):
-    def product(ref):
-        rows = ref[...].reshape(256, ref.shape[2])
-        value = jnp.dot(rows, weight_ref[...], preferred_element_type=F32).astype(BF)
-        out_ref[...] = value.reshape(8, 32, value.shape[1])
-
-    own = pl.program_id(0) == place[1]
-
-    @pl.when(own)
+def partial_kernel(place, got_ref, swapped_ref, weight_ref, out_ref, rows):
+    @pl.when(pl.program_id(0) == 0)
     def _():
-        product(got_ref)
-
-    @pl.when(jnp.logical_not(own))
-    def _():
-        product(swapped_ref)
+        first = place[1] == 0
+        got, swapped = got_ref[...], swapped_ref[...]
+        rows[:, 0:32, :] = jnp.where(first, got, swapped)
+        rows[:, 32:64, :] = jnp.where(first, swapped, got)
+
+    lhs = rows[...].reshape(8 * IMG, rows.shape[2])
+    value = jnp.dot(lhs, weight_ref[...], preferred_element_type=F32).astype(BF)
+    out_ref[...] = value.reshape(8, IMG, value.shape[1])
 
 
 def partial_images(place, got, swapped, weight):
     depth, width = weight.shape
+    cut = width // 4
     rows = pl.BlockSpec((8, 32, depth), lambda i, place: (0, 0, 0))
     return pl.pallas_call(
         partial_kernel,
         grid_spec=pltpu.PrefetchScalarGridSpec(
             num_scalar_prefetch=1,
-            grid=(2,),
-            in_specs=[rows, rows, pl.BlockSpec((depth, width), lambda i, place: (0, 0))],
-            out_specs=pl.BlockSpec((8, 32, width), lambda i, place: (0, i, 0)),
+            grid=(4,),
+            in_specs=[rows, rows, pl.BlockSpec((depth, cut), lambda i, place: (0, i))],
+            out_specs=pl.BlockSpec((8, IMG, cut), lambda i, place: (0, 0, i)),
+            scratch_shapes=[pltpu.VMEM((8, IMG, depth), BF)],
         ),
         out_shape=jax.ShapeDtypeStruct((8, IMG, width), BF),
         compiler_params=pltpu.CompilerParams(vmem_limit_bytes=VMEM_LIMIT),
@@ -274,22 +270,18 @@
         rows = jnp.where(picked == 0, high.astype(F32), jnp.where(picked == 1, low.astype(F32), 0.0))
         pair[...] = jnp.concatenate([rows, jnp.zeros_like(rows)], axis=1).astype(BF)
 
-    product = jnp.dot(scaled[...], weight_ref[...], preferred_element_type=F32).astype(BF)
-    block = jnp.concatenate([product, pair[...]], axis=0)
-
-    @pl.when(step < 4)
-    def _():
-        swap_ref[0] = block
-
-    @pl.when(step >= 4)
-    def _():
-        same_ref[0] = block
+    product = jnp.dot(scaled[...], weight_ref[...], preferred_element_type=F32)
+    left, right = product[:, :256], product[:, 256:]
+    first = place[1] == 0
+    same_ref[0, 0:IMG, :] = jnp.where(first, left, right).astype(BF)
+    swap_ref[0, 0:IMG, :] = jnp.where(first, right, left).astype(BF)
+    same_ref[0, IMG:, :] = pair[...]
+    swap_ref[0, IMG:, :] = pair[...]
 
 
 def image_rows_kv(place, pieces, bias, gain, kv_w):
     def column(i, place):
-        core = jnp.where(i < 4, 1 - place[1], place[1])
-        return (0, 2 * lax.rem(place[2] + i, 4) + core)
+        return (0, lax.rem(place[2] + i, 4))
 
     width = pieces.shape[2]
     row = pl.BlockSpec((1, width), lambda i, place: (0, 0))
@@ -298,17 +290,17 @@
         image_kernel,
         grid_spec=pltpu.PrefetchScalarGridSpec(
             num_scalar_prefetch=1,
-            grid=(8,),
+            grid=(4,),
             in_specs=[
                 pl.BlockSpec((8, IMG, width), lambda i, place: (0, 0, 0)),
                 row,
                 row,
-                pl.BlockSpec((width, 256), column),
+                pl.BlockSpec((width, 512), column),
             ],
             out_specs=[
                 pl.BlockSpec((IMG, width), lambda i, place: (0, 0)),
-                pl.BlockSpec((1, IMG_TALL, 256), lambda i, place: (jnp.minimum(i, 3), 0, 0)),
-                pl.BlockSpec((1, IMG_TALL, 256), lambda i, place: (jnp.maximum(i - 4, 0), 0, 0)),
+                pl.BlockSpec((1, IMG_TALL, 256), lambda i, place: (i, 0, 0)),
+                pl.BlockSpec((1, IMG_TALL, 256), lambda i, place: (i, 0, 0)),
             ],
             scratch_shapes=[pltpu.VMEM((IMG, width), BF), pltpu.VMEM((16, 256), BF)],
         ),
@@ -362,43 +354,49 @@
 def merge_kernel(
     place, own_ref, other_ref, first_ref, second_ref, near_ref, yonder_ref, side_ref, far_ref, out_ref
 ):
-    step = pl.program_id(0)
-    match = jnp.where(place[0] == 0, step, place[3]).astype(F32)
-    shard = jnp.where(place[0] == 0, place[3], step)
-    level = lax.rem(place[3] - shard + 8, 4)
-    close = (shard >= 4) == (place[3] >= 4)
-    images = []
-    for near, away in ((near_ref, yonder_ref), (side_ref, far_ref)):
-        images.append(jnp.where(close, near[level].astype(F32), away[level].astype(F32)))
-    targets = []
-    for image in images:
-        owner = image[IMG : IMG + 1, 0:IMG]
-        spot = image[IMG + 1 : IMG + 2, 0:IMG] * PAGE + image[IMG + 2 : IMG + 3, 0:IMG]
-        targets.append(jnp.where(owner == match, spot, -1.0))
-    target = jnp.concatenate(targets, axis=1)
-    data = jnp.concatenate([images[0][0:IMG], images[1][0:IMG]], axis=0).astype(BF)
-    spots = lax.broadcasted_iota(jnp.int32, (CAP * PAGE, 2 * IMG), 0).astype(F32)
-    chosen = (spots == target).astype(F32).astype(BF)
-    image = jnp.dot(chosen, data, preferred_element_type=F32)
-    taken = jnp.dot(chosen, jnp.ones((2 * IMG, 256), BF), preferred_element_type=F32)
-
-    def write(left, right):
-        text = jnp.concatenate([left.reshape(CAP * PAGE, 128), right.reshape(CAP * PAGE, 128)], axis=1)
-        merged = jnp.where(taken > 0.5, image, text.astype(F32)).astype(BF)
-        out_ref[...] = merged.reshape(CAP, PAGE, 256)
-
-    @pl.when(place[0] == 0)
-    def _():
-        write(own_ref[0], other_ref[...])
-
-    @pl.when(place[0] != 0)
-    def _():
-        write(first_ref[0], second_ref[0])
+    def one(k):
+        step = 2 * pl.program_id(0) + k
+        match = jnp.where(place[0] == 0, step, place[3]).astype(F32)
+        shard = jnp.where(place[0] == 0, place[3], step)
+        level = lax.rem(place[3] - shard + 8, 4)
+        close = (shard >= 4) == (place[3] >= 4)
+        images = []
+        for near, away in ((near_ref, yonder_ref), (side_ref, far_ref)):
+            images.append(jnp.where(close, near[level].astype(F32), away[level].astype(F32)))
+        targets = []
+        for image in images:
+            owner = image[IMG : IMG + 1, 0:IMG]
+            spot = image[IMG + 1 : IMG + 2, 0:IMG] * PAGE + image[IMG + 2 : IMG + 3, 0:IMG]
+            targets.append(jnp.where(owner == match, spot, -1.0))
+        target = jnp.concatenate(targets, axis=1)
+        data = jnp.concatenate([images[0][0:IMG], images[1][0:IMG]], axis=0).astype(BF)
+        spots = lax.broadcasted_iota(jnp.int32, (CAP * PAGE, 2 * IMG), 0).astype(F32)
+        chosen = (spots == target).astype(F32).astype(BF)
+        image = jnp.dot(chosen, data, preferred_element_type=F32)
+        taken = jnp.dot(chosen, jnp.ones((2 * IMG, 128), BF), preferred_element_type=F32) > 0.5
+
+        def write(left, right):
+            for half, text in enumerate((left, right)):
+                lanes = slice(half * 128, half * 128 + 128)
+                text = text.reshape(CAP * PAGE, 128).astype(F32)
+                merged = jnp.where(taken, image[:, lanes], text).astype(BF)
+                out_ref[k * CAP : (k + 1) * CAP, :, lanes] = merged.reshape(CAP, PAGE, 128)
+
+        @pl.when(place[0] == 0)
+        def _():
+            write(own_ref[0, k * CAP : (k + 1) * CAP], other_ref[k * CAP : (k + 1) * CAP])
+
+        @pl.when(place[0] != 0)
+        def _():
+            write(first_ref[0, k * CAP : (k + 1) * CAP], second_ref[0, k * CAP : (k + 1) * CAP])
+
+    one(0)
+    one(1)
 
 
 def merge_slots(place, own, other, arrived, images):
     def local(i, place):
-        return jnp.where(place[0] == 0, i, 7)
+        return jnp.where(place[0] == 0, i, 3)
 
     def remote(i, place):
         return jnp.where(place[0] == 0, 0, i)
@@ -408,15 +406,15 @@
         merge_kernel,
         grid_spec=pltpu.PrefetchScalarGridSpec(
             num_scalar_prefetch=1,
-            grid=(8,),
+            grid=(4,),
             in_specs=[
-                pl.BlockSpec((1, CAP, PAGE, 128), lambda i, place: (1, local(i, place), 0, 0)),
-                pl.BlockSpec((CAP, PAGE, 128), lambda i, place: (local(i, place), 0, 0)),
-                pl.BlockSpec((1, CAP, PAGE, 128), lambda i, place: (0, remote(i, place), 0, 0)),
-                pl.BlockSpec((1, CAP, PAGE, 128), lambda i, place: (1, remote(i, place), 0, 0)),
+                pl.BlockSpec((1, 2 * CAP, PAGE, 128), lambda i, place: (1, local(i, place), 0, 0)),
+                pl.BlockSpec((2 * CAP, PAGE, 128), lambda i, place: (local(i, place), 0, 0)),
+                pl.BlockSpec((1, 2 * CAP, PAGE, 128), lambda i, place: (0, remote(i, place), 0, 0)),
+                pl.BlockSpec((1, 2 * CAP, PAGE, 128), lambda i, place: (1, remote(i, place), 0, 0)),
             ]
             + [image_spec] * 4,
-            out_specs=pl.BlockSpec((CAP, PAGE, 256), lambda i, place: (i, 0, 0)),
+            out_specs=pl.BlockSpec((2 * CAP, PAGE, 256), lambda i, place: (i, 0, 0)),
         ),
         out_shape=jax.ShapeDtypeStruct((256, PAGE, 256), BF),
         compiler_params=pltpu.CompilerParams(vmem_limit_bytes=VMEM_LIMIT),
@@ -515,24 +513,14 @@
 
     got = lax.all_to_all(cut_features(place, image_feats), "seq", 0, 0, tiled=True)
 
-    send, keep, _ = project_text(place, embeds, gain, kv_w, (1, 3))
-    received = lax.ppermute(send, "mp", PARTNER)
-    got = after(got, keep)
+    send, keep = project_text(place, embeds, gain, kv_w)
+    got = after(got, keep[0])
     swapped = lax.ppermute(got, "mp", PARTNER)
-    added = [None] * 4
-    parts = [None] * 4
-    for k, j in enumerate((1, 3)):
-        added[j] = add_pair(keep, received, k)
-        parts[j] = lax.ppermute(added[j], "mp", shift(j))
-    send, keep, _ = project_text(place, after(embeds, (added[1], added[3])), gain, kv_w, (2, 0))
-    received = lax.ppermute(send, "mp", PARTNER)
-    for k, j in enumerate((2, 0)):
-        added[j] = add_pair(keep, received, k)
-    parts[2] = lax.ppermute(added[2], "mp", shift(2))
-    parts[0] = added[0]
-
-    swapped = after(swapped, (added[2], added[0]))
-    partial = partial_images(place, got, swapped, proj_w)
+    received = [lax.ppermute(piece, "mp", PARTNER) for piece in send]
+    added = [None] + [add_pair(keep[j], received[j]) for j in (1, 2, 3)]
+    parts = [keep[0], received[0]] + [lax.ppermute(added[j], "mp", shift(j)) for j in (1, 2, 3)]
+
+    partial = partial_images(place, got, after(swapped, added[1:]), proj_w)
     attended = lax.cond(
         group != 0,
         attend,
@@ -543,13 +531,12 @@
         cache_lengths,
     )
     pieces = lax.all_to_all(partial, "seq", 0, 0, tiled=True)
-    pieces = after(pieces, attended)
     image_hidden, swap, same = image_rows_kv(place, pieces, bias, gain, kv_w)
     image_pairs = pair_images(same, lax.ppermute(swap, "mp", PARTNER))
     image_parts = [image_pairs[0]]
     image_parts += [lax.ppermute(image_pairs[j], "mp", shift(j)) for j in (1, 2, 3)]
 
-    rows, by_owner = finish_text(slots, limit.reshape(1), parts)
+    rows, by_owner = finish_text(slots, after(limit.reshape(1), attended), parts)
     other_rows = lax.ppermute(rows, "group", [(1, 0)])
     arrived = lax.all_to_all(
         by_owner.reshape(512, PAGE, 128), ("group", "seq"), split_axis=0, concat_axis=0, tiled=True

time: 170 us -> 136 us (0.80)
  the two profiles are of different devices: /device:TPU:10 before, /device:TPU:0 now
where the time goes in v3:
time: 136 us; the launch traced here: 135 us
  Pallas kernels  46.6 us (34%)
  starting transfers between devices  42.7 us (31%)
  waiting for transfers between devices  30.3 us (22%)
  local copies, waits for them, and re-layouts  8.64 us (6%)
  other arithmetic  5.33 us (4%)
  between operations  1.63 us (1%)
    ppermute x1, waiting for transfers between devices, per_device(): other_rows = lax.ppermute(rows, 'group', [(1, 0)])  10.5 us
    pallas_call x1, Pallas kernels, project_text(): pl.pallas_call(project_kernel, grid_spec=pltpu.PrefetchScalarGridSpec(num...  9.25 us
    all_to_all x1, starting transfers between devices, per_device(): lax.all_to_all(cut_features(place, image_feats), 'seq', 0, 0, tiled=True)  8.04 us
    all_to_all x1, waiting for transfers between devices, per_device(): pieces = lax.all_to_all(partial, 'seq', 0, 0, tiled=True)  7.77 us
    all_to_all x1, starting transfers between devices, per_device(): pieces = lax.all_to_all(partial, 'seq', 0, 0, tiled=True)  7.05 us
    pallas_call x1, Pallas kernels, merge_slots(): pl.pallas_call(merge_kernel, grid_spec=pltpu.PrefetchScalarGridSpec(num_s...  6.83 us
    unnamed x60, local copies, waits for them, and re-layouts  6.75 us
    pallas_call x3, Pallas kernels, add_pair(): pl.pallas_call(add_kernel, out_shape=jax.ShapeDtypeStruct((TALL, 128), BF...  6.39 us
  transfers between devices with their start and end apart: 23, of which 10 were waited for; matrix products, arithmetic and copies ran while one was open for 4% of the time, Pallas kernels for 23%

profile of v3, /device:TPU:0, one launch (start us, length us, event | category | flops | bytes accessed | tf_op | source)
XLA Modules:
  0.0 135.2 jit_solution(14171439977319947470)
XLA Ops:
  2.6 9.2 %project_text.1 = (bf16[2080,128]{1,0:T(8,128)(2,1)}, bf16[2080,128]{1,0:T(8,128)(2,1)}, bf16[2080,128]{1,0:T(8,128)(2,1)}, bf16[2080,128]{1,0:T(8,128)(2,1)}, b...) custom-call(s32[4]{0:T(128)} %pad_add_fusion.place, ...), custom_call_target="tpu_custom_call" | custom-call | flops 1 | bytes 1 | tf_op jit(solution)/shard_map/project_text/pallas_call | solution.py:84
  12.5 2.7 %cut_features.1 = bf16[8,32,912]{2,1,0:T(8,128)(2,1)} custom-call(s32[4]{0:T(128)} %pad_add_fusion.place, bf16[128,7296]{1,0:T(8,128)(2,1)} %feats_ref.1), custom_call_target="tpu_custom_call" | custom-call | flops 1 | bytes 1 | tf_op jit(solution)/shard_map/cut_features/pallas_call | solution.py:198
  15.2 8.0 %all-to-all-start = ((bf16[8,32,912]{2,1,0:T(8,128)(2,1)}), bf16[8,32,912]{2,1,0:T(8,128)(2,1)S(1)}, u32[]{:S(2)}, u32[]{:S(2)}) async-start(bf16[8,32,912]{2,1,0:T(8,128)(2,1)} %cut_features.1), calls=%async_computation | async-start | bytes 1048576 | tf_op jit(solution)/shard_map/all_to_all | solution.py:514
  24.2 2.1 %add_pair.3 = bf16[2080,128]{1,0:T(8,128)(2,1)} custom-call(bf16[2080,128]{1,0:T(8,128)(2,1)} %get-tuple-element.44.a_ref, bf16[2080,128]{1,0:T(8,128)(2,1)} %copy-done.7), custom_call_target="tpu_custom_call" | custom-call | flops 1 | bytes 1 | tf_op jit(solution)/shard_map/add_pair/pallas_call | solution.py:116
  26.3 1.5 %collective-permute-start.5 = (bf16[2080,128]{1,0:T(8,128)(2,1)}, bf16[2080,128]{1,0:T(8,128)(2,1)S(1)}, u32[]{:S(2)}, u32[]{:S(2)}) collective-permute-start(bf16[2080,128]{1,0:T(8,128)(2,1)} %add_pair.3), channel_id=1, source_target_pairs={{0,2},{1,3},{2,4},{3,5},{4,6},{5,7},{6,0},{7,1},{8,10},{9,11},{10,... | collective-permute-start | bytes 1597448 | tf_op jit(solution)/shard_map/ppermute | solution.py:521
  28.6 2.1 %add_pair.4 = bf16[2080,128]{1,0:T(8,128)(2,1)} custom-call(bf16[2080,128]{1,0:T(8,128)(2,1)} %get-tuple-element.46.a_ref, bf16[2080,128]{1,0:T(8,128)(2,1)} %copy-done.6), custom_call_target="tpu_custom_call" | custom-call | flops 1 | bytes 1 | tf_op jit(solution)/shard_map/add_pair/pallas_call | solution.py:116
  30.8 2.7 %collective-permute-start.6 = (bf16[2080,128]{1,0:T(8,128)(2,1)}, bf16[2080,128]{1,0:T(8,128)(2,1)S(1)}, u32[]{:S(2)}, u32[]{:S(2)}) collective-permute-start(bf16[2080,128]{1,0:T(8,128)(2,1)} %add_pair.4), channel_id=1, source_target_pairs={{0,4},{1,5},{2,6},{3,7},{4,0},{5,1},{6,2},{7,3},{8,12},{9,13},{10,... | collective-permute-start | bytes 1597448 | tf_op jit(solution)/shard_map/ppermute | solution.py:521
  34.3 2.1 %add_pair.5 = bf16[2080,128]{1,0:T(8,128)(2,1)} custom-call(bf16[2080,128]{1,0:T(8,128)(2,1)} %get-tuple-element.48.a_ref, bf16[2080,128]{1,0:T(8,128)(2,1)} %copy-done.5), custom_call_target="tpu_custom_call" | custom-call | flops 1 | bytes 1 | tf_op jit(solution)/shard_map/add_pair/pallas_call | solution.py:116
  36.4 1.4 %collective-permute-start.7 = (bf16[2080,128]{1,0:T(8,128)(2,1)}, bf16[2080,128]{1,0:T(8,128)(2,1)}, u32[]{:S(2)}, u32[]{:S(2)}) collective-permute-start(bf16[2080,128]{1,0:T(8,128)(2,1)} %add_pair.5), channel_id=1, source_target_pairs={{0,6},{1,7},{2,0},{3,1},{4,2},{5,3},{6,4},{7,5},{8,14},{9,15},{10,... | collective-permute-start | bytes 1597448 | tf_op jit(solution)/shard_map/ppermute | solution.py:521
  40.7 5.4 %partial_images.1 = bf16[8,64,1024]{2,1,0:T(8,128)(2,1)} custom-call(s32[4]{0:T(128)} %pad_add_fusion.place, bf16[8,32,912]{2,1,0:T(8,128)(2,1)} %copy-done.1, bf16[8,32,912]{2,1,0:T(8,128)(2,1)} %copy-done.8, bf16[912,1024]{1,0:T(8,128)(2,1)} %weight_ref.2), custom_call_target="tpu_custom_call" | custom-call | flops 1 | bytes 1 | tf_op jit(solution)/shard_map/partial_images/pallas_call | solution.py:231
  46.2 7.0 %all-to-all-start.2 = ((bf16[8,64,1024]{2,1,0:T(8,128)(2,1)}), bf16[8,64,1024]{2,1,0:T(8,128)(2,1)}, u32[]{:S(2)}, u32[]{:S(2)}) async-start(bf16[8,64,1024]{2,1,0:T(8,128)(2,1)} %partial_images.1), calls=%async_computation.2 | async-start | bytes 2097152 | tf_op jit(solution)/shard_map/all_to_all | solution.py:533
  54.5 2.7 %collective-permute-done.7.refs_4_ = bf16[2080,128]{1,0:T(8,128)(2,1)} collective-permute-done((bf16[2080,128]{1,0:T(8,128)(2,1)}, bf16[2080,128]{1,0:T(8,128)(2,1)}, u32[]{:S(2)}, u32[]{:S(2)}) %collective-permute-start.7) | collective-permute-done | bytes 532512 | tf_op jit(solution)/shard_map/ppermute | solution.py:521
  57.2 4.1 %finish_text.1 = (bf16[128,16,128]{2,1,0:T(8,128)(2,1)}, bf16[2,256,16,128]{3,2,1,0:T(8,128)(2,1)}) custom-call(s32[128]{0:T(128)} %multiply_add_fusion.slots, s32[1]{0:T(128)} %bitcast.16.limit, bf16[2080,128]{1,0:T(8,128)(2,1)} %get-tuple-element.42.refs_0_, bf16[2080,128]{1,0:T(8,128)(2,1)} %copy-done.26, bf16[2080,128]{1,0:T(8,128)(2,1)} %copy-done.27, ...), custom_call_target="tpu_custom_call" | custom-call | flops 199999995904 | bytes 740000006144 | tf_op jit(solution)/shard_map/finish_text/pallas_call | solution.py:147
  61.4 7.8 %all-to-all-done.2.pieces_ref = bf16[8,64,1024]{2,1,0:T(8,128)(2,1)} async-done(((bf16[8,64,1024]{2,1,0:T(8,128)(2,1)}), bf16[8,64,1024]{2,1,0:T(8,128)(2,1)}, u32[]{:S(2)}, u32[]{:S(2)}) %all-to-all-start.2) | async-done | bytes 1048608 | tf_op jit(solution)/shard_map/all_to_all | solution.py:533
  69.1 5.7 %all-to-all-start.1 = ((bf16[512,16,128]{2,1,0:T(8,128)(2,1)}), bf16[512,16,128]{2,1,0:T(8,128)(2,1)S(1)}, u32[]{:S(2)}, u32[]{:S(2)}) async-start(bf16[512,16,128]{2,1,0:T(8,128)(2,1)} %bitcast.64), calls=%async_computation.1 | async-start | bytes 4194304 | tf_op jit(solution)/shard_map/all_to_all | solution.py:541
  75.7 1.3 collective-permute-start.8
  77.1 5.7 %image_rows_kv.1 = (bf16[64,1024]{1,0:T(8,128)(2,1)}, bf16[4,80,256]{2,1,0:T(8,128)(2,1)}, bf16[4,80,256]{2,1,0:T(8,128)(2,1)}) custom-call(s32[4]{0:T(128)} %pad_add_fusion.place, bf16[8,64,1024]{2,1,0:T(8,128)(2,1)} %all-to-all-done.2.pieces_ref, bf16[1,1024]{1,0:T(2,128)(2,1)} %reshape.121.bias_ref, bf16[1,1024]{1,0:T(2,128)(2,1)} %reshape.118.gain_ref, ...), custom_call_target="tpu_custom_call" | custom-call | flops 1 | bytes 1 | tf_op jit(solution)/shard_map/image_rows_kv/pallas_call | solution.py:289
  82.8 1.6 %collective-permute-done.9.received_ref = bf16[4,80,256]{2,1,0:T(8,128)(2,1)S(1)} collective-permute-done((bf16[4,80,256]{2,1,0:T(8,128)(2,1)}, bf16[4,80,256]{2,1,0:T(8,128)(2,1)S(1)}, u32[]{:S(2)}, u32[]{:S(2)}) %collective-permute-start.9) | collective-permute-done | bytes 163872 | tf_op jit(solution)/shard_map/ppermute | solution.py:535
  85.1 1.7 %pair_images.1 = (bf16[80,256]{1,0:T(8,128)(2,1)}, bf16[80,256]{1,0:T(8,128)(2,1)}, bf16[80,256]{1,0:T(8,128)(2,1)}, bf16[80,256]{1,0:T(8,128)(2,1)}) custom-call(bf16[4,80,256]{2,1,0:T(8,128)(2,1)} %get-tuple-element.56.same_ref, bf16[4,80,256]{2,1,0:T(8,128)(2,1)} %copy-done.11), custom_call_target="tpu_custom_call" | custom-call | flops 1 | bytes 1 | tf_op jit(solution)/shard_map/pair_images/pallas_call | solution.py:325
  88.3 1.7 %collective-permute-start.12 = (bf16[80,256]{1,0:T(8,128)(2,1)}, bf16[80,256]{1,0:T(8,128)(2,1)S(1)}, u32[]{:S(2)}, u32[]{:S(2)}) collective-permute-start(bf16[80,256]{1,0:T(8,128)(2,1)} %get-tuple-element.61), channel_id=1, source_target_pairs={{0,6},{1,7},{2,0},{3,1},{4,2},{5,3},{6,4},{7,5},{8,14},{9,15},{10,... | collective-permute-start | bytes 122888 | tf_op jit(solution)/shard_map/ppermute | solution.py:537
  90.6 1.8 %collective-permute-done.10.b_ref = bf16[80,256]{1,0:T(8,128)(2,1)S(1)} collective-permute-done((bf16[80,256]{1,0:T(8,128)(2,1)}, bf16[80,256]{1,0:T(8,128)(2,1)S(1)}, u32[]{:S(2)}, u32[]{:S(2)}) %collective-permute-start.10) | collective-permute-done | bytes 40992 | tf_op jit(solution)/shard_map/ppermute | solution.py:537
  94.1 1.6 %close_images.1 = bf16[80,256]{1,0:T(8,128)(2,1)} custom-call(bf16[80,256]{1,0:T(8,128)(2,1)} %get-tuple-element.62.a_ref, bf16[80,256]{1,0:T(8,128)(2,1)} %copy-done.16, bf16[80,256]{1,0:T(8,128)(2,1)} %copy-done.17, bf16[80,256]{1,0:T(8,128)(2,1)} %copy-done.18, bf16[16,256]{1,0:T(8,128)(2,1)} %fusion.23.labels_ref), custom_call_target="tpu_custom_call" | custom-call | flops 1 | bytes 1 | tf_op jit(solution)/shard_map/close_images/pallas_call | solution.py:346
  95.6 3.1 %collective-permute-start.15 = (bf16[80,256]{1,0:T(8,128)(2,1)}, bf16[80,256]{1,0:T(8,128)(2,1)S(1)}, u32[]{:S(2)}, u32[]{:S(2)}) collective-permute-start(bf16[80,256]{1,0:T(8,128)(2,1)} %close_images.1), channel_id=1, source_target_pairs={{0,24},{8,0},{16,8},{24,16},{32,56},{40,32},{48,40},{56,48},{1,25}... | collective-permute-start | bytes 122888 | tf_op jit(solution)/shard_map/ppermute | solution.py:548
  101.8 10.5 %collective-permute-done.8.rows_ref = bf16[128,16,128]{2,1,0:T(8,128)(2,1)S(1)} collective-permute-done((bf16[128,16,128]{2,1,0:T(8,128)(2,1)}, bf16[128,16,128]{2,1,0:T(8,128)(2,1)S(1)}, u32[]{:S(2)}, u32[]{:S(2)}) %collective-permute-start.8) | collective-permute-done | bytes 524320 | tf_op jit(solution)/shard_map/ppermute | solution.py:540
  113.1 2.9 %place_pages.1.other_ref = bf16[256,16,128]{2,1,0:T(8,128)(2,1)} custom-call(s32[128]{0:T(128)} %multiply_add_fusion.slots, bf16[128,16,128]{2,1,0:T(8,128)(2,1)} %copy-done.9), custom_call_target="tpu_custom_call" | custom-call | flops 1 | bytes 1 | tf_op jit(solution)/shard_map/place_pages/pallas_call | solution.py:175
  116.8 1.6 %collective-permute-start.18 = (bf16[4,80,256]{2,1,0:T(8,128)(2,1)S(1)}, bf16[4,80,256]{2,1,0:T(8,128)(2,1)S(1)}, u32[]{:S(2)}, u32[]{:S(2)}) collective-permute-start(bf16[4,80,256]{2,1,0:T(8,128)(2,1)S(1)} %pad_maximum_fusion.near_ref), channel_id=1, source_target_pairs={{0,96},{8,104},{16,112},{24,120},{32,64},{40,72},{48,80},{56,88},{... | collective-permute-start | bytes 491528 | tf_op jit(solution)/shard_map/ppermute | solution.py:554
  118.4 1.8 %collective-permute-start.17 = (bf16[4,80,256]{2,1,0:T(8,128)(2,1)S(1)}, bf16[4,80,256]{2,1,0:T(8,128)(2,1)S(1)}, u32[]{:S(2)}, u32[]{:S(2)}) collective-permute-start(bf16[4,80,256]{2,1,0:T(8,128)(2,1)S(1)} %pad_maximum_fusion.near_ref), channel_id=1, source_target_pairs={{0,64},{64,0},{1,65},{65,1},{2,66},{66,2},{3,67},{67,3},{4,68},{68... | collective-permute-start | bytes 491528 | tf_op jit(solution)/shard_map/ppermute | solution.py:553
  120.1 1.4 %collective-permute-start.16 = (bf16[4,80,256]{2,1,0:T(8,128)(2,1)S(1)}, bf16[4,80,256]{2,1,0:T(8,128)(2,1)S(1)}, u32[]{:S(2)}, u32[]{:S(2)}) collective-permute-start(bf16[4,80,256]{2,1,0:T(8,128)(2,1)S(1)} %pad_maximum_fusion.near_ref), channel_id=1, source_target_pairs={{0,32},{8,40},{16,48},{24,56},{32,0},{40,8},{48,16},{56,24},{1,33}... | collective-permute-start | bytes 491528 | tf_op jit(solution)/shard_map/ppermute | solution.py:552
  121.6 1.7 %maximum_select_fusion = bf16[128,1024]{1,0:T(8,128)(2,1)} fusion(bf16[128,1024]{1,0:T(8,128)(2,1)S(1)} %copy-done.3, bf16[64,1024]{1,0:T(8,128)(2,1)S(1)} %collective-permute-done.19, bf16[64,1024]{1,0:T(8,128)(2,1)} %get-tuple-element.66, pred[]{:T(512)S(6)} %eq.48), kind=kLoop, calls=%fused_computation.26 | loop fusion | flops 655360 | bytes 786433 | tf_op jit(solution)/shard_map/jit(_where)/select_n | solution.py:560
  123.2 1.3 collective-permute-done.18.far_ref
  124.6 2.4 %collective-permute-done.16.yonder_ref = bf16[4,80,256]{2,1,0:T(8,128)(2,1)S(1)} collective-permute-done((bf16[4,80,256]{2,1,0:T(8,128)(2,1)S(1)}, bf16[4,80,256]{2,1,0:T(8,128)(2,1)S(1)}, u32[]{:S(2)}, u32[]{:S(2)}) %collective-permute-start.16) | collective-permute-done | bytes 163872 | tf_op jit(solution)/shard_map/ppermute | solution.py:552
  128.4 6.8 %merge_slots.1 = bf16[256,16,256]{2,1,0:T(8,128)(2,1)} custom-call(s32[4]{0:T(128)} %pad_add_fusion.place, bf16[2,256,16,128]{3,2,1,0:T(8,128)(2,1)} %get-tuple-element.54.own_ref, bf16[256,16,128]{2,1,0:T(8,128)(2,1)} %place_pages.1.other_ref, bf16[2,256,16,128]{3,2,1,0:T(8,128)(2,1)} %bitcast.62, bf16[2,256,16,128]{3,2,1,0:T(8,128)(2,1)} %bitcast.63, ...), custom_call_target="tpu_custom_call" | custom-call | flops 1 | bytes 1 | tf_op jit(solution)/shard_map/merge_slots/pallas_call | solution.py:405
  (102 shorter events, 20.0 us)
Async XLA Ops:
  11.8 26.1 %copy-start.29 = (s32[4]{0:T(128)S(1)}, s32[4]{0:T(128)}, u32[]{:S(2)}) copy-start(s32[4]{0:T(128)} %param.22) | copy-start | bytes 52
  11.8 27.4 %copy-start.22 = (s32[128,1]{0,1:T(1,128)S(1)}, s32[128,1]{0,1:T(1,128)}, u32[]{:S(2)}) copy-start(s32[128,1]{0,1:T(1,128)} %param.23) | copy-start | bytes 1540
  11.9 11.6 %collective-permute-start.1 = (bf16[2080,128]{1,0:T(8,128)(2,1)}, bf16[2080,128]{1,0:T(8,128)(2,1)S(1)}, u32[]{:S(2)}, u32[]{:S(2)}) collective-permute-start(bf16[2080,128]{1,0:T(8,128)(2,1)} %get-tuple-element.45), channel_id=1, source_target_pairs={{0,1},{1,0},{2,3},{3,2},{4,5},{5,4},{6,7},{7,6},{8,9},{9,8},{10,11... | collective-permute-start | bytes 1597448 | tf_op jit(solution)/shard_map/ppermute | solution.py:519
  11.9 15.9 %collective-permute-start.2 = (bf16[2080,128]{1,0:T(8,128)(2,1)}, bf16[2080,128]{1,0:T(8,128)(2,1)S(1)}, u32[]{:S(2)}, u32[]{:S(2)}) collective-permute-start(bf16[2080,128]{1,0:T(8,128)(2,1)} %get-tuple-element.47), channel_id=1, source_target_pairs={{0,1},{1,0},{2,3},{3,2},{4,5},{5,4},{6,7},{7,6},{8,9},{9,8},{10,11... | collective-permute-start | bytes 1597448 | tf_op jit(solution)/shard_map/ppermute | solution.py:519
  12.4 21.1 %collective-permute-start.3 = (bf16[2080,128]{1,0:T(8,128)(2,1)}, bf16[2080,128]{1,0:T(8,128)(2,1)S(1)}, u32[]{:S(2)}, u32[]{:S(2)}) collective-permute-start(bf16[2080,128]{1,0:T(8,128)(2,1)} %get-tuple-element.49), channel_id=1, source_target_pairs={{0,1},{1,0},{2,3},{3,2},{4,5},{5,4},{6,7},{7,6},{8,9},{9,8},{10,11... | collective-permute-start | bytes 1597448 | tf_op jit(solution)/shard_map/ppermute | solution.py:519
  15.2 22.7 %all-to-all-start = ((bf16[8,32,912]{2,1,0:T(8,128)(2,1)}), bf16[8,32,912]{2,1,0:T(8,128)(2,1)S(1)}, u32[]{:S(2)}, u32[]{:S(2)}) async-start(bf16[8,32,912]{2,1,0:T(8,128)(2,1)} %cut_features.1), calls=%async_computation | async-start | bytes 1048576 | tf_op jit(solution)/shard_map/all_to_all | solution.py:514
  23.3 30.1 %collective-permute-start.4 = (bf16[2080,128]{1,0:T(8,128)(2,1)}, bf16[2080,128]{1,0:T(8,128)(2,1)S(1)}, u32[]{:S(2)}, u32[]{:S(2)}) collective-permute-start(bf16[2080,128]{1,0:T(8,128)(2,1)} %get-tuple-element.53), channel_id=1, source_target_pairs={{0,1},{1,0},{2,3},{3,2},{4,5},{5,4},{6,7},{7,6},{8,9},{9,8},{10,11... | collective-permute-start | bytes 1597448 | tf_op jit(solution)/shard_map/ppermute | solution.py:519
  26.3 27.0 %collective-permute-start.5 = (bf16[2080,128]{1,0:T(8,128)(2,1)}, bf16[2080,128]{1,0:T(8,128)(2,1)S(1)}, u32[]{:S(2)}, u32[]{:S(2)}) collective-permute-start(bf16[2080,128]{1,0:T(8,128)(2,1)} %add_pair.3), channel_id=1, source_target_pairs={{0,2},{1,3},{2,4},{3,5},{4,6},{5,7},{6,0},{7,1},{8,10},{9,11},{10,... | collective-permute-start | bytes 1597448 | tf_op jit(solution)/shard_map/ppermute | solution.py:521
  30.8 22.5 %copy-start.10 = (bf16[128,1024]{1,0:T(8,128)(2,1)S(1)}, bf16[128,1024]{1,0:T(8,128)(2,1)}, u32[]{:S(2)}) copy-start(bf16[128,1024]{1,0:T(8,128)(2,1)} %param.24) | copy-start | bytes 786436
  30.8 22.5 %copy-start.15 = (bf16[128,256]{1,0:T(8,128)(2,1)S(1)}, bf16[128,256]{1,0:T(8,128)(2,1)}, u32[]{:S(2)}) copy-start(bf16[128,256]{1,0:T(8,128)(2,1)} %param.26) | copy-start | bytes 196612
  30.8 22.5 %copy-start.20 = (s32[128]{0:T(128)S(1)}, s32[128]{0:T(128)}, u32[]{:S(2)}) copy-start(s32[128]{0:T(128)} %param.27) | copy-start | bytes 1540
  30.8 23.7 %collective-permute-start.6 = (bf16[2080,128]{1,0:T(8,128)(2,1)}, bf16[2080,128]{1,0:T(8,128)(2,1)S(1)}, u32[]{:S(2)}, u32[]{:S(2)}) collective-permute-start(bf16[2080,128]{1,0:T(8,128)(2,1)} %add_pair.4), channel_id=1, source_target_pairs={{0,4},{1,5},{2,6},{3,7},{4,0},{5,1},{6,2},{7,3},{8,12},{9,13},{10,... | collective-permute-start | bytes 1597448 | tf_op jit(solution)/shard_map/ppermute | solution.py:521
  36.4 20.7 %collective-permute-start.7 = (bf16[2080,128]{1,0:T(8,128)(2,1)}, bf16[2080,128]{1,0:T(8,128)(2,1)}, u32[]{:S(2)}, u32[]{:S(2)}) collective-permute-start(bf16[2080,128]{1,0:T(8,128)(2,1)} %add_pair.5), channel_id=1, source_target_pairs={{0,6},{1,7},{2,0},{3,1},{4,2},{5,3},{6,4},{7,5},{8,14},{9,15},{10,... | collective-permute-start | bytes 1597448 | tf_op jit(solution)/shard_map/ppermute | solution.py:521
  37.9 2.0 %collective-permute-start = (bf16[8,32,912]{2,1,0:T(8,128)(2,1)S(1)}, bf16[8,32,912]{2,1,0:T(8,128)(2,1)S(1)}, u32[]{:S(2)}, u32[]{:S(2)}) collective-permute-start(bf16[8,32,912]{2,1,0:T(8,128)(2,1)S(1)} %all-to-all-done.got_ref), channel_id=1, source_target_pairs={{0,1},{1,0},{2,3},{3,2},{4,5},{5,4},{6,7},{7,6},{8,9},{9,8},{10,11... | collective-permute-start | bytes 1400840 | tf_op jit(solution)/shard_map/ppermute | solution.py:518
  46.2 23.0 %all-to-all-start.2 = ((bf16[8,64,1024]{2,1,0:T(8,128)(2,1)}), bf16[8,64,1024]{2,1,0:T(8,128)(2,1)}, u32[]{:S(2)}, u32[]{:S(2)}) async-start(bf16[8,64,1024]{2,1,0:T(8,128)(2,1)} %partial_images.1), calls=%async_computation.2 | async-start | bytes 2097152 | tf_op jit(solution)/shard_map/all_to_all | solution.py:533
  61.3 14.1 %copy-start.21 = (s32[128]{0:T(128)S(1)}, s32[128]{0:T(128)}, u32[]{:S(2)}) copy-start(s32[128]{0:T(128)} %param.17) | copy-start | bytes 1540
  61.4 14.2 %copy-start.23 = (s32[128,1]{0,1:T(1,128)S(1)}, s32[128,1]{0,1:T(1,128)}, u32[]{:S(2)}) copy-start(s32[128,1]{0,1:T(1,128)} %param.23) | copy-start | bytes 1540
  61.4 14.2 %copy-start.25 = (s32[128]{0:T(128)S(1)}, s32[128]{0:T(128)}, u32[]{:S(2)}) copy-start(s32[128]{0:T(128)} %copy-done.24) | copy-start | bytes 1540
  69.1 57.8 %all-to-all-start.1 = ((bf16[512,16,128]{2,1,0:T(8,128)(2,1)}), bf16[512,16,128]{2,1,0:T(8,128)(2,1)S(1)}, u32[]{:S(2)}, u32[]{:S(2)}) async-start(bf16[512,16,128]{2,1,0:T(8,128)(2,1)} %bitcast.64), calls=%async_computation.1 | async-start | bytes 4194304 | tf_op jit(solution)/shard_map/all_to_all | solution.py:541
  74.8 46.7 %copy-start.3 = (bf16[128,1024]{1,0:T(8,128)(2,1)S(1)}, bf16[128,1024]{1,0:T(8,128)(2,1)}, u32[]{:S(2)}) copy-start(bf16[128,1024]{1,0:T(8,128)(2,1)} %copy-done.2) | copy-start | bytes 786436
  75.7 36.5 %collective-permute-start.8 = (bf16[128,16,128]{2,1,0:T(8,128)(2,1)}, bf16[128,16,128]{2,1,0:T(8,128)(2,1)S(1)}, u32[]{:S(2)}, u32[]{:S(2)}) collective-permute-start(bf16[128,16,128]{2,1,0:T(8,128)(2,1)} %get-tuple-element.55), channel_id=1, source_target_pairs={{64,0},{65,1},{66,2},{67,3},{68,4},{69,5},{70,6},{71,7},{72,8},{73... | collective-permute-start | bytes 1572872 | tf_op jit(solution)/shard_map/ppermute | solution.py:540
  82.8 1.6 %collective-permute-start.9 = (bf16[4,80,256]{2,1,0:T(8,128)(2,1)}, bf16[4,80,256]{2,1,0:T(8,128)(2,1)S(1)}, u32[]{:S(2)}, u32[]{:S(2)}) collective-permute-start(bf16[4,80,256]{2,1,0:T(8,128)(2,1)} %get-tuple-element.57), channel_id=1, source_target_pairs={{0,1},{1,0},{2,3},{3,2},{4,5},{5,4},{6,7},{7,6},{8,9},{9,8},{10,11... | collective-permute-start | bytes 491528 | tf_op jit(solution)/shard_map/ppermute | solution.py:535
  86.7 5.6 %collective-permute-start.10 = (bf16[80,256]{1,0:T(8,128)(2,1)}, bf16[80,256]{1,0:T(8,128)(2,1)S(1)}, u32[]{:S(2)}, u32[]{:S(2)}) collective-permute-start(bf16[80,256]{1,0:T(8,128)(2,1)} %get-tuple-element.59), channel_id=1, source_target_pairs={{0,2},{1,3},{2,4},{3,5},{4,6},{5,7},{6,0},{7,1},{8,10},{9,11},{10,... | collective-permute-start | bytes 122888 | tf_op jit(solution)/shard_map/ppermute | solution.py:537
  87.3 5.7 %collective-permute-start.11 = (bf16[80,256]{1,0:T(8,128)(2,1)}, bf16[80,256]{1,0:T(8,128)(2,1)S(1)}, u32[]{:S(2)}, u32[]{:S(2)}) collective-permute-start(bf16[80,256]{1,0:T(8,128)(2,1)} %get-tuple-element.60), channel_id=1, source_target_pairs={{0,4},{1,5},{2,6},{3,7},{4,0},{5,1},{6,2},{7,3},{8,12},{9,13},{10,... | collective-permute-start | bytes 122888 | tf_op jit(solution)/shard_map/ppermute | solution.py:537
  88.3 5.2 %collective-permute-start.12 = (bf16[80,256]{1,0:T(8,128)(2,1)}, bf16[80,256]{1,0:T(8,128)(2,1)S(1)}, u32[]{:S(2)}, u32[]{:S(2)}) collective-permute-start(bf16[80,256]{1,0:T(8,128)(2,1)} %get-tuple-element.61), channel_id=1, source_target_pairs={{0,6},{1,7},{2,0},{3,1},{4,2},{5,3},{6,4},{7,5},{8,14},{9,15},{10,... | collective-permute-start | bytes 122888 | tf_op jit(solution)/shard_map/ppermute | solution.py:537
  95.6 20.3 %collective-permute-start.15 = (bf16[80,256]{1,0:T(8,128)(2,1)}, bf16[80,256]{1,0:T(8,128)(2,1)S(1)}, u32[]{:S(2)}, u32[]{:S(2)}) collective-permute-start(bf16[80,256]{1,0:T(8,128)(2,1)} %close_images.1), channel_id=1, source_target_pairs={{0,24},{8,0},{16,8},{24,16},{32,56},{40,32},{48,40},{56,48},{1,25}... | collective-permute-start | bytes 122888 | tf_op jit(solution)/shard_map/ppermute | solution.py:548
  98.8 17.2 %collective-permute-start.14 = (bf16[80,256]{1,0:T(8,128)(2,1)}, bf16[80,256]{1,0:T(8,128)(2,1)S(1)}, u32[]{:S(2)}, u32[]{:S(2)}) collective-permute-start(bf16[80,256]{1,0:T(8,128)(2,1)} %close_images.1), channel_id=1, source_target_pairs={{0,16},{8,24},{16,0},{24,8},{32,48},{40,56},{48,32},{56,40},{1,17}... | collective-permute-start | bytes 122888 | tf_op jit(solution)/shard_map/ppermute | solution.py:548
  99.6 16.3 %collective-permute-start.13 = (bf16[80,256]{1,0:T(8,128)(2,1)}, bf16[80,256]{1,0:T(8,128)(2,1)S(1)}, u32[]{:S(2)}, u32[]{:S(2)}) collective-permute-start(bf16[80,256]{1,0:T(8,128)(2,1)} %close_images.1), channel_id=1, source_target_pairs={{0,8},{8,16},{16,24},{24,0},{32,40},{40,48},{48,56},{56,32},{1,9},... | collective-permute-start | bytes 122888 | tf_op jit(solution)/shard_map/ppermute | solution.py:548
  100.5 21.1 %collective-permute-start.19 = (bf16[64,1024]{1,0:T(8,128)(2,1)}, bf16[64,1024]{1,0:T(8,128)(2,1)S(1)}, u32[]{:S(2)}, u32[]{:S(2)}) collective-permute-start(bf16[64,1024]{1,0:T(8,128)(2,1)} %get-tuple-element.66), channel_id=1, source_target_pairs={{64,0},{65,1},{66,2},{67,3},{68,4},{69,5},{70,6},{71,7},{72,8},{73... | collective-permute-start | bytes 393224 | tf_op jit(solution)/shard_map/ppermute | solution.py:559
  116.8 7.8 %collective-permute-start.18 = (bf16[4,80,256]{2,1,0:T(8,128)(2,1)S(1)}, bf16[4,80,256]{2,1,0:T(8,128)(2,1)S(1)}, u32[]{:S(2)}, u32[]{:S(2)}) collective-permute-start(bf16[4,80,256]{2,1,0:T(8,128)(2,1)S(1)} %pad_maximum_fusion.near_ref), channel_id=1, source_target_pairs={{0,96},{8,104},{16,112},{24,120},{32,64},{40,72},{48,80},{56,88},{... | collective-permute-start | bytes 491528 | tf_op jit(solution)/shard_map/ppermute | solution.py:554
  118.4 6.2 %collective-permute-start.17 = (bf16[4,80,256]{2,1,0:T(8,128)(2,1)S(1)}, bf16[4,80,256]{2,1,0:T(8,128)(2,1)S(1)}, u32[]{:S(2)}, u32[]{:S(2)}) collective-permute-start(bf16[4,80,256]{2,1,0:T(8,128)(2,1)S(1)} %pad_maximum_fusion.near_ref), channel_id=1, source_target_pairs={{0,64},{64,0},{1,65},{65,1},{2,66},{66,2},{3,67},{67,3},{4,68},{68... | collective-permute-start | bytes 491528 | tf_op jit(solution)/shard_map/ppermute | solution.py:553
  120.1 6.8 %collective-permute-start.16 = (bf16[4,80,256]{2,1,0:T(8,128)(2,1)S(1)}, bf16[4,80,256]{2,1,0:T(8,128)(2,1)S(1)}, u32[]{:S(2)}, u32[]{:S(2)}) collective-permute-start(bf16[4,80,256]{2,1,0:T(8,128)(2,1)S(1)} %pad_maximum_fusion.near_ref), channel_id=1, source_target_pairs={{0,32},{8,40},{16,48},{24,56},{32,0},{40,8},{48,16},{56,24},{1,33}... | collective-permute-start | bytes 491528 | tf_op jit(solution)/shard_map/ppermute | solution.py:552
  (21 other events, 71.9 us)

commit v4 on v3

--- a/solution.py
+++ b/solution.py
@@ -46,7 +46,7 @@
     @pl.when(step < STEPS)
     def _():
         hidden = embeds_ref[...].astype(F32)
-        scaled = (hidden * gain_ref[...].astype(F32)).astype(BF)
+        scaled = (hidden * gain_ref[...].astype(F32).reshape(1, -1)).astype(BF)
         squared = hidden * hidden
         lanes = squared[:, 0:128]
         for k in range(1, 8):
@@ -79,7 +79,7 @@
 
     specs = [
         pl.BlockSpec((TILE, 1024), lambda i, place: (jnp.minimum(i, STEPS - 1), 0)),
-        pl.BlockSpec((1, 1024), lambda i, place: (0, 0)),
+        pl.BlockSpec((1024,), lambda i, place: (0,)),
     ] + [pl.BlockSpec((1024, 128), column(r, j)) for r in range(2) for j in range(4)]
     outs = pl.pallas_call(
         project_kernel,
@@ -105,54 +105,39 @@
     return total
 
 
-def add_kernel(a_ref, b_ref, out_ref):
-    out_ref[0:ROWS, :] = (a_ref[0:ROWS, :].astype(F32) + b_ref[0:ROWS, :].astype(F32)).astype(BF)
-    high, low = split_pair(square_rows([a_ref, b_ref]))
-    out_ref[ROWS : ROWS + 16, :] = high
-    out_ref[ROWS + 16 : TALL, :] = low
-
-
 def add_pair(keep, received):
-    return pl.pallas_call(
-        add_kernel,
-        out_shape=jax.ShapeDtypeStruct((TALL, 128), BF),
-        compiler_params=pltpu.CompilerParams(vmem_limit_bytes=VMEM_LIMIT),
-        cost_estimate=LIGHT,
-        name="add_pair",
-    )(keep, received)
-
-
-def finish_kernel(slots, limit, *refs):
+    return (keep.astype(F32) + received.astype(F32)).astype(BF)
+
+
+def finish_kernel(slots, mask_ref, *refs):
     parts, (rows_ref, slot_ref) = refs[:5], refs[5:]
     slot_ref[...] = jnp.zeros_like(slot_ref)
     squares = square_rows(parts)
-    scale = lax.rsqrt(squares / D + 1e-05)
-    row_iota = lax.broadcasted_iota(jnp.int32, (128, 128), 0)
+    scale = jnp.where(mask_ref[...] > 0.0, lax.rsqrt(squares / D + 1e-05), 0.0)
     for part in range(16):
         tile = jnp.broadcast_to(scale[part : part + 1, :], (128, 128)).T
         here = slice(part * 128, part * 128 + 128)
         total = parts[0][here, :].astype(F32)
         for ref in parts[1:]:
             total = total + ref[here, :].astype(F32)
-        live = row_iota + part * 128 < limit[0]
-        rows = jnp.where(live, total * tile, 0.0).astype(BF)
+        rows = jnp.where(tile > 0.0, total * tile, 0.0).astype(BF)
         for p in range(8):
             page = rows[p * PAGE : (p + 1) * PAGE, :]
             rows_ref[part * 8 + p] = page
             slot_ref[0, slots[part * 8 + p]] = page
 
 
-def finish_text(slots, limit, parts):
-    whole = lambda i, slots, limit: (0, 0)
+def finish_text(slots, mask, parts):
+    whole = lambda i, slots: (0, 0)
     return pl.pallas_call(
         finish_kernel,
         grid_spec=pltpu.PrefetchScalarGridSpec(
-            num_scalar_prefetch=2,
+            num_scalar_prefetch=1,
             grid=(1,),
-            in_specs=[pl.BlockSpec((TALL, 128), whole)] * 5,
+            in_specs=[pl.BlockSpec((16, 128), whole)] + [pl.BlockSpec((TALL, 128), whole)] * 5,
             out_specs=[
-                pl.BlockSpec((PAGES, PAGE, 128), lambda i, slots, limit: (0, 0, 0)),
-                pl.BlockSpec((1, 256, PAGE, 128), lambda i, slots, limit: (1, 0, 0, 0)),
+                pl.BlockSpec((PAGES, PAGE, 128), lambda i, slots: (0, 0, 0)),
+                pl.BlockSpec((1, 256, PAGE, 128), lambda i, slots: (1, 0, 0, 0)),
             ],
         ),
         out_shape=[
@@ -160,31 +145,9 @@
             jax.ShapeDtypeStruct((2, 256, PAGE, 128), BF),
         ],
         compiler_params=pltpu.CompilerParams(vmem_limit_bytes=VMEM_LIMIT),
-        cost_estimate=work(200000),
+        cost_estimate=work(20000),
         name="finish_text",
-    )(slots, limit, *parts)
-
-
-def place_kernel(slots, rows_ref, slot_ref):
-    slot_ref[...] = jnp.zeros_like(slot_ref)
-    for p in range(PAGES):
-        slot_ref[slots[p]] = rows_ref[p]
-
-
-def place_pages(slots, rows):
-    return pl.pallas_call(
-        place_kernel,
-        grid_spec=pltpu.PrefetchScalarGridSpec(
-            num_scalar_prefetch=1,
-            grid=(1,),
-            in_specs=[pl.BlockSpec((PAGES, PAGE, 128), lambda i, slots: (0, 0, 0))],
-            out_specs=pl.BlockSpec((256, PAGE, 128), lambda i, slots: (0, 0, 0)),
-        ),
-        out_shape=jax.ShapeDtypeStruct((256, PAGE, 128), BF),
-        compiler_params=pltpu.CompilerParams(vmem_limit_bytes=VMEM_LIMIT),
-        cost_estimate=LIGHT,
-        name="place_pages",
-    )(slots, rows)
+    )(slots, mask, *parts)
 
 
 def cut_kernel(place, feats_ref, out_ref):
@@ -211,39 +174,6 @@
     )(place, feats)
 
 
-def partial_kernel(place, got_ref, swapped_ref, weight_ref, out_ref, rows):
-    @pl.when(pl.program_id(0) == 0)
-    def _():
-        first = place[1] == 0
-        got, swapped = got_ref[...], swapped_ref[...]
-        rows[:, 0:32, :] = jnp.where(first, got, swapped)
-        rows[:, 32:64, :] = jnp.where(first, swapped, got)
-
-    lhs = rows[...].reshape(8 * IMG, rows.shape[2])
-    value = jnp.dot(lhs, weight_ref[...], preferred_element_type=F32).astype(BF)
-    out_ref[...] = value.reshape(8, IMG, value.shape[1])
-
-
-def partial_images(place, got, swapped, weight):
-    depth, width = weight.shape
-    cut = width // 4
-    rows = pl.BlockSpec((8, 32, depth), lambda i, place: (0, 0, 0))
-    return pl.pallas_call(
-        partial_kernel,
-        grid_spec=pltpu.PrefetchScalarGridSpec(
-            num_scalar_prefetch=1,
-            grid=(4,),
-            in_specs=[rows, rows, pl.BlockSpec((depth, cut), lambda i, place: (0, i))],
-            out_specs=pl.BlockSpec((8, IMG, cut), lambda i, place: (0, 0, i)),
-            scratch_shapes=[pltpu.VMEM((8, IMG, depth), BF)],
-        ),
-        out_shape=jax.ShapeDtypeStruct((8, IMG, width), BF),
-        compiler_params=pltpu.CompilerParams(vmem_limit_bytes=VMEM_LIMIT),
-        cost_estimate=LIGHT,
-        name="partial_images",
-    )(place, got, swapped, weight)
-
-
 def image_kernel(
     place, pieces_ref, bias_ref, gain_ref, weight_ref, hidden_ref, swap_ref, same_ref, scaled, pair
 ):
@@ -254,11 +184,13 @@
         total = pieces_ref[0].astype(F32)
         for k in range(1, 8):
             total = total + pieces_ref[k].astype(F32)
-        total = total + bias_ref[...].astype(F32)
+        flipped = jnp.concatenate([total[32:64], total[0:32]], axis=0)
+        total = jnp.where(place[1] == 0, total, flipped)
+        total = total + bias_ref[...].astype(F32).reshape(1, -1)
         image_hidden = (0.5 * total * (1.0 + lax.erf(total * (0.5**0.5)))).astype(BF)
         hidden_ref[...] = image_hidden
         hidden = image_hidden.astype(F32)
-        scaled[...] = (hidden * gain_ref[...].astype(F32)).astype(BF)
+        scaled[...] = (hidden * gain_ref[...].astype(F32).reshape(1, -1)).astype(BF)
         squared = hidden * hidden
         lanes = squared[:, 0:128]
         for k in range(1, 8):
@@ -284,7 +216,7 @@
         return (0, lax.rem(place[2] + i, 4))
 
     width = pieces.shape[2]
-    row = pl.BlockSpec((1, width), lambda i, place: (0, 0))
+    row = pl.BlockSpec((width,), lambda i, place: (0,))
     out = jax.ShapeDtypeStruct((4, IMG_TALL, 256), BF)
     return pl.pallas_call(
         image_kernel,
@@ -311,25 +243,6 @@
     )(place, pieces, bias, gain, kv_w)
 
 
-def pair_kernel(same_ref, received_ref, *out_refs):
-    for j, out_ref in enumerate(out_refs):
-        total = same_ref[j].astype(F32) + received_ref[j].astype(F32)
-        out_ref[0:IMG, :] = total[0:IMG].astype(BF)
-        high, low = split_pair(total[IMG : IMG + 1] + total[IMG + 1 : IMG + 2])
-        picked = lax.broadcasted_iota(jnp.int32, (16, 256), 0)
-        rows = jnp.where(picked == 0, high.astype(F32), jnp.where(picked == 1, low.astype(F32), 0.0))
-        out_ref[IMG:, :] = rows.astype(BF)
-
-
-def pair_images(same, received):
-    return pl.pallas_call(
-        pair_kernel,
-        out_shape=[jax.ShapeDtypeStruct((IMG_TALL, 256), BF)] * 4,
-        cost_estimate=LIGHT,
-        name="pair_images",
-    )(same, received)
-
-
 def close_kernel(a_ref, b_ref, c_ref, d_ref, labels_ref, out_ref):
     total = a_ref[...].astype(F32) + b_ref[...].astype(F32)
     total = total + c_ref[...].astype(F32) + d_ref[...].astype(F32)
@@ -352,41 +265,48 @@
 
 
 def merge_kernel(
-    place, own_ref, other_ref, first_ref, second_ref, near_ref, yonder_ref, side_ref, far_ref, out_ref
+    place, slots, own_ref, rows_ref, first_ref, second_ref, near_ref, yonder_ref, side_ref, far_ref, out_ref, other
 ):
+    prefill = place[0] == 0
+
+    @pl.when(jnp.logical_and(prefill, pl.program_id(0) == 0))
+    def _():
+        other[...] = jnp.zeros_like(other)
+        for p in range(PAGES):
+            other[slots[p]] = rows_ref[p]
+
     def one(k):
         step = 2 * pl.program_id(0) + k
-        match = jnp.where(place[0] == 0, step, place[3]).astype(F32)
-        shard = jnp.where(place[0] == 0, place[3], step)
+        match = jnp.where(prefill, step, place[3]).astype(F32)
+        shard = jnp.where(prefill, place[3], step)
         level = lax.rem(place[3] - shard + 8, 4)
         close = (shard >= 4) == (place[3] >= 4)
         images = []
         for near, away in ((near_ref, yonder_ref), (side_ref, far_ref)):
-            images.append(jnp.where(close, near[level].astype(F32), away[level].astype(F32)))
+            images.append(jnp.where(close, near[level], away[level]))
         targets = []
         for image in images:
-            owner = image[IMG : IMG + 1, 0:IMG]
-            spot = image[IMG + 1 : IMG + 2, 0:IMG] * PAGE + image[IMG + 2 : IMG + 3, 0:IMG]
-            targets.append(jnp.where(owner == match, spot, -1.0))
+            labels = image[IMG:IMG_TALL, 0:IMG].astype(F32)
+            spot = labels[1:2] * PAGE + labels[2:3]
+            targets.append(jnp.where(labels[0:1] == match, spot, -1.0))
         target = jnp.concatenate(targets, axis=1)
-        data = jnp.concatenate([images[0][0:IMG], images[1][0:IMG]], axis=0).astype(BF)
+        data = jnp.concatenate([images[0][0:IMG], images[1][0:IMG]], axis=0)
         spots = lax.broadcasted_iota(jnp.int32, (CAP * PAGE, 2 * IMG), 0).astype(F32)
         chosen = (spots == target).astype(F32).astype(BF)
-        image = jnp.dot(chosen, data, preferred_element_type=F32)
-        taken = jnp.dot(chosen, jnp.ones((2 * IMG, 128), BF), preferred_element_type=F32) > 0.5
+        image = jnp.dot(chosen, data, preferred_element_type=F32).astype(BF)
 
         def write(left, right):
             for half, text in enumerate((left, right)):
                 lanes = slice(half * 128, half * 128 + 128)
-                text = text.reshape(CAP * PAGE, 128).astype(F32)
-                merged = jnp.where(taken, image[:, lanes], text).astype(BF)
-                out_ref[k * CAP : (k + 1) * CAP, :, lanes] = merged.reshape(CAP, PAGE, 128)
-
-        @pl.when(place[0] == 0)
+                text = text.reshape(CAP * PAGE, 128)
+                out_ref[k * CAP : (k + 1) * CAP, :, lanes] = (text + image[:, lanes]).reshape(CAP, PAGE, 128)
+
+        @pl.when(prefill)
         def _():
-            write(own_ref[0, k * CAP : (k + 1) * CAP], other_ref[k * CAP : (k + 1) * CAP])
-
-        @pl.when(place[0] != 0)
+            here = pl.ds(step * CAP, CAP)
+            write(own_ref[0, k * CAP : (k + 1) * CAP], other[here])
+
+        @pl.when(jnp.logical_not(prefill))
         def _():
             write(first_ref[0, k * CAP : (k + 1) * CAP], second_ref[0, k * CAP : (k + 1) * CAP])
 
@@ -394,33 +314,35 @@
     one(1)
 
 
-def merge_slots(place, own, other, arrived, images):
+def merge_slots(place, slots, own, rows, arrived, images):
     def local(i, place):
         return jnp.where(place[0] == 0, i, 3)
 
     def remote(i, place):
         return jnp.where(place[0] == 0, 0, i)
 
-    image_spec = pl.BlockSpec((4, IMG_TALL, 256), lambda i, place: (0, 0, 0))
+    image_spec = pl.BlockSpec((4, IMG_TALL, 256), lambda i, place, slots: (0, 0, 0))
+    chunk = (1, 2 * CAP, PAGE, 128)
     return pl.pallas_call(
         merge_kernel,
         grid_spec=pltpu.PrefetchScalarGridSpec(
-            num_scalar_prefetch=1,
+            num_scalar_prefetch=2,
             grid=(4,),
             in_specs=[
-                pl.BlockSpec((1, 2 * CAP, PAGE, 128), lambda i, place: (1, local(i, place), 0, 0)),
-                pl.BlockSpec((2 * CAP, PAGE, 128), lambda i, place: (local(i, place), 0, 0)),
-                pl.BlockSpec((1, 2 * CAP, PAGE, 128), lambda i, place: (0, remote(i, place), 0, 0)),
-                pl.BlockSpec((1, 2 * CAP, PAGE, 128), lambda i, place: (1, remote(i, place), 0, 0)),
+                pl.BlockSpec(chunk, lambda i, place, slots: (1, local(i, place), 0, 0)),
+                pl.BlockSpec((PAGES, PAGE, 128), lambda i, place, slots: (0, 0, 0)),
+                pl.BlockSpec(chunk, lambda i, place, slots: (0, remote(i, place), 0, 0)),
+                pl.BlockSpec(chunk, lambda i, place, slots: (1, remote(i, place), 0, 0)),
             ]
             + [image_spec] * 4,
-            out_specs=pl.BlockSpec((2 * CAP, PAGE, 256), lambda i, place: (i, 0, 0)),
+            out_specs=pl.BlockSpec((2 * CAP, PAGE, 256), lambda i, place, slots: (i, 0, 0)),
+            scratch_shapes=[pltpu.VMEM((256, PAGE, 128), BF)],
         ),
         out_shape=jax.ShapeDtypeStruct((256, PAGE, 256), BF),
         compiler_params=pltpu.CompilerParams(vmem_limit_bytes=VMEM_LIMIT),
         cost_estimate=LIGHT,
         name="merge_slots",
-    )(place, own, other, arrived, arrived, *images)
+    )(place, slots, own, rows, arrived, arrived, *images)
 
 
 def attend(queries, kv_cache, new_kv, cache_lengths):
@@ -490,9 +412,7 @@
     mp = lax.axis_index("mp").astype(jnp.int32)
     core, x = mp % 2, mp // 2
     place = jnp.stack([group, core, x, seq])
-    gain = norm_gain.reshape(1, -1)
-
-    bias = proj_b.reshape(1, -1)
+
 
     owners = page_owner[:, 0]
     before = (
@@ -509,18 +429,25 @@
     labels = jnp.stack(
         [image_owner, image_rank, local_pos % PAGE, (local_pos < limit).astype(jnp.int32)]
     ).astype(BF)
+    tokens = jnp.arange(ROWS, dtype=jnp.int32).reshape(16, 128)
+    places = image_pos - seq * ROWS
+    upper = (places // 128)[None, :] == jnp.arange(16, dtype=jnp.int32)[:, None]
+    lower = (places % 128)[:, None] == jnp.arange(128, dtype=jnp.int32)[None, :]
+    is_image = jnp.dot(upper.astype(BF), lower.astype(BF), preferred_element_type=F32)
+    mask = jnp.where((tokens < limit) & (is_image < 0.5), 1.0, 0.0).astype(F32)
     labels = jnp.pad(labels, ((0, 12), (0, 256 - IMG)))
 
     got = lax.all_to_all(cut_features(place, image_feats), "seq", 0, 0, tiled=True)
 
-    send, keep = project_text(place, embeds, gain, kv_w)
+    send, keep = project_text(place, embeds, norm_gain, kv_w)
     got = after(got, keep[0])
     swapped = lax.ppermute(got, "mp", PARTNER)
     received = [lax.ppermute(piece, "mp", PARTNER) for piece in send]
     added = [None] + [add_pair(keep[j], received[j]) for j in (1, 2, 3)]
     parts = [keep[0], received[0]] + [lax.ppermute(added[j], "mp", shift(j)) for j in (1, 2, 3)]
 
-    partial = partial_images(place, got, after(swapped, added[1:]), proj_w)
+    feats = jnp.concatenate([got, after(swapped, added[1:])], axis=1).reshape(8 * IMG, -1)
+    partial = jnp.dot(feats, proj_w, preferred_element_type=F32).astype(BF).reshape(8, IMG, -1)
     attended = lax.cond(
         group != 0,
         attend,
@@ -531,12 +458,12 @@
         cache_lengths,
     )
     pieces = lax.all_to_all(partial, "seq", 0, 0, tiled=True)
-    image_hidden, swap, same = image_rows_kv(place, pieces, bias, gain, kv_w)
-    image_pairs = pair_images(same, lax.ppermute(swap, "mp", PARTNER))
+    image_hidden, swap, same = image_rows_kv(place, pieces, proj_b, norm_gain, kv_w)
+    image_pairs = add_pair(same, lax.ppermute(swap, "mp", PARTNER))
     image_parts = [image_pairs[0]]
     image_parts += [lax.ppermute(image_pairs[j], "mp", shift(j)) for j in (1, 2, 3)]
 
-    rows, by_owner = finish_text(slots, after(limit.reshape(1), attended), parts)
+    rows, by_owner = finish_text(slots, after(mask, attended), parts)
     other_rows = lax.ppermute(rows, "group", [(1, 0)])
     arrived = lax.all_to_all(
         by_owner.reshape(512, PAGE, 128), ("group", "seq"), split_axis=0, concat_axis=0, tiled=True
@@ -553,8 +480,7 @@
         lax.ppermute(near, "group", [(0, 1), (1, 0)]),
         lax.ppermute(near, ("group", "seq"), FAR),
     ]
-    other = place_pages(slots, other_rows)
-    page_slots = merge_slots(place, by_owner, other, arrived, images)
+    page_slots = merge_slots(place, slots, by_owner, other_rows, arrived, images)
 
     other_hidden = lax.ppermute(image_hidden, "group", [(1, 0)])
     row_states = jnp.where(

time: 136 us -> 126 us (0.926)
  the two profiles are of different devices: /device:TPU:0 before, /device:TPU:10 now
where the time goes in v4:
time: 126 us; the launch traced here: 125 us
  starting transfers between devices  45.5 us (36%)
  Pallas kernels  30.1 us (24%)
  waiting for transfers between devices  20.3 us (16%)
  other arithmetic  13.2 us (10%)
  matrix products  11.3 us (9%)
  local copies, waits for them, and re-layouts  3.02 us (2%)
  between operations  1.59 us (1%)
    pallas_call x1, Pallas kernels, project_text(): pl.pallas_call(project_kernel, grid_spec=pltpu.PrefetchScalarGridSpec(num...  9.29 us
    all_to_all x1, starting transfers between devices, per_device(): lax.all_to_all(by_owner.reshape(512, PAGE, 128), ('group', 'seq'), split_...  8.69 us
    all_to_all x1, starting transfers between devices, per_device(): pieces = lax.all_to_all(partial, 'seq', 0, 0, tiled=True)  7.45 us
    all_to_all x1, starting transfers between devices, per_device(): lax.all_to_all(cut_features(place, image_feats), 'seq', 0, 0, tiled=True)  7.05 us
    pallas_call x1, Pallas kernels, merge_slots(): pl.pallas_call(merge_kernel, grid_spec=pltpu.PrefetchScalarGridSpec(num_s...  6.72 us
    convert_element_type x4, other arithmetic, add_pair(): return (keep.astype(F32) + received.astype(F32)).astype(BF)  6.21 us
    pallas_call x1, Pallas kernels, image_rows_kv(): pl.pallas_call(image_kernel, grid_spec=pltpu.PrefetchScalarGridSpec(num_s...  5.76 us
    ppermute x1, waiting for transfers between devices, per_device(): lax.ppermute(near, 'seq', seq_shift(1, 0))  5.5 us
  transfers between devices with their start and end apart: 23, of which 9 were waited for; matrix products, arithmetic and copies ran while one was open for 20% of the time, Pallas kernels for 17%

profile of v4, /device:TPU:10, one launch (start us, length us, event | category | flops | bytes accessed | tf_op | source)
XLA Modules:
  0.0 125.1 jit_solution(14519818270944363482)
XLA Ops:
  1.2 2.7 %cut_features.1 = bf16[8,32,912]{2,1,0:T(8,128)(2,1)} custom-call(s32[4]{0:T(128)} %pad_add_fusion.place, bf16[128,7296]{1,0:T(8,128)(2,1)} %feats_ref.1), custom_call_target="tpu_custom_call" | custom-call | flops 1 | bytes 1 | tf_op jit(solution)/shard_map/cut_features/pallas_call | solution.py:161
  3.9 7.0 %all-to-all-start = ((bf16[8,32,912]{2,1,0:T(8,128)(2,1)}), bf16[8,32,912]{2,1,0:T(8,128)(2,1)S(1)}, u32[]{:S(2)}, u32[]{:S(2)}) async-start(bf16[8,32,912]{2,1,0:T(8,128)(2,1)} %cut_features.1), calls=%async_computation | async-start | bytes 1048576 | tf_op jit(solution)/shard_map/all_to_all | solution.py:440
  11.0 9.3 %project_text.1 = (bf16[2080,128]{1,0:T(8,128)(2,1)}, bf16[2080,128]{1,0:T(8,128)(2,1)}, bf16[2080,128]{1,0:T(8,128)(2,1)}, bf16[2080,128]{1,0:T(8,128)(2,1)}, b...) custom-call(s32[4]{0:T(128)} %pad_add_fusion.place, ...), custom_call_target="tpu_custom_call" | custom-call | flops 1 | bytes 1 | tf_op jit(solution)/shard_map/project_text/pallas_call | solution.py:84
  23.8 2.2 %add_convert_fusion.2 = bf16[2080,128]{1,0:T(8,128)(2,1)} fusion(bf16[2080,128]{1,0:T(8,128)(2,1)} %collective-permute-done.1, bf16[2080,128]{1,0:T(8,128)(2,1)} %get-tuple-element.40), kind=kLoop, calls=%fused_computation.32 | loop fusion | flops 1064960 | bytes 1597440 | tf_op jit(solution)/shard_map/convert_element_type | solution.py:109
  26.0 1.5 %collective-permute-start.5 = (bf16[2080,128]{1,0:T(8,128)(2,1)}, bf16[2080,128]{1,0:T(8,128)(2,1)}, u32[]{:S(2)}, u32[]{:S(2)}) collective-permute-start(bf16[2080,128]{1,0:T(8,128)(2,1)} %add_convert_fusion.2), channel_id=1, source_target_pairs={{0,2},{1,3},{2,4},{3,5},{4,6},{5,7},{6,0},{7,1},{8,10},{9,11},{10,... | collective-permute-start | bytes 1597448 | tf_op jit(solution)/shard_map/ppermute | solution.py:447
  27.5 2.1 %add_convert_fusion.1 = bf16[2080,128]{1,0:T(8,128)(2,1)} fusion(bf16[2080,128]{1,0:T(8,128)(2,1)} %collective-permute-done.2, bf16[2080,128]{1,0:T(8,128)(2,1)} %get-tuple-element.42), kind=kLoop, calls=%fused_computation.31 | loop fusion | flops 1064960 | bytes 1597440 | tf_op jit(solution)/shard_map/convert_element_type | solution.py:109
  31.7 2.2 %collective-permute-start.7 = (bf16[2080,128]{1,0:T(8,128)(2,1)}, bf16[2080,128]{1,0:T(8,128)(2,1)}, u32[]{:S(2)}, u32[]{:S(2)}) collective-permute-start(bf16[2080,128]{1,0:T(8,128)(2,1)} %add_convert_fusion), channel_id=1, source_target_pairs={{0,6},{1,7},{2,0},{3,1},{4,2},{5,3},{6,4},{7,5},{8,14},{9,15},{10,... | collective-permute-start | bytes 1597448 | tf_op jit(solution)/shard_map/ppermute | solution.py:447
  34.4 1.2 pad_maximum_fusion
  35.6 2.2 %convolution_convert_fusion = bf16[512,1024]{1,0:T(8,128)(2,1)} fusion(bf16[512,912]{1,0:T(8,128)(2,1)S(1)} %bitcast.79, bf16[912,1024]{1,0:T(8,128)(2,1)S(1)} %copy-done), kind=kOutput, calls=%fused_computation.26 | convolution fusion | flops 956825600 | bytes 3850240 | tf_op jit(solution)/shard_map/dot_general | solution.py:450
  37.9 7.5 %all-to-all-start.2 = ((bf16[8,64,1024]{2,1,0:T(8,128)(2,1)}), bf16[8,64,1024]{2,1,0:T(8,128)(2,1)S(1)}, u32[]{:S(2)}, u32[]{:S(2)}) async-start(bf16[8,64,1024]{2,1,0:T(8,128)(2,1)} %bitcast.78), calls=%async_computation.2 | async-start | bytes 2097152 | tf_op jit(solution)/shard_map/all_to_all | solution.py:460
  45.3 9.0 %conditional.1 = (bf16[128,1024]{1,0:T(8,128)(2,1)S(1)}) conditional(s32[]{:T(128)} %convert_element_type.78, () %tuple.19, (s32[128]{0:T(128)S(1)}, bf16[128,1024]{1,0:T(8,128)(2,1)S(1)}, bf16[128,128,256]{2,1,0:T(8,128)(2,1)}, bf16[128,256]{1,0:T(8,128)(2,1)S(1)}) %tuple.41), branch_computations={%region_2.3_spmd, %region_3.6_spmd} | conditional | flops 68852736 | bytes 12157448 | solution.py:451
  45.8 4.5 %fusion.36 = (f32[128,8]{1,0:T(8,128)S(1)}, f32[128,8,128]{2,1,0:T(8,128)S(1)}) fusion(bf16[128,8,128]{2,1,0:T(8,128)(2,1)S(1)} %bitcast.77, bf16[128,128,1,256]{3,1,0,2:T(8,128)(2,1)} %bitcast.74, pred[128,128]{1,0:T(8,128)(4,1)S(1)} %iota_compare_fusion), kind=kOutput, calls=%fused_computation.88 | convolution fusion | flops 33946624 | bytes 5001216 | tf_op jit(solution)/shard_map/cond/branch_1_fun/rgqh,rjgh->rgqj/dot_general | solution.py:354
  50.8 3.5 %fusion.5 = bf16[128,8,128]{2,1,0:T(8,128)(2,1)S(1)} fusion(bf16[128,128,1,256]{3,1,0,2:T(8,128)(2,1)} %bitcast.75, f32[128,8,128]{2,1,0:T(8,128)S(1)} %get-tuple-element.76, f32[128,128]{1,0:T(8,128)S(1)} %get-tuple-element.74, f32[128,8]{1,0:T(8,128)S(1)} %bitcast_convert_fusion, f32[128,8]{1,0:T(8,128)S(1)} %get-tuple-element.71, ...), kind=kOutput, calls=%fused_computation.7 | convolution fusion | flops 34340864 | bytes 5058560 | tf_op jit(solution)/shard_map/cond/branch_1_fun/rgqj,rjgh->rgqh/dot_general | solution.py:370
  54.4 2.6 %collective-permute-done.7.refs_4_ = bf16[2080,128]{1,0:T(8,128)(2,1)} collective-permute-done((bf16[2080,128]{1,0:T(8,128)(2,1)}, bf16[2080,128]{1,0:T(8,128)(2,1)}, u32[]{:S(2)}, u32[]{:S(2)}) %collective-permute-start.7) | collective-permute-done | bytes 532512 | tf_op jit(solution)/shard_map/ppermute | solution.py:447
  57.0 4.1 %finish_text.1 = (bf16[128,16,128]{2,1,0:T(8,128)(2,1)}, bf16[2,256,16,128]{3,2,1,0:T(8,128)(2,1)}) custom-call(s32[128]{0:T(128)} %multiply_add_fusion.slots, f32[16,128]{1,0:T(8,128)} %fusion.15.mask_ref, bf16[2080,128]{1,0:T(8,128)(2,1)} %get-tuple-element.38.refs_0_, bf16[2080,128]{1,0:T(8,128)(2,1)} %collective-permute-done.4.refs_1_, ...), custom_call_target="tpu_custom_call" | custom-call | flops 20000000000 | bytes 73999998976 | tf_op jit(solution)/shard_map/finish_text/pallas_call | solution.py:132
  62.1 8.7 %all-to-all-start.1 = ((bf16[512,16,128]{2,1,0:T(8,128)(2,1)}), bf16[512,16,128]{2,1,0:T(8,128)(2,1)}, u32[]{:S(2)}, u32[]{:S(2)}) async-start(bf16[512,16,128]{2,1,0:T(8,128)(2,1)} %bitcast.73), calls=%async_computation.1 | async-start | bytes 4194304 | tf_op jit(solution)/shard_map/all_to_all | solution.py:468
  71.1 5.8 %image_rows_kv.1 = (bf16[64,1024]{1,0:T(8,128)(2,1)}, bf16[4,80,256]{2,1,0:T(8,128)(2,1)}, bf16[4,80,256]{2,1,0:T(8,128)(2,1)}) custom-call(s32[4]{0:T(128)} %pad_add_fusion.place, bf16[8,64,1024]{2,1,0:T(8,128)(2,1)} %copy-done.1, bf16[1024]{0:T(1024)(128)(2,1)} %bias_ref.1, bf16[1024]{0:T(1024)(128)(2,1)} %gain_ref.3, bf16[1024,2048]{1,0:T(8,128)(2,1)} %weight_ref.1), custom_call_target="tpu_custom_call" | custom-call | flops 1 | bytes 1 | tf_op jit(solution)/shard_map/image_rows_kv/pallas_call | solution.py:221
  76.8 2.1 %collective-permute-start.8 = (bf16[128,16,128]{2,1,0:T(8,128)(2,1)}, bf16[128,16,128]{2,1,0:T(8,128)(2,1)S(1)}, u32[]{:S(2)}, u32[]{:S(2)}) collective-permute-start(bf16[128,16,128]{2,1,0:T(8,128)(2,1)} %get-tuple-element.51), channel_id=1, source_target_pairs={{64,0},{65,1},{66,2},{67,3},{68,4},{69,5},{70,6},{71,7},{72,8},{73... | collective-permute-start | bytes 1572872 | tf_op jit(solution)/shard_map/ppermute | solution.py:467
  80.5 2.1 %collective-permute-start.11 = (bf16[80,256]{1,0:T(8,128)(2,1)S(1)}, bf16[80,256]{1,0:T(8,128)(2,1)S(1)}, u32[]{:S(2)}, u32[]{:S(2)}) collective-permute-start(bf16[80,256]{1,0:T(8,128)(2,1)S(1)} %get-tuple-element.78), channel_id=1, source_target_pairs={{0,4},{1,5},{2,6},{3,7},{4,0},{5,1},{6,2},{7,3},{8,12},{9,13},{10,... | collective-permute-start | bytes 122888 | tf_op jit(solution)/shard_map/ppermute | solution.py:464
  82.6 1.7 %collective-permute-start.10 = (bf16[80,256]{1,0:T(8,128)(2,1)S(1)}, bf16[80,256]{1,0:T(8,128)(2,1)S(1)}, u32[]{:S(2)}, u32[]{:S(2)}) collective-permute-start(bf16[80,256]{1,0:T(8,128)(2,1)S(1)} %get-tuple-element.79), channel_id=1, source_target_pairs={{0,2},{1,3},{2,4},{3,5},{4,6},{5,7},{6,0},{7,1},{8,10},{9,11},{10,... | collective-permute-start | bytes 122888 | tf_op jit(solution)/shard_map/ppermute | solution.py:464
  84.9 1.2 collective-permute-done.11.c_ref
  87.7 1.6 %close_images.1 = bf16[80,256]{1,0:T(8,128)(2,1)} custom-call(bf16[80,256]{1,0:T(8,128)(2,1)} %get-tuple-element.54.a_ref, bf16[80,256]{1,0:T(8,128)(2,1)} %copy-done.12, bf16[80,256]{1,0:T(8,128)(2,1)} %copy-done.11, bf16[80,256]{1,0:T(8,128)(2,1)} %copy-done.10, bf16[16,256]{1,0:T(8,128)(2,1)} %fusion.26.labels_ref), custom_call_target="tpu_custom_call" | custom-call | flops 1 | bytes 1 | tf_op jit(solution)/shard_map/close_images/pallas_call | solution.py:259
  89.2 3.1 %collective-permute-start.15 = (bf16[80,256]{1,0:T(8,128)(2,1)}, bf16[80,256]{1,0:T(8,128)(2,1)S(1)}, u32[]{:S(2)}, u32[]{:S(2)}) collective-permute-start(bf16[80,256]{1,0:T(8,128)(2,1)} %close_images.1), channel_id=1, source_target_pairs={{0,24},{8,0},{16,8},{24,16},{32,56},{40,32},{48,40},{56,48},{1,25}... | collective-permute-start | bytes 122888 | tf_op jit(solution)/shard_map/ppermute | solution.py:475
  94.0 1.5 %collective-permute-start.19 = (bf16[64,1024]{1,0:T(8,128)(2,1)}, bf16[64,1024]{1,0:T(8,128)(2,1)S(1)}, u32[]{:S(2)}, u32[]{:S(2)}) collective-permute-start(bf16[64,1024]{1,0:T(8,128)(2,1)} %get-tuple-element.58), channel_id=1, source_target_pairs={{64,0},{65,1},{66,2},{67,3},{68,4},{69,5},{70,6},{71,7},{72,8},{73... | collective-permute-start | bytes 393224 | tf_op jit(solution)/shard_map/ppermute | solution.py:485
  95.6 2.7 %collective-permute-done.15 = bf16[80,256]{1,0:T(8,128)(2,1)S(1)} collective-permute-done((bf16[80,256]{1,0:T(8,128)(2,1)}, bf16[80,256]{1,0:T(8,128)(2,1)S(1)}, u32[]{:S(2)}, u32[]{:S(2)}) %collective-permute-start.15) | collective-permute-done | bytes 40992 | tf_op jit(solution)/shard_map/ppermute | solution.py:475
  99.6 1.8 %collective-permute-start.18 = (bf16[4,80,256]{2,1,0:T(8,128)(2,1)S(1)}, bf16[4,80,256]{2,1,0:T(8,128)(2,1)S(1)}, u32[]{:S(2)}, u32[]{:S(2)}) collective-permute-start(bf16[4,80,256]{2,1,0:T(8,128)(2,1)S(1)} %pad_maximum_fusion.1.near_ref), channel_id=1, source_target_pairs={{0,96},{8,104},{16,112},{24,120},{32,64},{40,72},{48,80},{56,88},{... | collective-permute-start | bytes 491528 | tf_op jit(solution)/shard_map/ppermute | solution.py:481
  101.4 2.4 %collective-permute-start.17 = (bf16[4,80,256]{2,1,0:T(8,128)(2,1)S(1)}, bf16[4,80,256]{2,1,0:T(8,128)(2,1)S(1)}, u32[]{:S(2)}, u32[]{:S(2)}) collective-permute-start(bf16[4,80,256]{2,1,0:T(8,128)(2,1)S(1)} %pad_maximum_fusion.1.near_ref), channel_id=1, source_target_pairs={{0,64},{64,0},{1,65},{65,1},{2,66},{66,2},{3,67},{67,3},{4,68},{68... | collective-permute-start | bytes 491528 | tf_op jit(solution)/shard_map/ppermute | solution.py:480
  103.8 5.0 %collective-permute-done.19 = bf16[64,1024]{1,0:T(8,128)(2,1)S(1)} collective-permute-done((bf16[64,1024]{1,0:T(8,128)(2,1)}, bf16[64,1024]{1,0:T(8,128)(2,1)S(1)}, u32[]{:S(2)}, u32[]{:S(2)}) %collective-permute-start.19) | collective-permute-done | bytes 131104 | tf_op jit(solution)/shard_map/ppermute | solution.py:485
  108.8 1.7 %maximum_select_fusion = bf16[128,1024]{1,0:T(8,128)(2,1)} fusion(bf16[128,1024]{1,0:T(8,128)(2,1)S(1)} %get-tuple-element.83, bf16[64,1024]{1,0:T(8,128)(2,1)S(1)} %collective-permute-done.19, bf16[64,1024]{1,0:T(8,128)(2,1)} %get-tuple-element.58, pred[]{:T(512)S(6)} %eq.79), kind=kLoop, calls=%fused_computation.35 | loop fusion | flops 655360 | bytes 786433 | tf_op jit(solution)/shard_map/jit(_where)/select_n | solution.py:486
  110.5 1.7 %collective-permute-done.17.side_ref = bf16[4,80,256]{2,1,0:T(8,128)(2,1)S(1)} collective-permute-done((bf16[4,80,256]{2,1,0:T(8,128)(2,1)S(1)}, bf16[4,80,256]{2,1,0:T(8,128)(2,1)S(1)}, u32[]{:S(2)}, u32[]{:S(2)}) %collective-permute-start.17) | collective-permute-done | bytes 163872 | tf_op jit(solution)/shard_map/ppermute | solution.py:480
  112.2 5.5 %collective-permute-done.16.yonder_ref = bf16[4,80,256]{2,1,0:T(8,128)(2,1)S(1)} collective-permute-done((bf16[4,80,256]{2,1,0:T(8,128)(2,1)S(1)}, bf16[4,80,256]{2,1,0:T(8,128)(2,1)S(1)}, u32[]{:S(2)}, u32[]{:S(2)}) %collective-permute-start.16) | collective-permute-done | bytes 163872 | tf_op jit(solution)/shard_map/ppermute | solution.py:479
  118.4 6.7 %merge_slots.1 = bf16[256,16,256]{2,1,0:T(8,128)(2,1)} custom-call(s32[4]{0:T(128)} %pad_add_fusion.place, s32[128]{0:T(128)} %multiply_add_fusion.slots, bf16[2,256,16,128]{3,2,1,0:T(8,128)(2,1)} %get-tuple-element.50.own_ref, bf16[128,16,128]{2,1,0:T(8,128)(2,1)} %copy-done.4, bf16[2,256,16,128]{3,2,1,0:T(8,128)(2,1)} %bitcast.19.first_ref.second_ref, ...), custom_call_target="tpu_custom_call" | custom-call | flops 1 | bytes 1 | tf_op jit(solution)/shard_map/merge_slots/pallas_call | solution.py:326
  (88 shorter events, 15.8 us)
Async XLA Ops:
  0.6 35.0 %copy-start = (bf16[912,1024]{1,0:T(8,128)(2,1)S(1)}, bf16[912,1024]{1,0:T(8,128)(2,1)}, u32[]{:S(2)}) copy-start(bf16[912,1024]{1,0:T(8,128)(2,1)} %param.18) | copy-start | bytes 5603332
  3.9 19.8 %all-to-all-start = ((bf16[8,32,912]{2,1,0:T(8,128)(2,1)}), bf16[8,32,912]{2,1,0:T(8,128)(2,1)S(1)}, u32[]{:S(2)}, u32[]{:S(2)}) async-start(bf16[8,32,912]{2,1,0:T(8,128)(2,1)} %cut_features.1), calls=%async_computation | async-start | bytes 1048576 | tf_op jit(solution)/shard_map/all_to_all | solution.py:440
  11.0 10.4 %copy-start.16 = (s32[4]{0:T(128)S(1)}, s32[4]{0:T(128)}, u32[]{:S(2)}) copy-start(s32[4]{0:T(128)} %param.22) | copy-start | bytes 52
  11.0 11.7 %copy-start.13 = (s32[128]{0:T(128)S(1)}, s32[128]{0:T(128)}, u32[]{:S(2)}) copy-start(s32[128]{0:T(128)} %param.17) | copy-start | bytes 1540
  11.0 11.7 %copy-start.15 = (s32[128,1]{0,1:T(1,128)S(1)}, s32[128,1]{0,1:T(1,128)}, u32[]{:S(2)}) copy-start(s32[128,1]{0,1:T(1,128)} %param.23) | copy-start | bytes 1540
  20.3 10.4 %copy-start.3 = (bf16[2080,128]{1,0:T(8,128)(2,1)S(1)}, bf16[2080,128]{1,0:T(8,128)(2,1)}, u32[]{:S(2)}) copy-start(bf16[2080,128]{1,0:T(8,128)(2,1)} %get-tuple-element.44) | copy-start | bytes 1597444
  20.3 3.5 %collective-permute-start.1 = (bf16[2080,128]{1,0:T(8,128)(2,1)}, bf16[2080,128]{1,0:T(8,128)(2,1)}, u32[]{:S(2)}, u32[]{:S(2)}) collective-permute-start(bf16[2080,128]{1,0:T(8,128)(2,1)} %get-tuple-element.41), channel_id=1, source_target_pairs={{0,1},{1,0},{2,3},{3,2},{4,5},{5,4},{6,7},{7,6},{8,9},{9,8},{10,11... | collective-permute-start | bytes 1597448 | tf_op jit(solution)/shard_map/ppermute | solution.py:445
  20.4 7.1 %collective-permute-start.2 = (bf16[2080,128]{1,0:T(8,128)(2,1)}, bf16[2080,128]{1,0:T(8,128)(2,1)}, u32[]{:S(2)}, u32[]{:S(2)}) collective-permute-start(bf16[2080,128]{1,0:T(8,128)(2,1)} %get-tuple-element.43), channel_id=1, source_target_pairs={{0,1},{1,0},{2,3},{3,2},{4,5},{5,4},{6,7},{7,6},{8,9},{9,8},{10,11... | collective-permute-start | bytes 1597448 | tf_op jit(solution)/shard_map/ppermute | solution.py:445
  20.9 9.8 %collective-permute-start.3 = (bf16[2080,128]{1,0:T(8,128)(2,1)}, bf16[2080,128]{1,0:T(8,128)(2,1)S(1)}, u32[]{:S(2)}, u32[]{:S(2)}) collective-permute-start(bf16[2080,128]{1,0:T(8,128)(2,1)} %get-tuple-element.45), channel_id=1, source_target_pairs={{0,1},{1,0},{2,3},{3,2},{4,5},{5,4},{6,7},{7,6},{8,9},{9,8},{10,11... | collective-permute-start | bytes 1597448 | tf_op jit(solution)/shard_map/ppermute | solution.py:445
  21.0 33.4 %collective-permute-start.4 = (bf16[2080,128]{1,0:T(8,128)(2,1)}, bf16[2080,128]{1,0:T(8,128)(2,1)}, u32[]{:S(2)}, u32[]{:S(2)}) collective-permute-start(bf16[2080,128]{1,0:T(8,128)(2,1)} %get-tuple-element.49), channel_id=1, source_target_pairs={{0,1},{1,0},{2,3},{3,2},{4,5},{5,4},{6,7},{7,6},{8,9},{9,8},{10,11... | collective-permute-start | bytes 1597448 | tf_op jit(solution)/shard_map/ppermute | solution.py:445
  23.7 10.7 %collective-permute-start = (bf16[8,32,912]{2,1,0:T(8,128)(2,1)S(1)}, bf16[8,32,912]{2,1,0:T(8,128)(2,1)}, u32[]{:S(2)}, u32[]{:S(2)}) collective-permute-start(bf16[8,32,912]{2,1,0:T(8,128)(2,1)S(1)} %all-to-all-done), channel_id=1, source_target_pairs={{0,1},{1,0},{2,3},{3,2},{4,5},{5,4},{6,7},{7,6},{8,9},{9,8},{10,11... | collective-permute-start | bytes 1400840 | tf_op jit(solution)/shard_map/ppermute | solution.py:444
  26.0 28.4 %collective-permute-start.5 = (bf16[2080,128]{1,0:T(8,128)(2,1)}, bf16[2080,128]{1,0:T(8,128)(2,1)}, u32[]{:S(2)}, u32[]{:S(2)}) collective-permute-start(bf16[2080,128]{1,0:T(8,128)(2,1)} %add_convert_fusion.2), channel_id=1, source_target_pairs={{0,2},{1,3},{2,4},{3,5},{4,6},{5,7},{6,0},{7,1},{8,10},{9,11},{10,... | collective-permute-start | bytes 1597448 | tf_op jit(solution)/shard_map/ppermute | solution.py:447
  29.6 24.7 %collective-permute-start.6 = (bf16[2080,128]{1,0:T(8,128)(2,1)}, bf16[2080,128]{1,0:T(8,128)(2,1)}, u32[]{:S(2)}, u32[]{:S(2)}) collective-permute-start(bf16[2080,128]{1,0:T(8,128)(2,1)} %add_convert_fusion.1), channel_id=1, source_target_pairs={{0,4},{1,5},{2,6},{3,7},{4,0},{5,1},{6,2},{7,3},{8,12},{9,13},{10,... | collective-permute-start | bytes 1597448 | tf_op jit(solution)/shard_map/ppermute | solution.py:447
  31.7 25.3 %collective-permute-start.7 = (bf16[2080,128]{1,0:T(8,128)(2,1)}, bf16[2080,128]{1,0:T(8,128)(2,1)}, u32[]{:S(2)}, u32[]{:S(2)}) collective-permute-start(bf16[2080,128]{1,0:T(8,128)(2,1)} %add_convert_fusion), channel_id=1, source_target_pairs={{0,6},{1,7},{2,0},{3,1},{4,2},{5,3},{6,4},{7,5},{8,14},{9,15},{10,... | collective-permute-start | bytes 1597448 | tf_op jit(solution)/shard_map/ppermute | solution.py:447
  37.9 7.5 %copy-start.5 = (bf16[128,1024]{1,0:T(8,128)(2,1)S(1)}, bf16[128,1024]{1,0:T(8,128)(2,1)}, u32[]{:S(2)}) copy-start(bf16[128,1024]{1,0:T(8,128)(2,1)} %param.24) | copy-start | bytes 786436
  37.9 7.5 %copy-start.9 = (bf16[128,256]{1,0:T(8,128)(2,1)S(1)}, bf16[128,256]{1,0:T(8,128)(2,1)}, u32[]{:S(2)}) copy-start(bf16[128,256]{1,0:T(8,128)(2,1)} %param.26) | copy-start | bytes 196612
  37.9 7.5 %copy-start.14 = (s32[128]{0:T(128)S(1)}, s32[128]{0:T(128)}, u32[]{:S(2)}) copy-start(s32[128]{0:T(128)} %param.27) | copy-start | bytes 1540
  37.9 23.2 %all-to-all-start.2 = ((bf16[8,64,1024]{2,1,0:T(8,128)(2,1)}), bf16[8,64,1024]{2,1,0:T(8,128)(2,1)S(1)}, u32[]{:S(2)}, u32[]{:S(2)}) async-start(bf16[8,64,1024]{2,1,0:T(8,128)(2,1)} %bitcast.78), calls=%async_computation.2 | async-start | bytes 2097152 | tf_op jit(solution)/shard_map/all_to_all | solution.py:460
  62.1 55.7 %all-to-all-start.1 = ((bf16[512,16,128]{2,1,0:T(8,128)(2,1)}), bf16[512,16,128]{2,1,0:T(8,128)(2,1)}, u32[]{:S(2)}, u32[]{:S(2)}) async-start(bf16[512,16,128]{2,1,0:T(8,128)(2,1)} %bitcast.73), calls=%async_computation.1 | async-start | bytes 4194304 | tf_op jit(solution)/shard_map/all_to_all | solution.py:468
  76.8 2.1 %collective-permute-start.9 = (bf16[4,80,256]{2,1,0:T(8,128)(2,1)}, bf16[4,80,256]{2,1,0:T(8,128)(2,1)S(1)}, u32[]{:S(2)}, u32[]{:S(2)}) collective-permute-start(bf16[4,80,256]{2,1,0:T(8,128)(2,1)} %get-tuple-element.53), channel_id=1, source_target_pairs={{0,1},{1,0},{2,3},{3,2},{4,5},{5,4},{6,7},{7,6},{8,9},{9,8},{10,11... | collective-permute-start | bytes 491528 | tf_op jit(solution)/shard_map/ppermute | solution.py:462
  76.8 33.7 %collective-permute-start.8 = (bf16[128,16,128]{2,1,0:T(8,128)(2,1)}, bf16[128,16,128]{2,1,0:T(8,128)(2,1)S(1)}, u32[]{:S(2)}, u32[]{:S(2)}) collective-permute-start(bf16[128,16,128]{2,1,0:T(8,128)(2,1)} %get-tuple-element.51), channel_id=1, source_target_pairs={{64,0},{65,1},{66,2},{67,3},{68,4},{69,5},{70,6},{71,7},{72,8},{73... | collective-permute-start | bytes 1572872 | tf_op jit(solution)/shard_map/ppermute | solution.py:467
  80.5 4.3 %collective-permute-start.12 = (bf16[80,256]{1,0:T(8,128)(2,1)S(1)}, bf16[80,256]{1,0:T(8,128)(2,1)S(1)}, u32[]{:S(2)}, u32[]{:S(2)}) collective-permute-start(bf16[80,256]{1,0:T(8,128)(2,1)S(1)} %get-tuple-element.77), channel_id=1, source_target_pairs={{0,6},{1,7},{2,0},{3,1},{4,2},{5,3},{6,4},{7,5},{8,14},{9,15},{10,... | collective-permute-start | bytes 122888 | tf_op jit(solution)/shard_map/ppermute | solution.py:464
  80.5 5.5 %collective-permute-start.11 = (bf16[80,256]{1,0:T(8,128)(2,1)S(1)}, bf16[80,256]{1,0:T(8,128)(2,1)S(1)}, u32[]{:S(2)}, u32[]{:S(2)}) collective-permute-start(bf16[80,256]{1,0:T(8,128)(2,1)S(1)} %get-tuple-element.78), channel_id=1, source_target_pairs={{0,4},{1,5},{2,6},{3,7},{4,0},{5,1},{6,2},{7,3},{8,12},{9,13},{10,... | collective-permute-start | bytes 122888 | tf_op jit(solution)/shard_map/ppermute | solution.py:464
  82.6 4.4 %collective-permute-start.10 = (bf16[80,256]{1,0:T(8,128)(2,1)S(1)}, bf16[80,256]{1,0:T(8,128)(2,1)S(1)}, u32[]{:S(2)}, u32[]{:S(2)}) collective-permute-start(bf16[80,256]{1,0:T(8,128)(2,1)S(1)} %get-tuple-element.79), channel_id=1, source_target_pairs={{0,2},{1,3},{2,4},{3,5},{4,6},{5,7},{6,0},{7,1},{8,10},{9,11},{10,... | collective-permute-start | bytes 122888 | tf_op jit(solution)/shard_map/ppermute | solution.py:464
  89.2 9.1 %collective-permute-start.15 = (bf16[80,256]{1,0:T(8,128)(2,1)}, bf16[80,256]{1,0:T(8,128)(2,1)S(1)}, u32[]{:S(2)}, u32[]{:S(2)}) collective-permute-start(bf16[80,256]{1,0:T(8,128)(2,1)} %close_images.1), channel_id=1, source_target_pairs={{0,24},{8,0},{16,8},{24,16},{32,56},{40,32},{48,40},{56,48},{1,25}... | collective-permute-start | bytes 122888 | tf_op jit(solution)/shard_map/ppermute | solution.py:475
  92.3 6.3 %collective-permute-start.14 = (bf16[80,256]{1,0:T(8,128)(2,1)}, bf16[80,256]{1,0:T(8,128)(2,1)S(1)}, u32[]{:S(2)}, u32[]{:S(2)}) collective-permute-start(bf16[80,256]{1,0:T(8,128)(2,1)} %close_images.1), channel_id=1, source_target_pairs={{0,16},{8,24},{16,0},{24,8},{32,48},{40,56},{48,32},{56,40},{1,17}... | collective-permute-start | bytes 122888 | tf_op jit(solution)/shard_map/ppermute | solution.py:475
  93.1 5.7 %collective-permute-start.13 = (bf16[80,256]{1,0:T(8,128)(2,1)}, bf16[80,256]{1,0:T(8,128)(2,1)S(1)}, u32[]{:S(2)}, u32[]{:S(2)}) collective-permute-start(bf16[80,256]{1,0:T(8,128)(2,1)} %close_images.1), channel_id=1, source_target_pairs={{0,8},{8,16},{16,24},{24,0},{32,40},{40,48},{48,56},{56,32},{1,9},... | collective-permute-start | bytes 122888 | tf_op jit(solution)/shard_map/ppermute | solution.py:475
  94.0 14.8 %collective-permute-start.19 = (bf16[64,1024]{1,0:T(8,128)(2,1)}, bf16[64,1024]{1,0:T(8,128)(2,1)S(1)}, u32[]{:S(2)}, u32[]{:S(2)}) collective-permute-start(bf16[64,1024]{1,0:T(8,128)(2,1)} %get-tuple-element.58), channel_id=1, source_target_pairs={{64,0},{65,1},{66,2},{67,3},{68,4},{69,5},{70,6},{71,7},{72,8},{73... | collective-permute-start | bytes 393224 | tf_op jit(solution)/shard_map/ppermute | solution.py:485
  99.6 18.1 %copy-start.2 = (bf16[4,80,256]{2,1,0:T(8,128)(2,1)}, bf16[4,80,256]{2,1,0:T(8,128)(2,1)S(1)}, u32[]{:S(2)}) copy-start(bf16[4,80,256]{2,1,0:T(8,128)(2,1)S(1)} %pad_maximum_fusion.1.near_ref) | copy-start | bytes 491524
  99.6 10.9 %collective-permute-start.18 = (bf16[4,80,256]{2,1,0:T(8,128)(2,1)S(1)}, bf16[4,80,256]{2,1,0:T(8,128)(2,1)S(1)}, u32[]{:S(2)}, u32[]{:S(2)}) collective-permute-start(bf16[4,80,256]{2,1,0:T(8,128)(2,1)S(1)} %pad_maximum_fusion.1.near_ref), channel_id=1, source_target_pairs={{0,96},{8,104},{16,112},{24,120},{32,64},{40,72},{48,80},{56,88},{... | collective-permute-start | bytes 491528 | tf_op jit(solution)/shard_map/ppermute | solution.py:481
  101.4 10.8 %collective-permute-start.17 = (bf16[4,80,256]{2,1,0:T(8,128)(2,1)S(1)}, bf16[4,80,256]{2,1,0:T(8,128)(2,1)S(1)}, u32[]{:S(2)}, u32[]{:S(2)}) collective-permute-start(bf16[4,80,256]{2,1,0:T(8,128)(2,1)S(1)} %pad_maximum_fusion.1.near_ref), channel_id=1, source_target_pairs={{0,64},{64,0},{1,65},{65,1},{2,66},{66,2},{3,67},{67,3},{4,68},{68... | collective-permute-start | bytes 491528 | tf_op jit(solution)/shard_map/ppermute | solution.py:480
  103.8 13.9 %collective-permute-start.16 = (bf16[4,80,256]{2,1,0:T(8,128)(2,1)S(1)}, bf16[4,80,256]{2,1,0:T(8,128)(2,1)S(1)}, u32[]{:S(2)}, u32[]{:S(2)}) collective-permute-start(bf16[4,80,256]{2,1,0:T(8,128)(2,1)S(1)} %pad_maximum_fusion.1.near_ref), channel_id=1, source_target_pairs={{0,32},{8,40},{16,48},{24,56},{32,0},{40,8},{48,16},{56,24},{1,33}... | collective-permute-start | bytes 491528 | tf_op jit(solution)/shard_map/ppermute | solution.py:479
  (8 other events, 25.5 us)

commit v5 on v4

--- a/solution.py
+++ b/solution.py
@@ -110,7 +110,7 @@
 
 
 def finish_kernel(slots, mask_ref, *refs):
-    parts, (rows_ref, slot_ref) = refs[:5], refs[5:]
+    parts, (rows_ref, slot_ref) = refs[:4], refs[4:]
     slot_ref[...] = jnp.zeros_like(slot_ref)
     squares = square_rows(parts)
     scale = jnp.where(mask_ref[...] > 0.0, lax.rsqrt(squares / D + 1e-05), 0.0)
@@ -134,7 +134,7 @@
         grid_spec=pltpu.PrefetchScalarGridSpec(
             num_scalar_prefetch=1,
             grid=(1,),
-            in_specs=[pl.BlockSpec((16, 128), whole)] + [pl.BlockSpec((TALL, 128), whole)] * 5,
+            in_specs=[pl.BlockSpec((16, 128), whole)] + [pl.BlockSpec((TALL, 128), whole)] * 4,
             out_specs=[
                 pl.BlockSpec((PAGES, PAGE, 128), lambda i, slots: (0, 0, 0)),
                 pl.BlockSpec((1, 256, PAGE, 128), lambda i, slots: (1, 0, 0, 0)),
@@ -175,7 +175,7 @@
 
 
 def image_kernel(
-    place, pieces_ref, bias_ref, gain_ref, weight_ref, hidden_ref, swap_ref, same_ref, scaled, pair
+    place, pieces_ref, bias_ref, gain_ref, weight_ref, hidden_ref, heads_ref, scaled, pair
 ):
     step = pl.program_id(0)
 
@@ -203,21 +203,14 @@
         pair[...] = jnp.concatenate([rows, jnp.zeros_like(rows)], axis=1).astype(BF)
 
     product = jnp.dot(scaled[...], weight_ref[...], preferred_element_type=F32)
-    left, right = product[:, :256], product[:, 256:]
-    first = place[1] == 0
-    same_ref[0, 0:IMG, :] = jnp.where(first, left, right).astype(BF)
-    swap_ref[0, 0:IMG, :] = jnp.where(first, right, left).astype(BF)
-    same_ref[0, IMG:, :] = pair[...]
-    swap_ref[0, IMG:, :] = pair[...]
+    for k in range(2):
+        heads_ref[k, 0:IMG, :] = product[:, 256 * k : 256 * (k + 1)].astype(BF)
+        heads_ref[k, IMG:, :] = pair[...]
 
 
 def image_rows_kv(place, pieces, bias, gain, kv_w):
-    def column(i, place):
-        return (0, lax.rem(place[2] + i, 4))
-
     width = pieces.shape[2]
     row = pl.BlockSpec((width,), lambda i, place: (0,))
-    out = jax.ShapeDtypeStruct((4, IMG_TALL, 256), BF)
     return pl.pallas_call(
         image_kernel,
         grid_spec=pltpu.PrefetchScalarGridSpec(
@@ -227,25 +220,28 @@
                 pl.BlockSpec((8, IMG, width), lambda i, place: (0, 0, 0)),
                 row,
                 row,
-                pl.BlockSpec((width, 512), column),
+                pl.BlockSpec((width, 512), lambda i, place: (0, i)),
             ],
             out_specs=[
                 pl.BlockSpec((IMG, width), lambda i, place: (0, 0)),
-                pl.BlockSpec((1, IMG_TALL, 256), lambda i, place: (i, 0, 0)),
-                pl.BlockSpec((1, IMG_TALL, 256), lambda i, place: (i, 0, 0)),
+                pl.BlockSpec((2, IMG_TALL, 256), lambda i, place: (i, 0, 0)),
             ],
             scratch_shapes=[pltpu.VMEM((IMG, width), BF), pltpu.VMEM((16, 256), BF)],
         ),
-        out_shape=[jax.ShapeDtypeStruct((IMG, width), BF), out, out],
+        out_shape=[
+            jax.ShapeDtypeStruct((IMG, width), BF),
+            jax.ShapeDtypeStruct((8, IMG_TALL, 256), BF),
+        ],
         compiler_params=pltpu.CompilerParams(vmem_limit_bytes=VMEM_LIMIT),
         cost_estimate=LIGHT,
         name="image_rows_kv",
     )(place, pieces, bias, gain, kv_w)
 
 
-def close_kernel(a_ref, b_ref, c_ref, d_ref, labels_ref, out_ref):
-    total = a_ref[...].astype(F32) + b_ref[...].astype(F32)
-    total = total + c_ref[...].astype(F32) + d_ref[...].astype(F32)
+def close_kernel(parts_ref, labels_ref, out_ref):
+    total = parts_ref[0].astype(F32)
+    for k in range(1, 8):
+        total = total + parts_ref[k].astype(F32)
     squares = total[IMG : IMG + 1, 0:128] + total[IMG + 1 : IMG + 2, 0:128]
     scale = lax.rsqrt(squares / D + 1e-05)
     scale = jnp.where(labels_ref[3:4, 0:128].astype(F32) > 0.5, scale, 0.0)
@@ -261,7 +257,7 @@
         out_shape=jax.ShapeDtypeStruct((IMG_TALL, 256), BF),
         cost_estimate=LIGHT,
         name="close_images",
-    )(*parts, labels)
+    )(parts, labels)
 
 
 def merge_kernel(
@@ -443,34 +439,27 @@
     got = after(got, keep[0])
     swapped = lax.ppermute(got, "mp", PARTNER)
     received = [lax.ppermute(piece, "mp", PARTNER) for piece in send]
-    added = [None] + [add_pair(keep[j], received[j]) for j in (1, 2, 3)]
-    parts = [keep[0], received[0]] + [lax.ppermute(added[j], "mp", shift(j)) for j in (1, 2, 3)]
-
-    feats = jnp.concatenate([got, after(swapped, added[1:])], axis=1).reshape(8 * IMG, -1)
+
+    feats = jnp.concatenate([got, swapped], axis=1).reshape(8 * IMG, -1)
     partial = jnp.dot(feats, proj_w, preferred_element_type=F32).astype(BF).reshape(8, IMG, -1)
-    attended = lax.cond(
-        group != 0,
-        attend,
-        lambda *unused: jnp.zeros(queries.shape, BF),
-        after(queries, partial),
-        kv_cache,
-        new_kv,
-        cache_lengths,
-    )
     pieces = lax.all_to_all(partial, "seq", 0, 0, tiled=True)
-    image_hidden, swap, same = image_rows_kv(place, pieces, proj_b, norm_gain, kv_w)
-    image_pairs = add_pair(same, lax.ppermute(swap, "mp", PARTNER))
-    image_parts = [image_pairs[0]]
-    image_parts += [lax.ppermute(image_pairs[j], "mp", shift(j)) for j in (1, 2, 3)]
-
-    rows, by_owner = finish_text(slots, after(mask, attended), parts)
+
+    added = [None] + [add_pair(after(keep[j], partial), received[j]) for j in (1, 2, 3)]
+    base = keep[0].astype(F32) + after(received[0], added[1:]).astype(F32)
+    parts = [base] + [lax.ppermute(added[j], "mp", shift(j)) for j in (1, 2, 3)]
+
+    image_hidden, heads = image_rows_kv(
+        place, after(pieces, base), proj_b, norm_gain, kv_w
+    )
+    image_parts = lax.all_to_all(heads, "mp", 0, 0, tiled=True)
+    image_block = close_images(image_parts, labels)
+
+    rows, by_owner = finish_text(slots, after(mask, image_block), parts)
     other_rows = lax.ppermute(rows, "group", [(1, 0)])
     arrived = lax.all_to_all(
         by_owner.reshape(512, PAGE, 128), ("group", "seq"), split_axis=0, concat_axis=0, tiled=True
     ).reshape(2, 256, PAGE, 128)
 
-    image_parts = after(image_parts, by_owner)
-    image_block = close_images(image_parts, labels)
     near = jnp.stack(
         [image_block] + [lax.ppermute(image_block, "seq", seq_shift(0, k)) for k in (1, 2, 3)]
     )
@@ -480,6 +469,15 @@
         lax.ppermute(near, "group", [(0, 1), (1, 0)]),
         lax.ppermute(near, ("group", "seq"), FAR),
     ]
+    attended = lax.cond(
+        group != 0,
+        attend,
+        lambda *unused: jnp.zeros(queries.shape, BF),
+        after(queries, near),
+        kv_cache,
+        new_kv,
+        cache_lengths,
+    )
     page_slots = merge_slots(place, slots, by_owner, other_rows, arrived, images)
 
     other_hidden = lax.ppermute(image_hidden, "group", [(1, 0)])

time: 126 us -> 140 us (1.11); the launches traced: 125 us -> 138 us
  waiting for transfers between devices: 20.3 us -> 31.9 us
    ppermute x3, waiting for transfers between devices: 3.25 us -> 17.9 us  [per_device(): lax.ppermute(image_block, 'seq', seq_shift(0, k))]
    all_to_all x0 -> x1, waiting for transfers between devices: none -> 7.2 us  [per_device(): image_parts = lax.all_to_all(heads, 'mp', 0, 0, tiled=True)]
    ppermute x1, waiting for transfers between devices: 5.03 us -> 0.01 us  [per_device(): other_hidden = lax.ppermute(image_hidden, 'group', [(1, 0)])]
    all_to_all x0 -> x1, starting transfers between devices: none -> 4.83 us  [per_device(): image_parts = lax.all_to_all(heads, 'mp', 0, 0, tiled=True)]
    ppermute x7 -> x3, waiting for transfers between devices: 4.8 us -> 0.01 us  [per_device(): parts = [base] + [lax.ppermute(added[j], 'mp', shift(j)) for j in (1, 2, 3)]]
    ppermute x7 -> x3, starting transfers between devices: 8.49 us -> 4.83 us  [per_device(): parts = [base] + [lax.ppermute(added[j], 'mp', shift(j)) for j in (1, 2, 3)]]
    ppermute x1, waiting for transfers between devices: 5.5 us -> 1.86 us  [per_device(): lax.ppermute(near, 'seq', seq_shift(1, 0))]
    all_to_all x1, waiting for transfers between devices: 0.01 us -> 3.44 us  [per_device(): pieces = lax.all_to_all(partial, 'seq', 0, 0, tiled=True)]
  transfers between devices with their start and end apart: 23 -> 20, of which waited for: 9 -> 6; matrix products, arithmetic and copies ran while one was open for 20% -> 17% of each run, Pallas kernels for 17% -> 12%
where the time goes in v5:
time: 140 us; the launch traced here: 138 us
  starting transfers between devices  46.8 us (33%)
  waiting for transfers between devices  31.9 us (23%)
  Pallas kernels  30.1 us (22%)
  other arithmetic  12.8 us (9%)
  matrix products  11.4 us (8%)
  local copies, waits for them, and re-layouts  2.76 us (2%)
  between operations  1.56 us (1%)
    ppermute x3, waiting for transfers between devices, per_device(): lax.ppermute(image_block, 'seq', seq_shift(0, k))  17.9 us
    pallas_call x1, Pallas kernels, project_text(): pl.pallas_call(project_kernel, grid_spec=pltpu.PrefetchScalarGridSpec(num...  9.29 us
    all_to_all x1, starting transfers between devices, per_device(): lax.all_to_all(by_owner.reshape(512, PAGE, 128), ('group', 'seq'), split_...  8.42 us
    all_to_all x1, starting transfers between devices, per_device(): pieces = lax.all_to_all(partial, 'seq', 0, 0, tiled=True)  7.46 us
    all_to_all x1, waiting for transfers between devices, per_device(): image_parts = lax.all_to_all(heads, 'mp', 0, 0, tiled=True)  7.2 us
    all_to_all x1, starting transfers between devices, per_device(): lax.all_to_all(cut_features(place, image_feats), 'seq', 0, 0, tiled=True)  7.05 us
    pallas_call x1, Pallas kernels, merge_slots(): pl.pallas_call(merge_kernel, grid_spec=pltpu.PrefetchScalarGridSpec(num_s...  6.72 us
    pallas_call x1, Pallas kernels, image_rows_kv(): pl.pallas_call(image_kernel, grid_spec=pltpu.PrefetchScalarGridSpec(num_s...  5.75 us
  transfers between devices with their start and end apart: 20, of which 6 were waited for; matrix products, arithmetic and copies ran while one was open for 17% of the time, Pallas kernels for 12%

profile of v5, /device:TPU:10, one launch (start us, length us, event | category | flops | bytes accessed | tf_op | source)
XLA Modules:
  0.0 137.6 jit_solution(3643339070506554681)
XLA Ops:
  1.3 2.7 %cut_features.1 = bf16[8,32,912]{2,1,0:T(8,128)(2,1)} custom-call(s32[4]{0:T(128)} %pad_add_fusion.place, bf16[128,7296]{1,0:T(8,128)(2,1)} %feats_ref.1), custom_call_target="tpu_custom_call" | custom-call | flops 1 | bytes 1 | tf_op jit(solution)/shard_map/cut_features/pallas_call | solution.py:161
  4.0 7.0 %all-to-all-start = ((bf16[8,32,912]{2,1,0:T(8,128)(2,1)}), bf16[8,32,912]{2,1,0:T(8,128)(2,1)S(1)}, u32[]{:S(2)}, u32[]{:S(2)}) async-start(bf16[8,32,912]{2,1,0:T(8,128)(2,1)} %cut_features.1), calls=%async_computation | async-start | bytes 1048576 | tf_op jit(solution)/shard_map/all_to_all | solution.py:436
  11.1 9.3 %project_text.1 = (bf16[2080,128]{1,0:T(8,128)(2,1)}, bf16[2080,128]{1,0:T(8,128)(2,1)}, bf16[2080,128]{1,0:T(8,128)(2,1)}, bf16[2080,128]{1,0:T(8,128)(2,1)}, b...) custom-call(s32[4]{0:T(128)} %pad_add_fusion.place, ...), custom_call_target="tpu_custom_call" | custom-call | flops 1 | bytes 1 | tf_op jit(solution)/shard_map/project_text/pallas_call | solution.py:84
  23.9 1.5 %collective-permute-done = bf16[8,32,912]{2,1,0:T(8,128)(2,1)S(1)} collective-permute-done((bf16[8,32,912]{2,1,0:T(8,128)(2,1)S(1)}, bf16[8,32,912]{2,1,0:T(8,128)(2,1)S(1)}, u32[]{:S(2)}, u32[]{:S(2)}) %collective-permute-start) | collective-permute-done | bytes 466976 | tf_op jit(solution)/shard_map/ppermute | solution.py:440
  25.5 2.3 %convolution_convert_fusion = bf16[512,1024]{1,0:T(8,128)(2,1)} fusion(bf16[512,912]{1,0:T(8,128)(2,1)S(1)} %bitcast.71, bf16[912,1024]{1,0:T(8,128)(2,1)S(1)} %copy-done), kind=kOutput, calls=%fused_computation.26 | convolution fusion | flops 956825600 | bytes 3850240 | tf_op jit(solution)/shard_map/dot_general | solution.py:444
  27.8 7.5 %all-to-all-start.1 = ((bf16[8,64,1024]{2,1,0:T(8,128)(2,1)}), bf16[8,64,1024]{2,1,0:T(8,128)(2,1)S(1)}, u32[]{:S(2)}, u32[]{:S(2)}) async-start(bf16[8,64,1024]{2,1,0:T(8,128)(2,1)} %bitcast.70), calls=%async_computation.1 | async-start | bytes 2097152 | tf_op jit(solution)/shard_map/all_to_all | solution.py:445
  35.3 2.2 %add_convert_fusion.2 = bf16[2080,128]{1,0:T(8,128)(2,1)} fusion(bf16[2080,128]{1,0:T(8,128)(2,1)} %collective-permute-done.2, bf16[2080,128]{1,0:T(8,128)(2,1)} %get-tuple-element.41), kind=kLoop, calls=%fused_computation.33 | loop fusion | flops 1064960 | bytes 1597440 | tf_op jit(solution)/shard_map/convert_element_type | solution.py:109
  37.5 1.5 %collective-permute-start.5 = (bf16[2080,128]{1,0:T(8,128)(2,1)}, bf16[2080,128]{1,0:T(8,128)(2,1)}, u32[]{:S(2)}, u32[]{:S(2)}) collective-permute-start(bf16[2080,128]{1,0:T(8,128)(2,1)} %add_convert_fusion.2), channel_id=1, source_target_pairs={{0,2},{1,3},{2,4},{3,5},{4,6},{5,7},{6,0},{7,1},{8,10},{9,11},{10,... | collective-permute-start | bytes 1597448 | tf_op jit(solution)/shard_map/ppermute | solution.py:449
  39.0 2.0 %add_convert_fusion.1 = bf16[2080,128]{1,0:T(8,128)(2,1)} fusion(bf16[2080,128]{1,0:T(8,128)(2,1)} %collective-permute-done.3, bf16[2080,128]{1,0:T(8,128)(2,1)S(1)} %copy-done.5), kind=kLoop, calls=%fused_computation.32 | loop fusion | flops 1064960 | bytes 1597440 | tf_op jit(solution)/shard_map/convert_element_type | solution.py:109
  41.0 1.1 collective-permute-start.6
  42.1 1.2 add_convert_fusion
  43.3 2.2 %collective-permute-start.7 = (bf16[2080,128]{1,0:T(8,128)(2,1)S(1)}, bf16[2080,128]{1,0:T(8,128)(2,1)}, u32[]{:S(2)}, u32[]{:S(2)}) collective-permute-start(bf16[2080,128]{1,0:T(8,128)(2,1)S(1)} %add_convert_fusion), channel_id=1, source_target_pairs={{0,6},{1,7},{2,0},{3,1},{4,2},{5,3},{6,4},{7,5},{8,14},{9,15},{10,... | collective-permute-start | bytes 1597448 | tf_op jit(solution)/shard_map/ppermute | solution.py:449
  45.5 2.1 %convert_add_fusion.refs_0_ = f32[2080,128]{1,0:T(8,128)} fusion(bf16[2080,128]{1,0:T(8,128)(2,1)} %collective-permute-done.1, bf16[2080,128]{1,0:T(8,128)(2,1)S(1)} %copy-done.6), kind=kLoop, calls=%fused_computation.30 | loop fusion | flops 798720 | bytes 2129920 | tf_op jit(solution)/shard_map/add | solution.py:448
  47.7 3.4 %all-to-all-done.1.pieces_ref = bf16[8,64,1024]{2,1,0:T(8,128)(2,1)S(1)} async-done(((bf16[8,64,1024]{2,1,0:T(8,128)(2,1)}), bf16[8,64,1024]{2,1,0:T(8,128)(2,1)S(1)}, u32[]{:S(2)}, u32[]{:S(2)}) %all-to-all-start.1) | async-done | bytes 1048608 | tf_op jit(solution)/shard_map/all_to_all | solution.py:445
  52.1 5.7 %image_rows_kv.1 = (bf16[64,1024]{1,0:T(8,128)(2,1)}, bf16[8,80,256]{2,1,0:T(8,128)(2,1)}) custom-call(s32[4]{0:T(128)} %pad_add_fusion.place, bf16[8,64,1024]{2,1,0:T(8,128)(2,1)} %copy-done.1, bf16[1024]{0:T(1024)(128)(2,1)} %bias_ref.1, bf16[1024]{0:T(1024)(128)(2,1)} %gain_ref.3, bf16[1024,2048]{1,0:T(8,128)(2,1)} %weight_ref.1), custom_call_target="tpu_custom_call" | custom-call | flops 1 | bytes 1 | tf_op jit(solution)/shard_map/image_rows_kv/pallas_call | solution.py:214
  57.8 4.8 %all-to-all-start.2 = ((bf16[8,80,256]{2,1,0:T(8,128)(2,1)}), bf16[8,80,256]{2,1,0:T(8,128)(2,1)S(1)}, u32[]{:S(2)}, u32[]{:S(2)}) async-start(bf16[8,80,256]{2,1,0:T(8,128)(2,1)} %get-tuple-element.51), calls=%async_computation.2 | async-start | bytes 655360 | tf_op jit(solution)/shard_map/all_to_all | solution.py:454
  64.1 7.2 %all-to-all-done.2.parts_ref = bf16[8,80,256]{2,1,0:T(8,128)(2,1)S(1)} async-done(((bf16[8,80,256]{2,1,0:T(8,128)(2,1)}), bf16[8,80,256]{2,1,0:T(8,128)(2,1)S(1)}, u32[]{:S(2)}, u32[]{:S(2)}) %all-to-all-start.2) | async-done | bytes 327712 | tf_op jit(solution)/shard_map/all_to_all | solution.py:454
  72.0 1.7 %close_images.1 = bf16[80,256]{1,0:T(8,128)(2,1)} custom-call(bf16[8,80,256]{2,1,0:T(8,128)(2,1)} %copy-done.2, bf16[16,256]{1,0:T(8,128)(2,1)} %fusion.26.labels_ref), custom_call_target="tpu_custom_call" | custom-call | flops 1 | bytes 1 | tf_op jit(solution)/shard_map/close_images/pallas_call | solution.py:255
  73.7 4.0 %finish_text.1 = (bf16[128,16,128]{2,1,0:T(8,128)(2,1)}, bf16[2,256,16,128]{3,2,1,0:T(8,128)(2,1)}) custom-call(s32[128]{0:T(128)} %multiply_add_fusion.slots, f32[16,128]{1,0:T(8,128)} %fusion.15.mask_ref, f32[2080,128]{1,0:T(8,128)} %convert_add_fusion.refs_0_, bf16[2080,128]{1,0:T(8,128)(2,1)} %collective-permute-done.5.refs_1_, ...), custom_call_target="tpu_custom_call" | custom-call | flops 20000000000 | bytes 73999998976 | tf_op jit(solution)/shard_map/finish_text/pallas_call | solution.py:132
  77.7 8.4 %all-to-all-start.3 = ((bf16[512,16,128]{2,1,0:T(8,128)(2,1)}), bf16[512,16,128]{2,1,0:T(8,128)(2,1)}, u32[]{:S(2)}, u32[]{:S(2)}) async-start(bf16[512,16,128]{2,1,0:T(8,128)(2,1)} %bitcast.65), calls=%async_computation.3 | async-start | bytes 4194304 | tf_op jit(solution)/shard_map/all_to_all | solution.py:459
  86.2 2.1 %collective-permute-start.8 = (bf16[128,16,128]{2,1,0:T(8,128)(2,1)}, bf16[128,16,128]{2,1,0:T(8,128)(2,1)S(1)}, u32[]{:S(2)}, u32[]{:S(2)}) collective-permute-start(bf16[128,16,128]{2,1,0:T(8,128)(2,1)} %get-tuple-element.54), channel_id=1, source_target_pairs={{64,0},{65,1},{66,2},{67,3},{68,4},{69,5},{70,6},{71,7},{72,8},{73... | collective-permute-start | bytes 1572872 | tf_op jit(solution)/shard_map/ppermute | solution.py:458
  88.3 3.1 %collective-permute-start.11 = (bf16[80,256]{1,0:T(8,128)(2,1)S(1)}, bf16[80,256]{1,0:T(8,128)(2,1)S(1)}, u32[]{:S(2)}, u32[]{:S(2)}) collective-permute-start(bf16[80,256]{1,0:T(8,128)(2,1)S(1)} %copy-done.9), channel_id=1, source_target_pairs={{0,24},{8,0},{16,8},{24,16},{32,56},{40,32},{48,40},{56,48},{1,25}... | collective-permute-start | bytes 122888 | tf_op jit(solution)/shard_map/ppermute | solution.py:464
  93.1 1.9 %collective-permute-start.15 = (bf16[64,1024]{1,0:T(8,128)(2,1)S(1)}, bf16[64,1024]{1,0:T(8,128)(2,1)}, u32[]{:S(2)}, u32[]{:S(2)}) collective-permute-start(bf16[64,1024]{1,0:T(8,128)(2,1)S(1)} %copy-done.12), channel_id=1, source_target_pairs={{64,0},{65,1},{66,2},{67,3},{68,4},{69,5},{70,6},{71,7},{72,8},{73... | collective-permute-start | bytes 393224 | tf_op jit(solution)/shard_map/ppermute | solution.py:483
  95.1 16.5 %collective-permute-done.11 = bf16[80,256]{1,0:T(8,128)(2,1)S(1)} collective-permute-done((bf16[80,256]{1,0:T(8,128)(2,1)S(1)}, bf16[80,256]{1,0:T(8,128)(2,1)S(1)}, u32[]{:S(2)}, u32[]{:S(2)}) %collective-permute-start.11) | collective-permute-done | bytes 40992 | tf_op jit(solution)/shard_map/ppermute | solution.py:464
  111.6 1.3 collective-permute-done.9
  114.0 2.8 %collective-permute-start.13 = (bf16[4,80,256]{2,1,0:T(8,128)(2,1)S(1)}, bf16[4,80,256]{2,1,0:T(8,128)(2,1)S(1)}, u32[]{:S(2)}, u32[]{:S(2)}) collective-permute-start(bf16[4,80,256]{2,1,0:T(8,128)(2,1)S(1)} %pad_maximum_fusion.1.near_ref), channel_id=1, source_target_pairs={{0,64},{64,0},{1,65},{65,1},{2,66},{66,2},{3,67},{67,3},{4,68},{68... | collective-permute-start | bytes 491528 | tf_op jit(solution)/shard_map/ppermute | solution.py:469
  117.2 9.2 %conditional.1 = (bf16[128,1024]{1,0:T(8,128)(2,1)S(1)}) conditional(s32[]{:T(128)} %convert_element_type.87, () %tuple.29, (s32[128]{0:T(128)S(1)}, bf16[128,1024]{1,0:T(8,128)(2,1)S(1)}, bf16[128,128,256]{2,1,0:T(8,128)(2,1)}, bf16[128,256]{1,0:T(8,128)(2,1)}) %tuple.43), branch_computations={%region_4.5_spmd, %region_5.8_spmd} | conditional | flops 68852736 | bytes 12419620 | solution.py:472
  117.5 4.6 %fusion.36 = (f32[128,8]{1,0:T(8,128)S(1)}, f32[128,8,128]{2,1,0:T(8,128)S(1)}) fusion(bf16[128,8,128]{2,1,0:T(8,128)(2,1)S(1)} %bitcast.68, bf16[128,128,1,256]{3,1,0,2:T(8,128)(2,1)} %bitcast.66, pred[128,128]{1,0:T(8,128)(4,1)S(1)} %iota_compare_fusion), kind=kOutput, calls=%fused_computation.84 | convolution fusion | flops 33946624 | bytes 5001216 | tf_op jit(solution)/shard_map/cond/branch_1_fun/rgqh,rjgh->rgqj/dot_general | solution.py:350
  122.9 3.5 %fusion.5 = bf16[128,8,128]{2,1,0:T(8,128)(2,1)S(1)} fusion(bf16[128,128,1,256]{3,1,0,2:T(8,128)(2,1)} %bitcast.67, f32[128,8,128]{2,1,0:T(8,128)S(1)} %get-tuple-element.74, f32[128,128]{1,0:T(8,128)S(1)} %get-tuple-element.72, f32[128,8]{1,0:T(8,128)S(1)} %bitcast_convert_fusion, f32[128,8]{1,0:T(8,128)S(1)} %get-tuple-element.69, ...), kind=kOutput, calls=%fused_computation.7 | convolution fusion | flops 34340864 | bytes 5058560 | tf_op jit(solution)/shard_map/cond/branch_1_fun/rgqj,rjgh->rgqh/dot_general | solution.py:366
  126.4 1.7 %maximum_select_fusion = bf16[128,1024]{1,0:T(8,128)(2,1)} fusion(bf16[128,1024]{1,0:T(8,128)(2,1)S(1)} %get-tuple-element.77, bf16[64,1024]{1,0:T(8,128)(2,1)} %collective-permute-done.15, bf16[64,1024]{1,0:T(8,128)(2,1)S(1)} %copy-done.12, pred[]{:T(512)S(6)} %eq.79), kind=kLoop, calls=%fused_computation.35 | loop fusion | flops 655360 | bytes 786433 | tf_op jit(solution)/shard_map/jit(_where)/select_n | solution.py:484
  128.1 1.9 %collective-permute-done.12.yonder_ref = bf16[4,80,256]{2,1,0:T(8,128)(2,1)S(1)} collective-permute-done((bf16[4,80,256]{2,1,0:T(8,128)(2,1)S(1)}, bf16[4,80,256]{2,1,0:T(8,128)(2,1)S(1)}, u32[]{:S(2)}, u32[]{:S(2)}) %collective-permute-start.12) | collective-permute-done | bytes 163872 | tf_op jit(solution)/shard_map/ppermute | solution.py:468
  130.9 6.7 %merge_slots.1 = bf16[256,16,256]{2,1,0:T(8,128)(2,1)} custom-call(s32[4]{0:T(128)} %pad_add_fusion.place, s32[128]{0:T(128)} %multiply_add_fusion.slots, bf16[2,256,16,128]{3,2,1,0:T(8,128)(2,1)} %get-tuple-element.53.own_ref, bf16[128,16,128]{2,1,0:T(8,128)(2,1)} %copy-done.7, bf16[2,256,16,128]{3,2,1,0:T(8,128)(2,1)} %bitcast.23.first_ref.second_ref, ...), custom_call_target="tpu_custom_call" | custom-call | flops 1 | bytes 1 | tf_op jit(solution)/shard_map/merge_slots/pallas_call | solution.py:322
  (83 shorter events, 11.7 us)
Async XLA Ops:
  0.6 24.9 %copy-start = (bf16[912,1024]{1,0:T(8,128)(2,1)S(1)}, bf16[912,1024]{1,0:T(8,128)(2,1)}, u32[]{:S(2)}) copy-start(bf16[912,1024]{1,0:T(8,128)(2,1)} %param.18) | copy-start | bytes 5603332
  4.0 18.5 %all-to-all-start = ((bf16[8,32,912]{2,1,0:T(8,128)(2,1)}), bf16[8,32,912]{2,1,0:T(8,128)(2,1)S(1)}, u32[]{:S(2)}, u32[]{:S(2)}) async-start(bf16[8,32,912]{2,1,0:T(8,128)(2,1)} %cut_features.1), calls=%async_computation | async-start | bytes 1048576 | tf_op jit(solution)/shard_map/all_to_all | solution.py:436
  11.0 10.4 %copy-start.15 = (s32[128,1]{0,1:T(1,128)S(1)}, s32[128,1]{0,1:T(1,128)}, u32[]{:S(2)}) copy-start(s32[128,1]{0,1:T(1,128)} %param.23) | copy-start | bytes 1540
  11.0 10.6 %copy-start.14 = (s32[128]{0:T(128)S(1)}, s32[128]{0:T(128)}, u32[]{:S(2)}) copy-start(s32[128]{0:T(128)} %param.17) | copy-start | bytes 1540
  11.1 11.5 %copy-start.17 = (s32[4]{0:T(128)S(1)}, s32[4]{0:T(128)}, u32[]{:S(2)}) copy-start(s32[4]{0:T(128)} %param.22) | copy-start | bytes 52
  20.4 25.2 %collective-permute-start.1 = (bf16[2080,128]{1,0:T(8,128)(2,1)}, bf16[2080,128]{1,0:T(8,128)(2,1)}, u32[]{:S(2)}, u32[]{:S(2)}) collective-permute-start(bf16[2080,128]{1,0:T(8,128)(2,1)} %get-tuple-element.39), channel_id=1, source_target_pairs={{0,1},{1,0},{2,3},{3,2},{4,5},{5,4},{6,7},{7,6},{8,9},{9,8},{10,11... | collective-permute-start | bytes 1597448 | tf_op jit(solution)/shard_map/ppermute | solution.py:441
  20.5 14.8 %collective-permute-start.2 = (bf16[2080,128]{1,0:T(8,128)(2,1)}, bf16[2080,128]{1,0:T(8,128)(2,1)}, u32[]{:S(2)}, u32[]{:S(2)}) collective-permute-start(bf16[2080,128]{1,0:T(8,128)(2,1)} %get-tuple-element.42), channel_id=1, source_target_pairs={{0,1},{1,0},{2,3},{3,2},{4,5},{5,4},{6,7},{7,6},{8,9},{9,8},{10,11... | collective-permute-start | bytes 1597448 | tf_op jit(solution)/shard_map/ppermute | solution.py:441
  21.0 18.1 %collective-permute-start.3 = (bf16[2080,128]{1,0:T(8,128)(2,1)}, bf16[2080,128]{1,0:T(8,128)(2,1)}, u32[]{:S(2)}, u32[]{:S(2)}) collective-permute-start(bf16[2080,128]{1,0:T(8,128)(2,1)} %get-tuple-element.45), channel_id=1, source_target_pairs={{0,1},{1,0},{2,3},{3,2},{4,5},{5,4},{6,7},{7,6},{8,9},{9,8},{10,11... | collective-permute-start | bytes 1597448 | tf_op jit(solution)/shard_map/ppermute | solution.py:441
  21.0 21.1 %collective-permute-start.4 = (bf16[2080,128]{1,0:T(8,128)(2,1)}, bf16[2080,128]{1,0:T(8,128)(2,1)}, u32[]{:S(2)}, u32[]{:S(2)}) collective-permute-start(bf16[2080,128]{1,0:T(8,128)(2,1)} %get-tuple-element.48), channel_id=1, source_target_pairs={{0,1},{1,0},{2,3},{3,2},{4,5},{5,4},{6,7},{7,6},{8,9},{9,8},{10,11... | collective-permute-start | bytes 1597448 | tf_op jit(solution)/shard_map/ppermute | solution.py:441
  22.5 2.9 %collective-permute-start = (bf16[8,32,912]{2,1,0:T(8,128)(2,1)S(1)}, bf16[8,32,912]{2,1,0:T(8,128)(2,1)S(1)}, u32[]{:S(2)}, u32[]{:S(2)}) collective-permute-start(bf16[8,32,912]{2,1,0:T(8,128)(2,1)S(1)} %all-to-all-done), channel_id=1, source_target_pairs={{0,1},{1,0},{2,3},{3,2},{4,5},{5,4},{6,7},{7,6},{8,9},{9,8},{10,11... | collective-permute-start | bytes 1400840 | tf_op jit(solution)/shard_map/ppermute | solution.py:440
  27.8 11.2 %copy-start.5 = (bf16[2080,128]{1,0:T(8,128)(2,1)S(1)}, bf16[2080,128]{1,0:T(8,128)(2,1)}, u32[]{:S(2)}) copy-start(bf16[2080,128]{1,0:T(8,128)(2,1)} %get-tuple-element.44) | copy-start | bytes 1597444
  27.8 23.3 %all-to-all-start.1 = ((bf16[8,64,1024]{2,1,0:T(8,128)(2,1)}), bf16[8,64,1024]{2,1,0:T(8,128)(2,1)S(1)}, u32[]{:S(2)}, u32[]{:S(2)}) async-start(bf16[8,64,1024]{2,1,0:T(8,128)(2,1)} %bitcast.70), calls=%async_computation.1 | async-start | bytes 2097152 | tf_op jit(solution)/shard_map/all_to_all | solution.py:445
  35.3 6.9 %copy-start.4 = (bf16[2080,128]{1,0:T(8,128)(2,1)S(1)}, bf16[2080,128]{1,0:T(8,128)(2,1)}, u32[]{:S(2)}) copy-start(bf16[2080,128]{1,0:T(8,128)(2,1)} %get-tuple-element.47) | copy-start | bytes 1597444
  35.3 10.3 %copy-start.6 = (bf16[2080,128]{1,0:T(8,128)(2,1)S(1)}, bf16[2080,128]{1,0:T(8,128)(2,1)}, u32[]{:S(2)}) copy-start(bf16[2080,128]{1,0:T(8,128)(2,1)} %get-tuple-element.37) | copy-start | bytes 1597444
  37.5 36.2 %collective-permute-start.5 = (bf16[2080,128]{1,0:T(8,128)(2,1)}, bf16[2080,128]{1,0:T(8,128)(2,1)}, u32[]{:S(2)}, u32[]{:S(2)}) collective-permute-start(bf16[2080,128]{1,0:T(8,128)(2,1)} %add_convert_fusion.2), channel_id=1, source_target_pairs={{0,2},{1,3},{2,4},{3,5},{4,6},{5,7},{6,0},{7,1},{8,10},{9,11},{10,... | collective-permute-start | bytes 1597448 | tf_op jit(solution)/shard_map/ppermute | solution.py:449
  41.0 32.7 %collective-permute-start.6 = (bf16[2080,128]{1,0:T(8,128)(2,1)}, bf16[2080,128]{1,0:T(8,128)(2,1)}, u32[]{:S(2)}, u32[]{:S(2)}) collective-permute-start(bf16[2080,128]{1,0:T(8,128)(2,1)} %add_convert_fusion.1), channel_id=1, source_target_pairs={{0,4},{1,5},{2,6},{3,7},{4,0},{5,1},{6,2},{7,3},{8,12},{9,13},{10,... | collective-permute-start | bytes 1597448 | tf_op jit(solution)/shard_map/ppermute | solution.py:449
  43.3 30.4 %collective-permute-start.7 = (bf16[2080,128]{1,0:T(8,128)(2,1)S(1)}, bf16[2080,128]{1,0:T(8,128)(2,1)}, u32[]{:S(2)}, u32[]{:S(2)}) collective-permute-start(bf16[2080,128]{1,0:T(8,128)(2,1)S(1)} %add_convert_fusion), channel_id=1, source_target_pairs={{0,6},{1,7},{2,0},{3,1},{4,2},{5,3},{6,4},{7,5},{8,14},{9,15},{10,... | collective-permute-start | bytes 1597448 | tf_op jit(solution)/shard_map/ppermute | solution.py:449
  57.8 13.4 %all-to-all-start.2 = ((bf16[8,80,256]{2,1,0:T(8,128)(2,1)}), bf16[8,80,256]{2,1,0:T(8,128)(2,1)S(1)}, u32[]{:S(2)}, u32[]{:S(2)}) async-start(bf16[8,80,256]{2,1,0:T(8,128)(2,1)} %get-tuple-element.51), calls=%async_computation.2 | async-start | bytes 655360 | tf_op jit(solution)/shard_map/all_to_all | solution.py:454
  77.7 10.5 %copy-start.9 = (bf16[80,256]{1,0:T(8,128)(2,1)S(1)}, bf16[80,256]{1,0:T(8,128)(2,1)}, u32[]{:S(2)}) copy-start(bf16[80,256]{1,0:T(8,128)(2,1)} %close_images.1) | copy-start | bytes 122884
  77.7 15.4 %copy-start.12 = (bf16[64,1024]{1,0:T(8,128)(2,1)S(1)}, bf16[64,1024]{1,0:T(8,128)(2,1)}, u32[]{:S(2)}) copy-start(bf16[64,1024]{1,0:T(8,128)(2,1)} %get-tuple-element.55) | copy-start | bytes 393220
  77.7 39.4 %copy-start.8 = (bf16[128,1024]{1,0:T(8,128)(2,1)S(1)}, bf16[128,1024]{1,0:T(8,128)(2,1)}, u32[]{:S(2)}) copy-start(bf16[128,1024]{1,0:T(8,128)(2,1)} %param.24) | copy-start | bytes 786436
  77.7 39.4 %copy-start.16 = (s32[128]{0:T(128)S(1)}, s32[128]{0:T(128)}, u32[]{:S(2)}) copy-start(s32[128]{0:T(128)} %param.27) | copy-start | bytes 1540
  77.7 52.2 %all-to-all-start.3 = ((bf16[512,16,128]{2,1,0:T(8,128)(2,1)}), bf16[512,16,128]{2,1,0:T(8,128)(2,1)}, u32[]{:S(2)}, u32[]{:S(2)}) async-start(bf16[512,16,128]{2,1,0:T(8,128)(2,1)} %bitcast.65), calls=%async_computation.3 | async-start | bytes 4194304 | tf_op jit(solution)/shard_map/all_to_all | solution.py:459
  86.2 43.8 %collective-permute-start.8 = (bf16[128,16,128]{2,1,0:T(8,128)(2,1)}, bf16[128,16,128]{2,1,0:T(8,128)(2,1)S(1)}, u32[]{:S(2)}, u32[]{:S(2)}) collective-permute-start(bf16[128,16,128]{2,1,0:T(8,128)(2,1)} %get-tuple-element.54), channel_id=1, source_target_pairs={{64,0},{65,1},{66,2},{67,3},{68,4},{69,5},{70,6},{71,7},{72,8},{73... | collective-permute-start | bytes 1572872 | tf_op jit(solution)/shard_map/ppermute | solution.py:458
  88.3 23.3 %collective-permute-start.11 = (bf16[80,256]{1,0:T(8,128)(2,1)S(1)}, bf16[80,256]{1,0:T(8,128)(2,1)S(1)}, u32[]{:S(2)}, u32[]{:S(2)}) collective-permute-start(bf16[80,256]{1,0:T(8,128)(2,1)S(1)} %copy-done.9), channel_id=1, source_target_pairs={{0,24},{8,0},{16,8},{24,16},{32,56},{40,32},{48,40},{56,48},{1,25}... | collective-permute-start | bytes 122888 | tf_op jit(solution)/shard_map/ppermute | solution.py:464
  91.4 20.2 %collective-permute-start.10 = (bf16[80,256]{1,0:T(8,128)(2,1)S(1)}, bf16[80,256]{1,0:T(8,128)(2,1)S(1)}, u32[]{:S(2)}, u32[]{:S(2)}) collective-permute-start(bf16[80,256]{1,0:T(8,128)(2,1)S(1)} %copy-done.9), channel_id=1, source_target_pairs={{0,16},{8,24},{16,0},{24,8},{32,48},{40,56},{48,32},{56,40},{1,17}... | collective-permute-start | bytes 122888 | tf_op jit(solution)/shard_map/ppermute | solution.py:464
  92.3 20.7 %collective-permute-start.9 = (bf16[80,256]{1,0:T(8,128)(2,1)S(1)}, bf16[80,256]{1,0:T(8,128)(2,1)S(1)}, u32[]{:S(2)}, u32[]{:S(2)}) collective-permute-start(bf16[80,256]{1,0:T(8,128)(2,1)S(1)} %copy-done.9), channel_id=1, source_target_pairs={{0,8},{8,16},{16,24},{24,0},{32,40},{40,48},{48,56},{56,32},{1,9},... | collective-permute-start | bytes 122888 | tf_op jit(solution)/shard_map/ppermute | solution.py:464
  93.1 33.3 %collective-permute-start.15 = (bf16[64,1024]{1,0:T(8,128)(2,1)S(1)}, bf16[64,1024]{1,0:T(8,128)(2,1)}, u32[]{:S(2)}, u32[]{:S(2)}) collective-permute-start(bf16[64,1024]{1,0:T(8,128)(2,1)S(1)} %copy-done.12), channel_id=1, source_target_pairs={{64,0},{65,1},{66,2},{67,3},{68,4},{69,5},{70,6},{71,7},{72,8},{73... | collective-permute-start | bytes 393224 | tf_op jit(solution)/shard_map/ppermute | solution.py:483
  113.0 17.0 %collective-permute-start.12 = (bf16[4,80,256]{2,1,0:T(8,128)(2,1)S(1)}, bf16[4,80,256]{2,1,0:T(8,128)(2,1)S(1)}, u32[]{:S(2)}, u32[]{:S(2)}) collective-permute-start(bf16[4,80,256]{2,1,0:T(8,128)(2,1)S(1)} %pad_maximum_fusion.1.near_ref), channel_id=1, source_target_pairs={{0,32},{8,40},{16,48},{24,56},{32,0},{40,8},{48,16},{56,24},{1,33}... | collective-permute-start | bytes 491528 | tf_op jit(solution)/shard_map/ppermute | solution.py:468
  114.0 15.9 %collective-permute-start.13 = (bf16[4,80,256]{2,1,0:T(8,128)(2,1)S(1)}, bf16[4,80,256]{2,1,0:T(8,128)(2,1)S(1)}, u32[]{:S(2)}, u32[]{:S(2)}) collective-permute-start(bf16[4,80,256]{2,1,0:T(8,128)(2,1)S(1)} %pad_maximum_fusion.1.near_ref), channel_id=1, source_target_pairs={{0,64},{64,0},{1,65},{65,1},{2,66},{66,2},{3,67},{67,3},{4,68},{68... | collective-permute-start | bytes 491528 | tf_op jit(solution)/shard_map/ppermute | solution.py:469
  116.8 13.2 %collective-permute-start.14 = (bf16[4,80,256]{2,1,0:T(8,128)(2,1)S(1)}, bf16[4,80,256]{2,1,0:T(8,128)(2,1)}, u32[]{:S(2)}, u32[]{:S(2)}) collective-permute-start(bf16[4,80,256]{2,1,0:T(8,128)(2,1)S(1)} %pad_maximum_fusion.1.near_ref), channel_id=1, source_target_pairs={{0,96},{8,104},{16,112},{24,120},{32,64},{40,72},{48,80},{56,88},{... | collective-permute-start | bytes 491528 | tf_op jit(solution)/shard_map/ppermute | solution.py:470
  117.5 4.6 %copy-start.13 = (bf16[128,256]{1,0:T(8,128)(2,1)S(1)}, bf16[128,256]{1,0:T(8,128)(2,1)}, u32[]{:S(2)}) copy-start(bf16[128,256]{1,0:T(8,128)(2,1)} %get-tuple-element.62) | copy-start | bytes 196612 | tf_op jit(solution)/shard_map/cond
  (6 other events, 8.2 us)

commit v6 on v5

--- a/solution.py
+++ b/solution.py
@@ -110,8 +110,8 @@
 
 
 def finish_kernel(slots, mask_ref, *refs):
-    parts, (rows_ref, slot_ref) = refs[:4], refs[4:]
-    slot_ref[...] = jnp.zeros_like(slot_ref)
+    parts, rows_ref, stack_ref, moved = refs[:4], refs[4], refs[5], refs[6:]
+    stack_ref[...] = jnp.zeros_like(stack_ref)
     squares = square_rows(parts)
     scale = jnp.where(mask_ref[...] > 0.0, lax.rsqrt(squares / D + 1e-05), 0.0)
     for part in range(16):
@@ -124,7 +124,9 @@
         for p in range(8):
             page = rows[p * PAGE : (p + 1) * PAGE, :]
             rows_ref[part * 8 + p] = page
-            slot_ref[0, slots[part * 8 + p]] = page
+            stack_ref[slots[part * 8 + p]] = page
+    for k, ref in enumerate(moved):
+        ref[...] = stack_ref[64 * (k + 1) : 64 * (k + 2)]
 
 
 def finish_text(slots, mask, parts):
@@ -136,13 +138,12 @@
             grid=(1,),
             in_specs=[pl.BlockSpec((16, 128), whole)] + [pl.BlockSpec((TALL, 128), whole)] * 4,
             out_specs=[
-                pl.BlockSpec((PAGES, PAGE, 128), lambda i, slots: (0, 0, 0)),
-                pl.BlockSpec((1, 256, PAGE, 128), lambda i, slots: (1, 0, 0, 0)),
+                pl.BlockSpec((count, PAGE, 128), lambda i, slots: (0, 0, 0))
+                for count in (PAGES, 256, 64, 64, 64)
             ],
         ),
         out_shape=[
-            jax.ShapeDtypeStruct((PAGES, PAGE, 128), BF),
-            jax.ShapeDtypeStruct((2, 256, PAGE, 128), BF),
+            jax.ShapeDtypeStruct((count, PAGE, 128), BF) for count in (PAGES, 256, 64, 64, 64)
         ],
         compiler_params=pltpu.CompilerParams(vmem_limit_bytes=VMEM_LIMIT),
         cost_estimate=work(20000),
@@ -247,8 +248,9 @@
     scale = jnp.where(labels_ref[3:4, 0:128].astype(F32) > 0.5, scale, 0.0)
     tile = jnp.broadcast_to(scale, (128, 128)).T[0:IMG]
     tile = jnp.concatenate([tile, tile], axis=1)
-    out_ref[0:IMG, :] = jnp.where(tile > 0.0, total[0:IMG] * tile, 0.0).astype(BF)
-    out_ref[IMG:, :] = labels_ref[...]
+    rows = jnp.where(tile > 0.0, total[0:IMG] * tile, 0.0).astype(BF)
+    block = jnp.concatenate([rows, labels_ref[...]], axis=0)
+    out_ref[...] = block
 
 
 def close_images(parts, labels):
@@ -261,84 +263,108 @@
 
 
 def merge_kernel(
-    place, slots, own_ref, rows_ref, first_ref, second_ref, near_ref, yonder_ref, side_ref, far_ref, out_ref, other
+    place,
+    slots,
+    own_ref,
+    rows_ref,
+    next_ref,
+    cross_ref,
+    stay_ref,
+    other_ref,
+    image0,
+    image1,
+    image2,
+    image3,
+    out_ref,
+    placed,
 ):
     prefill = place[0] == 0
-
-    @pl.when(jnp.logical_and(prefill, pl.program_id(0) == 0))
+    step = pl.program_id(0)
+    here, there = place[3] // 4, 1 - place[3] // 4
+
+    @pl.when(jnp.logical_and(prefill, step == 0))
     def _():
-        other[...] = jnp.zeros_like(other)
+        placed[...] = jnp.zeros_like(placed)
         for p in range(PAGES):
-            other[slots[p]] = rows_ref[p]
-
-    def one(k):
-        step = 2 * pl.program_id(0) + k
-        match = jnp.where(prefill, step, place[3]).astype(F32)
-        shard = jnp.where(prefill, place[3], step)
-        level = lax.rem(place[3] - shard + 8, 4)
-        close = (shard >= 4) == (place[3] >= 4)
-        images = []
-        for near, away in ((near_ref, yonder_ref), (side_ref, far_ref)):
-            images.append(jnp.where(close, near[level], away[level]))
+            placed[slots[p]] = rows_ref[p]
+
+    spots = lax.broadcasted_iota(jnp.int32, (CAP * PAGE, 2 * IMG), 0).astype(F32)
+
+    def one(images, owner, upper, left, right):
         targets = []
         for image in images:
-            labels = image[IMG:IMG_TALL, 0:IMG].astype(F32)
+            labels = image[0, IMG:IMG_TALL, 0:IMG].astype(F32)
             spot = labels[1:2] * PAGE + labels[2:3]
-            targets.append(jnp.where(labels[0:1] == match, spot, -1.0))
+            targets.append(jnp.where(labels[0:1] == owner.astype(F32), spot, -1.0))
         target = jnp.concatenate(targets, axis=1)
-        data = jnp.concatenate([images[0][0:IMG], images[1][0:IMG]], axis=0)
-        spots = lax.broadcasted_iota(jnp.int32, (CAP * PAGE, 2 * IMG), 0).astype(F32)
+        data = jnp.concatenate([images[0][0, 0:IMG, :], images[1][0, 0:IMG, :]], axis=0)
         chosen = (spots == target).astype(F32).astype(BF)
         image = jnp.dot(chosen, data, preferred_element_type=F32).astype(BF)
-
-        def write(left, right):
-            for half, text in enumerate((left, right)):
-                lanes = slice(half * 128, half * 128 + 128)
-                text = text.reshape(CAP * PAGE, 128)
-                out_ref[k * CAP : (k + 1) * CAP, :, lanes] = (text + image[:, lanes]).reshape(CAP, PAGE, 128)
-
-        @pl.when(prefill)
-        def _():
-            here = pl.ds(step * CAP, CAP)
-            write(own_ref[0, k * CAP : (k + 1) * CAP], other[here])
-
-        @pl.when(jnp.logical_not(prefill))
-        def _():
-            write(first_ref[0, k * CAP : (k + 1) * CAP], second_ref[0, k * CAP : (k + 1) * CAP])
-
-    one(0)
-    one(1)
-
-
-def merge_slots(place, slots, own, rows, arrived, images):
-    def local(i, place):
-        return jnp.where(place[0] == 0, i, 3)
-
-    def remote(i, place):
-        return jnp.where(place[0] == 0, 0, i)
-
-    image_spec = pl.BlockSpec((4, IMG_TALL, 256), lambda i, place, slots: (0, 0, 0))
-    chunk = (1, 2 * CAP, PAGE, 128)
-    return pl.pallas_call(
+        for half, text in enumerate((left, right)):
+            lanes = slice(half * 128, half * 128 + 128)
+            merged = text.reshape(CAP * PAGE, 128) + image[:, lanes]
+            out_ref[upper, 0, :, :, lanes] = merged.reshape(CAP, PAGE, 128)
+
+    @pl.when(prefill)
+    def _():
+        level = lax.rem(place[3] + step, 4)
+        for k, upper in enumerate((here, there)):
+            start = (2 * step + k) * CAP
+            one((image0, image1), upper * 4 + level, upper, own_ref[k], placed[pl.ds(start, CAP)])
+
+    @pl.when(jnp.logical_not(prefill))
+    def _():
+        one((image0, image1), place[3], here, next_ref[0], stay_ref[0])
+        one((image2, image3), place[3], there, cross_ref[0], other_ref[0])
+
+
+def merge_slots(place, slots, stack, rows, blocks, images):
+    def level(i, place):
+        return lax.rem(jnp.where(place[0] == 0, place[3] + i, place[3] + 8 - i), 4)
+
+    def image_spec(apart):
+        def index(i, place, slots):
+            y = place[3] // 4
+            y = 1 - y if apart else y
+            return (jnp.where(place[0] == 0, place[3], 4 * y + level(i, place)), 0, 0)
+
+        return pl.BlockSpec((1, IMG_TALL, 256), index)
+
+    def local(i, place, slots):
+        return (jnp.where(place[0] == 0, i, 0), 0, 0, 0)
+
+    def remote(i, place, slots):
+        return (jnp.where(place[0] == 0, 0, i), 0, 0, 0)
+
+    chunk = pl.BlockSpec((1, CAP, PAGE, 128), remote)
+    result = pl.pallas_call(
         merge_kernel,
         grid_spec=pltpu.PrefetchScalarGridSpec(
             num_scalar_prefetch=2,
             grid=(4,),
             in_specs=[
-                pl.BlockSpec(chunk, lambda i, place, slots: (1, local(i, place), 0, 0)),
+                pl.BlockSpec((2, CAP, PAGE, 128), local),
                 pl.BlockSpec((PAGES, PAGE, 128), lambda i, place, slots: (0, 0, 0)),
-                pl.BlockSpec(chunk, lambda i, place, slots: (0, remote(i, place), 0, 0)),
-                pl.BlockSpec(chunk, lambda i, place, slots: (1, remote(i, place), 0, 0)),
-            ]
-            + [image_spec] * 4,
-            out_specs=pl.BlockSpec((2 * CAP, PAGE, 256), lambda i, place, slots: (i, 0, 0)),
+                chunk,
+                chunk,
+                chunk,
+                chunk,
+                image_spec(False),
+                image_spec(False),
+                image_spec(True),
+                image_spec(True),
+            ],
+            out_specs=pl.BlockSpec(
+                (2, 1, CAP, PAGE, 256), lambda i, place, slots: (0, level(i, place), 0, 0, 0)
+            ),
             scratch_shapes=[pltpu.VMEM((256, PAGE, 128), BF)],
         ),
-        out_shape=jax.ShapeDtypeStruct((256, PAGE, 256), BF),
+        out_shape=jax.ShapeDtypeStruct((2, 4, CAP, PAGE, 256), BF),
         compiler_params=pltpu.CompilerParams(vmem_limit_bytes=VMEM_LIMIT),
         cost_estimate=LIGHT,
         name="merge_slots",
-    )(place, slots, own, rows, arrived, arrived, *images)
+    )(place, slots, stack.reshape(8, CAP, PAGE, 128), rows, *blocks, *images, *images)
+    return result.reshape(256, PAGE, 256)
 
 
 def attend(queries, kv_cache, new_kv, cache_lengths):
@@ -381,7 +407,8 @@
     return [(i, (i // 4 + y) % 2 * 4 + (i + z) % 4) for i in range(8)]
 
 
-FAR = [(g * 8 + i, (1 - g) * 8 + (i + 4) % 8) for g in range(2) for i in range(8)]
+CROSS = [(i, 8 + (i + 4) % 8) for i in range(8)]
+AWAY = [(8 + i, 8 + (i + 4) % 8) for i in range(8)]
 
 
 def after(value, other):
@@ -415,7 +442,8 @@
         jnp.arange(PAGES, dtype=jnp.int32)[None, :] < jnp.arange(PAGES, dtype=jnp.int32)[:, None]
     )
     page_rank = jnp.sum((before & (owners[:, None] == owners[None, :])).astype(jnp.int32), axis=1)
-    slots = owners * CAP + page_rank
+    distance = 2 * ((owners % 4 - seq % 4) % 4) + (owners // 4 != seq // 4).astype(jnp.int32)
+    slots = distance * CAP + page_rank
     live = jnp.sum(jnp.where(jnp.arange(4, dtype=jnp.int32) == seq // 2, prompt_lengths, 0))
     limit = live - (seq % 2) * ROWS
     local_pos = lax.dynamic_slice(image_pos, (group * IMG,), (IMG,)) - seq * ROWS
@@ -440,47 +468,44 @@
     swapped = lax.ppermute(got, "mp", PARTNER)
     received = [lax.ppermute(piece, "mp", PARTNER) for piece in send]
 
-    feats = jnp.concatenate([got, swapped], axis=1).reshape(8 * IMG, -1)
+    added = [None] + [add_pair(keep[j], received[j]) for j in (1, 2, 3)]
+    base = keep[0].astype(F32) + after(received[0], added[1:]).astype(F32)
+    parts = [base] + [lax.ppermute(added[j], "mp", shift(j)) for j in (1, 2, 3)]
+
+    feats = jnp.concatenate([got, after(swapped, base)], axis=1).reshape(8 * IMG, -1)
     partial = jnp.dot(feats, proj_w, preferred_element_type=F32).astype(BF).reshape(8, IMG, -1)
     pieces = lax.all_to_all(partial, "seq", 0, 0, tiled=True)
 
-    added = [None] + [add_pair(after(keep[j], partial), received[j]) for j in (1, 2, 3)]
-    base = keep[0].astype(F32) + after(received[0], added[1:]).astype(F32)
-    parts = [base] + [lax.ppermute(added[j], "mp", shift(j)) for j in (1, 2, 3)]
-
-    image_hidden, heads = image_rows_kv(
-        place, after(pieces, base), proj_b, norm_gain, kv_w
-    )
-    image_parts = lax.all_to_all(heads, "mp", 0, 0, tiled=True)
-    image_block = close_images(image_parts, labels)
-
-    rows, by_owner = finish_text(slots, after(mask, image_block), parts)
-    other_rows = lax.ppermute(rows, "group", [(1, 0)])
-    arrived = lax.all_to_all(
-        by_owner.reshape(512, PAGE, 128), ("group", "seq"), split_axis=0, concat_axis=0, tiled=True
-    ).reshape(2, 256, PAGE, 128)
-
-    near = jnp.stack(
-        [image_block] + [lax.ppermute(image_block, "seq", seq_shift(0, k)) for k in (1, 2, 3)]
-    )
-    images = [
-        near,
-        lax.ppermute(near, "seq", seq_shift(1, 0)),
-        lax.ppermute(near, "group", [(0, 1), (1, 0)]),
-        lax.ppermute(near, ("group", "seq"), FAR),
-    ]
     attended = lax.cond(
         group != 0,
         attend,
         lambda *unused: jnp.zeros(queries.shape, BF),
-        after(queries, near),
+        after(queries, partial),
         kv_cache,
         new_kv,
         cache_lengths,
     )
-    page_slots = merge_slots(place, slots, by_owner, other_rows, arrived, images)
-
+    rows, stack, *moved = finish_text(slots, after(mask, attended), parts)
+    image_hidden, heads = image_rows_kv(place, after(pieces, stack), proj_b, norm_gain, kv_w)
+    levels = [stack[:64]] + [
+        lax.ppermute(moved[k - 1], "seq", seq_shift(0, k)) for k in (1, 2, 3)
+    ]
+    levels = [piece.reshape(2, CAP, PAGE, 128) for piece in after(levels, heads)]
+    stay = jnp.stack([piece[0] for piece in levels])
+    leave = jnp.stack([piece[1] for piece in levels])
+    neighbour = lax.ppermute(stay, "group", [(0, 1)])
+    cross = lax.ppermute(leave, ("group", "seq"), CROSS)
+    away = lax.ppermute(leave, ("group", "seq"), AWAY)
+    other_rows = lax.ppermute(rows, "group", [(1, 0)])
+
+    image_parts = lax.all_to_all(heads, "mp", 0, 0, tiled=True)
+    image_copies = close_images(after(image_parts, (stay, leave)), labels)
+    images = lax.all_gather(image_copies, "seq", axis=0)
+    other_images = lax.ppermute(images, "group", [(0, 1), (1, 0)])
     other_hidden = lax.ppermute(image_hidden, "group", [(1, 0)])
+
+    page_slots = merge_slots(place, slots, stack, other_rows, (neighbour, cross, stay, away), (images, other_images))
+
     row_states = jnp.where(
         group == 0, jnp.concatenate([image_hidden, other_hidden], axis=0), attended
     )

time: 140 us -> 153 us (1.093); the launches traced: 138 us -> 152 us
  blocking collectives: 0 us -> 35.1 us
  waiting for transfers between devices: 31.9 us -> 6.49 us
  local copies, waits for them, and re-layouts: 2.76 us -> 5.68 us
  other arithmetic: 12.8 us -> 14.4 us
    all_gather x0 -> x1, blocking collectives: none -> 35.1 us  [per_device(): images = lax.all_gather(image_copies, 'seq', axis=0)]
    ppermute x6 -> x7, waiting for transfers between devices: 19.7 us -> 5.34 us  [the longest x1 5.33 us: per_device(): other_images = lax.ppermute(images, 'group', [(0, 1), (1, 0)])]
    all_to_all x1 -> x0, starting transfers between devices: 8.42 us -> none  [per_device(): lax.all_to_all(by_owner.reshape(512, PAGE, 128), ('group', 'seq'), split_...]
    all_to_all x1, waiting for transfers between devices: 7.2 us -> 0.01 us  [per_device(): image_parts = lax.all_to_all(heads, 'mp', 0, 0, tiled=True)]
    ppermute x1, starting transfers between devices: 1.94 us -> 6.42 us  [per_device(): other_hidden = lax.ppermute(image_hidden, 'group', [(1, 0)])]
    ppermute x6 -> x7, starting transfers between devices: 9.03 us -> 13.2 us  [the longest x3 6.27 us: per_device(): lax.ppermute(moved[k - 1], 'seq', seq_shift(0, k))]
    all_to_all x1, waiting for transfers between devices: 3.44 us -> 0.01 us  [per_device(): pieces = lax.all_to_all(partial, 'seq', 0, 0, tiled=True)]
    slice x0 -> x3, local copies, waits for them, and re-layouts: none -> 3.11 us  [the longest x2 2.14 us: per_device(): leave = jnp.stack([piece[1] for piece in levels])]
  transfers between devices with their start and end apart: 20 -> 20, of which waited for: 6 -> 2; matrix products, arithmetic and copies ran while one was open for 17% -> 19% of each run, Pallas kernels for 12% -> 14%
where the time goes in v6:
time: 153 us; the launch traced here: 152 us
  starting transfers between devices  48.1 us (31%)
  blocking collectives  35.1 us (23%)
  Pallas kernels  29.4 us (19%)
  other arithmetic  14.4 us (9%)
  matrix products  11.3 us (7%)
  waiting for transfers between devices  6.49 us (4%)
  local copies, waits for them, and re-layouts  5.68 us (4%)
  between operations  1.61 us (1%)
    all_gather x1, blocking collectives, per_device(): images = lax.all_gather(image_copies, 'seq', axis=0)  35.1 us
    pallas_call x1, Pallas kernels, project_text(): pl.pallas_call(project_kernel, grid_spec=pltpu.PrefetchScalarGridSpec(num...  9.28 us
    all_to_all x1, starting transfers between devices, per_device(): pieces = lax.all_to_all(partial, 'seq', 0, 0, tiled=True)  7.45 us
    all_to_all x1, starting transfers between devices, per_device(): lax.all_to_all(cut_features(place, image_feats), 'seq', 0, 0, tiled=True)  7.05 us
    ppermute x1, starting transfers between devices, per_device(): other_hidden = lax.ppermute(image_hidden, 'group', [(1, 0)])  6.42 us
    ppermute x3, starting transfers between devices, per_device(): lax.ppermute(moved[k - 1], 'seq', seq_shift(0, k))  6.27 us
    convert_element_type x3, other arithmetic, add_pair(): return (keep.astype(F32) + received.astype(F32)).astype(BF)  6.11 us
    pallas_call x1, Pallas kernels, merge_slots(): pl.pallas_call(merge_kernel, grid_spec=pltpu.PrefetchScalarGridSpec(num_s...  5.81 us
  transfers between devices with their start and end apart: 20, of which 2 were waited for; matrix products, arithmetic and copies ran while one was open for 19% of the time, Pallas kernels for 14%

profile of v6, /device:TPU:10, one launch (start us, length us, event | category | flops | bytes accessed | tf_op | source)
XLA Modules:
  0.0 152.2 jit_solution(4439778797004203650)
XLA Ops:
  1.2 2.7 %cut_features.1 = bf16[8,32,912]{2,1,0:T(8,128)(2,1)} custom-call(s32[4]{0:T(128)} %pad_add_fusion.place, bf16[128,7296]{1,0:T(8,128)(2,1)} %feats_ref.1), custom_call_target="tpu_custom_call" | custom-call | flops 1 | bytes 1 | tf_op jit(solution)/shard_map/cut_features/pallas_call | solution.py:162
  3.9 7.0 %all-to-all-start = ((bf16[8,32,912]{2,1,0:T(8,128)(2,1)}), bf16[8,32,912]{2,1,0:T(8,128)(2,1)S(1)}, u32[]{:S(2)}, u32[]{:S(2)}) async-start(bf16[8,32,912]{2,1,0:T(8,128)(2,1)} %cut_features.1), calls=%async_computation | async-start | bytes 1048576 | tf_op jit(solution)/shard_map/all_to_all | solution.py:464
  11.0 9.3 %project_text.1 = (bf16[2080,128]{1,0:T(8,128)(2,1)}, bf16[2080,128]{1,0:T(8,128)(2,1)}, bf16[2080,128]{1,0:T(8,128)(2,1)}, bf16[2080,128]{1,0:T(8,128)(2,1)}, b...) custom-call(s32[4]{0:T(128)} %pad_add_fusion.place, ...), custom_call_target="tpu_custom_call" | custom-call | flops 1 | bytes 1 | tf_op jit(solution)/shard_map/project_text/pallas_call | solution.py:84
  24.5 2.1 %add_convert_fusion.2 = bf16[2080,128]{1,0:T(8,128)(2,1)} fusion(bf16[2080,128]{1,0:T(8,128)(2,1)} %collective-permute-done.2, bf16[2080,128]{1,0:T(8,128)(2,1)} %get-tuple-element.46), kind=kLoop, calls=%fused_computation.33 | loop fusion | flops 1064960 | bytes 1597440 | tf_op jit(solution)/shard_map/convert_element_type | solution.py:109
  26.7 1.5 collective-permute-start.5
  28.2 2.0 %add_convert_fusion.1 = bf16[2080,128]{1,0:T(8,128)(2,1)} fusion(bf16[2080,128]{1,0:T(8,128)(2,1)} %collective-permute-done.3, bf16[2080,128]{1,0:T(8,128)(2,1)S(1)} %copy-done.7), kind=kLoop, calls=%fused_computation.32 | loop fusion | flops 1064960 | bytes 1597440 | tf_op jit(solution)/shard_map/convert_element_type | solution.py:109
  31.3 2.0 %add_convert_fusion = bf16[2080,128]{1,0:T(8,128)(2,1)} fusion(bf16[2080,128]{1,0:T(8,128)(2,1)} %collective-permute-done.4, bf16[2080,128]{1,0:T(8,128)(2,1)S(1)} %copy-done.6), kind=kLoop, calls=%fused_computation.31 | loop fusion | flops 1064960 | bytes 1597440 | tf_op jit(solution)/shard_map/convert_element_type | solution.py:109
  33.2 2.2 %collective-permute-start.7 = (bf16[2080,128]{1,0:T(8,128)(2,1)}, bf16[2080,128]{1,0:T(8,128)(2,1)}, u32[]{:S(2)}, u32[]{:S(2)}) collective-permute-start(bf16[2080,128]{1,0:T(8,128)(2,1)} %add_convert_fusion), channel_id=1, source_target_pairs={{0,6},{1,7},{2,0},{3,1},{4,2},{5,3},{6,4},{7,5},{8,14},{9,15},{10,... | collective-permute-start | bytes 1597448 | tf_op jit(solution)/shard_map/ppermute | solution.py:473
  35.4 2.1 %convert_add_fusion.refs_0_ = f32[2080,128]{1,0:T(8,128)} fusion(bf16[2080,128]{1,0:T(8,128)(2,1)} %collective-permute-done.1, bf16[2080,128]{1,0:T(8,128)(2,1)S(1)} %copy-done.8), kind=kLoop, calls=%fused_computation.30 | loop fusion | flops 798720 | bytes 2129920 | tf_op jit(solution)/shard_map/add | solution.py:472
  37.7 2.2 %convolution_convert_fusion = bf16[512,1024]{1,0:T(8,128)(2,1)} fusion(bf16[512,912]{1,0:T(8,128)(2,1)S(1)} %bitcast.88, bf16[912,1024]{1,0:T(8,128)(2,1)S(1)} %copy-done), kind=kOutput, calls=%fused_computation.26 | convolution fusion | flops 956825600 | bytes 3850240 | tf_op jit(solution)/shard_map/dot_general | solution.py:476
  39.9 7.5 %all-to-all-start.1 = ((bf16[8,64,1024]{2,1,0:T(8,128)(2,1)}), bf16[8,64,1024]{2,1,0:T(8,128)(2,1)S(1)}, u32[]{:S(2)}, u32[]{:S(2)}) async-start(bf16[8,64,1024]{2,1,0:T(8,128)(2,1)} %bitcast.87), calls=%async_computation.1 | async-start | bytes 2097152 | tf_op jit(solution)/shard_map/all_to_all | solution.py:477
  47.4 9.0 %conditional.1 = (bf16[128,1024]{1,0:T(8,128)(2,1)S(1)}) conditional(s32[]{:T(128)} %convert_element_type.79, () %tuple.22, (s32[128]{0:T(128)S(1)}, bf16[128,1024]{1,0:T(8,128)(2,1)S(1)}, bf16[128,128,256]{2,1,0:T(8,128)(2,1)}, bf16[128,256]{1,0:T(8,128)(2,1)S(1)}) %tuple.52), branch_computations={%region_2.3_spmd, %region_3.6_spmd} | conditional | flops 68852736 | bytes 12157448 | solution.py:479
  47.9 4.5 %fusion.40 = (f32[128,8]{1,0:T(8,128)S(1)}, f32[128,8,128]{2,1,0:T(8,128)S(1)}) fusion(bf16[128,8,128]{2,1,0:T(8,128)(2,1)S(1)} %bitcast.86, bf16[128,128,1,256]{3,1,0,2:T(8,128)(2,1)} %bitcast.81, pred[128,128]{1,0:T(8,128)(4,1)S(1)} %iota_compare_fusion), kind=kOutput, calls=%fused_computation.107 | convolution fusion | flops 33946624 | bytes 5001216 | tf_op jit(solution)/shard_map/cond/branch_1_fun/rgqh,rjgh->rgqj/dot_general | solution.py:376
  52.9 3.5 %fusion.5 = bf16[128,8,128]{2,1,0:T(8,128)(2,1)S(1)} fusion(bf16[128,128,1,256]{3,1,0,2:T(8,128)(2,1)} %bitcast.82, f32[128,8,128]{2,1,0:T(8,128)S(1)} %get-tuple-element.86, f32[128,128]{1,0:T(8,128)S(1)} %get-tuple-element.84, f32[128,8]{1,0:T(8,128)S(1)} %bitcast_convert_fusion, f32[128,8]{1,0:T(8,128)S(1)} %get-tuple-element.81, ...), kind=kOutput, calls=%fused_computation.7 | convolution fusion | flops 34340864 | bytes 5058560 | tf_op jit(solution)/shard_map/cond/branch_1_fun/rgqj,rjgh->rgqh/dot_general | solution.py:392
  56.4 1.1 collective-permute-done.7.refs_3_
  57.5 4.2 %finish_text.1 = (bf16[128,16,128]{2,1,0:T(8,128)(2,1)}, bf16[256,16,128]{2,1,0:T(8,128)(2,1)}, bf16[64,16,128]{2,1,0:T(8,128)(2,1)}, bf16[64,16,128]{2,1,0:T(8,128)(2,1)}, bf16[64,16,128]{2,1,0:T(8,128)(2,1)}) custom-call(s32[128]{0:T(128)} %multiply_add_fusion.slots, f32[16,128]{1,0:T(8,128)} %fusion.15.mask_ref, f32[2080,128]{1,0:T(8,128)} %convert_add_fusion.refs_0_, ...), custom_call_target="tpu_custom_call" | custom-call | flops 20000000000 | bytes 73999998976 | tf_op jit(solution)/shard_map/finish_text/pallas_call | solution.py:134
  61.8 2.1 %collective-permute-start.9 = (bf16[64,16,128]{2,1,0:T(8,128)(2,1)}, bf16[64,16,128]{2,1,0:T(8,128)(2,1)}, u32[]{:S(2)}, u32[]{:S(2)}) collective-permute-start(bf16[64,16,128]{2,1,0:T(8,128)(2,1)} %get-tuple-element.58), channel_id=1, source_target_pairs={{0,8},{8,16},{16,24},{24,0},{32,40},{40,48},{48,56},{56,32},{1,9},... | collective-permute-start | bytes 786440 | tf_op jit(solution)/shard_map/ppermute | solution.py:491
  63.9 2.7 %collective-permute-start.10 = (bf16[64,16,128]{2,1,0:T(8,128)(2,1)}, bf16[64,16,128]{2,1,0:T(8,128)(2,1)}, u32[]{:S(2)}, u32[]{:S(2)}) collective-permute-start(bf16[64,16,128]{2,1,0:T(8,128)(2,1)} %get-tuple-element.59), channel_id=1, source_target_pairs={{0,16},{8,24},{16,0},{24,8},{32,48},{40,56},{48,32},{56,40},{1,17}... | collective-permute-start | bytes 786440 | tf_op jit(solution)/shard_map/ppermute | solution.py:491
  66.6 1.5 collective-permute-start.11
  69.2 4.1 %collective-permute-start.8 = (bf16[128,16,128]{2,1,0:T(8,128)(2,1)}, bf16[128,16,128]{2,1,0:T(8,128)(2,1)}, u32[]{:S(2)}, u32[]{:S(2)}) collective-permute-start(bf16[128,16,128]{2,1,0:T(8,128)(2,1)} %get-tuple-element.57), channel_id=1, source_target_pairs={{64,0},{65,1},{66,2},{67,3},{68,4},{69,5},{70,6},{71,7},{72,8},{73... | collective-permute-start | bytes 1572872 | tf_op jit(solution)/shard_map/ppermute | solution.py:499
  74.3 5.7 %image_rows_kv.1 = (bf16[64,1024]{1,0:T(8,128)(2,1)}, bf16[8,80,256]{2,1,0:T(8,128)(2,1)}) custom-call(s32[4]{0:T(128)} %pad_add_fusion.place, bf16[8,64,1024]{2,1,0:T(8,128)(2,1)} %copy-done.1, bf16[1024]{0:T(1024)(128)(2,1)} %bias_ref.1, bf16[1024]{0:T(1024)(128)(2,1)} %gain_ref.3, bf16[1024,2048]{1,0:T(8,128)(2,1)} %weight_ref.1), custom_call_target="tpu_custom_call" | custom-call | flops 1 | bytes 1 | tf_op jit(solution)/shard_map/image_rows_kv/pallas_call | solution.py:215
  80.0 3.9 %all-to-all-start.2 = ((bf16[8,80,256]{2,1,0:T(8,128)(2,1)}), bf16[8,80,256]{2,1,0:T(8,128)(2,1)S(1)}, u32[]{:S(2)}, u32[]{:S(2)}) async-start(bf16[8,80,256]{2,1,0:T(8,128)(2,1)} %get-tuple-element.62), calls=%async_computation.2 | async-start | bytes 655360 | tf_op jit(solution)/shard_map/all_to_all | solution.py:501
  85.0 1.1 slice_bitcast_fusion.14
  87.0 4.3 %collective-permute-start.14 = (bf16[4,32,16,128]{3,2,1,0:T(8,128)(2,1)}, bf16[4,32,16,128]{3,2,1,0:T(8,128)(2,1)}, u32[]{:S(2)}, u32[]{:S(2)}) collective-permute-start(bf16[4,32,16,128]{3,2,1,0:T(8,128)(2,1)} %pad_maximum_fusion.2), channel_id=1, source_target_pairs={{64,96},{72,104},{80,112},{88,120},{96,64},{104,72},{112,80},{120,... | collective-permute-start | bytes 1572872 | tf_op jit(solution)/shard_map/ppermute | solution.py:498
  91.2 1.3 collective-permute-start.13
  92.6 1.3 collective-permute-start.12
  94.5 6.4 %collective-permute-start.16 = (bf16[64,1024]{1,0:T(8,128)(2,1)}, bf16[64,1024]{1,0:T(8,128)(2,1)S(1)}, u32[]{:S(2)}, u32[]{:S(2)}) collective-permute-start(bf16[64,1024]{1,0:T(8,128)(2,1)} %get-tuple-element.68), channel_id=1, source_target_pairs={{64,0},{65,1},{66,2},{67,3},{68,4},{69,5},{70,6},{71,7},{72,8},{73... | collective-permute-start | bytes 393224 | tf_op jit(solution)/shard_map/ppermute | solution.py:505
  101.7 1.7 %close_images.1 = bf16[80,256]{1,0:T(8,128)(2,1)} custom-call(bf16[8,80,256]{2,1,0:T(8,128)(2,1)} %copy-done.4, bf16[16,256]{1,0:T(8,128)(2,1)} %fusion.26.labels_ref), custom_call_target="tpu_custom_call" | custom-call | flops 1 | bytes 1 | tf_op jit(solution)/shard_map/close_images/pallas_call | solution.py:257
  103.4 35.1 %all-gather = bf16[640,256]{1,0:T(8,128)(2,1)S(1)} all-gather(bf16[80,256]{1,0:T(8,128)(2,1)} %close_images.1), channel_id=2, replica_groups=mesh['group'=2,'seq'=8,'mp'=8] {'seq'}, dimensions={0}, use_global_device_ids=true | all-gather | bytes 368640 | tf_op jit(solution)/shard_map/all_gather | solution.py:503
  138.6 1.7 %maximum_select_fusion = bf16[128,1024]{1,0:T(8,128)(2,1)} fusion(bf16[128,1024]{1,0:T(8,128)(2,1)S(1)} %get-tuple-element.101, bf16[64,1024]{1,0:T(8,128)(2,1)S(1)} %collective-permute-done.16, bf16[64,1024]{1,0:T(8,128)(2,1)} %get-tuple-element.68, pred[]{:T(512)S(6)} %eq.82), kind=kLoop, calls=%fused_computation.37 | loop fusion | flops 655360 | bytes 786433 | tf_op jit(solution)/shard_map/jit(_where)/select_n | solution.py:509
  140.4 5.3 %collective-permute-done.15.image1.image3 = bf16[8,80,256]{2,1,0:T(8,128)(2,1)S(1)} collective-permute-done((bf16[8,80,256]{2,1,0:T(8,128)(2,1)S(1)}, bf16[8,80,256]{2,1,0:T(8,128)(2,1)S(1)}, u32[]{:S(2)}, u32[]{:S(2)}) %collective-permute-start.15) | collective-permute-done | bytes 327712 | tf_op jit(solution)/shard_map/ppermute | solution.py:504
  146.4 5.8 %merge_slots.1 = bf16[2,4,32,16,256]{4,3,2,1,0:T(8,128)(2,1)} custom-call(s32[4]{0:T(128)} %pad_add_fusion.place, s32[128]{0:T(128)} %multiply_add_fusion.slots, bf16[8,32,16,128]{3,2,1,0:T(8,128)(2,1)} %bitcast.84, bf16[128,16,128]{2,1,0:T(8,128)(2,1)} %collective-permute-done.8.rows_ref, bf16[4,32,16,128]{3,2,1,0:T(8,128)(2,1)} %collective-permute-done.12.next_ref, ...), custom_call_target="tpu_custom_call" | custom-call | flops 1 | bytes 1 | tf_op jit(solution)/shard_map/merge_slots/pallas_call | solution.py:340
  (82 shorter events, 12.5 us)
Async XLA Ops:
  0.6 37.0 %copy-start = (bf16[912,1024]{1,0:T(8,128)(2,1)S(1)}, bf16[912,1024]{1,0:T(8,128)(2,1)}, u32[]{:S(2)}) copy-start(bf16[912,1024]{1,0:T(8,128)(2,1)} %param.18) | copy-start | bytes 5603332
  3.9 20.5 %all-to-all-start = ((bf16[8,32,912]{2,1,0:T(8,128)(2,1)}), bf16[8,32,912]{2,1,0:T(8,128)(2,1)S(1)}, u32[]{:S(2)}, u32[]{:S(2)}) async-start(bf16[8,32,912]{2,1,0:T(8,128)(2,1)} %cut_features.1), calls=%async_computation | async-start | bytes 1048576 | tf_op jit(solution)/shard_map/all_to_all | solution.py:464
  10.9 10.4 %copy-start.11 = (s32[128,1]{0,1:T(1,128)S(1)}, s32[128,1]{0,1:T(1,128)}, u32[]{:S(2)}) copy-start(s32[128,1]{0,1:T(1,128)} %param.23) | copy-start | bytes 1540
  10.9 10.6 %copy-start.12 = (s32[128]{0:T(128)S(1)}, s32[128]{0:T(128)}, u32[]{:S(2)}) copy-start(s32[128]{0:T(128)} %param.17) | copy-start | bytes 1540
  11.0 10.7 %copy-start.14 = (s32[4]{0:T(128)S(1)}, s32[4]{0:T(128)}, u32[]{:S(2)}) copy-start(s32[4]{0:T(128)} %param.22) | copy-start | bytes 52
  20.3 7.9 %copy-start.7 = (bf16[2080,128]{1,0:T(8,128)(2,1)S(1)}, bf16[2080,128]{1,0:T(8,128)(2,1)}, u32[]{:S(2)}) copy-start(bf16[2080,128]{1,0:T(8,128)(2,1)} %get-tuple-element.48) | copy-start | bytes 1597444
  20.3 11.0 %copy-start.6 = (bf16[2080,128]{1,0:T(8,128)(2,1)S(1)}, bf16[2080,128]{1,0:T(8,128)(2,1)}, u32[]{:S(2)}) copy-start(bf16[2080,128]{1,0:T(8,128)(2,1)} %get-tuple-element.50) | copy-start | bytes 1597444
  20.3 15.1 %collective-permute-start.1 = (bf16[2080,128]{1,0:T(8,128)(2,1)}, bf16[2080,128]{1,0:T(8,128)(2,1)}, u32[]{:S(2)}, u32[]{:S(2)}) collective-permute-start(bf16[2080,128]{1,0:T(8,128)(2,1)} %get-tuple-element.45), channel_id=1, source_target_pairs={{0,1},{1,0},{2,3},{3,2},{4,5},{5,4},{6,7},{7,6},{8,9},{9,8},{10,11... | collective-permute-start | bytes 1597448 | tf_op jit(solution)/shard_map/ppermute | solution.py:469
  20.4 4.2 %collective-permute-start.2 = (bf16[2080,128]{1,0:T(8,128)(2,1)}, bf16[2080,128]{1,0:T(8,128)(2,1)}, u32[]{:S(2)}, u32[]{:S(2)}) collective-permute-start(bf16[2080,128]{1,0:T(8,128)(2,1)} %get-tuple-element.47), channel_id=1, source_target_pairs={{0,1},{1,0},{2,3},{3,2},{4,5},{5,4},{6,7},{7,6},{8,9},{9,8},{10,11... | collective-permute-start | bytes 1597448 | tf_op jit(solution)/shard_map/ppermute | solution.py:469
  20.9 7.3 %collective-permute-start.3 = (bf16[2080,128]{1,0:T(8,128)(2,1)}, bf16[2080,128]{1,0:T(8,128)(2,1)}, u32[]{:S(2)}, u32[]{:S(2)}) collective-permute-start(bf16[2080,128]{1,0:T(8,128)(2,1)} %get-tuple-element.49), channel_id=1, source_target_pairs={{0,1},{1,0},{2,3},{3,2},{4,5},{5,4},{6,7},{7,6},{8,9},{9,8},{10,11... | collective-permute-start | bytes 1597448 | tf_op jit(solution)/shard_map/ppermute | solution.py:469
  21.0 10.3 %collective-permute-start.4 = (bf16[2080,128]{1,0:T(8,128)(2,1)}, bf16[2080,128]{1,0:T(8,128)(2,1)}, u32[]{:S(2)}, u32[]{:S(2)}) collective-permute-start(bf16[2080,128]{1,0:T(8,128)(2,1)} %get-tuple-element.51), channel_id=1, source_target_pairs={{0,1},{1,0},{2,3},{3,2},{4,5},{5,4},{6,7},{7,6},{8,9},{9,8},{10,11... | collective-permute-start | bytes 1597448 | tf_op jit(solution)/shard_map/ppermute | solution.py:469
  24.4 13.1 %collective-permute-start = (bf16[8,32,912]{2,1,0:T(8,128)(2,1)S(1)}, bf16[8,32,912]{2,1,0:T(8,128)(2,1)S(1)}, u32[]{:S(2)}, u32[]{:S(2)}) collective-permute-start(bf16[8,32,912]{2,1,0:T(8,128)(2,1)S(1)} %all-to-all-done), channel_id=1, source_target_pairs={{0,1},{1,0},{2,3},{3,2},{4,5},{5,4},{6,7},{7,6},{8,9},{9,8},{10,11... | collective-permute-start | bytes 1400840 | tf_op jit(solution)/shard_map/ppermute | solution.py:468
  26.7 8.7 %copy-start.8 = (bf16[2080,128]{1,0:T(8,128)(2,1)S(1)}, bf16[2080,128]{1,0:T(8,128)(2,1)}, u32[]{:S(2)}) copy-start(bf16[2080,128]{1,0:T(8,128)(2,1)} %get-tuple-element.43) | copy-start | bytes 1597444
  26.7 29.7 %collective-permute-start.5 = (bf16[2080,128]{1,0:T(8,128)(2,1)}, bf16[2080,128]{1,0:T(8,128)(2,1)}, u32[]{:S(2)}, u32[]{:S(2)}) collective-permute-start(bf16[2080,128]{1,0:T(8,128)(2,1)} %add_convert_fusion.2), channel_id=1, source_target_pairs={{0,2},{1,3},{2,4},{3,5},{4,6},{5,7},{6,0},{7,1},{8,10},{9,11},{10,... | collective-permute-start | bytes 1597448 | tf_op jit(solution)/shard_map/ppermute | solution.py:473
  30.2 26.3 %collective-permute-start.6 = (bf16[2080,128]{1,0:T(8,128)(2,1)}, bf16[2080,128]{1,0:T(8,128)(2,1)}, u32[]{:S(2)}, u32[]{:S(2)}) collective-permute-start(bf16[2080,128]{1,0:T(8,128)(2,1)} %add_convert_fusion.1), channel_id=1, source_target_pairs={{0,4},{1,5},{2,6},{3,7},{4,0},{5,1},{6,2},{7,3},{8,12},{9,13},{10,... | collective-permute-start | bytes 1597448 | tf_op jit(solution)/shard_map/ppermute | solution.py:473
  33.2 24.3 %collective-permute-start.7 = (bf16[2080,128]{1,0:T(8,128)(2,1)}, bf16[2080,128]{1,0:T(8,128)(2,1)}, u32[]{:S(2)}, u32[]{:S(2)}) collective-permute-start(bf16[2080,128]{1,0:T(8,128)(2,1)} %add_convert_fusion), channel_id=1, source_target_pairs={{0,6},{1,7},{2,0},{3,1},{4,2},{5,3},{6,4},{7,5},{8,14},{9,15},{10,... | collective-permute-start | bytes 1597448 | tf_op jit(solution)/shard_map/ppermute | solution.py:473
  39.9 7.5 %copy-start.9 = (bf16[128,1024]{1,0:T(8,128)(2,1)S(1)}, bf16[128,1024]{1,0:T(8,128)(2,1)}, u32[]{:S(2)}) copy-start(bf16[128,1024]{1,0:T(8,128)(2,1)} %param.24) | copy-start | bytes 786436
  39.9 7.5 %copy-start.10 = (bf16[128,256]{1,0:T(8,128)(2,1)S(1)}, bf16[128,256]{1,0:T(8,128)(2,1)}, u32[]{:S(2)}) copy-start(bf16[128,256]{1,0:T(8,128)(2,1)} %param.26) | copy-start | bytes 196612
  39.9 7.5 %copy-start.13 = (s32[128]{0:T(128)S(1)}, s32[128]{0:T(128)}, u32[]{:S(2)}) copy-start(s32[128]{0:T(128)} %param.27) | copy-start | bytes 1540
  39.9 33.4 %all-to-all-start.1 = ((bf16[8,64,1024]{2,1,0:T(8,128)(2,1)}), bf16[8,64,1024]{2,1,0:T(8,128)(2,1)S(1)}, u32[]{:S(2)}, u32[]{:S(2)}) async-start(bf16[8,64,1024]{2,1,0:T(8,128)(2,1)} %bitcast.87), calls=%async_computation.1 | async-start | bytes 2097152 | tf_op jit(solution)/shard_map/all_to_all | solution.py:477
  61.8 22.2 %collective-permute-start.9 = (bf16[64,16,128]{2,1,0:T(8,128)(2,1)}, bf16[64,16,128]{2,1,0:T(8,128)(2,1)}, u32[]{:S(2)}, u32[]{:S(2)}) collective-permute-start(bf16[64,16,128]{2,1,0:T(8,128)(2,1)} %get-tuple-element.58), channel_id=1, source_target_pairs={{0,8},{8,16},{16,24},{24,0},{32,40},{40,48},{48,56},{56,32},{1,9},... | collective-permute-start | bytes 786440 | tf_op jit(solution)/shard_map/ppermute | solution.py:491
  63.9 20.0 %collective-permute-start.10 = (bf16[64,16,128]{2,1,0:T(8,128)(2,1)}, bf16[64,16,128]{2,1,0:T(8,128)(2,1)}, u32[]{:S(2)}, u32[]{:S(2)}) collective-permute-start(bf16[64,16,128]{2,1,0:T(8,128)(2,1)} %get-tuple-element.59), channel_id=1, source_target_pairs={{0,16},{8,24},{16,0},{24,8},{32,48},{40,56},{48,32},{56,40},{1,17}... | collective-permute-start | bytes 786440 | tf_op jit(solution)/shard_map/ppermute | solution.py:491
  66.6 17.4 %collective-permute-start.11 = (bf16[64,16,128]{2,1,0:T(8,128)(2,1)}, bf16[64,16,128]{2,1,0:T(8,128)(2,1)}, u32[]{:S(2)}, u32[]{:S(2)}) collective-permute-start(bf16[64,16,128]{2,1,0:T(8,128)(2,1)} %get-tuple-element.60), channel_id=1, source_target_pairs={{0,24},{8,0},{16,8},{24,16},{32,56},{40,32},{48,40},{56,48},{1,25}... | collective-permute-start | bytes 786440 | tf_op jit(solution)/shard_map/ppermute | solution.py:491
  69.2 71.1 %collective-permute-start.8 = (bf16[128,16,128]{2,1,0:T(8,128)(2,1)}, bf16[128,16,128]{2,1,0:T(8,128)(2,1)}, u32[]{:S(2)}, u32[]{:S(2)}) collective-permute-start(bf16[128,16,128]{2,1,0:T(8,128)(2,1)} %get-tuple-element.57), channel_id=1, source_target_pairs={{64,0},{65,1},{66,2},{67,3},{68,4},{69,5},{70,6},{71,7},{72,8},{73... | collective-permute-start | bytes 1572872 | tf_op jit(solution)/shard_map/ppermute | solution.py:499
  80.0 21.0 %all-to-all-start.2 = ((bf16[8,80,256]{2,1,0:T(8,128)(2,1)}), bf16[8,80,256]{2,1,0:T(8,128)(2,1)S(1)}, u32[]{:S(2)}, u32[]{:S(2)}) async-start(bf16[8,80,256]{2,1,0:T(8,128)(2,1)} %get-tuple-element.62), calls=%async_computation.2 | async-start | bytes 655360 | tf_op jit(solution)/shard_map/all_to_all | solution.py:501
  87.0 53.4 %collective-permute-start.14 = (bf16[4,32,16,128]{3,2,1,0:T(8,128)(2,1)}, bf16[4,32,16,128]{3,2,1,0:T(8,128)(2,1)}, u32[]{:S(2)}, u32[]{:S(2)}) collective-permute-start(bf16[4,32,16,128]{3,2,1,0:T(8,128)(2,1)} %pad_maximum_fusion.2), channel_id=1, source_target_pairs={{64,96},{72,104},{80,112},{88,120},{96,64},{104,72},{112,80},{120,... | collective-permute-start | bytes 1572872 | tf_op jit(solution)/shard_map/ppermute | solution.py:498
  91.2 49.1 %collective-permute-start.13 = (bf16[4,32,16,128]{3,2,1,0:T(8,128)(2,1)}, bf16[4,32,16,128]{3,2,1,0:T(8,128)(2,1)}, u32[]{:S(2)}, u32[]{:S(2)}) collective-permute-start(bf16[4,32,16,128]{3,2,1,0:T(8,128)(2,1)} %pad_maximum_fusion.2), channel_id=1, source_target_pairs={{0,96},{8,104},{16,112},{24,120},{32,64},{40,72},{48,80},{56,88},{... | collective-permute-start | bytes 1572872 | tf_op jit(solution)/shard_map/ppermute | solution.py:497
  92.6 53.1 %copy-start.3 = (bf16[4,32,16,128]{3,2,1,0:T(8,128)(2,1)}, bf16[4,32,16,128]{3,2,1,0:T(8,128)(2,1)S(1)}, u32[]{:S(2)}) copy-start(bf16[4,32,16,128]{3,2,1,0:T(8,128)(2,1)S(1)} %pad_maximum_fusion.1.stay_ref) | copy-start | bytes 1572868
  92.6 47.7 %collective-permute-start.12 = (bf16[4,32,16,128]{3,2,1,0:T(8,128)(2,1)S(1)}, bf16[4,32,16,128]{3,2,1,0:T(8,128)(2,1)}, u32[]{:S(2)}, u32[]{:S(2)}) collective-permute-start(bf16[4,32,16,128]{3,2,1,0:T(8,128)(2,1)S(1)} %pad_maximum_fusion.1.stay_ref), channel_id=1, source_target_pairs={{0,64},{1,65},{2,66},{3,67},{4,68},{5,69},{6,70},{7,71},{8,72},{9,... | collective-permute-start | bytes 1572872 | tf_op jit(solution)/shard_map/ppermute | solution.py:496
  94.5 44.0 %collective-permute-start.16 = (bf16[64,1024]{1,0:T(8,128)(2,1)}, bf16[64,1024]{1,0:T(8,128)(2,1)S(1)}, u32[]{:S(2)}, u32[]{:S(2)}) collective-permute-start(bf16[64,1024]{1,0:T(8,128)(2,1)} %get-tuple-element.68), channel_id=1, source_target_pairs={{64,0},{65,1},{66,2},{67,3},{68,4},{69,5},{70,6},{71,7},{72,8},{73... | collective-permute-start | bytes 393224 | tf_op jit(solution)/shard_map/ppermute | solution.py:505
  138.5 7.2 %copy-start.2 = (bf16[640,256]{1,0:T(8,128)(2,1)}, bf16[640,256]{1,0:T(8,128)(2,1)S(1)}, u32[]{:S(2)}) copy-start(bf16[640,256]{1,0:T(8,128)(2,1)S(1)} %all-gather) | copy-start | bytes 983044
  138.5 7.1 %collective-permute-start.15 = (bf16[8,80,256]{2,1,0:T(8,128)(2,1)S(1)}, bf16[8,80,256]{2,1,0:T(8,128)(2,1)S(1)}, u32[]{:S(2)}, u32[]{:S(2)}) collective-permute-start(bf16[8,80,256]{2,1,0:T(8,128)(2,1)S(1)} %bitcast.78), channel_id=1, source_target_pairs={{0,64},{64,0},{1,65},{65,1},{2,66},{66,2},{3,67},{67,3},{4,68},{68... | collective-permute-start | bytes 983048 | tf_op jit(solution)/shard_map/ppermute | solution.py:504
  (3 other events, 2.4 us)

commit v7 on v4

--- a/solution.py
+++ b/solution.py
@@ -265,84 +265,107 @@
 
 
 def merge_kernel(
-    place, slots, own_ref, rows_ref, first_ref, second_ref, near_ref, yonder_ref, side_ref, far_ref, out_ref, other
+    place,
+    slots,
+    own_near,
+    own_far,
+    rows_ref,
+    key_near,
+    value_near,
+    key_far,
+    value_far,
+    near_ref,
+    side_ref,
+    yonder_ref,
+    far_ref,
+    out_ref,
+    placed,
 ):
     prefill = place[0] == 0
-
-    @pl.when(jnp.logical_and(prefill, pl.program_id(0) == 0))
+    step = pl.program_id(0)
+    here, there = place[3] // 4, 1 - place[3] // 4
+    level = lax.rem(place[3] + 8 - step, 4)
+
+    @pl.when(jnp.logical_and(prefill, step == 0))
     def _():
-        other[...] = jnp.zeros_like(other)
+        placed[...] = jnp.zeros_like(placed)
         for p in range(PAGES):
-            other[slots[p]] = rows_ref[p]
-
-    def one(k):
-        step = 2 * pl.program_id(0) + k
-        match = jnp.where(prefill, step, place[3]).astype(F32)
-        shard = jnp.where(prefill, place[3], step)
-        level = lax.rem(place[3] - shard + 8, 4)
-        close = (shard >= 4) == (place[3] >= 4)
-        images = []
-        for near, away in ((near_ref, yonder_ref), (side_ref, far_ref)):
-            images.append(jnp.where(close, near[level], away[level]))
+            placed[slots[p]] = rows_ref[p]
+
+    spots = lax.broadcasted_iota(jnp.int32, (CAP * PAGE, 2 * IMG), 0).astype(F32)
+
+    def one(images, owner, upper, left, right):
         targets = []
         for image in images:
-            labels = image[IMG:IMG_TALL, 0:IMG].astype(F32)
+            labels = image[0, IMG:IMG_TALL, 0:IMG].astype(F32)
             spot = labels[1:2] * PAGE + labels[2:3]
-            targets.append(jnp.where(labels[0:1] == match, spot, -1.0))
+            targets.append(jnp.where(labels[0:1] == owner.astype(F32), spot, -1.0))
         target = jnp.concatenate(targets, axis=1)
-        data = jnp.concatenate([images[0][0:IMG], images[1][0:IMG]], axis=0)
-        spots = lax.broadcasted_iota(jnp.int32, (CAP * PAGE, 2 * IMG), 0).astype(F32)
+        data = jnp.concatenate([images[0][0, 0:IMG, :], images[1][0, 0:IMG, :]], axis=0)
         chosen = (spots == target).astype(F32).astype(BF)
         image = jnp.dot(chosen, data, preferred_element_type=F32).astype(BF)
-
-        def write(left, right):
-            for half, text in enumerate((left, right)):
-                lanes = slice(half * 128, half * 128 + 128)
-                text = text.reshape(CAP * PAGE, 128)
-                out_ref[k * CAP : (k + 1) * CAP, :, lanes] = (text + image[:, lanes]).reshape(CAP, PAGE, 128)
-
-        @pl.when(prefill)
-        def _():
-            here = pl.ds(step * CAP, CAP)
-            write(own_ref[0, k * CAP : (k + 1) * CAP], other[here])
-
-        @pl.when(jnp.logical_not(prefill))
-        def _():
-            write(first_ref[0, k * CAP : (k + 1) * CAP], second_ref[0, k * CAP : (k + 1) * CAP])
-
-    one(0)
-    one(1)
+        for half, text in enumerate((left, right)):
+            lanes = slice(half * 128, half * 128 + 128)
+            merged = text.reshape(CAP * PAGE, 128) + image[:, lanes]
+            out_ref[upper, 0, :, :, lanes] = merged.reshape(CAP, PAGE, 128)
+
+    @pl.when(prefill)
+    def _():
+        for own_ref, upper in ((own_near, here), (own_far, there)):
+            owner = upper * 4 + level
+            one((near_ref, side_ref), owner, upper, own_ref[0], placed[pl.ds(owner * CAP, CAP)])
+
+    @pl.when(jnp.logical_not(prefill))
+    def _():
+        one((near_ref, side_ref), place[3], here, key_near[0], value_near[0])
+        one((yonder_ref, far_ref), place[3], there, key_far[0], value_far[0])
 
 
 def merge_slots(place, slots, own, rows, arrived, images):
-    def local(i, place):
-        return jnp.where(place[0] == 0, i, 3)
-
-    def remote(i, place):
-        return jnp.where(place[0] == 0, 0, i)
-
-    image_spec = pl.BlockSpec((4, IMG_TALL, 256), lambda i, place, slots: (0, 0, 0))
-    chunk = (1, 2 * CAP, PAGE, 128)
-    return pl.pallas_call(
+    def level(i, place):
+        return lax.rem(place[3] + 8 - i, 4)
+
+    def chunk(base, apart, prefill):
+        def index(i, place, slots):
+            y = place[3] // 4
+            y = 1 - y if apart else y
+            used = (place[0] == 0) == prefill
+            return (base + jnp.where(used, 4 * y + level(i, place), 0), 0, 0, 0)
+
+        return pl.BlockSpec((1, CAP, PAGE, 128), index)
+
+    image_spec = pl.BlockSpec(
+        (1, IMG_TALL, 256), lambda i, place, slots: (jnp.where(place[0] == 0, 0, i), 0, 0)
+    )
+    own = own.reshape(16, CAP, PAGE, 128)
+    arrived = arrived.reshape(16, CAP, PAGE, 128)
+    near, yonder, side, far = images
+    result = pl.pallas_call(
         merge_kernel,
         grid_spec=pltpu.PrefetchScalarGridSpec(
             num_scalar_prefetch=2,
             grid=(4,),
             in_specs=[
-                pl.BlockSpec(chunk, lambda i, place, slots: (1, local(i, place), 0, 0)),
+                chunk(8, False, True),
+                chunk(8, True, True),
                 pl.BlockSpec((PAGES, PAGE, 128), lambda i, place, slots: (0, 0, 0)),
-                pl.BlockSpec(chunk, lambda i, place, slots: (0, remote(i, place), 0, 0)),
-                pl.BlockSpec(chunk, lambda i, place, slots: (1, remote(i, place), 0, 0)),
+                chunk(0, False, False),
+                chunk(8, False, False),
+                chunk(0, True, False),
+                chunk(8, True, False),
             ]
             + [image_spec] * 4,
-            out_specs=pl.BlockSpec((2 * CAP, PAGE, 256), lambda i, place, slots: (i, 0, 0)),
+            out_specs=pl.BlockSpec(
+                (2, 1, CAP, PAGE, 256), lambda i, place, slots: (0, level(i, place), 0, 0, 0)
+            ),
             scratch_shapes=[pltpu.VMEM((256, PAGE, 128), BF)],
         ),
-        out_shape=jax.ShapeDtypeStruct((256, PAGE, 256), BF),
+        out_shape=jax.ShapeDtypeStruct((2, 4, CAP, PAGE, 256), BF),
         compiler_params=pltpu.CompilerParams(vmem_limit_bytes=VMEM_LIMIT),
         cost_estimate=LIGHT,
         name="merge_slots",
-    )(place, slots, own, rows, arrived, arrived, *images)
+    )(place, slots, own, own, rows, arrived, arrived, arrived, arrived, near, side, yonder, far)
+    return result.reshape(256, PAGE, 256)
 
 
 def attend(queries, kv_cache, new_kv, cache_lengths):
@@ -385,7 +408,8 @@
     return [(i, (i // 4 + y) % 2 * 4 + (i + z) % 4) for i in range(8)]
 
 
-FAR = [(g * 8 + i, (1 - g) * 8 + (i + 4) % 8) for g in range(2) for i in range(8)]
+FAR = [(i, 8 + (i + 4) % 8) for i in range(8)]
+AWAY = [(8 + i, 8 + (i + 4) % 8) for i in range(8)]
 
 
 def after(value, other):
@@ -476,7 +500,7 @@
     )
     images = [
         near,
-        lax.ppermute(near, "seq", seq_shift(1, 0)),
+        lax.ppermute(near, ("group", "seq"), AWAY),
         lax.ppermute(near, "group", [(0, 1), (1, 0)]),
         lax.ppermute(near, ("group", "seq"), FAR),
     ]

time: 126 us -> 124 us (0.984)
  waiting for transfers between devices: 20.3 us -> 15.5 us
  starting transfers between devices: 45.5 us -> 48.1 us
    ppermute x1, starting transfers between devices: 0.01 us -> 4.84 us  [per_device(): lax.ppermute(near, ('group', 'seq'), AWAY)]
    ppermute x1, waiting for transfers between devices: 5.03 us -> 2.43 us  [per_device(): other_hidden = lax.ppermute(image_hidden, 'group', [(1, 0)])]
    ppermute x1, starting transfers between devices: 2.37 us -> 0.63 us  [per_device(): lax.ppermute(near, 'group', [(0, 1), (1, 0)])]
    ppermute x1, waiting for transfers between devices: 1.71 us -> 0.01 us  [per_device(): lax.ppermute(near, 'group', [(0, 1), (1, 0)])]
  transfers between devices with their start and end apart: 23 -> 23, of which waited for: 9 -> 8; matrix products, arithmetic and copies ran while one was open for 20% -> 20% of each run, Pallas kernels for 17% -> 17%
where the time goes in v7:
time: 124 us; the launch traced here: 122 us
  starting transfers between devices  48.1 us (39%)
  Pallas kernels  29.3 us (24%)
  waiting for transfers between devices  15.5 us (12%)
  other arithmetic  13.2 us (11%)
  matrix products  11.3 us (9%)
  local copies, waits for them, and re-layouts  3.07 us (2%)
  between operations  1.6 us (1%)
    pallas_call x1, Pallas kernels, project_text(): pl.pallas_call(project_kernel, grid_spec=pltpu.PrefetchScalarGridSpec(num...  9.29 us
    all_to_all x1, starting transfers between devices, per_device(): lax.all_to_all(by_owner.reshape(512, PAGE, 128), ('group', 'seq'), split_...  8.69 us
    all_to_all x1, starting transfers between devices, per_device(): pieces = lax.all_to_all(partial, 'seq', 0, 0, tiled=True)  7.45 us
    all_to_all x1, starting transfers between devices, per_device(): lax.all_to_all(cut_features(place, image_feats), 'seq', 0, 0, tiled=True)  7.05 us
    convert_element_type x4, other arithmetic, add_pair(): return (keep.astype(F32) + received.astype(F32)).astype(BF)  6.21 us
    pallas_call x1, Pallas kernels, merge_slots(): pl.pallas_call(merge_kernel, grid_spec=pltpu.PrefetchScalarGridSpec(num_s...  5.89 us
    pallas_call x1, Pallas kernels, image_rows_kv(): pl.pallas_call(image_kernel, grid_spec=pltpu.PrefetchScalarGridSpec(num_s...  5.76 us
    ppermute x1, waiting for transfers between devices, per_device(): lax.ppermute(near, ('group', 'seq'), AWAY)  4.96 us
  transfers between devices with their start and end apart: 23, of which 8 were waited for; matrix products, arithmetic and copies ran while one was open for 20% of the time, Pallas kernels for 17%

profile of v7, /device:TPU:10, one launch (start us, length us, event | category | flops | bytes accessed | tf_op | source)
XLA Modules:
  0.0 122.1 jit_solution(2143631189400881658)
XLA Ops:
  1.2 2.7 %cut_features.1 = bf16[8,32,912]{2,1,0:T(8,128)(2,1)} custom-call(s32[4]{0:T(128)} %pad_add_fusion.place, bf16[128,7296]{1,0:T(8,128)(2,1)} %feats_ref.1), custom_call_target="tpu_custom_call" | custom-call | flops 1 | bytes 1 | tf_op jit(solution)/shard_map/cut_features/pallas_call | solution.py:161
  3.9 7.0 %all-to-all-start = ((bf16[8,32,912]{2,1,0:T(8,128)(2,1)}), bf16[8,32,912]{2,1,0:T(8,128)(2,1)S(1)}, u32[]{:S(2)}, u32[]{:S(2)}) async-start(bf16[8,32,912]{2,1,0:T(8,128)(2,1)} %cut_features.1), calls=%async_computation | async-start | bytes 1048576 | tf_op jit(solution)/shard_map/all_to_all | solution.py:464
  11.0 9.3 %project_text.1 = (bf16[2080,128]{1,0:T(8,128)(2,1)}, bf16[2080,128]{1,0:T(8,128)(2,1)}, bf16[2080,128]{1,0:T(8,128)(2,1)}, bf16[2080,128]{1,0:T(8,128)(2,1)}, b...) custom-call(s32[4]{0:T(128)} %pad_add_fusion.place, ...), custom_call_target="tpu_custom_call" | custom-call | flops 1 | bytes 1 | tf_op jit(solution)/shard_map/project_text/pallas_call | solution.py:84
  23.8 2.2 %add_convert_fusion.2 = bf16[2080,128]{1,0:T(8,128)(2,1)} fusion(bf16[2080,128]{1,0:T(8,128)(2,1)} %collective-permute-done.1, bf16[2080,128]{1,0:T(8,128)(2,1)} %get-tuple-element.40), kind=kLoop, calls=%fused_computation.32 | loop fusion | flops 1064960 | bytes 1597440 | tf_op jit(solution)/shard_map/convert_element_type | solution.py:109
  26.0 1.5 %collective-permute-start.5 = (bf16[2080,128]{1,0:T(8,128)(2,1)}, bf16[2080,128]{1,0:T(8,128)(2,1)}, u32[]{:S(2)}, u32[]{:S(2)}) collective-permute-start(bf16[2080,128]{1,0:T(8,128)(2,1)} %add_convert_fusion.2), channel_id=1, source_target_pairs={{0,2},{1,3},{2,4},{3,5},{4,6},{5,7},{6,0},{7,1},{8,10},{9,11},{10,... | collective-permute-start | bytes 1597448 | tf_op jit(solution)/shard_map/ppermute | solution.py:471
  27.5 2.1 %add_convert_fusion.1 = bf16[2080,128]{1,0:T(8,128)(2,1)} fusion(bf16[2080,128]{1,0:T(8,128)(2,1)} %collective-permute-done.2, bf16[2080,128]{1,0:T(8,128)(2,1)} %get-tuple-element.42), kind=kLoop, calls=%fused_computation.31 | loop fusion | flops 1064960 | bytes 1597440 | tf_op jit(solution)/shard_map/convert_element_type | solution.py:109
  29.6 1.1 collective-permute-start.6
  31.7 2.2 %collective-permute-start.7 = (bf16[2080,128]{1,0:T(8,128)(2,1)}, bf16[2080,128]{1,0:T(8,128)(2,1)}, u32[]{:S(2)}, u32[]{:S(2)}) collective-permute-start(bf16[2080,128]{1,0:T(8,128)(2,1)} %add_convert_fusion), channel_id=1, source_target_pairs={{0,6},{1,7},{2,0},{3,1},{4,2},{5,3},{6,4},{7,5},{8,14},{9,15},{10,... | collective-permute-start | bytes 1597448 | tf_op jit(solution)/shard_map/ppermute | solution.py:471
  34.4 1.2 pad_maximum_fusion
  35.6 2.2 %convolution_convert_fusion = bf16[512,1024]{1,0:T(8,128)(2,1)} fusion(bf16[512,912]{1,0:T(8,128)(2,1)S(1)} %bitcast.84, bf16[912,1024]{1,0:T(8,128)(2,1)S(1)} %copy-done), kind=kOutput, calls=%fused_computation.26 | convolution fusion | flops 956825600 | bytes 3850240 | tf_op jit(solution)/shard_map/dot_general | solution.py:474
  37.9 7.5 %all-to-all-start.2 = ((bf16[8,64,1024]{2,1,0:T(8,128)(2,1)}), bf16[8,64,1024]{2,1,0:T(8,128)(2,1)S(1)}, u32[]{:S(2)}, u32[]{:S(2)}) async-start(bf16[8,64,1024]{2,1,0:T(8,128)(2,1)} %bitcast.83), calls=%async_computation.2 | async-start | bytes 2097152 | tf_op jit(solution)/shard_map/all_to_all | solution.py:484
  45.3 9.0 %conditional.1 = (bf16[128,1024]{1,0:T(8,128)(2,1)S(1)}) conditional(s32[]{:T(128)} %convert_element_type.78, () %tuple.19, (s32[128]{0:T(128)S(1)}, bf16[128,1024]{1,0:T(8,128)(2,1)S(1)}, bf16[128,128,256]{2,1,0:T(8,128)(2,1)}, bf16[128,256]{1,0:T(8,128)(2,1)S(1)}) %tuple.41), branch_computations={%region_2.3_spmd, %region_3.6_spmd} | conditional | flops 68852736 | bytes 12157448 | solution.py:475
  45.8 4.5 %fusion.36 = (f32[128,8]{1,0:T(8,128)S(1)}, f32[128,8,128]{2,1,0:T(8,128)S(1)}) fusion(bf16[128,8,128]{2,1,0:T(8,128)(2,1)S(1)} %bitcast.82, bf16[128,128,1,256]{3,1,0,2:T(8,128)(2,1)} %bitcast.79, pred[128,128]{1,0:T(8,128)(4,1)S(1)} %iota_compare_fusion), kind=kOutput, calls=%fused_computation.88 | convolution fusion | flops 33946624 | bytes 5001216 | tf_op jit(solution)/shard_map/cond/branch_1_fun/rgqh,rjgh->rgqj/dot_general | solution.py:377
  50.8 3.5 %fusion.5 = bf16[128,8,128]{2,1,0:T(8,128)(2,1)S(1)} fusion(bf16[128,128,1,256]{3,1,0,2:T(8,128)(2,1)} %bitcast.80, f32[128,8,128]{2,1,0:T(8,128)S(1)} %get-tuple-element.76, f32[128,128]{1,0:T(8,128)S(1)} %get-tuple-element.74, f32[128,8]{1,0:T(8,128)S(1)} %bitcast_convert_fusion, f32[128,8]{1,0:T(8,128)S(1)} %get-tuple-element.71, ...), kind=kOutput, calls=%fused_computation.7 | convolution fusion | flops 34340864 | bytes 5058560 | tf_op jit(solution)/shard_map/cond/branch_1_fun/rgqj,rjgh->rgqh/dot_general | solution.py:393
  54.4 2.6 %collective-permute-done.7.refs_4_ = bf16[2080,128]{1,0:T(8,128)(2,1)} collective-permute-done((bf16[2080,128]{1,0:T(8,128)(2,1)}, bf16[2080,128]{1,0:T(8,128)(2,1)}, u32[]{:S(2)}, u32[]{:S(2)}) %collective-permute-start.7) | collective-permute-done | bytes 532512 | tf_op jit(solution)/shard_map/ppermute | solution.py:471
  57.0 4.1 %finish_text.1 = (bf16[128,16,128]{2,1,0:T(8,128)(2,1)}, bf16[2,256,16,128]{3,2,1,0:T(8,128)(2,1)}) custom-call(s32[128]{0:T(128)} %multiply_add_fusion.slots, f32[16,128]{1,0:T(8,128)} %fusion.15.mask_ref, bf16[2080,128]{1,0:T(8,128)(2,1)} %get-tuple-element.38.refs_0_, bf16[2080,128]{1,0:T(8,128)(2,1)} %collective-permute-done.4.refs_1_, ...), custom_call_target="tpu_custom_call" | custom-call | flops 20000000000 | bytes 73999998976 | tf_op jit(solution)/shard_map/finish_text/pallas_call | solution.py:132
  62.1 8.7 %all-to-all-start.1 = ((bf16[512,16,128]{2,1,0:T(8,128)(2,1)}), bf16[512,16,128]{2,1,0:T(8,128)(2,1)}, u32[]{:S(2)}, u32[]{:S(2)}) async-start(bf16[512,16,128]{2,1,0:T(8,128)(2,1)} %bitcast.75), calls=%async_computation.1 | async-start | bytes 4194304 | tf_op jit(solution)/shard_map/all_to_all | solution.py:492
  71.1 5.8 %image_rows_kv.1 = (bf16[64,1024]{1,0:T(8,128)(2,1)}, bf16[4,80,256]{2,1,0:T(8,128)(2,1)}, bf16[4,80,256]{2,1,0:T(8,128)(2,1)}) custom-call(s32[4]{0:T(128)} %pad_add_fusion.place, bf16[8,64,1024]{2,1,0:T(8,128)(2,1)} %copy-done.1, bf16[1024]{0:T(1024)(128)(2,1)} %bias_ref.1, bf16[1024]{0:T(1024)(128)(2,1)} %gain_ref.3, bf16[1024,2048]{1,0:T(8,128)(2,1)} %weight_ref.1), custom_call_target="tpu_custom_call" | custom-call | flops 1 | bytes 1 | tf_op jit(solution)/shard_map/image_rows_kv/pallas_call | solution.py:221
  76.8 2.1 %collective-permute-start.8 = (bf16[128,16,128]{2,1,0:T(8,128)(2,1)}, bf16[128,16,128]{2,1,0:T(8,128)(2,1)S(1)}, u32[]{:S(2)}, u32[]{:S(2)}) collective-permute-start(bf16[128,16,128]{2,1,0:T(8,128)(2,1)} %get-tuple-element.51), channel_id=1, source_target_pairs={{64,0},{65,1},{66,2},{67,3},{68,4},{69,5},{70,6},{71,7},{72,8},{73... | collective-permute-start | bytes 1572872 | tf_op jit(solution)/shard_map/ppermute | solution.py:491
  80.5 2.1 %collective-permute-start.11 = (bf16[80,256]{1,0:T(8,128)(2,1)S(1)}, bf16[80,256]{1,0:T(8,128)(2,1)S(1)}, u32[]{:S(2)}, u32[]{:S(2)}) collective-permute-start(bf16[80,256]{1,0:T(8,128)(2,1)S(1)} %get-tuple-element.78), channel_id=1, source_target_pairs={{0,4},{1,5},{2,6},{3,7},{4,0},{5,1},{6,2},{7,3},{8,12},{9,13},{10,... | collective-permute-start | bytes 122888 | tf_op jit(solution)/shard_map/ppermute | solution.py:488
  82.6 1.7 %collective-permute-start.10 = (bf16[80,256]{1,0:T(8,128)(2,1)S(1)}, bf16[80,256]{1,0:T(8,128)(2,1)S(1)}, u32[]{:S(2)}, u32[]{:S(2)}) collective-permute-start(bf16[80,256]{1,0:T(8,128)(2,1)S(1)} %get-tuple-element.79), channel_id=1, source_target_pairs={{0,2},{1,3},{2,4},{3,5},{4,6},{5,7},{6,0},{7,1},{8,10},{9,11},{10,... | collective-permute-start | bytes 122888 | tf_op jit(solution)/shard_map/ppermute | solution.py:488
  84.9 1.2 collective-permute-done.11.c_ref
  87.7 1.6 %close_images.1 = bf16[80,256]{1,0:T(8,128)(2,1)} custom-call(bf16[80,256]{1,0:T(8,128)(2,1)} %get-tuple-element.54.a_ref, bf16[80,256]{1,0:T(8,128)(2,1)} %copy-done.12, bf16[80,256]{1,0:T(8,128)(2,1)} %copy-done.11, bf16[80,256]{1,0:T(8,128)(2,1)} %copy-done.10, bf16[16,256]{1,0:T(8,128)(2,1)} %fusion.26.labels_ref), custom_call_target="tpu_custom_call" | custom-call | flops 1 | bytes 1 | tf_op jit(solution)/shard_map/close_images/pallas_call | solution.py:259
  89.2 3.1 %collective-permute-start.15 = (bf16[80,256]{1,0:T(8,128)(2,1)}, bf16[80,256]{1,0:T(8,128)(2,1)S(1)}, u32[]{:S(2)}, u32[]{:S(2)}) collective-permute-start(bf16[80,256]{1,0:T(8,128)(2,1)} %close_images.1), channel_id=1, source_target_pairs={{0,24},{8,0},{16,8},{24,16},{32,56},{40,32},{48,40},{56,48},{1,25}... | collective-permute-start | bytes 122888 | tf_op jit(solution)/shard_map/ppermute | solution.py:499
  94.0 1.5 %collective-permute-start.19 = (bf16[64,1024]{1,0:T(8,128)(2,1)}, bf16[64,1024]{1,0:T(8,128)(2,1)S(1)}, u32[]{:S(2)}, u32[]{:S(2)}) collective-permute-start(bf16[64,1024]{1,0:T(8,128)(2,1)} %get-tuple-element.58), channel_id=1, source_target_pairs={{64,0},{65,1},{66,2},{67,3},{68,4},{69,5},{70,6},{71,7},{72,8},{73... | collective-permute-start | bytes 393224 | tf_op jit(solution)/shard_map/ppermute | solution.py:509
  95.6 2.7 %collective-permute-done.15 = bf16[80,256]{1,0:T(8,128)(2,1)S(1)} collective-permute-done((bf16[80,256]{1,0:T(8,128)(2,1)}, bf16[80,256]{1,0:T(8,128)(2,1)S(1)}, u32[]{:S(2)}, u32[]{:S(2)}) %collective-permute-start.15) | collective-permute-done | bytes 40992 | tf_op jit(solution)/shard_map/ppermute | solution.py:499
  99.6 1.3 %collective-permute-start.18 = (bf16[4,80,256]{2,1,0:T(8,128)(2,1)S(1)}, bf16[4,80,256]{2,1,0:T(8,128)(2,1)S(1)}, u32[]{:S(2)}, u32[]{:S(2)}) collective-permute-start(bf16[4,80,256]{2,1,0:T(8,128)(2,1)S(1)} %pad_maximum_fusion.1.near_ref), channel_id=1, source_target_pairs={{0,96},{8,104},{16,112},{24,120},{32,64},{40,72},{48,80},{56,88},{... | collective-permute-start | bytes 491528 | tf_op jit(solution)/shard_map/ppermute | solution.py:505
  100.9 4.8 %collective-permute-start.17 = (bf16[4,80,256]{2,1,0:T(8,128)(2,1)S(1)}, bf16[4,80,256]{2,1,0:T(8,128)(2,1)S(1)}, u32[]{:S(2)}, u32[]{:S(2)}) collective-permute-start(bf16[4,80,256]{2,1,0:T(8,128)(2,1)S(1)} %pad_maximum_fusion.1.near_ref), channel_id=1, source_target_pairs={{64,96},{72,104},{80,112},{88,120},{96,64},{104,72},{112,80},{120,... | collective-permute-start | bytes 491528 | tf_op jit(solution)/shard_map/ppermute | solution.py:503
  106.4 2.4 %collective-permute-done.19 = bf16[64,1024]{1,0:T(8,128)(2,1)S(1)} collective-permute-done((bf16[64,1024]{1,0:T(8,128)(2,1)}, bf16[64,1024]{1,0:T(8,128)(2,1)S(1)}, u32[]{:S(2)}, u32[]{:S(2)}) %collective-permute-start.19) | collective-permute-done | bytes 131104 | tf_op jit(solution)/shard_map/ppermute | solution.py:509
  108.8 1.7 %maximum_select_fusion = bf16[128,1024]{1,0:T(8,128)(2,1)} fusion(bf16[128,1024]{1,0:T(8,128)(2,1)S(1)} %get-tuple-element.83, bf16[64,1024]{1,0:T(8,128)(2,1)S(1)} %collective-permute-done.19, bf16[64,1024]{1,0:T(8,128)(2,1)} %get-tuple-element.58, pred[]{:T(512)S(6)} %eq.79), kind=kLoop, calls=%fused_computation.35 | loop fusion | flops 655360 | bytes 786433 | tf_op jit(solution)/shard_map/jit(_where)/select_n | solution.py:510
  110.5 5.0 %collective-permute-done.17.yonder_ref = bf16[4,80,256]{2,1,0:T(8,128)(2,1)S(1)} collective-permute-done((bf16[4,80,256]{2,1,0:T(8,128)(2,1)S(1)}, bf16[4,80,256]{2,1,0:T(8,128)(2,1)S(1)}, u32[]{:S(2)}, u32[]{:S(2)}) %collective-permute-start.17) | collective-permute-done | bytes 163872 | tf_op jit(solution)/shard_map/ppermute | solution.py:503
  116.2 5.9 %merge_slots.1 = bf16[2,4,32,16,256]{4,3,2,1,0:T(8,128)(2,1)} custom-call(s32[4]{0:T(128)} %pad_add_fusion.place, s32[128]{0:T(128)} %multiply_add_fusion.slots, bf16[16,32,16,128]{3,2,1,0:T(8,128)(2,1)} %bitcast.76, bf16[16,32,16,128]{3,2,1,0:T(8,128)(2,1)} %bitcast.77, bf16[128,16,128]{2,1,0:T(8,128)(2,1)} %copy-done.4, ...), custom_call_target="tpu_custom_call" | custom-call | flops 1 | bytes 1 | tf_op jit(solution)/shard_map/merge_slots/pallas_call | solution.py:343
  (88 shorter events, 15.3 us)
Async XLA Ops:
  0.6 35.0 %copy-start = (bf16[912,1024]{1,0:T(8,128)(2,1)S(1)}, bf16[912,1024]{1,0:T(8,128)(2,1)}, u32[]{:S(2)}) copy-start(bf16[912,1024]{1,0:T(8,128)(2,1)} %param.18) | copy-start | bytes 5603332
  3.9 19.8 %all-to-all-start = ((bf16[8,32,912]{2,1,0:T(8,128)(2,1)}), bf16[8,32,912]{2,1,0:T(8,128)(2,1)S(1)}, u32[]{:S(2)}, u32[]{:S(2)}) async-start(bf16[8,32,912]{2,1,0:T(8,128)(2,1)} %cut_features.1), calls=%async_computation | async-start | bytes 1048576 | tf_op jit(solution)/shard_map/all_to_all | solution.py:464
  11.0 10.4 %copy-start.16 = (s32[4]{0:T(128)S(1)}, s32[4]{0:T(128)}, u32[]{:S(2)}) copy-start(s32[4]{0:T(128)} %param.22) | copy-start | bytes 52
  11.0 11.7 %copy-start.13 = (s32[128]{0:T(128)S(1)}, s32[128]{0:T(128)}, u32[]{:S(2)}) copy-start(s32[128]{0:T(128)} %param.17) | copy-start | bytes 1540
  11.0 11.7 %copy-start.15 = (s32[128,1]{0,1:T(1,128)S(1)}, s32[128,1]{0,1:T(1,128)}, u32[]{:S(2)}) copy-start(s32[128,1]{0,1:T(1,128)} %param.23) | copy-start | bytes 1540
  20.3 10.4 %copy-start.3 = (bf16[2080,128]{1,0:T(8,128)(2,1)S(1)}, bf16[2080,128]{1,0:T(8,128)(2,1)}, u32[]{:S(2)}) copy-start(bf16[2080,128]{1,0:T(8,128)(2,1)} %get-tuple-element.44) | copy-start | bytes 1597444
  20.3 3.5 %collective-permute-start.1 = (bf16[2080,128]{1,0:T(8,128)(2,1)}, bf16[2080,128]{1,0:T(8,128)(2,1)}, u32[]{:S(2)}, u32[]{:S(2)}) collective-permute-start(bf16[2080,128]{1,0:T(8,128)(2,1)} %get-tuple-element.41), channel_id=1, source_target_pairs={{0,1},{1,0},{2,3},{3,2},{4,5},{5,4},{6,7},{7,6},{8,9},{9,8},{10,11... | collective-permute-start | bytes 1597448 | tf_op jit(solution)/shard_map/ppermute | solution.py:469
  20.4 7.1 %collective-permute-start.2 = (bf16[2080,128]{1,0:T(8,128)(2,1)}, bf16[2080,128]{1,0:T(8,128)(2,1)}, u32[]{:S(2)}, u32[]{:S(2)}) collective-permute-start(bf16[2080,128]{1,0:T(8,128)(2,1)} %get-tuple-element.43), channel_id=1, source_target_pairs={{0,1},{1,0},{2,3},{3,2},{4,5},{5,4},{6,7},{7,6},{8,9},{9,8},{10,11... | collective-permute-start | bytes 1597448 | tf_op jit(solution)/shard_map/ppermute | solution.py:469
  20.9 9.8 %collective-permute-start.3 = (bf16[2080,128]{1,0:T(8,128)(2,1)}, bf16[2080,128]{1,0:T(8,128)(2,1)S(1)}, u32[]{:S(2)}, u32[]{:S(2)}) collective-permute-start(bf16[2080,128]{1,0:T(8,128)(2,1)} %get-tuple-element.45), channel_id=1, source_target_pairs={{0,1},{1,0},{2,3},{3,2},{4,5},{5,4},{6,7},{7,6},{8,9},{9,8},{10,11... | collective-permute-start | bytes 1597448 | tf_op jit(solution)/shard_map/ppermute | solution.py:469
  21.0 33.4 %collective-permute-start.4 = (bf16[2080,128]{1,0:T(8,128)(2,1)}, bf16[2080,128]{1,0:T(8,128)(2,1)}, u32[]{:S(2)}, u32[]{:S(2)}) collective-permute-start(bf16[2080,128]{1,0:T(8,128)(2,1)} %get-tuple-element.49), channel_id=1, source_target_pairs={{0,1},{1,0},{2,3},{3,2},{4,5},{5,4},{6,7},{7,6},{8,9},{9,8},{10,11... | collective-permute-start | bytes 1597448 | tf_op jit(solution)/shard_map/ppermute | solution.py:469
  23.7 10.7 %collective-permute-start = (bf16[8,32,912]{2,1,0:T(8,128)(2,1)S(1)}, bf16[8,32,912]{2,1,0:T(8,128)(2,1)}, u32[]{:S(2)}, u32[]{:S(2)}) collective-permute-start(bf16[8,32,912]{2,1,0:T(8,128)(2,1)S(1)} %all-to-all-done), channel_id=1, source_target_pairs={{0,1},{1,0},{2,3},{3,2},{4,5},{5,4},{6,7},{7,6},{8,9},{9,8},{10,11... | collective-permute-start | bytes 1400840 | tf_op jit(solution)/shard_map/ppermute | solution.py:468
  26.0 28.4 %collective-permute-start.5 = (bf16[2080,128]{1,0:T(8,128)(2,1)}, bf16[2080,128]{1,0:T(8,128)(2,1)}, u32[]{:S(2)}, u32[]{:S(2)}) collective-permute-start(bf16[2080,128]{1,0:T(8,128)(2,1)} %add_convert_fusion.2), channel_id=1, source_target_pairs={{0,2},{1,3},{2,4},{3,5},{4,6},{5,7},{6,0},{7,1},{8,10},{9,11},{10,... | collective-permute-start | bytes 1597448 | tf_op jit(solution)/shard_map/ppermute | solution.py:471
  29.6 24.7 %collective-permute-start.6 = (bf16[2080,128]{1,0:T(8,128)(2,1)}, bf16[2080,128]{1,0:T(8,128)(2,1)}, u32[]{:S(2)}, u32[]{:S(2)}) collective-permute-start(bf16[2080,128]{1,0:T(8,128)(2,1)} %add_convert_fusion.1), channel_id=1, source_target_pairs={{0,4},{1,5},{2,6},{3,7},{4,0},{5,1},{6,2},{7,3},{8,12},{9,13},{10,... | collective-permute-start | bytes 1597448 | tf_op jit(solution)/shard_map/ppermute | solution.py:471
  31.7 25.3 %collective-permute-start.7 = (bf16[2080,128]{1,0:T(8,128)(2,1)}, bf16[2080,128]{1,0:T(8,128)(2,1)}, u32[]{:S(2)}, u32[]{:S(2)}) collective-permute-start(bf16[2080,128]{1,0:T(8,128)(2,1)} %add_convert_fusion), channel_id=1, source_target_pairs={{0,6},{1,7},{2,0},{3,1},{4,2},{5,3},{6,4},{7,5},{8,14},{9,15},{10,... | collective-permute-start | bytes 1597448 | tf_op jit(solution)/shard_map/ppermute | solution.py:471
  37.9 7.5 %copy-start.5 = (bf16[128,1024]{1,0:T(8,128)(2,1)S(1)}, bf16[128,1024]{1,0:T(8,128)(2,1)}, u32[]{:S(2)}) copy-start(bf16[128,1024]{1,0:T(8,128)(2,1)} %param.24) | copy-start | bytes 786436
  37.9 7.5 %copy-start.9 = (bf16[128,256]{1,0:T(8,128)(2,1)S(1)}, bf16[128,256]{1,0:T(8,128)(2,1)}, u32[]{:S(2)}) copy-start(bf16[128,256]{1,0:T(8,128)(2,1)} %param.26) | copy-start | bytes 196612
  37.9 7.5 %copy-start.14 = (s32[128]{0:T(128)S(1)}, s32[128]{0:T(128)}, u32[]{:S(2)}) copy-start(s32[128]{0:T(128)} %param.27) | copy-start | bytes 1540
  37.9 23.2 %all-to-all-start.2 = ((bf16[8,64,1024]{2,1,0:T(8,128)(2,1)}), bf16[8,64,1024]{2,1,0:T(8,128)(2,1)S(1)}, u32[]{:S(2)}, u32[]{:S(2)}) async-start(bf16[8,64,1024]{2,1,0:T(8,128)(2,1)} %bitcast.83), calls=%async_computation.2 | async-start | bytes 2097152 | tf_op jit(solution)/shard_map/all_to_all | solution.py:484
  62.1 53.4 %all-to-all-start.1 = ((bf16[512,16,128]{2,1,0:T(8,128)(2,1)}), bf16[512,16,128]{2,1,0:T(8,128)(2,1)}, u32[]{:S(2)}, u32[]{:S(2)}) async-start(bf16[512,16,128]{2,1,0:T(8,128)(2,1)} %bitcast.75), calls=%async_computation.1 | async-start | bytes 4194304 | tf_op jit(solution)/shard_map/all_to_all | solution.py:492
  76.8 2.1 %collective-permute-start.9 = (bf16[4,80,256]{2,1,0:T(8,128)(2,1)}, bf16[4,80,256]{2,1,0:T(8,128)(2,1)S(1)}, u32[]{:S(2)}, u32[]{:S(2)}) collective-permute-start(bf16[4,80,256]{2,1,0:T(8,128)(2,1)} %get-tuple-element.53), channel_id=1, source_target_pairs={{0,1},{1,0},{2,3},{3,2},{4,5},{5,4},{6,7},{7,6},{8,9},{9,8},{10,11... | collective-permute-start | bytes 491528 | tf_op jit(solution)/shard_map/ppermute | solution.py:486
  76.8 33.7 %collective-permute-start.8 = (bf16[128,16,128]{2,1,0:T(8,128)(2,1)}, bf16[128,16,128]{2,1,0:T(8,128)(2,1)S(1)}, u32[]{:S(2)}, u32[]{:S(2)}) collective-permute-start(bf16[128,16,128]{2,1,0:T(8,128)(2,1)} %get-tuple-element.51), channel_id=1, source_target_pairs={{64,0},{65,1},{66,2},{67,3},{68,4},{69,5},{70,6},{71,7},{72,8},{73... | collective-permute-start | bytes 1572872 | tf_op jit(solution)/shard_map/ppermute | solution.py:491
  80.5 4.3 %collective-permute-start.12 = (bf16[80,256]{1,0:T(8,128)(2,1)S(1)}, bf16[80,256]{1,0:T(8,128)(2,1)S(1)}, u32[]{:S(2)}, u32[]{:S(2)}) collective-permute-start(bf16[80,256]{1,0:T(8,128)(2,1)S(1)} %get-tuple-element.77), channel_id=1, source_target_pairs={{0,6},{1,7},{2,0},{3,1},{4,2},{5,3},{6,4},{7,5},{8,14},{9,15},{10,... | collective-permute-start | bytes 122888 | tf_op jit(solution)/shard_map/ppermute | solution.py:488
  80.5 5.5 %collective-permute-start.11 = (bf16[80,256]{1,0:T(8,128)(2,1)S(1)}, bf16[80,256]{1,0:T(8,128)(2,1)S(1)}, u32[]{:S(2)}, u32[]{:S(2)}) collective-permute-start(bf16[80,256]{1,0:T(8,128)(2,1)S(1)} %get-tuple-element.78), channel_id=1, source_target_pairs={{0,4},{1,5},{2,6},{3,7},{4,0},{5,1},{6,2},{7,3},{8,12},{9,13},{10,... | collective-permute-start | bytes 122888 | tf_op jit(solution)/shard_map/ppermute | solution.py:488
  82.6 4.4 %collective-permute-start.10 = (bf16[80,256]{1,0:T(8,128)(2,1)S(1)}, bf16[80,256]{1,0:T(8,128)(2,1)S(1)}, u32[]{:S(2)}, u32[]{:S(2)}) collective-permute-start(bf16[80,256]{1,0:T(8,128)(2,1)S(1)} %get-tuple-element.79), channel_id=1, source_target_pairs={{0,2},{1,3},{2,4},{3,5},{4,6},{5,7},{6,0},{7,1},{8,10},{9,11},{10,... | collective-permute-start | bytes 122888 | tf_op jit(solution)/shard_map/ppermute | solution.py:488
  89.2 9.1 %collective-permute-start.15 = (bf16[80,256]{1,0:T(8,128)(2,1)}, bf16[80,256]{1,0:T(8,128)(2,1)S(1)}, u32[]{:S(2)}, u32[]{:S(2)}) collective-permute-start(bf16[80,256]{1,0:T(8,128)(2,1)} %close_images.1), channel_id=1, source_target_pairs={{0,24},{8,0},{16,8},{24,16},{32,56},{40,32},{48,40},{56,48},{1,25}... | collective-permute-start | bytes 122888 | tf_op jit(solution)/shard_map/ppermute | solution.py:499
  92.3 6.3 %collective-permute-start.14 = (bf16[80,256]{1,0:T(8,128)(2,1)}, bf16[80,256]{1,0:T(8,128)(2,1)S(1)}, u32[]{:S(2)}, u32[]{:S(2)}) collective-permute-start(bf16[80,256]{1,0:T(8,128)(2,1)} %close_images.1), channel_id=1, source_target_pairs={{0,16},{8,24},{16,0},{24,8},{32,48},{40,56},{48,32},{56,40},{1,17}... | collective-permute-start | bytes 122888 | tf_op jit(solution)/shard_map/ppermute | solution.py:499
  93.1 5.7 %collective-permute-start.13 = (bf16[80,256]{1,0:T(8,128)(2,1)}, bf16[80,256]{1,0:T(8,128)(2,1)S(1)}, u32[]{:S(2)}, u32[]{:S(2)}) collective-permute-start(bf16[80,256]{1,0:T(8,128)(2,1)} %close_images.1), channel_id=1, source_target_pairs={{0,8},{8,16},{16,24},{24,0},{32,40},{40,48},{48,56},{56,32},{1,9},... | collective-permute-start | bytes 122888 | tf_op jit(solution)/shard_map/ppermute | solution.py:499
  94.0 14.8 %collective-permute-start.19 = (bf16[64,1024]{1,0:T(8,128)(2,1)}, bf16[64,1024]{1,0:T(8,128)(2,1)S(1)}, u32[]{:S(2)}, u32[]{:S(2)}) collective-permute-start(bf16[64,1024]{1,0:T(8,128)(2,1)} %get-tuple-element.58), channel_id=1, source_target_pairs={{64,0},{65,1},{66,2},{67,3},{68,4},{69,5},{70,6},{71,7},{72,8},{73... | collective-permute-start | bytes 393224 | tf_op jit(solution)/shard_map/ppermute | solution.py:509
  99.6 15.9 %copy-start.2 = (bf16[4,80,256]{2,1,0:T(8,128)(2,1)}, bf16[4,80,256]{2,1,0:T(8,128)(2,1)S(1)}, u32[]{:S(2)}) copy-start(bf16[4,80,256]{2,1,0:T(8,128)(2,1)S(1)} %pad_maximum_fusion.1.near_ref) | copy-start | bytes 491524
  99.6 10.9 %collective-permute-start.18 = (bf16[4,80,256]{2,1,0:T(8,128)(2,1)S(1)}, bf16[4,80,256]{2,1,0:T(8,128)(2,1)S(1)}, u32[]{:S(2)}, u32[]{:S(2)}) collective-permute-start(bf16[4,80,256]{2,1,0:T(8,128)(2,1)S(1)} %pad_maximum_fusion.1.near_ref), channel_id=1, source_target_pairs={{0,96},{8,104},{16,112},{24,120},{32,64},{40,72},{48,80},{56,88},{... | collective-permute-start | bytes 491528 | tf_op jit(solution)/shard_map/ppermute | solution.py:505
  100.9 14.6 %collective-permute-start.17 = (bf16[4,80,256]{2,1,0:T(8,128)(2,1)S(1)}, bf16[4,80,256]{2,1,0:T(8,128)(2,1)S(1)}, u32[]{:S(2)}, u32[]{:S(2)}) collective-permute-start(bf16[4,80,256]{2,1,0:T(8,128)(2,1)S(1)} %pad_maximum_fusion.1.near_ref), channel_id=1, source_target_pairs={{64,96},{72,104},{80,112},{88,120},{96,64},{104,72},{112,80},{120,... | collective-permute-start | bytes 491528 | tf_op jit(solution)/shard_map/ppermute | solution.py:503
  105.8 9.7 %collective-permute-start.16 = (bf16[4,80,256]{2,1,0:T(8,128)(2,1)S(1)}, bf16[4,80,256]{2,1,0:T(8,128)(2,1)S(1)}, u32[]{:S(2)}, u32[]{:S(2)}) collective-permute-start(bf16[4,80,256]{2,1,0:T(8,128)(2,1)S(1)} %pad_maximum_fusion.1.near_ref), channel_id=1, source_target_pairs={{0,64},{64,0},{1,65},{65,1},{2,66},{66,2},{3,67},{67,3},{4,68},{68... | collective-permute-start | bytes 491528 | tf_op jit(solution)/shard_map/ppermute | solution.py:504
  (8 other events, 16.2 us)

commit v8 on v7

--- a/solution.py
+++ b/solution.py
@@ -175,7 +175,7 @@
 
 
 def image_kernel(
-    place, pieces_ref, bias_ref, gain_ref, weight_ref, hidden_ref, swap_ref, same_ref, scaled, pair
+    place, pieces_ref, bias_ref, gain_ref, weight_ref, other_ref, hidden_ref, swap_ref, same_ref, scaled, pair
 ):
     step = pl.program_id(0)
 
@@ -202,18 +202,19 @@
         rows = jnp.where(picked == 0, high.astype(F32), jnp.where(picked == 1, low.astype(F32), 0.0))
         pair[...] = jnp.concatenate([rows, jnp.zeros_like(rows)], axis=1).astype(BF)
 
-    product = jnp.dot(scaled[...], weight_ref[...], preferred_element_type=F32)
-    left, right = product[:, :256], product[:, 256:]
     first = place[1] == 0
-    same_ref[0, 0:IMG, :] = jnp.where(first, left, right).astype(BF)
-    swap_ref[0, 0:IMG, :] = jnp.where(first, right, left).astype(BF)
-    same_ref[0, IMG:, :] = pair[...]
-    swap_ref[0, IMG:, :] = pair[...]
+    for k, weight in enumerate((weight_ref, other_ref)):
+        product = jnp.dot(scaled[...], weight[...], preferred_element_type=F32)
+        left, right = product[:, :256], product[:, 256:]
+        same_ref[k, 0:IMG, :] = jnp.where(first, left, right).astype(BF)
+        swap_ref[k, 0:IMG, :] = jnp.where(first, right, left).astype(BF)
+        same_ref[k, IMG:, :] = pair[...]
+        swap_ref[k, IMG:, :] = pair[...]
 
 
 def image_rows_kv(place, pieces, bias, gain, kv_w):
-    def column(i, place):
-        return (0, lax.rem(place[2] + i, 4))
+    def column(k):
+        return lambda i, place: (0, lax.rem(place[2] + 2 * i + k, 4))
 
     width = pieces.shape[2]
     row = pl.BlockSpec((width,), lambda i, place: (0,))
@@ -222,17 +223,18 @@
         image_kernel,
         grid_spec=pltpu.PrefetchScalarGridSpec(
             num_scalar_prefetch=1,
-            grid=(4,),
+            grid=(2,),
             in_specs=[
                 pl.BlockSpec((8, IMG, width), lambda i, place: (0, 0, 0)),
                 row,
                 row,
-                pl.BlockSpec((width, 512), column),
+                pl.BlockSpec((width, 512), column(0)),
+                pl.BlockSpec((width, 512), column(1)),
             ],
             out_specs=[
                 pl.BlockSpec((IMG, width), lambda i, place: (0, 0)),
-                pl.BlockSpec((1, IMG_TALL, 256), lambda i, place: (i, 0, 0)),
-                pl.BlockSpec((1, IMG_TALL, 256), lambda i, place: (i, 0, 0)),
+                pl.BlockSpec((2, IMG_TALL, 256), lambda i, place: (i, 0, 0)),
+                pl.BlockSpec((2, IMG_TALL, 256), lambda i, place: (i, 0, 0)),
             ],
             scratch_shapes=[pltpu.VMEM((IMG, width), BF), pltpu.VMEM((16, 256), BF)],
         ),
@@ -240,7 +242,7 @@
         compiler_params=pltpu.CompilerParams(vmem_limit_bytes=VMEM_LIMIT),
         cost_estimate=LIGHT,
         name="image_rows_kv",
-    )(place, pieces, bias, gain, kv_w)
+    )(place, pieces, bias, gain, kv_w, kv_w)
 
 
 def close_kernel(a_ref, b_ref, c_ref, d_ref, labels_ref, out_ref):

time: 124 us -> 124 us (level)
  transfers between devices with their start and end apart: 23 -> 23, of which waited for: 8 -> 7; matrix products, arithmetic and copies ran while one was open for 20% -> 20% of each run, Pallas kernels for 17% -> 16%
where the time goes in v8:
time: 124 us; the launch traced here: 122 us
  starting transfers between devices  48.3 us (39%)
  Pallas kernels  28.1 us (23%)
  waiting for transfers between devices  16.4 us (13%)
  other arithmetic  13.2 us (11%)
  matrix products  11.3 us (9%)
  local copies, waits for them, and re-layouts  3.07 us (2%)
  between operations  1.61 us (1%)
    pallas_call x1, Pallas kernels, project_text(): pl.pallas_call(project_kernel, grid_spec=pltpu.PrefetchScalarGridSpec(num...  9.29 us
    all_to_all x1, starting transfers between devices, per_device(): lax.all_to_all(by_owner.reshape(512, PAGE, 128), ('group', 'seq'), split_...  8.69 us
    all_to_all x1, starting transfers between devices, per_device(): pieces = lax.all_to_all(partial, 'seq', 0, 0, tiled=True)  7.45 us
    all_to_all x1, starting transfers between devices, per_device(): lax.all_to_all(cut_features(place, image_feats), 'seq', 0, 0, tiled=True)  7.05 us
    convert_element_type x4, other arithmetic, add_pair(): return (keep.astype(F32) + received.astype(F32)).astype(BF)  6.21 us
    pallas_call x1, Pallas kernels, merge_slots(): pl.pallas_call(merge_kernel, grid_spec=pltpu.PrefetchScalarGridSpec(num_s...  5.89 us
    ppermute x1, starting transfers between devices, per_device(): lax.ppermute(near, ('group', 'seq'), AWAY)  5.07 us
    ppermute x1, waiting for transfers between devices, per_device(): lax.ppermute(near, ('group', 'seq'), AWAY)  4.96 us
  transfers between devices with their start and end apart: 23, of which 7 were waited for; matrix products, arithmetic and copies ran while one was open for 20% of the time, Pallas kernels for 16%

profile of v8, /device:TPU:10, one launch (start us, length us, event | category | flops | bytes accessed | tf_op | source)
XLA Modules:
  0.0 122.1 jit_solution(10967465720365959738)
XLA Ops:
  1.2 2.7 %cut_features.1 = bf16[8,32,912]{2,1,0:T(8,128)(2,1)} custom-call(s32[4]{0:T(128)} %pad_add_fusion.place, bf16[128,7296]{1,0:T(8,128)(2,1)} %feats_ref.1), custom_call_target="tpu_custom_call" | custom-call | flops 1 | bytes 1 | tf_op jit(solution)/shard_map/cut_features/pallas_call | solution.py:161
  3.9 7.0 %all-to-all-start = ((bf16[8,32,912]{2,1,0:T(8,128)(2,1)}), bf16[8,32,912]{2,1,0:T(8,128)(2,1)S(1)}, u32[]{:S(2)}, u32[]{:S(2)}) async-start(bf16[8,32,912]{2,1,0:T(8,128)(2,1)} %cut_features.1), calls=%async_computation | async-start | bytes 1048576 | tf_op jit(solution)/shard_map/all_to_all | solution.py:466
  11.0 9.3 %project_text.1 = (bf16[2080,128]{1,0:T(8,128)(2,1)}, bf16[2080,128]{1,0:T(8,128)(2,1)}, bf16[2080,128]{1,0:T(8,128)(2,1)}, bf16[2080,128]{1,0:T(8,128)(2,1)}, b...) custom-call(s32[4]{0:T(128)} %pad_add_fusion.place, ...), custom_call_target="tpu_custom_call" | custom-call | flops 1 | bytes 1 | tf_op jit(solution)/shard_map/project_text/pallas_call | solution.py:84
  23.8 2.2 %add_convert_fusion.2 = bf16[2080,128]{1,0:T(8,128)(2,1)} fusion(bf16[2080,128]{1,0:T(8,128)(2,1)} %collective-permute-done.1, bf16[2080,128]{1,0:T(8,128)(2,1)} %get-tuple-element.40), kind=kLoop, calls=%fused_computation.32 | loop fusion | flops 1064960 | bytes 1597440 | tf_op jit(solution)/shard_map/convert_element_type | solution.py:109
  26.0 1.5 %collective-permute-start.5 = (bf16[2080,128]{1,0:T(8,128)(2,1)}, bf16[2080,128]{1,0:T(8,128)(2,1)}, u32[]{:S(2)}, u32[]{:S(2)}) collective-permute-start(bf16[2080,128]{1,0:T(8,128)(2,1)} %add_convert_fusion.2), channel_id=1, source_target_pairs={{0,2},{1,3},{2,4},{3,5},{4,6},{5,7},{6,0},{7,1},{8,10},{9,11},{10,... | collective-permute-start | bytes 1597448 | tf_op jit(solution)/shard_map/ppermute | solution.py:473
  27.5 2.1 %add_convert_fusion.1 = bf16[2080,128]{1,0:T(8,128)(2,1)} fusion(bf16[2080,128]{1,0:T(8,128)(2,1)} %collective-permute-done.2, bf16[2080,128]{1,0:T(8,128)(2,1)} %get-tuple-element.42), kind=kLoop, calls=%fused_computation.31 | loop fusion | flops 1064960 | bytes 1597440 | tf_op jit(solution)/shard_map/convert_element_type | solution.py:109
  29.6 1.1 collective-permute-start.6
  31.7 2.2 %collective-permute-start.7 = (bf16[2080,128]{1,0:T(8,128)(2,1)}, bf16[2080,128]{1,0:T(8,128)(2,1)}, u32[]{:S(2)}, u32[]{:S(2)}) collective-permute-start(bf16[2080,128]{1,0:T(8,128)(2,1)} %add_convert_fusion), channel_id=1, source_target_pairs={{0,6},{1,7},{2,0},{3,1},{4,2},{5,3},{6,4},{7,5},{8,14},{9,15},{10,... | collective-permute-start | bytes 1597448 | tf_op jit(solution)/shard_map/ppermute | solution.py:473
  34.4 1.2 pad_maximum_fusion
  35.6 2.2 %convolution_convert_fusion = bf16[512,1024]{1,0:T(8,128)(2,1)} fusion(bf16[512,912]{1,0:T(8,128)(2,1)S(1)} %bitcast.84, bf16[912,1024]{1,0:T(8,128)(2,1)S(1)} %copy-done), kind=kOutput, calls=%fused_computation.26 | convolution fusion | flops 956825600 | bytes 3850240 | tf_op jit(solution)/shard_map/dot_general | solution.py:476
  37.9 7.5 %all-to-all-start.2 = ((bf16[8,64,1024]{2,1,0:T(8,128)(2,1)}), bf16[8,64,1024]{2,1,0:T(8,128)(2,1)S(1)}, u32[]{:S(2)}, u32[]{:S(2)}) async-start(bf16[8,64,1024]{2,1,0:T(8,128)(2,1)} %bitcast.83), calls=%async_computation.2 | async-start | bytes 2097152 | tf_op jit(solution)/shard_map/all_to_all | solution.py:486
  45.3 9.0 %conditional.1 = (bf16[128,1024]{1,0:T(8,128)(2,1)S(1)}) conditional(s32[]{:T(128)} %convert_element_type.78, () %tuple.19, (s32[128]{0:T(128)S(1)}, bf16[128,1024]{1,0:T(8,128)(2,1)S(1)}, bf16[128,128,256]{2,1,0:T(8,128)(2,1)}, bf16[128,256]{1,0:T(8,128)(2,1)S(1)}) %tuple.41), branch_computations={%region_2.3_spmd, %region_3.6_spmd} | conditional | flops 68852736 | bytes 12157448 | solution.py:477
  45.8 4.5 %fusion.36 = (f32[128,8]{1,0:T(8,128)S(1)}, f32[128,8,128]{2,1,0:T(8,128)S(1)}) fusion(bf16[128,8,128]{2,1,0:T(8,128)(2,1)S(1)} %bitcast.82, bf16[128,128,1,256]{3,1,0,2:T(8,128)(2,1)} %bitcast.79, pred[128,128]{1,0:T(8,128)(4,1)S(1)} %iota_compare_fusion), kind=kOutput, calls=%fused_computation.88 | convolution fusion | flops 33946624 | bytes 5001216 | tf_op jit(solution)/shard_map/cond/branch_1_fun/rgqh,rjgh->rgqj/dot_general | solution.py:379
  50.8 3.5 %fusion.5 = bf16[128,8,128]{2,1,0:T(8,128)(2,1)S(1)} fusion(bf16[128,128,1,256]{3,1,0,2:T(8,128)(2,1)} %bitcast.80, f32[128,8,128]{2,1,0:T(8,128)S(1)} %get-tuple-element.76, f32[128,128]{1,0:T(8,128)S(1)} %get-tuple-element.74, f32[128,8]{1,0:T(8,128)S(1)} %bitcast_convert_fusion, f32[128,8]{1,0:T(8,128)S(1)} %get-tuple-element.71, ...), kind=kOutput, calls=%fused_computation.7 | convolution fusion | flops 34340864 | bytes 5058560 | tf_op jit(solution)/shard_map/cond/branch_1_fun/rgqj,rjgh->rgqh/dot_general | solution.py:395
  54.4 2.6 %collective-permute-done.7.refs_4_ = bf16[2080,128]{1,0:T(8,128)(2,1)} collective-permute-done((bf16[2080,128]{1,0:T(8,128)(2,1)}, bf16[2080,128]{1,0:T(8,128)(2,1)}, u32[]{:S(2)}, u32[]{:S(2)}) %collective-permute-start.7) | collective-permute-done | bytes 532512 | tf_op jit(solution)/shard_map/ppermute | solution.py:473
  57.0 4.1 %finish_text.1 = (bf16[128,16,128]{2,1,0:T(8,128)(2,1)}, bf16[2,256,16,128]{3,2,1,0:T(8,128)(2,1)}) custom-call(s32[128]{0:T(128)} %multiply_add_fusion.slots, f32[16,128]{1,0:T(8,128)} %fusion.15.mask_ref, bf16[2080,128]{1,0:T(8,128)(2,1)} %get-tuple-element.38.refs_0_, bf16[2080,128]{1,0:T(8,128)(2,1)} %collective-permute-done.4.refs_1_, ...), custom_call_target="tpu_custom_call" | custom-call | flops 20000000000 | bytes 73999998976 | tf_op jit(solution)/shard_map/finish_text/pallas_call | solution.py:132
  62.1 8.7 %all-to-all-start.1 = ((bf16[512,16,128]{2,1,0:T(8,128)(2,1)}), bf16[512,16,128]{2,1,0:T(8,128)(2,1)}, u32[]{:S(2)}, u32[]{:S(2)}) async-start(bf16[512,16,128]{2,1,0:T(8,128)(2,1)} %bitcast.75), calls=%async_computation.1 | async-start | bytes 4194304 | tf_op jit(solution)/shard_map/all_to_all | solution.py:494
  71.1 4.6 %image_rows_kv.1 = (bf16[64,1024]{1,0:T(8,128)(2,1)}, bf16[4,80,256]{2,1,0:T(8,128)(2,1)}, bf16[4,80,256]{2,1,0:T(8,128)(2,1)}) custom-call(s32[4]{0:T(128)} %pad_add_fusion.place, bf16[8,64,1024]{2,1,0:T(8,128)(2,1)} %copy-done.1, bf16[1024]{0:T(1024)(128)(2,1)} %bias_ref.1, bf16[1024]{0:T(1024)(128)(2,1)} %gain_ref.3, bf16[1024,2048]{1,0:T(8,128)(2,1)} %other_ref.1, ...), custom_call_target="tpu_custom_call" | custom-call | flops 1 | bytes 1 | tf_op jit(solution)/shard_map/image_rows_kv/pallas_call | solution.py:222
  75.7 2.1 %collective-permute-start.8 = (bf16[128,16,128]{2,1,0:T(8,128)(2,1)}, bf16[128,16,128]{2,1,0:T(8,128)(2,1)S(1)}, u32[]{:S(2)}, u32[]{:S(2)}) collective-permute-start(bf16[128,16,128]{2,1,0:T(8,128)(2,1)} %get-tuple-element.51), channel_id=1, source_target_pairs={{64,0},{65,1},{66,2},{67,3},{68,4},{69,5},{70,6},{71,7},{72,8},{73... | collective-permute-start | bytes 1572872 | tf_op jit(solution)/shard_map/ppermute | solution.py:493
  79.4 2.1 %collective-permute-start.11 = (bf16[80,256]{1,0:T(8,128)(2,1)S(1)}, bf16[80,256]{1,0:T(8,128)(2,1)S(1)}, u32[]{:S(2)}, u32[]{:S(2)}) collective-permute-start(bf16[80,256]{1,0:T(8,128)(2,1)S(1)} %get-tuple-element.78), channel_id=1, source_target_pairs={{0,4},{1,5},{2,6},{3,7},{4,0},{5,1},{6,2},{7,3},{8,12},{9,13},{10,... | collective-permute-start | bytes 122888 | tf_op jit(solution)/shard_map/ppermute | solution.py:490
  81.5 1.7 %collective-permute-start.10 = (bf16[80,256]{1,0:T(8,128)(2,1)S(1)}, bf16[80,256]{1,0:T(8,128)(2,1)S(1)}, u32[]{:S(2)}, u32[]{:S(2)}) collective-permute-start(bf16[80,256]{1,0:T(8,128)(2,1)S(1)} %get-tuple-element.79), channel_id=1, source_target_pairs={{0,2},{1,3},{2,4},{3,5},{4,6},{5,7},{6,0},{7,1},{8,10},{9,11},{10,... | collective-permute-start | bytes 122888 | tf_op jit(solution)/shard_map/ppermute | solution.py:490
  83.7 1.2 collective-permute-done.11.c_ref
  86.5 1.6 %close_images.1 = bf16[80,256]{1,0:T(8,128)(2,1)} custom-call(bf16[80,256]{1,0:T(8,128)(2,1)} %get-tuple-element.54.a_ref, bf16[80,256]{1,0:T(8,128)(2,1)} %copy-done.12, bf16[80,256]{1,0:T(8,128)(2,1)} %copy-done.11, bf16[80,256]{1,0:T(8,128)(2,1)} %copy-done.10, bf16[16,256]{1,0:T(8,128)(2,1)} %fusion.26.labels_ref), custom_call_target="tpu_custom_call" | custom-call | flops 1 | bytes 1 | tf_op jit(solution)/shard_map/close_images/pallas_call | solution.py:261
  88.1 3.1 %collective-permute-start.15 = (bf16[80,256]{1,0:T(8,128)(2,1)}, bf16[80,256]{1,0:T(8,128)(2,1)S(1)}, u32[]{:S(2)}, u32[]{:S(2)}) collective-permute-start(bf16[80,256]{1,0:T(8,128)(2,1)} %close_images.1), channel_id=1, source_target_pairs={{0,24},{8,0},{16,8},{24,16},{32,56},{40,32},{48,40},{56,48},{1,25}... | collective-permute-start | bytes 122888 | tf_op jit(solution)/shard_map/ppermute | solution.py:501
  92.9 1.5 %collective-permute-start.19 = (bf16[64,1024]{1,0:T(8,128)(2,1)}, bf16[64,1024]{1,0:T(8,128)(2,1)S(1)}, u32[]{:S(2)}, u32[]{:S(2)}) collective-permute-start(bf16[64,1024]{1,0:T(8,128)(2,1)} %get-tuple-element.58), channel_id=1, source_target_pairs={{64,0},{65,1},{66,2},{67,3},{68,4},{69,5},{70,6},{71,7},{72,8},{73... | collective-permute-start | bytes 393224 | tf_op jit(solution)/shard_map/ppermute | solution.py:511
  94.4 3.5 %collective-permute-done.15 = bf16[80,256]{1,0:T(8,128)(2,1)S(1)} collective-permute-done((bf16[80,256]{1,0:T(8,128)(2,1)}, bf16[80,256]{1,0:T(8,128)(2,1)S(1)}, u32[]{:S(2)}, u32[]{:S(2)}) %collective-permute-start.15) | collective-permute-done | bytes 40992 | tf_op jit(solution)/shard_map/ppermute | solution.py:501
  99.1 1.3 %collective-permute-start.18 = (bf16[4,80,256]{2,1,0:T(8,128)(2,1)S(1)}, bf16[4,80,256]{2,1,0:T(8,128)(2,1)S(1)}, u32[]{:S(2)}, u32[]{:S(2)}) collective-permute-start(bf16[4,80,256]{2,1,0:T(8,128)(2,1)S(1)} %pad_maximum_fusion.1.near_ref), channel_id=1, source_target_pairs={{0,96},{8,104},{16,112},{24,120},{32,64},{40,72},{48,80},{56,88},{... | collective-permute-start | bytes 491528 | tf_op jit(solution)/shard_map/ppermute | solution.py:507
  100.4 5.1 %collective-permute-start.17 = (bf16[4,80,256]{2,1,0:T(8,128)(2,1)S(1)}, bf16[4,80,256]{2,1,0:T(8,128)(2,1)S(1)}, u32[]{:S(2)}, u32[]{:S(2)}) collective-permute-start(bf16[4,80,256]{2,1,0:T(8,128)(2,1)S(1)} %pad_maximum_fusion.1.near_ref), channel_id=1, source_target_pairs={{64,96},{72,104},{80,112},{88,120},{96,64},{104,72},{112,80},{120,... | collective-permute-start | bytes 491528 | tf_op jit(solution)/shard_map/ppermute | solution.py:505
  106.1 2.7 %collective-permute-done.19 = bf16[64,1024]{1,0:T(8,128)(2,1)S(1)} collective-permute-done((bf16[64,1024]{1,0:T(8,128)(2,1)}, bf16[64,1024]{1,0:T(8,128)(2,1)S(1)}, u32[]{:S(2)}, u32[]{:S(2)}) %collective-permute-start.19) | collective-permute-done | bytes 131104 | tf_op jit(solution)/shard_map/ppermute | solution.py:511
  108.8 1.7 %maximum_select_fusion = bf16[128,1024]{1,0:T(8,128)(2,1)} fusion(bf16[128,1024]{1,0:T(8,128)(2,1)S(1)} %get-tuple-element.83, bf16[64,1024]{1,0:T(8,128)(2,1)S(1)} %collective-permute-done.19, bf16[64,1024]{1,0:T(8,128)(2,1)} %get-tuple-element.58, pred[]{:T(512)S(6)} %eq.79), kind=kLoop, calls=%fused_computation.35 | loop fusion | flops 655360 | bytes 786433 | tf_op jit(solution)/shard_map/jit(_where)/select_n | solution.py:512
  110.5 5.0 %collective-permute-done.17.yonder_ref = bf16[4,80,256]{2,1,0:T(8,128)(2,1)S(1)} collective-permute-done((bf16[4,80,256]{2,1,0:T(8,128)(2,1)S(1)}, bf16[4,80,256]{2,1,0:T(8,128)(2,1)S(1)}, u32[]{:S(2)}, u32[]{:S(2)}) %collective-permute-start.17) | collective-permute-done | bytes 163872 | tf_op jit(solution)/shard_map/ppermute | solution.py:505
  116.2 5.9 %merge_slots.1 = bf16[2,4,32,16,256]{4,3,2,1,0:T(8,128)(2,1)} custom-call(s32[4]{0:T(128)} %pad_add_fusion.place, s32[128]{0:T(128)} %multiply_add_fusion.slots, bf16[16,32,16,128]{3,2,1,0:T(8,128)(2,1)} %bitcast.76, bf16[16,32,16,128]{3,2,1,0:T(8,128)(2,1)} %bitcast.77, bf16[128,16,128]{2,1,0:T(8,128)(2,1)} %copy-done.4, ...), custom_call_target="tpu_custom_call" | custom-call | flops 1 | bytes 1 | tf_op jit(solution)/shard_map/merge_slots/pallas_call | solution.py:345
  (88 shorter events, 15.2 us)
Async XLA Ops:
  0.6 35.0 %copy-start = (bf16[912,1024]{1,0:T(8,128)(2,1)S(1)}, bf16[912,1024]{1,0:T(8,128)(2,1)}, u32[]{:S(2)}) copy-start(bf16[912,1024]{1,0:T(8,128)(2,1)} %param.18) | copy-start | bytes 5603332
  3.9 19.8 %all-to-all-start = ((bf16[8,32,912]{2,1,0:T(8,128)(2,1)}), bf16[8,32,912]{2,1,0:T(8,128)(2,1)S(1)}, u32[]{:S(2)}, u32[]{:S(2)}) async-start(bf16[8,32,912]{2,1,0:T(8,128)(2,1)} %cut_features.1), calls=%async_computation | async-start | bytes 1048576 | tf_op jit(solution)/shard_map/all_to_all | solution.py:466
  11.0 10.4 %copy-start.16 = (s32[4]{0:T(128)S(1)}, s32[4]{0:T(128)}, u32[]{:S(2)}) copy-start(s32[4]{0:T(128)} %param.22) | copy-start | bytes 52
  11.0 11.7 %copy-start.13 = (s32[128]{0:T(128)S(1)}, s32[128]{0:T(128)}, u32[]{:S(2)}) copy-start(s32[128]{0:T(128)} %param.17) | copy-start | bytes 1540
  11.0 11.7 %copy-start.15 = (s32[128,1]{0,1:T(1,128)S(1)}, s32[128,1]{0,1:T(1,128)}, u32[]{:S(2)}) copy-start(s32[128,1]{0,1:T(1,128)} %param.23) | copy-start | bytes 1540
  20.3 10.4 %copy-start.3 = (bf16[2080,128]{1,0:T(8,128)(2,1)S(1)}, bf16[2080,128]{1,0:T(8,128)(2,1)}, u32[]{:S(2)}) copy-start(bf16[2080,128]{1,0:T(8,128)(2,1)} %get-tuple-element.44) | copy-start | bytes 1597444
  20.3 3.5 %collective-permute-start.1 = (bf16[2080,128]{1,0:T(8,128)(2,1)}, bf16[2080,128]{1,0:T(8,128)(2,1)}, u32[]{:S(2)}, u32[]{:S(2)}) collective-permute-start(bf16[2080,128]{1,0:T(8,128)(2,1)} %get-tuple-element.41), channel_id=1, source_target_pairs={{0,1},{1,0},{2,3},{3,2},{4,5},{5,4},{6,7},{7,6},{8,9},{9,8},{10,11... | collective-permute-start | bytes 1597448 | tf_op jit(solution)/shard_map/ppermute | solution.py:471
  20.4 7.1 %collective-permute-start.2 = (bf16[2080,128]{1,0:T(8,128)(2,1)}, bf16[2080,128]{1,0:T(8,128)(2,1)}, u32[]{:S(2)}, u32[]{:S(2)}) collective-permute-start(bf16[2080,128]{1,0:T(8,128)(2,1)} %get-tuple-element.43), channel_id=1, source_target_pairs={{0,1},{1,0},{2,3},{3,2},{4,5},{5,4},{6,7},{7,6},{8,9},{9,8},{10,11... | collective-permute-start | bytes 1597448 | tf_op jit(solution)/shard_map/ppermute | solution.py:471
  20.9 9.8 %collective-permute-start.3 = (bf16[2080,128]{1,0:T(8,128)(2,1)}, bf16[2080,128]{1,0:T(8,128)(2,1)S(1)}, u32[]{:S(2)}, u32[]{:S(2)}) collective-permute-start(bf16[2080,128]{1,0:T(8,128)(2,1)} %get-tuple-element.45), channel_id=1, source_target_pairs={{0,1},{1,0},{2,3},{3,2},{4,5},{5,4},{6,7},{7,6},{8,9},{9,8},{10,11... | collective-permute-start | bytes 1597448 | tf_op jit(solution)/shard_map/ppermute | solution.py:471
  21.0 33.4 %collective-permute-start.4 = (bf16[2080,128]{1,0:T(8,128)(2,1)}, bf16[2080,128]{1,0:T(8,128)(2,1)}, u32[]{:S(2)}, u32[]{:S(2)}) collective-permute-start(bf16[2080,128]{1,0:T(8,128)(2,1)} %get-tuple-element.49), channel_id=1, source_target_pairs={{0,1},{1,0},{2,3},{3,2},{4,5},{5,4},{6,7},{7,6},{8,9},{9,8},{10,11... | collective-permute-start | bytes 1597448 | tf_op jit(solution)/shard_map/ppermute | solution.py:471
  23.7 10.7 %collective-permute-start = (bf16[8,32,912]{2,1,0:T(8,128)(2,1)S(1)}, bf16[8,32,912]{2,1,0:T(8,128)(2,1)}, u32[]{:S(2)}, u32[]{:S(2)}) collective-permute-start(bf16[8,32,912]{2,1,0:T(8,128)(2,1)S(1)} %all-to-all-done), channel_id=1, source_target_pairs={{0,1},{1,0},{2,3},{3,2},{4,5},{5,4},{6,7},{7,6},{8,9},{9,8},{10,11... | collective-permute-start | bytes 1400840 | tf_op jit(solution)/shard_map/ppermute | solution.py:470
  26.0 28.4 %collective-permute-start.5 = (bf16[2080,128]{1,0:T(8,128)(2,1)}, bf16[2080,128]{1,0:T(8,128)(2,1)}, u32[]{:S(2)}, u32[]{:S(2)}) collective-permute-start(bf16[2080,128]{1,0:T(8,128)(2,1)} %add_convert_fusion.2), channel_id=1, source_target_pairs={{0,2},{1,3},{2,4},{3,5},{4,6},{5,7},{6,0},{7,1},{8,10},{9,11},{10,... | collective-permute-start | bytes 1597448 | tf_op jit(solution)/shard_map/ppermute | solution.py:473
  29.6 24.7 %collective-permute-start.6 = (bf16[2080,128]{1,0:T(8,128)(2,1)}, bf16[2080,128]{1,0:T(8,128)(2,1)}, u32[]{:S(2)}, u32[]{:S(2)}) collective-permute-start(bf16[2080,128]{1,0:T(8,128)(2,1)} %add_convert_fusion.1), channel_id=1, source_target_pairs={{0,4},{1,5},{2,6},{3,7},{4,0},{5,1},{6,2},{7,3},{8,12},{9,13},{10,... | collective-permute-start | bytes 1597448 | tf_op jit(solution)/shard_map/ppermute | solution.py:473
  31.7 25.3 %collective-permute-start.7 = (bf16[2080,128]{1,0:T(8,128)(2,1)}, bf16[2080,128]{1,0:T(8,128)(2,1)}, u32[]{:S(2)}, u32[]{:S(2)}) collective-permute-start(bf16[2080,128]{1,0:T(8,128)(2,1)} %add_convert_fusion), channel_id=1, source_target_pairs={{0,6},{1,7},{2,0},{3,1},{4,2},{5,3},{6,4},{7,5},{8,14},{9,15},{10,... | collective-permute-start | bytes 1597448 | tf_op jit(solution)/shard_map/ppermute | solution.py:473
  37.9 7.5 %copy-start.5 = (bf16[128,1024]{1,0:T(8,128)(2,1)S(1)}, bf16[128,1024]{1,0:T(8,128)(2,1)}, u32[]{:S(2)}) copy-start(bf16[128,1024]{1,0:T(8,128)(2,1)} %param.24) | copy-start | bytes 786436
  37.9 7.5 %copy-start.9 = (bf16[128,256]{1,0:T(8,128)(2,1)S(1)}, bf16[128,256]{1,0:T(8,128)(2,1)}, u32[]{:S(2)}) copy-start(bf16[128,256]{1,0:T(8,128)(2,1)} %param.26) | copy-start | bytes 196612
  37.9 7.5 %copy-start.14 = (s32[128]{0:T(128)S(1)}, s32[128]{0:T(128)}, u32[]{:S(2)}) copy-start(s32[128]{0:T(128)} %param.27) | copy-start | bytes 1540
  37.9 23.2 %all-to-all-start.2 = ((bf16[8,64,1024]{2,1,0:T(8,128)(2,1)}), bf16[8,64,1024]{2,1,0:T(8,128)(2,1)S(1)}, u32[]{:S(2)}, u32[]{:S(2)}) async-start(bf16[8,64,1024]{2,1,0:T(8,128)(2,1)} %bitcast.83), calls=%async_computation.2 | async-start | bytes 2097152 | tf_op jit(solution)/shard_map/all_to_all | solution.py:486
  62.1 53.4 %all-to-all-start.1 = ((bf16[512,16,128]{2,1,0:T(8,128)(2,1)}), bf16[512,16,128]{2,1,0:T(8,128)(2,1)}, u32[]{:S(2)}, u32[]{:S(2)}) async-start(bf16[512,16,128]{2,1,0:T(8,128)(2,1)} %bitcast.75), calls=%async_computation.1 | async-start | bytes 4194304 | tf_op jit(solution)/shard_map/all_to_all | solution.py:494
  75.7 2.1 %collective-permute-start.9 = (bf16[4,80,256]{2,1,0:T(8,128)(2,1)}, bf16[4,80,256]{2,1,0:T(8,128)(2,1)S(1)}, u32[]{:S(2)}, u32[]{:S(2)}) collective-permute-start(bf16[4,80,256]{2,1,0:T(8,128)(2,1)} %get-tuple-element.53), channel_id=1, source_target_pairs={{0,1},{1,0},{2,3},{3,2},{4,5},{5,4},{6,7},{7,6},{8,9},{9,8},{10,11... | collective-permute-start | bytes 491528 | tf_op jit(solution)/shard_map/ppermute | solution.py:488
  75.7 34.8 %collective-permute-start.8 = (bf16[128,16,128]{2,1,0:T(8,128)(2,1)}, bf16[128,16,128]{2,1,0:T(8,128)(2,1)S(1)}, u32[]{:S(2)}, u32[]{:S(2)}) collective-permute-start(bf16[128,16,128]{2,1,0:T(8,128)(2,1)} %get-tuple-element.51), channel_id=1, source_target_pairs={{64,0},{65,1},{66,2},{67,3},{68,4},{69,5},{70,6},{71,7},{72,8},{73... | collective-permute-start | bytes 1572872 | tf_op jit(solution)/shard_map/ppermute | solution.py:493
  79.4 4.3 %collective-permute-start.12 = (bf16[80,256]{1,0:T(8,128)(2,1)S(1)}, bf16[80,256]{1,0:T(8,128)(2,1)S(1)}, u32[]{:S(2)}, u32[]{:S(2)}) collective-permute-start(bf16[80,256]{1,0:T(8,128)(2,1)S(1)} %get-tuple-element.77), channel_id=1, source_target_pairs={{0,6},{1,7},{2,0},{3,1},{4,2},{5,3},{6,4},{7,5},{8,14},{9,15},{10,... | collective-permute-start | bytes 122888 | tf_op jit(solution)/shard_map/ppermute | solution.py:490
  79.4 5.5 %collective-permute-start.11 = (bf16[80,256]{1,0:T(8,128)(2,1)S(1)}, bf16[80,256]{1,0:T(8,128)(2,1)S(1)}, u32[]{:S(2)}, u32[]{:S(2)}) collective-permute-start(bf16[80,256]{1,0:T(8,128)(2,1)S(1)} %get-tuple-element.78), channel_id=1, source_target_pairs={{0,4},{1,5},{2,6},{3,7},{4,0},{5,1},{6,2},{7,3},{8,12},{9,13},{10,... | collective-permute-start | bytes 122888 | tf_op jit(solution)/shard_map/ppermute | solution.py:490
  81.5 4.4 %collective-permute-start.10 = (bf16[80,256]{1,0:T(8,128)(2,1)S(1)}, bf16[80,256]{1,0:T(8,128)(2,1)S(1)}, u32[]{:S(2)}, u32[]{:S(2)}) collective-permute-start(bf16[80,256]{1,0:T(8,128)(2,1)S(1)} %get-tuple-element.79), channel_id=1, source_target_pairs={{0,2},{1,3},{2,4},{3,5},{4,6},{5,7},{6,0},{7,1},{8,10},{9,11},{10,... | collective-permute-start | bytes 122888 | tf_op jit(solution)/shard_map/ppermute | solution.py:490
  88.1 9.8 %collective-permute-start.15 = (bf16[80,256]{1,0:T(8,128)(2,1)}, bf16[80,256]{1,0:T(8,128)(2,1)S(1)}, u32[]{:S(2)}, u32[]{:S(2)}) collective-permute-start(bf16[80,256]{1,0:T(8,128)(2,1)} %close_images.1), channel_id=1, source_target_pairs={{0,24},{8,0},{16,8},{24,16},{32,56},{40,32},{48,40},{56,48},{1,25}... | collective-permute-start | bytes 122888 | tf_op jit(solution)/shard_map/ppermute | solution.py:501
  91.2 7.1 %collective-permute-start.14 = (bf16[80,256]{1,0:T(8,128)(2,1)}, bf16[80,256]{1,0:T(8,128)(2,1)S(1)}, u32[]{:S(2)}, u32[]{:S(2)}) collective-permute-start(bf16[80,256]{1,0:T(8,128)(2,1)} %close_images.1), channel_id=1, source_target_pairs={{0,16},{8,24},{16,0},{24,8},{32,48},{40,56},{48,32},{56,40},{1,17}... | collective-permute-start | bytes 122888 | tf_op jit(solution)/shard_map/ppermute | solution.py:501
  92.0 6.3 %collective-permute-start.13 = (bf16[80,256]{1,0:T(8,128)(2,1)}, bf16[80,256]{1,0:T(8,128)(2,1)S(1)}, u32[]{:S(2)}, u32[]{:S(2)}) collective-permute-start(bf16[80,256]{1,0:T(8,128)(2,1)} %close_images.1), channel_id=1, source_target_pairs={{0,8},{8,16},{16,24},{24,0},{32,40},{40,48},{48,56},{56,32},{1,9},... | collective-permute-start | bytes 122888 | tf_op jit(solution)/shard_map/ppermute | solution.py:501
  92.9 16.0 %collective-permute-start.19 = (bf16[64,1024]{1,0:T(8,128)(2,1)}, bf16[64,1024]{1,0:T(8,128)(2,1)S(1)}, u32[]{:S(2)}, u32[]{:S(2)}) collective-permute-start(bf16[64,1024]{1,0:T(8,128)(2,1)} %get-tuple-element.58), channel_id=1, source_target_pairs={{64,0},{65,1},{66,2},{67,3},{68,4},{69,5},{70,6},{71,7},{72,8},{73... | collective-permute-start | bytes 393224 | tf_op jit(solution)/shard_map/ppermute | solution.py:511
  99.1 16.4 %copy-start.2 = (bf16[4,80,256]{2,1,0:T(8,128)(2,1)}, bf16[4,80,256]{2,1,0:T(8,128)(2,1)S(1)}, u32[]{:S(2)}) copy-start(bf16[4,80,256]{2,1,0:T(8,128)(2,1)S(1)} %pad_maximum_fusion.1.near_ref) | copy-start | bytes 491524
  99.1 11.4 %collective-permute-start.18 = (bf16[4,80,256]{2,1,0:T(8,128)(2,1)S(1)}, bf16[4,80,256]{2,1,0:T(8,128)(2,1)S(1)}, u32[]{:S(2)}, u32[]{:S(2)}) collective-permute-start(bf16[4,80,256]{2,1,0:T(8,128)(2,1)S(1)} %pad_maximum_fusion.1.near_ref), channel_id=1, source_target_pairs={{0,96},{8,104},{16,112},{24,120},{32,64},{40,72},{48,80},{56,88},{... | collective-permute-start | bytes 491528 | tf_op jit(solution)/shard_map/ppermute | solution.py:507
  100.4 15.1 %collective-permute-start.17 = (bf16[4,80,256]{2,1,0:T(8,128)(2,1)S(1)}, bf16[4,80,256]{2,1,0:T(8,128)(2,1)S(1)}, u32[]{:S(2)}, u32[]{:S(2)}) collective-permute-start(bf16[4,80,256]{2,1,0:T(8,128)(2,1)S(1)} %pad_maximum_fusion.1.near_ref), channel_id=1, source_target_pairs={{64,96},{72,104},{80,112},{88,120},{96,64},{104,72},{112,80},{120,... | collective-permute-start | bytes 491528 | tf_op jit(solution)/shard_map/ppermute | solution.py:505
  105.5 10.0 %collective-permute-start.16 = (bf16[4,80,256]{2,1,0:T(8,128)(2,1)S(1)}, bf16[4,80,256]{2,1,0:T(8,128)(2,1)S(1)}, u32[]{:S(2)}, u32[]{:S(2)}) collective-permute-start(bf16[4,80,256]{2,1,0:T(8,128)(2,1)S(1)} %pad_maximum_fusion.1.near_ref), channel_id=1, source_target_pairs={{0,64},{64,0},{1,65},{65,1},{2,66},{66,2},{3,67},{67,3},{4,68},{68... | collective-permute-start | bytes 491528 | tf_op jit(solution)/shard_map/ppermute | solution.py:506
  (8 other events, 16.2 us)
